TPU v7x, 32 devices: a whole 2x2x4 slice. The times are simulated.
32 devices in a mesh: dp: 8 (over z, x), expert: 4 (over y, core).
Axes of the slice: x: 2, y: 2, z: 4, core: 2. Of those that a mesh axis runs over, the one named last changes fastest.
Arguments:
- tokens: bfloat16 [32, 1024, 768], P(('dp', 'expert')), may hold values from -6 to 6
- resid_logits: bfloat16 [32, 1024, 12], P(('dp', 'expert')), may hold values from -3 to 3
- routes: int32 [32, 1024, 2], P(('dp', 'expert')), may hold values from 0 to 11, all different within a row; in each aligned block of 1024 rows (0 to 1023, 1024 to 2047, ..., all dimensions but the last counted through in order) at most 256 rows name the same one
- doc_ids: int32 [32, 1024], P(('dp', 'expert')), may hold values from 0 to 3, never falling along the last dimension, each value on 1 to 512 neighbouring positions
- w_qkv: bfloat16 [768, 2304], P('dp'), may hold values from -0.21875 to 0.21875
- w_out: bfloat16 [768, 768], P('dp'), may hold values from -1.75 to 1.75
- gain_attn: bfloat16 [768], P('dp'), may hold values from 0.25 to 1.75
- gain_ffn: bfloat16 [768], P('dp'), may hold values from 0.25 to 1.75
- w_router: bfloat16 [768, 12], P('dp'), may hold values from -0.15625 to 0.15625
- w_const: bfloat16 [768, 4], P('dp'), may hold values from -0.21875 to 0.21875
- v_const: bfloat16 [768, 2], P('dp'), may hold values from -5 to 5
- w_gate_up: bfloat16 [8, 768, 4096], P('expert', 'dp'), may hold values from -0.21875 to 0.21875
- w_down: bfloat16 [8, 2048, 768], P('expert', 'dp'), may hold values from -0.1875 to 0.1875
- out_grad: bfloat16 [32, 1024, 768], P(('dp', 'expert')), may hold values from -6 to 6
Outputs:
- output: bfloat16 [32, 1024, 768], P(('dp', 'expert'))
- token_grad: bfloat16 [32, 1024, 768], P(('dp', 'expert'))
- logit_grad: bfloat16 [32, 1024, 12], P(('dp', 'expert'))
- grad_w_qkv: float32 [768, 2304], P('dp')
- grad_w_out: float32 [768, 768], P('dp')
- grad_gain_attn: float32 [768], P('dp')
- grad_gain_ffn: float32 [768], P('dp')
- grad_w_router: float32 [768, 12], P('dp')
- grad_w_const: float32 [768, 4], P('dp')
- grad_v_const: float32 [768, 2], P('dp')
- grad_w_gate_up: float32 [8, 768, 4096], P('expert', 'dp')
- grad_w_down: float32 [8, 2048, 768], P('expert', 'dp')
Inputs may be any that keep to these rules, and one draw needn't show every extreme that they name: A token's two routes differ. Numbers below 8 are feed-forward experts, 8 the zero expert, 9 the copy expert, 10 + k constant expert k. Among the tokens of one device no number is named more than 256 times. `doc_ids`: Non-decreasing along each sequence; a document covers 1 to 512 positions.
All inputs are finite; a program needn't handle non-finite values.
Results may differ from a plain program's by a relative error of at most 0.02.
Values may be sent and summed in bfloat16 or wider, within the bound.
A program may use at most 320 MiB of HBM per device.

v0:
```python
import jax
import jax.numpy as jnp
from jax import lax
from jax.sharding import PartitionSpec as P

HEADS = 12
BLOCK = 256
CAP = 256


epsilon = 1e-06
highest = lax.Precision.HIGHEST


def normalize(values, gain_vec):
    row_scale = lax.rsqrt(jnp.mean(values * values, -1, keepdims=True) + epsilon)
    return (values * row_scale * gain_vec, row_scale)


def normalize_back(values, row_scale, gain_vec, grad_out):
    weighted = grad_out * gain_vec
    grad_gain = jnp.sum(grad_out * values * row_scale, 0)
    grad_in = row_scale * weighted - values * row_scale**3 * jnp.mean(
        weighted * values, -1, keepdims=True
    )
    return (grad_in, grad_gain)


def rotary_tables(row_count, length, head_dim):
    half_dim = head_dim // 2
    frequency = 10000.0 ** (-jnp.arange(half_dim, dtype=jnp.float32) / half_dim)
    positions = (jnp.arange(row_count) % length).astype(jnp.float32)
    angles = positions[:, None] * frequency[None, :]
    return (jnp.cos(angles)[:, None, :], jnp.sin(angles)[:, None, :])


def rotate(values, cosine_table, sine_table):
    half_dim = values.shape[-1] // 2
    first_half = values[..., :half_dim]
    second_half = values[..., half_dim:]
    return jnp.concatenate(
        [
            first_half * cosine_table - second_half * sine_table,
            second_half * cosine_table + first_half * sine_table,
        ],
        -1,
    )


def rotate_back(grad_vals, cosine_table, sine_table):
    half_dim = grad_vals.shape[-1] // 2
    first_half = grad_vals[..., :half_dim]
    second_half = grad_vals[..., half_dim:]
    return jnp.concatenate(
        [
            first_half * cosine_table + second_half * sine_table,
            second_half * cosine_table - first_half * sine_table,
        ],
        -1,
    )


def softmax_last(values):
    row_peak = jnp.max(values, -1, keepdims=True)
    shifted = jnp.exp(values - row_peak)
    return shifted / jnp.sum(shifted, -1, keepdims=True)


def block_scores(query_rows, keys_all, docs_rows, docs_all, first_row, score_scale):
    row_pos = first_row + jnp.arange(query_rows.shape[0])
    key_pos = jnp.arange(keys_all.shape[0])
    allowed = (docs_rows[:, None] == docs_all[None, :]) & (
        row_pos[:, None] // BLOCK >= key_pos[None, :] // BLOCK
    )
    scores = (
        jnp.einsum("qhd,khd->hqk", query_rows, keys_all, preferred_element_type=jnp.float32)
        * score_scale
    )
    return jnp.where(allowed[None], scores, -1e30)


def attend_forward(query_seq, key_seq, value_seq, docs_seq, score_scale):
    length = query_seq.shape[0]
    step_rows = min(512, length)
    outs_list = []
    lse_list = []
    for first_row in range(0, length, step_rows):
        last_row = first_row + step_rows
        scores = block_scores(
            query_seq[first_row:last_row],
            key_seq,
            docs_seq[first_row:last_row],
            docs_seq,
            first_row,
            score_scale,
        )
        row_peak = jnp.max(scores, -1, keepdims=True)
        shifted = jnp.exp(scores - row_peak)
        row_total = jnp.sum(shifted, -1, keepdims=True)
        prob_low = (shifted / row_total).astype(jnp.bfloat16)
        outs_list.append(
            jnp.einsum("hqk,khd->qhd", prob_low, value_seq, preferred_element_type=jnp.float32)
        )
        lse_list.append(row_peak + jnp.log(row_total))
    return (jnp.concatenate(outs_list, 0), jnp.concatenate(lse_list, 1))


def attend_backward(query_seq, key_seq, value_seq, docs_seq, lse_seq, grad_seq, score_scale):
    length = query_seq.shape[0]
    step_rows = min(512, length)
    grad_key = jnp.zeros(key_seq.shape, jnp.float32)
    grad_value = jnp.zeros(value_seq.shape, jnp.float32)
    query_grads = []
    for first_row in range(0, length, step_rows):
        last_row = first_row + step_rows
        rows_query = query_seq[first_row:last_row]
        rows_grad = grad_seq[first_row:last_row]
        scores = block_scores(
            rows_query, key_seq, docs_seq[first_row:last_row], docs_seq, first_row, score_scale
        )
        probs_full = jnp.exp(scores - lse_seq[:, first_row:last_row])
        prob_low = probs_full.astype(jnp.bfloat16)
        grad_probs = jnp.einsum(
            "qhd,khd->hqk", rows_grad, value_seq, preferred_element_type=jnp.float32
        )
        grad_value = grad_value + jnp.einsum(
            "hqk,qhd->khd", prob_low, rows_grad, preferred_element_type=jnp.float32
        )
        inner_sum = jnp.sum(probs_full * grad_probs, -1, keepdims=True)
        grad_scores = (probs_full * (grad_probs - inner_sum)).astype(jnp.bfloat16)
        query_grads.append(
            jnp.einsum("hqk,khd->qhd", grad_scores, key_seq, preferred_element_type=jnp.float32)
            * score_scale
        )
        grad_key = (
            grad_key
            + jnp.einsum(
                "hqk,qhd->khd", grad_scores, rows_query, preferred_element_type=jnp.float32
            )
            * score_scale
        )
    return (jnp.concatenate(query_grads, 0), grad_key, grad_value)


def shards(
    tokens,
    resid_logits,
    routes,
    doc_ids,
    w_qkv,
    w_out,
    gain_attn,
    gain_ffn,
    w_router,
    w_const,
    v_const,
    w_gate_up,
    w_down,
    out_grad,
):
    seq_count, length, model_width = tokens.shape
    row_count = seq_count * length
    pair_count = 2 * row_count
    head_dim = model_width // HEADS
    score_scale = head_dim ** (-0.5)
    choice_count = resid_logits.shape[-1]
    qkv_full, out_full, gain_one, gain_two, router_full, const_full, vector_full = (
        lax.all_gather(w_qkv, "dp", axis=0, tiled=True),
        lax.all_gather(w_out, "dp", axis=0, tiled=True),
        lax.all_gather(gain_attn, "dp", axis=0, tiled=True),
        lax.all_gather(gain_ffn, "dp", axis=0, tiled=True),
        lax.all_gather(w_router, "dp", axis=0, tiled=True),
        lax.all_gather(w_const, "dp", axis=0, tiled=True),
        lax.all_gather(v_const, "dp", axis=0, tiled=True),
    )
    gate_up_full, down_full = (
        lax.all_gather(w_gate_up, "dp", axis=1, tiled=True),
        lax.all_gather(w_down, "dp", axis=1, tiled=True),
    )
    local_count = gate_up_full.shape[0]
    owner_count = lax.axis_size("expert")
    expert_count = owner_count * local_count
    hidden_count = down_full.shape[1]
    const_count = vector_full.shape[1]
    gain_first = gain_one.astype(jnp.float32)
    gain_second = gain_two.astype(jnp.float32)
    inputs = tokens.reshape(row_count, model_width).astype(jnp.float32)
    normed_float, scale_one = normalize(inputs, gain_first)
    normed_one = normed_float.astype(jnp.bfloat16)
    projected = jnp.dot(normed_one, qkv_full, preferred_element_type=jnp.float32)
    cosine_table, sine_table = rotary_tables(row_count, length, head_dim)
    head_shape = (row_count, HEADS, head_dim)
    queries = rotate(
        projected[:, :model_width].reshape(head_shape), cosine_table, sine_table
    ).astype(jnp.bfloat16)
    keys_all = rotate(
        projected[:, model_width : 2 * model_width].reshape(head_shape), cosine_table, sine_table
    ).astype(jnp.bfloat16)
    values_all = projected[:, 2 * model_width :].reshape(head_shape).astype(jnp.bfloat16)
    shape_seq = (seq_count, length, HEADS, head_dim)
    attended, log_sums = lax.map(
        lambda seq_items: attend_forward(
            seq_items[0], seq_items[1], seq_items[2], seq_items[3], score_scale
        ),
        (
            queries.reshape(shape_seq),
            keys_all.reshape(shape_seq),
            values_all.reshape(shape_seq),
            doc_ids,
        ),
    )
    attended = attended.reshape(row_count, model_width).astype(jnp.bfloat16)
    branch = jnp.dot(attended, out_full, preferred_element_type=jnp.float32)
    middle = inputs + branch
    normed_two, scale_two = normalize(middle, gain_second)
    normed_low = normed_two.astype(jnp.bfloat16)
    normed_back = normed_low.astype(jnp.float32)
    logits = jnp.dot(
        normed_low, router_full, preferred_element_type=jnp.float32
    ) + resid_logits.reshape(row_count, choice_count).astype(jnp.float32)
    route_rows = routes.reshape(row_count, 2)
    picked = route_rows[:, :, None] == jnp.arange(choice_count)[None, None, :]
    route_logits = jnp.sum(jnp.where(picked, logits[:, None, :], 0.0), -1)
    gate_weights = softmax_last(route_logits)
    flat_routes = route_rows.reshape(pair_count)
    one_hot = picked.reshape(pair_count, choice_count).astype(jnp.int32)
    slot_rank = jnp.sum((jnp.cumsum(one_hot, 0) - one_hot) * one_hot, 1)
    destination = jnp.where(
        flat_routes < expert_count, flat_routes * CAP + slot_rank, expert_count * CAP
    )
    slot_pair = (
        jnp.full((expert_count * CAP + 1,), pair_count, jnp.int32)
        .at[destination]
        .set(jnp.arange(pair_count, dtype=jnp.int32))[: expert_count * CAP]
    )
    zero_row = jnp.zeros((1, model_width), jnp.bfloat16)
    padded_in = jnp.concatenate([normed_low, zero_row], 0)
    send_rows = padded_in[slot_pair // 2].reshape(owner_count, local_count * CAP, model_width)
    arrived = lax.all_to_all(send_rows, "expert", split_axis=0, concat_axis=0, tiled=True).reshape(
        owner_count, local_count, CAP, model_width
    )
    gate_up = jnp.einsum(
        "secd,edf->secf", arrived, gate_up_full, preferred_element_type=jnp.float32
    )
    gate_part = gate_up[..., :hidden_count]
    up_part = gate_up[..., hidden_count:]
    squashed = lax.logistic(gate_part)
    silu_gate = gate_part * squashed
    activated = (silu_gate * up_part).astype(jnp.bfloat16)
    expert_out = jnp.einsum(
        "secf,efd->secd", activated, down_full, preferred_element_type=jnp.float32
    ).astype(jnp.bfloat16)
    returned = lax.all_to_all(
        expert_out.reshape(owner_count, local_count * CAP, model_width),
        "expert",
        split_axis=0,
        concat_axis=0,
        tiled=True,
    ).reshape(expert_count * CAP, model_width)
    padded_out = jnp.concatenate([returned, zero_row], 0)
    pair_out = padded_out[destination].reshape(row_count, 2, model_width).astype(jnp.float32)
    mixing = softmax_last(
        jnp.dot(normed_low, const_full, preferred_element_type=jnp.float32).reshape(
            row_count, const_count, 2
        )
    )
    vectors = vector_full.astype(jnp.float32).T
    const_val = mixing[..., 0:1] * normed_back[:, None, :] + mixing[..., 1:2] * vectors[None, :, :]
    copy_hit = (route_rows == expert_count + 1).astype(jnp.float32)
    const_hit = (
        route_rows[:, :, None] == expert_count + 2 + jnp.arange(const_count)[None, None, :]
    ).astype(jnp.float32)
    copy_weight = jnp.sum(gate_weights * copy_hit, -1)
    const_weight = jnp.sum(gate_weights[:, :, None] * const_hit, 1)
    expert_mix = (
        jnp.sum(gate_weights[:, :, None] * pair_out, 1)
        + copy_weight[:, None] * normed_back
        + jnp.sum(const_weight[:, :, None] * const_val, 1)
    )
    output = (middle + expert_mix).astype(jnp.bfloat16).reshape(tokens.shape)
    grad_final = out_grad.reshape(row_count, model_width).astype(jnp.float32)
    dot_copy = jnp.sum(grad_final * normed_back, -1)
    dot_const = jnp.sum(grad_final[:, None, :] * const_val, -1)
    grad_gates = (
        jnp.sum(pair_out * grad_final[:, None, :], -1)
        + copy_hit * dot_copy[:, None]
        + jnp.sum(const_hit * dot_const[:, None, :], -1)
    )
    grad_route = gate_weights * (grad_gates - jnp.sum(gate_weights * grad_gates, -1, keepdims=True))
    grad_logits = jnp.sum(jnp.where(picked, grad_route[:, :, None], 0.0), 1)
    logit_grad = grad_logits.astype(jnp.bfloat16).reshape(resid_logits.shape)
    grad_router = jnp.dot(normed_back.T, grad_logits, precision=highest)
    grad_normed = jnp.dot(grad_logits, router_full.astype(jnp.float32).T, precision=highest)
    grad_normed = grad_normed + copy_weight[:, None] * grad_final
    grad_const_val = const_weight[:, :, None] * grad_final[:, None, :]
    grad_mix_first = jnp.sum(grad_const_val * normed_back[:, None, :], -1)
    grad_mix_second = jnp.sum(grad_const_val * vectors[None, :, :], -1)
    mix_term = mixing[..., 0] * mixing[..., 1] * (grad_mix_first - grad_mix_second)
    grad_mix_logits = jnp.stack([mix_term, -mix_term], -1).reshape(row_count, 2 * const_count)
    grad_const = jnp.dot(normed_back.T, grad_mix_logits, precision=highest)
    grad_normed = (
        grad_normed
        + jnp.dot(grad_mix_logits, const_full.astype(jnp.float32).T, precision=highest)
        + jnp.sum(grad_const_val * mixing[..., 0:1], 1)
    )
    grad_vector = jnp.dot(grad_final.T, const_weight * mixing[..., 1], precision=highest)
    pair_grads = (
        (gate_weights[:, :, None] * grad_final[:, None, :])
        .reshape(pair_count, model_width)
        .astype(jnp.bfloat16)
    )
    padded_grad = jnp.concatenate([pair_grads, zero_row], 0)
    send_grads = padded_grad[slot_pair].reshape(owner_count, local_count * CAP, model_width)
    arrived_grad = lax.all_to_all(
        send_grads, "expert", split_axis=0, concat_axis=0, tiled=True
    ).reshape(owner_count, local_count, CAP, model_width)
    gate_up_back, down_back = (
        lax.all_gather(w_gate_up, "dp", axis=1, tiled=True),
        lax.all_gather(w_down, "dp", axis=1, tiled=True),
    )
    grad_down = jnp.einsum(
        "secf,secd->efd", activated, arrived_grad, preferred_element_type=jnp.float32
    )
    grad_act = jnp.einsum(
        "secd,efd->secf", arrived_grad, down_back, preferred_element_type=jnp.float32
    )
    grad_gate = grad_act * up_part * squashed * (1.0 + gate_part * (1.0 - squashed))
    grad_up = grad_act * silu_gate
    grad_gate_up = jnp.concatenate([grad_gate, grad_up], -1).astype(jnp.bfloat16)
    grad_expert_gu = jnp.einsum(
        "secd,secf->edf", arrived, grad_gate_up, preferred_element_type=jnp.float32
    )
    grad_rows = jnp.einsum(
        "secf,edf->secd", grad_gate_up, gate_up_back, preferred_element_type=jnp.float32
    ).astype(jnp.bfloat16)
    back_rows = lax.all_to_all(
        grad_rows.reshape(owner_count, local_count * CAP, model_width),
        "expert",
        split_axis=0,
        concat_axis=0,
        tiled=True,
    ).reshape(expert_count * CAP, model_width)
    padded_back = jnp.concatenate([back_rows, zero_row], 0)
    grad_normed = grad_normed + jnp.sum(
        padded_back[destination].reshape(row_count, 2, model_width).astype(jnp.float32), 1
    )
    grad_expert_gu, grad_expert_down = (
        lax.psum_scatter(
            grad_expert_gu.astype(jnp.bfloat16), "dp", scatter_dimension=1, tiled=True
        ).astype(jnp.float32),
        lax.psum_scatter(
            grad_down.astype(jnp.bfloat16), "dp", scatter_dimension=1, tiled=True
        ).astype(jnp.float32),
    )
    grad_middle, grad_gain_two = normalize_back(middle, scale_two, gain_second, grad_normed)
    grad_middle = grad_middle + grad_final
    grad_branch = grad_middle.astype(jnp.bfloat16)
    grad_out_w = lax.dot_general(
        attended, grad_branch, (((0,), (0,)), ((), ())), preferred_element_type=jnp.float32
    )
    grad_attended = lax.dot_general(
        grad_branch, out_full, (((1,), (1,)), ((), ())), preferred_element_type=jnp.float32
    ).astype(jnp.bfloat16)
    grad_query, grad_key, grad_value = lax.map(
        lambda seq_items: attend_backward(
            seq_items[0],
            seq_items[1],
            seq_items[2],
            seq_items[3],
            seq_items[4],
            seq_items[5],
            score_scale,
        ),
        (
            queries.reshape(shape_seq),
            keys_all.reshape(shape_seq),
            values_all.reshape(shape_seq),
            doc_ids,
            log_sums,
            grad_attended.reshape(shape_seq),
        ),
    )
    grad_query = rotate_back(grad_query.reshape(head_shape), cosine_table, sine_table)
    grad_key = rotate_back(grad_key.reshape(head_shape), cosine_table, sine_table)
    grad_projected = jnp.concatenate(
        [
            grad_query.reshape(row_count, model_width),
            grad_key.reshape(row_count, model_width),
            grad_value.reshape(row_count, model_width),
        ],
        -1,
    ).astype(jnp.bfloat16)
    grad_qkv = lax.dot_general(
        normed_one, grad_projected, (((0,), (0,)), ((), ())), preferred_element_type=jnp.float32
    )
    grad_normed_one = lax.dot_general(
        grad_projected, qkv_full, (((1,), (1,)), ((), ())), preferred_element_type=jnp.float32
    )
    grad_inputs, grad_gain_one = normalize_back(inputs, scale_one, gain_first, grad_normed_one)
    token_grad = (grad_inputs + grad_middle).astype(jnp.bfloat16).reshape(tokens.shape)
    sum_qkv, sum_out, sum_gain_one, sum_gain_two, sum_router, sum_const, sum_vector = (
        lax.psum(grad_qkv.astype(jnp.bfloat16), "expert").astype(jnp.float32),
        lax.psum(grad_out_w.astype(jnp.bfloat16), "expert").astype(jnp.float32),
        lax.psum(grad_gain_one.astype(jnp.bfloat16), "expert").astype(jnp.float32),
        lax.psum(grad_gain_two.astype(jnp.bfloat16), "expert").astype(jnp.float32),
        lax.psum(grad_router.astype(jnp.bfloat16), "expert").astype(jnp.float32),
        lax.psum(grad_const.astype(jnp.bfloat16), "expert").astype(jnp.float32),
        lax.psum(grad_vector.astype(jnp.bfloat16), "expert").astype(jnp.float32),
    )
    part_qkv, part_out, part_gain_one, part_gain_two, part_router, part_const, part_vector = (
        lax.psum_scatter(
            sum_qkv.astype(jnp.bfloat16), "dp", scatter_dimension=0, tiled=True
        ).astype(jnp.float32),
        lax.psum_scatter(
            sum_out.astype(jnp.bfloat16), "dp", scatter_dimension=0, tiled=True
        ).astype(jnp.float32),
        lax.psum_scatter(
            sum_gain_one.astype(jnp.bfloat16), "dp", scatter_dimension=0, tiled=True
        ).astype(jnp.float32),
        lax.psum_scatter(
            sum_gain_two.astype(jnp.bfloat16), "dp", scatter_dimension=0, tiled=True
        ).astype(jnp.float32),
        lax.psum_scatter(
            sum_router.astype(jnp.bfloat16), "dp", scatter_dimension=0, tiled=True
        ).astype(jnp.float32),
        lax.psum_scatter(
            sum_const.astype(jnp.bfloat16), "dp", scatter_dimension=0, tiled=True
        ).astype(jnp.float32),
        lax.psum_scatter(
            sum_vector.astype(jnp.bfloat16), "dp", scatter_dimension=0, tiled=True
        ).astype(jnp.float32),
    )
    return (
        output,
        token_grad,
        logit_grad,
        part_qkv,
        part_out,
        part_gain_one,
        part_gain_two,
        part_router,
        part_const,
        part_vector,
        grad_expert_gu,
        grad_expert_down,
    )


def solution(mesh):
    placed = (
        P(("dp", "expert"), None, None),
        P(("dp", "expert"), None, None),
        P(("dp", "expert"), None, None),
        P(("dp", "expert"), None),
        P("dp", None),
        P("dp", None),
        P("dp"),
        P("dp"),
        P("dp", None),
        P("dp", None),
        P("dp", None),
        P("expert", "dp", None),
        P("expert", "dp", None),
        P(("dp", "expert"), None, None),
    )
    return jax.shard_map(
        shards,
        mesh=mesh,
        in_specs=placed,
        out_specs=(
            P(("dp", "expert"), None, None),
            P(("dp", "expert"), None, None),
            P(("dp", "expert"), None, None),
            P("dp", None),
            P("dp", None),
            P("dp"),
            P("dp"),
            P("dp", None),
            P("dp", None),
            P("dp", None),
            P("expert", "dp", None),
            P("expert", "dp", None),
        ),
        check_vma=False,
    )
```

profile of v0, /device:TPU:19, one launch (start us, length us, event | category | flops | bytes accessed | tf_op | source)
XLA Modules:
  0.0 1447.6 jit_solution(5113885428531245413)
XLA Ops:
  16.8 12.8 all-reduce.9
  31.2 24.3 %all-gather = bf16[8,96,12]{1,2,0:T(8,128)(2,1)S(1)} all-gather(bf16[1,96,12]{1,2,0:T(8,128)(2,1)S(1)} %bitcast.227), channel_id=1, replica_groups=mesh['dp'=8,'expert'=4] {'dp'}, dimensions={0}, use_global_device_ids=true | all-gather | bytes 20736 | tf_op jit(solution)/shard_map/all_gather | solution.py:172
  62.7 8.6 mul.685
  77.3 8.1 scatter_custom_fusion
  86.0 14.4 all-gather.1
  101.1 13.7 all-gather.2
  141.7 10.7 fusion.24
  152.4 10.7 fusion.25
  163.1 12.0 fusion
  175.2 12.9 fusion.60
  213.9 9.4 gather_fusion
  223.3 21.2 %all-to-all-start = ((bf16[4,512,768]{2,1,0:T(8,128)(2,1)}), bf16[4,512,768]{2,1,0:T(8,128)(2,1)}, u32[]{:S(2)}, u32[]{:S(2)}) async-start(bf16[4,512,768]{2,1,0:T(8,128)(2,1)} %bitcast.199), calls=%async_computation | async-start | bytes 6291456 | tf_op jit(solution)/shard_map/all_to_all | solution.py:239
  255.4 9.4 gather_fusion.2
  266.0 14.7 %all-to-all-done = bf16[4,512,768]{2,1,0:T(8,128)(2,1)} async-done(((bf16[4,512,768]{2,1,0:T(8,128)(2,1)}), bf16[4,512,768]{2,1,0:T(8,128)(2,1)}, u32[]{:S(2)}, u32[]{:S(2)}) %all-to-all-start) | async-done | bytes 3145760 | tf_op jit(solution)/shard_map/all_to_all | solution.py:239
  285.7 8.6 all-gather.12.cloned.1.call-done
  294.3 24.3 %convolution_bitcast_fusion = f32[4,2,256,4096]{3,2,0,1:T(8,128)} fusion(bf16[2,768,4096]{2,1,0:T(8,128)(2,1)} %all-gather.12.cloned.1.call-done, bf16[4,2,256,768]{3,2,1,0:T(8,128)(2,1)} %bitcast.19), kind=kOutput, calls=%fused_computation.34 | convolution fusion | flops 12884901888 | bytes 49283072 | tf_op jit(solution)/shard_map/secd,edf->secf/dot_general | solution.py:242
  321.7 72.1 %all-gather.14.cloned.1.call-done = bf16[2,2048,768]{2,1,0:T(8,128)(2,1)} async-done(((bf16[2,256,768]{2,1,0:T(8,128)(2,1)}), bf16[2,2048,768]{2,1,0:T(8,128)(2,1)}) %all-gather.14.cloned.1.call-update) | async-done | bytes 6291472 | tf_op jit(solution)/shard_map/all_gather | solution.py:178
  393.8 24.4 %fusion.6 = (bf16[4,2,256,2048]{3,2,0,1:T(8,128)(2,1)}, bf16[4,2,256,2048]{3,2,0,1:T(8,128)(2,1)}, bf16[4,2,256,2048]{3,2,0,1:T(8,128)(2,1)}) fusion(f32[4,2,256,4096]{3,2,0,1:T(8,128)} %convolution_bitcast_fusion, bf16[2,2048,768]{2,1,0:T(8,128)(2,1)} %all-gather.14.cloned.1.call-done, bf16[4,2,256,768]{3,2,1,0:T(8,128)(2,1)S(1)} %bitcast.201), kind=kOutput, calls=%fused_computation.27 | convolution fusion | flops 6505365504 | bytes 68157440 | tf_op jit(solution)/shard_map/secd,efd->secf/dot_general | solution.py:324
  418.2 10.9 convert_bitcast_fusion.1
  436.0 20.6 %convert_bitcast_fusion = bf16[4,2,256,768]{3,2,0,1:T(8,128)(2,1)} fusion(bf16[2,768,4096]{2,1,0:T(8,128)(2,1)} %all-gather.12.cloned.1.call-done, bf16[4,2,256,2048]{3,2,0,1:T(8,128)(2,1)} %get-tuple-element.95, bf16[4,2,256,2048]{3,2,0,1:T(8,128)(2,1)} %get-tuple-element.94), kind=kOutput, calls=%fused_computation.90 | convolution fusion | flops 12920029184 | bytes 32505856 | tf_op jit(solution)/shard_map/secf,edf->secd/dot_general | solution.py:333
  460.3 11.7 all-to-all-done.1
  481.5 9.4 gather_fusion.1
  499.0 47.9 %fusion.26 = (f32[1024,2]{1,0:T(8,128)}, f32[1024,2]{1,0:T(8,128)}, f32[1024,768]{1,0:T(8,128)}, f32[1024,768]{1,0:T(8,128)}, f32[1024,2]{1,0:T(8,128)}, /*index=5*/f32[1024,768]{1,0:T(8,128)}, f32[1024,2]{1,0:T(8,128)}) fusion(f32[1024,768]{1,0:T(8,128)S(1)} %copy-done.8, f32[1024,768]{1,0:T(8,128)} %convert_element_type.269, f32[1024,2]{1,0:T(8,128)} %copy.209, ...), kind=kLoop, calls=%fused_computation.56 | loop fusion | flops 25944064 | bytes 22091776 | tf_op jit(solution)/shard_map/reduce_sum | solution.py:296
  558.1 9.4 gather_fusion.3
  567.5 8.0 reshape.733
  575.6 12.1 reduce_sum.282
  601.1 18.6 %multiply_reduce_fusion.1 = (f32[12,512]{1,0:T(8,128)S(1)}, f32[12,512,1024]{2,1,0:T(8,128)}) fusion(f32[12,512]{1,0:T(8,128)S(1)} %copy-done.52, f32[12,512,1024]{2,1,0:T(8,128)} %get-tuple-element.134, pred[512,1024]{1,0:T(8,128)(4,1)} %copy-done.29, bf16[512,12,64]{0,2,1:T(8,128)(2,1)} %bitcast.203, bf16[1024,12,64]{0,2,1:T(8,128)(2,1)} %bitcast.193), kind=kOutput, calls=%fused_computation.10 | convolution fusion | flops 836757504 | bytes 53264384 | tf_op jit(solution)/shard_map/while/body/eval_jaxpr/qhd,khd->hqk/dot_general | solution.py:123
  619.7 18.2 %multiply_reduce_fusion = (f32[12,512]{1,0:T(8,128)S(1)}, f32[12,512,1024]{2,1,0:T(8,128)}) fusion(f32[12,512]{1,0:T(8,128)S(1)} %copy-done.53, f32[12,512,1024]{2,1,0:T(8,128)} %get-tuple-element.132, pred[512,1024]{1,0:T(8,128)(4,1)} %copy-done.11, bf16[512,12,64]{0,2,1:T(8,128)(2,1)} %bitcast.205, bf16[1024,12,64]{0,2,1:T(8,128)(2,1)} %bitcast.194), kind=kOutput, calls=%fused_computation.7 | convolution fusion | flops 836757504 | bytes 53264384 | tf_op jit(solution)/shard_map/while/body/eval_jaxpr/qhd,khd->hqk/dot_general | solution.py:123
  637.8 42.7 %multiply_convert_fusion = (bf16[12,512,1024]{2,1,0:T(8,128)(2,1)}, bf16[12,512,1024]{2,1,0:T(8,128)(2,1)}) fusion(f32[12,512,1024]{2,1,0:T(8,128)} %get-tuple-element.139, f32[12,512]{1,0:T(8,128)S(1)} %get-tuple-element.138, f32[12,512]{1,0:T(8,128)S(1)} %copy-done.53, f32[12,512,1024]{2,1,0:T(8,128)} %get-tuple-element.132, ...), kind=kLoop, calls=%fused_computation.6 | loop fusion | flops 75497472 | bytes 126976000 | tf_op jit(solution)/shard_map/while/body/eval_jaxpr/convert_element_type | solution.py:130
  680.6 8.7 fusion.118
  689.3 9.7 multiply_bitcast_fusion.2
  699.1 13.2 fusion.11
  714.7 10.3 multiply_bitcast_fusion.1
  725.0 8.8 multiply_bitcast_fusion
  740.1 13.4 add_convert_fusion
  754.7 8.8 convolution_convert_fusion
  769.1 25.9 %reduce-scatter.20.cloned.1.call-done = bf16[96,768]{1,0:T(8,128)(2,1)} async-done(((bf16[768,768]{1,0:T(8,128)(2,1)}), bf16[96,768]{1,0:T(8,128)(2,1)}) %reduce-scatter.20.cloned.1.call-update) | async-done | bytes 147472 | tf_op jit(solution)/shard_map/reduce_scatter | solution.py:414
  795.0 84.2 %reduce-scatter.18.cloned.1.call-done = bf16[96,2304]{1,0:T(8,128)(2,1)} async-done(((bf16[768,2304]{1,0:T(8,128)(2,1)}), bf16[96,2304]{1,0:T(8,128)(2,1)}) %reduce-scatter.18.cloned.1.call-update) | async-done | bytes 442384 | tf_op jit(solution)/shard_map/reduce_scatter | solution.py:411
  879.3 12.2 bitcast_convert_fusion.1
  891.6 21.2 %bitcast_convert_fusion = bf16[2,768,4096]{2,1,0:T(8,128)(2,1)} fusion(bf16[4,2,256,768]{3,2,1,0:T(8,128)(2,1)} %bitcast.19, bf16[4,2,256,2048]{3,2,0,1:T(8,128)(2,1)} %get-tuple-element.95, bf16[4,2,256,2048]{3,2,0,1:T(8,128)(2,1)} %get-tuple-element.94), kind=kOutput, calls=%fused_computation.5 | convolution fusion | flops 12924747776 | bytes 32505856 | tf_op jit(solution)/shard_map/secd,secf->edf/dot_general | solution.py:330
  913.4 27.2 %reduce-scatter.26.cloned.1.call-done = bf16[96,2]{1,0:T(8,128)(2,1)} async-done(((bf16[768,2]{1,0:T(8,128)(2,1)}), bf16[96,2]{1,0:T(8,128)(2,1)}) %reduce-scatter.26.cloned.1.call-update) | async-done | bytes 400
  941.5 8.9 fusion.42
  950.3 11.2 all-reduce.8
  966.0 38.6 %reduce-scatter.24.cloned.1.call-done = bf16[96,4]{1,0:T(8,128)(2,1)} async-done(((bf16[768,4]{1,0:T(8,128)(2,1)}), bf16[96,4]{1,0:T(8,128)(2,1)}) %reduce-scatter.24.cloned.1.call-update) | async-done | bytes 784
  1005.4 63.2 %reduce-scatter.22.cloned.1.call-done = bf16[96,12]{1,0:T(8,128)(2,1)} async-done(((bf16[768,12]{1,0:T(8,128)(2,1)}), bf16[96,12]{1,0:T(8,128)(2,1)}) %reduce-scatter.22.cloned.1.call-update) | async-done | bytes 2320
  1079.8 25.6 %all-reduce.14.cloned.1.call-done = (bf16[96,2304]{1,0:T(8,128)(2,1)}, bf16[96,768]{1,0:T(8,128)(2,1)}) async-done(((bf16[96,2304]{1,0:T(8,128)(2,1)}, bf16[96,768]{1,0:T(8,128)(2,1)}), (bf16[96,2304]{1,0:T(8,128)(2,1)}, bf16[96,768]{1,0:T(8,128)(2,1)})) %all-reduce.14.cloned.1.call-update) | async-done | bytes 589840 | tf_op jit(solution)/shard_map/psum | solution.py:402
  1109.1 118.1 %reduce-scatter.16.cloned.1.call-done = bf16[2,256,768]{2,1,0:T(8,128)(2,1)} async-done(((bf16[2,2048,768]{2,1,0:T(8,128)(2,1)}), bf16[2,256,768]{2,1,0:T(8,128)(2,1)}) %reduce-scatter.16.cloned.1.call-update) | async-done | bytes 786448 | tf_op jit(solution)/shard_map/reduce_scatter | solution.py:351
  1229.6 207.5 %reduce-scatter.14.cloned.1.call-done = bf16[2,96,4096]{2,1,0:T(8,128)(2,1)} async-done(((bf16[2,768,4096]{2,1,0:T(8,128)(2,1)}), bf16[2,96,4096]{2,1,0:T(8,128)(2,1)}) %reduce-scatter.14.cloned.1.call-update) | async-done | bytes 1572880 | tf_op jit(solution)/shard_map/reduce_scatter | solution.py:348
  (373 shorter events, 192.1 us)
Async XLA Ops:
  7.2 22.4 %copy-start.31 = (bf16[1,1024,768]{2,1,0:T(8,128)(2,1)S(1)}, bf16[1,1024,768]{2,1,0:T(8,128)(2,1)}, u32[]{:S(2)}) copy-start(bf16[1,1024,768]{2,1,0:T(8,128)(2,1)} %param.14) | copy-start | bytes 4718596
  7.2 23.3 %copy-start.82 = (s32[1,1024]{1,0:T(1,128)S(1)}, s32[1,1024]{1,0:T(1,128)}, u32[]{:S(2)}) copy-start(s32[1,1024]{1,0:T(1,128)} %param.17) | copy-start | bytes 12292
  7.2 23.9 %copy-start.87 = (bf16[96,12]{0,1:T(8,128)(2,1)S(1)}, bf16[96,12]{0,1:T(8,128)(2,1)}, u32[]{:S(2)}) copy-start(bf16[96,12]{0,1:T(8,128)(2,1)} %param.22) | copy-start | bytes 6916
  7.3 49.0 %copy-start.2 = (bf16[1,1024,768]{2,1,0:T(8,128)(2,1)S(1)}, bf16[1,1024,768]{2,1,0:T(8,128)(2,1)}, u32[]{:S(2)}) copy-start(bf16[1,1024,768]{2,1,0:T(8,128)(2,1)} %param.27) | copy-start | bytes 4718596
  7.3 109.8 %all-gather.8.cloned.1.call-start = ((), (), s32[]{:S(2)}) async-start(), calls=%async_computation.11 | async-start | bytes 3981312 | tf_op jit(solution)/shard_map/all_gather | solution.py:168
  8.0 198.4 %all-gather.10.cloned.1.call-start = ((), (), s32[]{:S(2)}) async-start(), calls=%async_computation.12 | async-start | bytes 1327104 | tf_op jit(solution)/shard_map/all_gather | solution.py:169
  8.8 285.5 %all-gather.12.cloned.1.call-start = ((), (), s32[]{:S(2)}) async-start(), calls=%async_computation.13 | async-start | bytes 14155776 | tf_op jit(solution)/shard_map/all_gather | solution.py:177
  9.5 384.3 %all-gather.14.cloned.1.call-start = ((), (), s32[]{:S(2)}) async-start(), calls=%async_computation.14 | async-start | bytes 7077888 | tf_op jit(solution)/shard_map/all_gather | solution.py:178
  29.6 87.5 %copy-start.83 = (f32[768]{0:T(1024)}, f32[768]{0:T(1024)S(1)}, u32[]{:S(2)}) copy-start(f32[768]{0:T(1024)S(1)} %convert_element_type.251) | copy-start | bytes 9220
  30.6 86.5 %copy-start.79 = (f32[1024]{0:T(1024)}, f32[1024]{0:T(1024)S(1)}, u32[]{:S(2)}) copy-start(f32[1024]{0:T(1024)S(1)} %get-tuple-element.124) | copy-start | bytes 12292
  62.7 23.3 %copy-start.91 = (bf16[96,4]{0,1:T(4,128)(2,1)S(1)}, bf16[96,4]{0,1:T(4,128)(2,1)}, u32[]{:S(2)}) copy-start(bf16[96,4]{0,1:T(4,128)(2,1)} %param.23) | copy-start | bytes 2308
  62.7 38.3 %copy-start.92 = (bf16[96,2]{0,1:T(2,128)(2,1)S(1)}, bf16[96,2]{0,1:T(2,128)(2,1)}, u32[]{:S(2)}) copy-start(bf16[96,2]{0,1:T(2,128)(2,1)} %param.24) | copy-start | bytes 1156
  71.3 45.8 %copy-start.32 = (bf16[1,1024,768]{2,1,0:T(8,128)(2,1)S(1)}, bf16[1,1024,768]{2,1,0:T(8,128)(2,1)}, u32[]{:S(2)}) copy-start(bf16[1,1024,768]{2,1,0:T(8,128)(2,1)} %param.14) | copy-start | bytes 4718596
  116.0 21.2 %copy-start.43 = (f32[1024,32]{0,1:T(8,128)}, f32[1024,32]{0,1:T(8,128)S(1)}, u32[]{:S(2)}) copy-start(f32[1024,32]{0,1:T(8,128)S(1)} %get-tuple-element.121) | copy-start | bytes 393220
  116.0 21.2 %copy-start.45 = (f32[1024,32]{0,1:T(8,128)}, f32[1024,32]{0,1:T(8,128)S(1)}, u32[]{:S(2)}) copy-start(f32[1024,32]{0,1:T(8,128)S(1)} %get-tuple-element.122) | copy-start | bytes 393220
  117.1 58.1 %copy-start.29 = (pred[512,1024]{1,0:T(8,128)(4,1)}, pred[512,1024]{1,0:T(8,128)(4,1)S(1)}, u32[]{:S(2)}) copy-start(pred[512,1024]{1,0:T(8,128)(4,1)S(1)} %get-tuple-element.119) | copy-start | bytes 1572868
  117.1 81.3 %copy-start.11 = (pred[512,1024]{1,0:T(8,128)(4,1)}, pred[512,1024]{1,0:T(8,128)(4,1)S(1)}, u32[]{:S(2)}) copy-start(pred[512,1024]{1,0:T(8,128)(4,1)S(1)} %get-tuple-element.120) | copy-start | bytes 1572868
  137.1 61.2 %copy-start.10 = (bf16[1024,768]{0,1:T(8,128)(2,1)}, bf16[1024,768]{0,1:T(8,128)(2,1)S(1)}, u32[]{:S(2)}) copy-start(bf16[1024,768]{0,1:T(8,128)(2,1)S(1)} %copy.198) | copy-start | bytes 4718596
  213.2 34.4 %copy-start = (bf16[1024,768]{1,0:T(8,128)(2,1)}, bf16[1024,768]{1,0:T(8,128)(2,1)S(1)}, u32[]{:S(2)}) copy-start(bf16[1024,768]{1,0:T(8,128)(2,1)S(1)} %get-tuple-element.93) | copy-start | bytes 4718596
  223.3 21.2 %copy-start.56 = (bf16[768,12]{0,1:T(8,128)(2,1)S(1)}, bf16[768,12]{0,1:T(8,128)(2,1)}, u32[]{:S(2)}) copy-start(bf16[768,12]{0,1:T(8,128)(2,1)} %reshape.783) | copy-start | bytes 55300
  223.3 21.2 %copy-start.74 = (bf16[1,1024,12]{1,2,0:T(8,128)(2,1)S(1)}, bf16[1,1024,12]{1,2,0:T(8,128)(2,1)}, u32[]{:S(2)}) copy-start(bf16[1,1024,12]{1,2,0:T(8,128)(2,1)} %param.15) | copy-start | bytes 73732
  223.3 21.7 %copy-start.50 = (s32[1,1024,2]{1,2,0:T(2,128)S(1)}, s32[1,1024,2]{1,2,0:T(2,128)}, u32[]{:S(2)}) copy-start(s32[1,1024,2]{1,2,0:T(2,128)} %param.16) | copy-start | bytes 24580
  223.3 57.4 %all-to-all-start = ((bf16[4,512,768]{2,1,0:T(8,128)(2,1)}), bf16[4,512,768]{2,1,0:T(8,128)(2,1)}, u32[]{:S(2)}, u32[]{:S(2)}) async-start(bf16[4,512,768]{2,1,0:T(8,128)(2,1)} %bitcast.199), calls=%async_computation | async-start | bytes 6291456 | tf_op jit(solution)/shard_map/all_to_all | solution.py:239
  280.7 41.0 %all-to-all-start.2 = ((bf16[4,512,768]{2,1,0:T(8,128)(2,1)}), bf16[4,512,768]{2,1,0:T(8,128)(2,1)S(1)}, u32[]{:S(2)}, u32[]{:S(2)}) async-start(bf16[4,512,768]{2,1,0:T(8,128)(2,1)} %bitcast.200), calls=%async_computation.2 | async-start | bytes 6291456 | tf_op jit(solution)/shard_map/all_to_all | solution.py:314
  321.7 96.5 %copy-start.36 = (bf16[4,512,768]{2,1,0:T(8,128)(2,1)}, bf16[4,512,768]{2,1,0:T(8,128)(2,1)S(1)}, u32[]{:S(2)}) copy-start(bf16[4,512,768]{2,1,0:T(8,128)(2,1)S(1)} %all-to-all-done.2) | copy-start | bytes 9437188
  431.1 41.0 %all-to-all-start.1 = ((bf16[4,512,768]{2,1,0:T(8,128)(2,1)}), bf16[4,512,768]{2,1,0:T(8,128)(2,1)S(1)}, u32[]{:S(2)}, u32[]{:S(2)}) async-start(bf16[4,512,768]{2,1,0:T(8,128)(2,1)} %bitcast.196), calls=%async_computation.1 | async-start | bytes 6291456 | tf_op jit(solution)/shard_map/all_to_all | solution.py:253
  473.8 82.2 %all-to-all-start.3 = ((bf16[4,512,768]{2,1,0:T(8,128)(2,1)}), bf16[4,512,768]{2,1,0:T(8,128)(2,1)}, u32[]{:S(2)}, u32[]{:S(2)}) async-start(bf16[4,512,768]{2,1,0:T(8,128)(2,1)} %bitcast.42), calls=%async_computation.3 | async-start | bytes 6291456 | tf_op jit(solution)/shard_map/all_to_all | solution.py:336
  479.3 315.6 %reduce-scatter.20.cloned.1.call-start = ((), (), s32[]{:S(2)}) async-start(), calls=%async_computation.18 | async-start | bytes 1327104 | tf_op jit(solution)/shard_map/reduce_scatter | solution.py:414
  498.9 52.9 %copy-start.59 = (f32[1024,2,2]{0,1,2:T(2,128)S(1)}, f32[1024,2,2]{0,1,2:T(2,128)}, u32[]{:S(2)}) copy-start(f32[1024,2,2]{0,1,2:T(2,128)} %copy-done.58) | copy-start | bytes 49156
  498.9 53.0 %copy-start.51 = (s32[1,1024,2]{1,2,0:T(2,128)S(1)}, s32[1,1024,2]{1,2,0:T(2,128)}, u32[]{:S(2)}) copy-start(s32[1,1024,2]{1,2,0:T(2,128)} %param.16) | copy-start | bytes 24580
  498.9 53.0 %copy-start.89 = (s32[2]{0:T(128)S(1)}, s32[2]{0:T(128)}, u32[]{:S(2)}) copy-start(s32[2]{0:T(128)} %iota_add_fusion.1) | copy-start | bytes 28
  498.9 53.1 %copy-start.55 = (f32[1024,2]{0,1:T(2,128)S(1)}, f32[1024,2]{0,1:T(2,128)}, u32[]{:S(2)}) copy-start(f32[1024,2]{0,1:T(2,128)} %copy-done.54) | copy-start | bytes 24580
  498.9 53.1 %copy-start.62 = (f32[1024]{0:T(1024)S(1)}, f32[1024]{0:T(1024)}, u32[]{:S(2)}) copy-start(f32[1024]{0:T(1024)} %copy-done.61) | copy-start | bytes 12292
  498.9 53.1 %copy-start.67 = (f32[1024]{0:T(1024)S(1)}, f32[1024]{0:T(1024)}, u32[]{:S(2)}) copy-start(f32[1024]{0:T(1024)} %copy-done.66) | copy-start | bytes 12292
  498.9 53.1 %copy-start.85 = (f32[1024]{0:T(1024)S(1)}, f32[1024]{0:T(1024)}, u32[]{:S(2)}) copy-start(f32[1024]{0:T(1024)} %get-tuple-element.92) | copy-start | bytes 12292
  498.9 54.0 %copy-start.57 = (bf16[768,12]{0,1:T(8,128)(2,1)S(1)}, bf16[768,12]{0,1:T(8,128)(2,1)}, u32[]{:S(2)}) copy-start(bf16[768,12]{0,1:T(8,128)(2,1)} %reshape.783) | copy-start | bytes 55300
  601.1 18.6 %copy-start.53 = (f32[12,512]{1,0:T(8,128)S(1)}, f32[12,512]{1,0:T(8,128)}, u32[]{:S(2)}) copy-start(f32[12,512]{1,0:T(8,128)} %log_add_fusion) | copy-start | bytes 73732
  637.8 42.7 %copy-start.14 = (bf16[1024,12,32]{0,2,1:T(8,128)(2,1)S(1)}, bf16[1024,12,32]{0,2,1:T(8,128)(2,1)}, u32[]{:S(2)}) copy-start(bf16[1024,12,32]{0,2,1:T(8,128)(2,1)} %copy-done.13) | copy-start | bytes 2359300
  637.8 42.7 %copy-start.17 = (bf16[1024,12,32]{0,2,1:T(8,128)(2,1)S(1)}, bf16[1024,12,32]{0,2,1:T(8,128)(2,1)}, u32[]{:S(2)}) copy-start(bf16[1024,12,32]{0,2,1:T(8,128)(2,1)} %copy-done.16) | copy-start | bytes 2359300
  733.9 145.3 %reduce-scatter.18.cloned.1.call-start = ((), (), s32[]{:S(2)}) async-start(), calls=%async_computation.17 | async-start | bytes 3981312 | tf_op jit(solution)/shard_map/reduce_scatter | solution.py:411
  763.5 177.1 %reduce-scatter.26.cloned.1.call-start = ((), (), s32[]{:S(2)}) async-start(), calls=%async_computation.21 | async-start | bytes 221184
  765.8 238.8 %reduce-scatter.24.cloned.1.call-start = ((), (), s32[]{:S(2)}) async-start(), calls=%async_computation.20 | async-start | bytes 221184
  767.4 301.2 %reduce-scatter.22.cloned.1.call-start = ((), (), s32[]{:S(2)}) async-start(), calls=%async_computation.19 | async-start | bytes 221184
  769.1 336.4 %all-reduce.14.cloned.1.call-start = ((), (), s32[]{:S(2)}) async-start(), calls=%async_computation.22 | async-start | bytes 1179648 | tf_op jit(solution)/shard_map/psum | solution.py:402
  879.2 348.0 %reduce-scatter.16.cloned.1.call-start = ((), (), s32[]{:S(2)}) async-start(), calls=%async_computation.16 | async-start | bytes 7077888 | tf_op jit(solution)/shard_map/reduce_scatter | solution.py:351
  891.5 545.6 %reduce-scatter.14.cloned.1.call-start = ((), (), s32[]{:S(2)}) async-start(), calls=%async_computation.15 | async-start | bytes 14155776 | tf_op jit(solution)/shard_map/reduce_scatter | solution.py:348
  941.4 20.9 %copy-start.21 = (f32[1024,768]{1,0:T(8,128)S(1)}, f32[1024,768]{1,0:T(8,128)}, u32[]{:S(2)}) copy-start(f32[1024,768]{1,0:T(8,128)} %copy-done.19) | copy-start | bytes 9437188
  941.4 20.9 %copy-start.78 = (f32[1024]{0:T(1024)S(1)}, f32[1024]{0:T(1024)}, u32[]{:S(2)}) copy-start(f32[1024]{0:T(1024)} %get-tuple-element.123) | copy-start | bytes 12292
  (71 other events, 516.5 us)
Sparse Core Ops, SparseCore 0:
  10.3 64.7 all-gather.7
  77.2 39.0 all-gather.9
  118.5 175.7 all-gather.11
  296.3 97.4 all-gather.13
  734.0 60.9 reduce-scatter.19
  798.5 80.6 reduce-scatter.17
  882.5 58.1 reduce-scatter.25
  944.5 60.1 reduce-scatter.23
  1008.5 60.0 reduce-scatter.21
  1070.9 34.5 all-reduce.13
  1109.1 118.1 reduce-scatter.15
  1230.7 206.3 reduce-scatter.13
where the time goes:
time: 1460 us; the launch traced here: 1450 us
  waiting for transfers between devices  703 us (48%)
  matrix products  301 us (21%)
  other arithmetic  168 us (12%)
  local copies, waits for them, and re-layouts  137 us (9%)
  blocking collectives  84.1 us (6%)
  starting transfers between devices  37.1 us (3%)
  between operations  17 us (1%)
    reduce_scatter x1, waiting for transfers between devices, shards(): lax.psum_scatter(grad_expert_gu.astype(jnp.bfloat16), 'dp', scatter_dimen...  207 us
    unnamed x15, waiting for transfers between devices  132 us
    reduce_scatter x1, waiting for transfers between devices, shards(): lax.psum_scatter(grad_down.astype(jnp.bfloat16), 'dp', scatter_dimension=...  118 us
    reduce_scatter x1, waiting for transfers between devices, shards(): lax.psum_scatter(sum_qkv.astype(jnp.bfloat16), 'dp', scatter_dimension=0,...  84.2 us
    all_gather x1, waiting for transfers between devices, shards(): lax.all_gather(w_down, 'dp', axis=1, tiled=True)  72.1 us
    reduce_sum x1, other arithmetic, shards(): grad_mix_first = jnp.sum(grad_const_val * normed_back[:, None, :], -1)  47.9 us
    convert_element_type x1, other arithmetic, attend_backward(): grad_scores = (probs_full * (grad_probs - inner_sum)).astype(jnp.bfloat16)  42.7 us
    dot_general x2, matrix products, attend_backward(): jnp.einsum('qhd,khd->hqk', rows_grad, value_seq, preferred_element_type=j...  36.7 us
  transfers between devices with their start and end apart: 16, of which 13 were waited for; matrix products, arithmetic and copies ran while one was open for 26% of the time, Pallas kernels for 0%

commit v1 on v0

--- a/solution.py
+++ b/solution.py
@@ -164,15 +164,25 @@
     head_dim = model_width // HEADS
     score_scale = head_dim ** (-0.5)
     choice_count = resid_logits.shape[-1]
-    qkv_full, out_full, gain_one, gain_two, router_full, const_full, vector_full = (
-        lax.all_gather(w_qkv, "dp", axis=0, tiled=True),
-        lax.all_gather(w_out, "dp", axis=0, tiled=True),
-        lax.all_gather(gain_attn, "dp", axis=0, tiled=True),
-        lax.all_gather(gain_ffn, "dp", axis=0, tiled=True),
-        lax.all_gather(w_router, "dp", axis=0, tiled=True),
-        lax.all_gather(w_const, "dp", axis=0, tiled=True),
-        lax.all_gather(v_const, "dp", axis=0, tiled=True),
-    )
+    width_qkv = w_qkv.shape[1]
+    width_out = w_out.shape[1]
+    small_parts = [w_router, w_const, v_const, gain_attn[:, None], gain_ffn[:, None]]
+    small_width = sum(part.shape[1] for part in small_parts)
+    pad_width = -(width_qkv + width_out + small_width) % 128
+    packed = jnp.concatenate(
+        [w_qkv, w_out] + small_parts + [jnp.zeros((w_qkv.shape[0], pad_width), jnp.bfloat16)], 1
+    )
+    packed_full = lax.all_gather(packed, "dp", axis=0, tiled=True)
+    qkv_full = packed_full[:, :width_qkv]
+    out_full = packed_full[:, width_qkv : width_qkv + width_out]
+    small_full = packed_full[:, width_qkv + width_out :]
+    router_width, const_width = w_router.shape[1], w_const.shape[1]
+    router_full = small_full[:, :router_width]
+    const_full = small_full[:, router_width : router_width + const_width]
+    first = router_width + const_width
+    vector_full = small_full[:, first : first + v_const.shape[1]]
+    first = first + v_const.shape[1]
+    gain_one, gain_two = small_full[:, first], small_full[:, first + 1]
     gate_up_full, down_full = (
         lax.all_gather(w_gate_up, "dp", axis=1, tiled=True),
         lax.all_gather(w_down, "dp", axis=1, tiled=True),
@@ -314,15 +324,11 @@
     arrived_grad = lax.all_to_all(
         send_grads, "expert", split_axis=0, concat_axis=0, tiled=True
     ).reshape(owner_count, local_count, CAP, model_width)
-    gate_up_back, down_back = (
-        lax.all_gather(w_gate_up, "dp", axis=1, tiled=True),
-        lax.all_gather(w_down, "dp", axis=1, tiled=True),
-    )
     grad_down = jnp.einsum(
         "secf,secd->efd", activated, arrived_grad, preferred_element_type=jnp.float32
     )
     grad_act = jnp.einsum(
-        "secd,efd->secf", arrived_grad, down_back, preferred_element_type=jnp.float32
+        "secd,efd->secf", arrived_grad, down_full, preferred_element_type=jnp.float32
     )
     grad_gate = grad_act * up_part * squashed * (1.0 + gate_part * (1.0 - squashed))
     grad_up = grad_act * silu_gate
@@ -331,7 +337,7 @@
         "secd,secf->edf", arrived, grad_gate_up, preferred_element_type=jnp.float32
     )
     grad_rows = jnp.einsum(
-        "secf,edf->secd", grad_gate_up, gate_up_back, preferred_element_type=jnp.float32
+        "secf,edf->secd", grad_gate_up, gate_up_full, preferred_element_type=jnp.float32
     ).astype(jnp.bfloat16)
     back_rows = lax.all_to_all(
         grad_rows.reshape(owner_count, local_count * CAP, model_width),
@@ -344,14 +350,17 @@
     grad_normed = grad_normed + jnp.sum(
         padded_back[destination].reshape(row_count, 2, model_width).astype(jnp.float32), 1
     )
-    grad_expert_gu, grad_expert_down = (
-        lax.psum_scatter(
-            grad_expert_gu.astype(jnp.bfloat16), "dp", scatter_dimension=1, tiled=True
-        ).astype(jnp.float32),
-        lax.psum_scatter(
-            grad_down.astype(jnp.bfloat16), "dp", scatter_dimension=1, tiled=True
-        ).astype(jnp.float32),
-    )
+    grad_expert_gu = grad_expert_gu.astype(jnp.bfloat16)
+    grad_down = grad_down.astype(jnp.bfloat16)
+    grad_normed, grad_expert_gu, grad_down = lax.optimization_barrier(
+        (grad_normed, grad_expert_gu, grad_down)
+    )
+    grad_expert_down = lax.psum_scatter(
+        grad_down, "dp", scatter_dimension=1, tiled=True
+    ).astype(jnp.float32)
+    grad_expert_gu = lax.psum_scatter(
+        grad_expert_gu, "dp", scatter_dimension=1, tiled=True
+    ).astype(jnp.float32)
     grad_middle, grad_gain_two = normalize_back(middle, scale_two, gain_second, grad_normed)
     grad_middle = grad_middle + grad_final
     grad_branch = grad_middle.astype(jnp.bfloat16)
@@ -398,38 +407,29 @@
     )
     grad_inputs, grad_gain_one = normalize_back(inputs, scale_one, gain_first, grad_normed_one)
     token_grad = (grad_inputs + grad_middle).astype(jnp.bfloat16).reshape(tokens.shape)
-    sum_qkv, sum_out, sum_gain_one, sum_gain_two, sum_router, sum_const, sum_vector = (
-        lax.psum(grad_qkv.astype(jnp.bfloat16), "expert").astype(jnp.float32),
-        lax.psum(grad_out_w.astype(jnp.bfloat16), "expert").astype(jnp.float32),
-        lax.psum(grad_gain_one.astype(jnp.bfloat16), "expert").astype(jnp.float32),
-        lax.psum(grad_gain_two.astype(jnp.bfloat16), "expert").astype(jnp.float32),
-        lax.psum(grad_router.astype(jnp.bfloat16), "expert").astype(jnp.float32),
-        lax.psum(grad_const.astype(jnp.bfloat16), "expert").astype(jnp.float32),
-        lax.psum(grad_vector.astype(jnp.bfloat16), "expert").astype(jnp.float32),
-    )
-    part_qkv, part_out, part_gain_one, part_gain_two, part_router, part_const, part_vector = (
-        lax.psum_scatter(
-            sum_qkv.astype(jnp.bfloat16), "dp", scatter_dimension=0, tiled=True
-        ).astype(jnp.float32),
-        lax.psum_scatter(
-            sum_out.astype(jnp.bfloat16), "dp", scatter_dimension=0, tiled=True
-        ).astype(jnp.float32),
-        lax.psum_scatter(
-            sum_gain_one.astype(jnp.bfloat16), "dp", scatter_dimension=0, tiled=True
-        ).astype(jnp.float32),
-        lax.psum_scatter(
-            sum_gain_two.astype(jnp.bfloat16), "dp", scatter_dimension=0, tiled=True
-        ).astype(jnp.float32),
-        lax.psum_scatter(
-            sum_router.astype(jnp.bfloat16), "dp", scatter_dimension=0, tiled=True
-        ).astype(jnp.float32),
-        lax.psum_scatter(
-            sum_const.astype(jnp.bfloat16), "dp", scatter_dimension=0, tiled=True
-        ).astype(jnp.float32),
-        lax.psum_scatter(
-            sum_vector.astype(jnp.bfloat16), "dp", scatter_dimension=0, tiled=True
-        ).astype(jnp.float32),
-    )
+    small_grads = [
+        grad_router,
+        grad_const,
+        grad_vector,
+        grad_gain_one[:, None],
+        grad_gain_two[:, None],
+    ]
+    packed_grads = jnp.concatenate(
+        [part.astype(jnp.bfloat16) for part in [grad_qkv, grad_out_w] + small_grads]
+        + [jnp.zeros((model_width, pad_width), jnp.bfloat16)],
+        1,
+    )
+    packed_part = lax.psum_scatter(packed_grads, "dp", scatter_dimension=0, tiled=True)
+    packed_part = lax.psum(packed_part, "expert").astype(jnp.float32)
+    part_qkv = packed_part[:, :width_qkv]
+    part_out = packed_part[:, width_qkv : width_qkv + width_out]
+    small_part = packed_part[:, width_qkv + width_out :]
+    part_router = small_part[:, :router_width]
+    part_const = small_part[:, router_width : router_width + const_width]
+    first = router_width + const_width
+    part_vector = small_part[:, first : first + v_const.shape[1]]
+    first = first + v_const.shape[1]
+    part_gain_one, part_gain_two = small_part[:, first], small_part[:, first + 1]
     return (
         output,
         token_grad,

time: 1460 us -> 1270 us (0.87)
  waiting for transfers between devices: 703 us -> 617 us
  blocking collectives: 84.1 us -> 0 us
  starting transfers between devices: 37.1 us -> 22.5 us
    unnamed x15 -> x7, waiting for transfers between devices: 132 us -> 2.64 us
    all_gather x3 -> x0, blocking collectives: 52.4 us -> none  [the longest x1 24.3 us: shards(): lax.all_gather(w_router, 'dp', axis=0, tiled=True)]
    all_gather x2 -> x1, waiting for transfers between devices: 0.04 us -> 42.1 us  [shards(): packed_full = lax.all_gather(packed, 'dp', axis=0, tiled=True)]
    unnamed x2 -> x0, blocking collectives: 24 us -> none
    all_to_all x1, waiting for transfers between devices: 0.01 us -> 19.5 us  [shards(): lax.all_to_all(grad_rows.reshape(owner_count, local_count * CAP, model_wi...]
    reduce_scatter x4 -> x3, waiting for transfers between devices: 436 us -> 420 us  [the longest x1 208 us: shards(): lax.psum_scatter(grad_expert_gu, 'dp', scatter_dimension=1, tiled=True)]
    all_to_all x1, starting transfers between devices: 21.2 us -> 5.69 us  [shards(): lax.all_to_all(send_rows, 'expert', split_axis=0, concat_axis=0, tiled=True)]
  transfers between devices with their start and end apart: 16 -> 11, of which waited for: 13 -> 9; matrix products, arithmetic and copies ran while one was open for 26% -> 21% of each run, Pallas kernels for 0% -> 0%
where the time goes in v1:
time: 1270 us
  waiting for transfers between devices  617 us (49%)
  matrix products  294 us (23%)
  other arithmetic  168 us (13%)
  local copies, waits for them, and re-layouts  148 us (12%)
  starting transfers between devices  22.5 us (2%)
  between operations  15.7 us (1%)
    reduce_scatter x1, waiting for transfers between devices, shards(): lax.psum_scatter(grad_expert_gu, 'dp', scatter_dimension=1, tiled=True)  208 us
    reduce_scatter x1, waiting for transfers between devices, shards(): lax.psum_scatter(grad_down, 'dp', scatter_dimension=1, tiled=True)  113 us
    reduce_scatter x1, waiting for transfers between devices, shards(): lax.psum_scatter(packed_grads, 'dp', scatter_dimension=0, tiled=True)  98.5 us
    all_gather x1, waiting for transfers between devices, shards(): lax.all_gather(w_down, 'dp', axis=1, tiled=True)  75.4 us
    reduce_sum x1, other arithmetic, shards(): grad_mix_first = jnp.sum(grad_const_val * normed_back[:, None, :], -1)  47.7 us
    all_gather x1, waiting for transfers between devices, shards(): packed_full = lax.all_gather(packed, 'dp', axis=0, tiled=True)  42.1 us
    convert_element_type x1, other arithmetic, attend_backward(): grad_scores = (probs_full * (grad_probs - inner_sum)).astype(jnp.bfloat16)  41.7 us
    dot_general x2, matrix products, attend_backward(): jnp.einsum('qhd,khd->hqk', rows_grad, value_seq, preferred_element_type=j...  39.3 us
  transfers between devices with their start and end apart: 11, of which 9 were waited for; matrix products, arithmetic and copies ran while one was open for 21% of the time, Pallas kernels for 0%

profile of v1, /device:TPU:19, one launch (start us, length us, event | category | flops | bytes accessed | tf_op | source)
XLA Modules:
  0.0 1265.8 jit_solution(9050178818104521452)
XLA Ops:
  26.0 8.2 scatter_custom_fusion
  36.9 4.7 mul.667
  41.6 8.6 mul.685
  52.5 42.1 %all-gather.4.cloned.1.call-done = bf16[768,3200]{1,0:T(8,128)(2,1)} async-done(((bf16[96,3200]{1,0:T(8,128)(2,1)}), bf16[768,3200]{1,0:T(8,128)(2,1)}) %all-gather.4.cloned.1.call-update) | async-done | bytes 4915216 | tf_op jit(solution)/shard_map/all_gather | solution.py:175
  96.5 6.0 fusion.46
  121.0 11.4 fusion.25
  132.4 14.5 %fusion.24 = (f32[12,512]{1,0:T(8,128)}, f32[12,512,1024]{2,1,0:T(8,128)}) fusion(pred[512,1024]{1,0:T(8,128)(4,1)S(1)} %get-tuple-element.214, bf16[1024,12,32]{0,2,1:T(8,128)(2,1)} %copy-done.27, bf16[1024,12,32]{0,2,1:T(8,128)(2,1)} %copy-done.24, bf16[1024,12,32]{0,2,1:T(8,128)(2,1)} %copy-done.17, bf16[1024,12,32]{0,2,1:T(8,128)(2,1)} %copy-done.14), kind=kOutput, calls=%fused_computation.48 | convolution fusion | flops 828893184 | bytes 28860416 | tf_op jit(solution)/shard_map/while/body/eval_jaxpr/qhd,khd->hqk/dot_general | solution.py:76
  146.9 12.7 %fusion.1 = f32[12,512]{1,0:T(8,128)S(1)} fusion(f32[12,512]{1,0:T(8,128)} %get-tuple-element.224, f32[12,512,1024]{2,1,0:T(8,128)} %get-tuple-element.225, pred[512,1024]{1,0:T(8,128)(4,1)S(1)} %get-tuple-element.215), kind=kLoop, calls=%fused_computation.19 | loop fusion | flops 25159680 | bytes 25739264 | tf_op jit(solution)/shard_map/while/body/eval_jaxpr/reduce_sum | solution.py:99
  159.7 8.5 fusion.64
  168.2 14.1 %fusion = f32[12,512]{1,0:T(8,128)S(1)} fusion(f32[12,512]{1,0:T(8,128)} %get-tuple-element.226, f32[12,512,1024]{2,1,0:T(8,128)} %get-tuple-element.227, pred[512,1024]{1,0:T(8,128)(4,1)S(1)} %get-tuple-element.214), kind=kLoop, calls=%fused_computation.18 | loop fusion | flops 25159680 | bytes 25739264 | tf_op jit(solution)/shard_map/while/body/eval_jaxpr/reduce_sum | solution.py:99
  184.4 7.9 fusion.63
  201.6 9.4 gather_fusion
  211.1 5.7 all-to-all-start
  228.4 9.4 gather_fusion.2
  237.9 15.1 %all-to-all-done = bf16[4,512,768]{2,1,0:T(8,128)(2,1)} async-done(((bf16[4,512,768]{2,1,0:T(8,128)(2,1)}), bf16[4,512,768]{2,1,0:T(8,128)(2,1)}, u32[]{:S(2)}, u32[]{:S(2)}) %all-to-all-start) | async-done | bytes 3145760 | tf_op jit(solution)/shard_map/all_to_all | solution.py:249
  257.5 13.8 %all-gather.6.cloned.1.call-done = bf16[2,768,4096]{2,1,0:T(8,128)(2,1)} async-done(((bf16[2,96,4096]{2,1,0:T(8,128)(2,1)}), bf16[2,768,4096]{2,1,0:T(8,128)(2,1)}) %all-gather.6.cloned.1.call-update) | async-done | bytes 12582928 | tf_op jit(solution)/shard_map/all_gather | solution.py:187
  271.3 24.2 %convolution_bitcast_fusion = f32[4,2,256,4096]{3,2,0,1:T(8,128)} fusion(bf16[2,768,4096]{2,1,0:T(8,128)(2,1)} %all-gather.6.cloned.1.call-done, bf16[4,2,256,768]{3,2,1,0:T(8,128)(2,1)} %bitcast.19), kind=kOutput, calls=%fused_computation.34 | convolution fusion | flops 12884901888 | bytes 49283072 | tf_op jit(solution)/shard_map/secd,edf->secf/dot_general | solution.py:252
  295.5 75.4 %all-gather.8.cloned.1.call-done = bf16[2,2048,768]{2,1,0:T(8,128)(2,1)} async-done(((bf16[2,256,768]{2,1,0:T(8,128)(2,1)}), bf16[2,2048,768]{2,1,0:T(8,128)(2,1)}) %all-gather.8.cloned.1.call-update) | async-done | bytes 6291472 | tf_op jit(solution)/shard_map/all_gather | solution.py:188
  370.9 24.5 %fusion.6 = (bf16[4,2,256,2048]{3,2,0,1:T(8,128)(2,1)}, bf16[4,2,256,2048]{3,2,0,1:T(8,128)(2,1)}, bf16[4,2,256,2048]{3,2,0,1:T(8,128)(2,1)}) fusion(f32[4,2,256,4096]{3,2,0,1:T(8,128)} %convolution_bitcast_fusion, bf16[2,2048,768]{2,1,0:T(8,128)(2,1)} %all-gather.8.cloned.1.call-done, bf16[4,2,256,768]{3,2,1,0:T(8,128)(2,1)S(1)} %bitcast.182), kind=kOutput, calls=%fused_computation.27 | convolution fusion | flops 6505365504 | bytes 68157440 | tf_op jit(solution)/shard_map/secd,efd->secf/dot_general | solution.py:330
  395.4 19.7 %convert_bitcast_fusion = bf16[4,2,256,768]{3,2,0,1:T(8,128)(2,1)S(1)} fusion(bf16[2,768,4096]{2,1,0:T(8,128)(2,1)} %all-gather.6.cloned.1.call-done, bf16[4,2,256,2048]{3,2,0,1:T(8,128)(2,1)} %get-tuple-element.190, bf16[4,2,256,2048]{3,2,0,1:T(8,128)(2,1)} %get-tuple-element.189), kind=kOutput, calls=%fused_computation.90 | convolution fusion | flops 12920029184 | bytes 32505856 | tf_op jit(solution)/shard_map/secf,edf->secd/dot_general | solution.py:339
  417.0 6.2 all-to-all-start.3
  427.0 10.9 convert_bitcast_fusion.1
  439.8 19.5 %all-to-all-done.3 = bf16[4,512,768]{2,1,0:T(8,128)(2,1)} async-done(((bf16[4,512,768]{2,1,0:T(8,128)(2,1)}), bf16[4,512,768]{2,1,0:T(8,128)(2,1)}, u32[]{:S(2)}, u32[]{:S(2)}) %all-to-all-start.3) | async-done | bytes 3145760 | tf_op jit(solution)/shard_map/all_to_all | solution.py:342
  459.4 5.8 all-to-all-start.1
  465.2 15.1 %bitcast_convert_fusion.1 = bf16[2,2048,768]{2,1,0:T(8,128)(2,1)} fusion(bf16[4,2,256,2048]{3,2,0,1:T(8,128)(2,1)} %get-tuple-element.191, bf16[4,2,256,768]{3,2,1,0:T(8,128)(2,1)S(1)} %bitcast.183), kind=kOutput, calls=%fused_computation.37 | convolution fusion | flops 6445596672 | bytes 17825792 | tf_op jit(solution)/shard_map/secf,secd->efd/dot_general | solution.py:327
  480.3 21.1 %bitcast_convert_fusion = bf16[2,768,4096]{2,1,0:T(8,128)(2,1)} fusion(bf16[4,2,256,768]{3,2,1,0:T(8,128)(2,1)} %bitcast.19, bf16[4,2,256,2048]{3,2,0,1:T(8,128)(2,1)} %get-tuple-element.190, bf16[4,2,256,2048]{3,2,0,1:T(8,128)(2,1)} %get-tuple-element.189), kind=kOutput, calls=%fused_computation.5 | convolution fusion | flops 12924747776 | bytes 32505856 | tf_op jit(solution)/shard_map/secd,secf->edf/dot_general | solution.py:336
  507.3 9.4 gather_fusion.3
  516.7 10.8 gather_fusion.1
  527.5 4.8 reshape.764
  532.3 47.7 %fusion.26 = (f32[1024,2]{1,0:T(8,128)}, f32[1024,2]{1,0:T(8,128)S(1)}, f32[1024,768]{1,0:T(8,128)}, f32[1024,768]{1,0:T(8,128)}, f32[1024,2]{1,0:T(8,128)S(1)}, /*index=5*/f32[1024,768]{1,0:T(8,128)}, f32[1024,2]{1,0:T(8,128)S(1)}) fusion(f32[1024,768]{1,0:T(8,128)} %copy-done.9, f32[1024,768]{1,0:T(8,128)} %convert_element_type.275, f32[1024,2]{1,0:T(8,128)} %copy.298, ...), kind=kLoop, calls=%fused_computation.56 | loop fusion | flops 25944064 | bytes 22091776 | tf_op jit(solution)/shard_map/reduce_sum | solution.py:306
  584.4 7.8 reshape.765
  592.2 12.1 reduce_sum.282
  606.8 5.7 add_add_fusion
  624.2 13.1 %fusion.11 = f32[12,64,1024]{2,1,0:T(8,128)} fusion(bf16[512,12,64]{0,2,1:T(8,128)(2,1)S(1)} %bitcast.186, f32[12,512]{1,0:T(8,128)S(1)} %log_add_fusion, f32[12,512,1024]{2,1,0:T(8,128)} %get-tuple-element.225, pred[512,1024]{1,0:T(8,128)(4,1)S(1)} %copy-done.13), kind=kOutput, calls=%fused_computation.35 | convolution fusion | flops 830472192 | bytes 29646848 | tf_op jit(solution)/shard_map/while/body/eval_jaxpr/hqk,qhd->khd/dot_general | solution.py:126
  637.3 17.7 %multiply_reduce_fusion = (f32[12,512]{1,0:T(8,128)S(1)}, f32[12,512,1024]{2,1,0:T(8,128)}) fusion(f32[12,512]{1,0:T(8,128)S(1)} %log_add_fusion, f32[12,512,1024]{2,1,0:T(8,128)} %get-tuple-element.225, pred[512,1024]{1,0:T(8,128)(4,1)S(1)} %copy-done.13, bf16[512,12,64]{0,2,1:T(8,128)(2,1)} %bitcast.187, bf16[1024,12,64]{0,2,1:T(8,128)(2,1)S(1)} %bitcast.175), kind=kOutput, calls=%fused_computation.7 | convolution fusion | flops 836757504 | bytes 53264384 | tf_op jit(solution)/shard_map/while/body/eval_jaxpr/qhd,khd->hqk/dot_general | solution.py:123
  655.0 21.6 %multiply_reduce_fusion.1 = (f32[12,512]{1,0:T(8,128)S(1)}, f32[12,512,1024]{2,1,0:T(8,128)}) fusion(f32[12,512]{1,0:T(8,128)S(1)} %log_add_fusion.1, f32[12,512,1024]{2,1,0:T(8,128)} %get-tuple-element.227, pred[512,1024]{1,0:T(8,128)(4,1)S(1)} %copy-done.31, bf16[512,12,64]{0,2,1:T(8,128)(2,1)S(1)} %bitcast.184, bf16[1024,12,64]{0,2,1:T(8,128)(2,1)S(1)} %bitcast.176), kind=kOutput, calls=%fused_computation.10 | convolution fusion | flops 836757504 | bytes 53264384 | tf_op jit(solution)/shard_map/while/body/eval_jaxpr/qhd,khd->hqk/dot_general | solution.py:123
  676.6 41.7 %multiply_convert_fusion = (bf16[12,512,1024]{2,1,0:T(8,128)(2,1)}, bf16[12,512,1024]{2,1,0:T(8,128)(2,1)}) fusion(f32[12,512,1024]{2,1,0:T(8,128)} %get-tuple-element.231, f32[12,512]{1,0:T(8,128)S(1)} %get-tuple-element.230, f32[12,512]{1,0:T(8,128)S(1)} %log_add_fusion, f32[12,512,1024]{2,1,0:T(8,128)} %get-tuple-element.225, ...), kind=kLoop, calls=%fused_computation.6 | loop fusion | flops 75497472 | bytes 126976000 | tf_op jit(solution)/shard_map/while/body/eval_jaxpr/convert_element_type | solution.py:130
  718.4 9.8 multiply_bitcast_fusion.2
  728.2 6.9 fusion.128
  737.6 13.3 %add_convert_fusion = bf16[12,64,1024]{2,1,0:T(8,128)(2,1)S(1)} fusion(f32[12,64,1024]{2,1,0:T(8,128)} %fusion.11, bf16[512,12,64]{0,2,1:T(8,128)(2,1)} %bitcast.185, f32[12,512]{1,0:T(8,128)S(1)} %log_add_fusion.1, f32[12,512,1024]{2,1,0:T(8,128)} %get-tuple-element.227, pred[512,1024]{1,0:T(8,128)(4,1)} %copy-done.30), kind=kOutput, calls=%fused_computation.86 | convolution fusion | flops 832045056 | bytes 31219712 | tf_op jit(solution)/shard_map/while/body/eval_jaxpr/hqk,qhd->khd/dot_general | solution.py:126
  751.0 8.6 multiply_bitcast_fusion.1
  759.6 7.1 multiply_bitcast_fusion
  773.7 6.0 fusion.42
  781.3 7.9 concatenate.66
  789.3 98.5 %reduce-scatter.4.cloned.1.call-done = bf16[96,3200]{1,0:T(8,128)(2,1)} async-done(((bf16[768,3200]{1,0:T(8,128)(2,1)}), bf16[96,3200]{1,0:T(8,128)(2,1)}) %reduce-scatter.4.cloned.1.call-update) | async-done | bytes 614416 | tf_op jit(solution)/shard_map/reduce_scatter | solution.py:422
  894.0 29.0 %all-reduce.6.cloned.1.call-done = bf16[96,3200]{1,0:T(8,128)(2,1)} async-done(((bf16[96,3200]{1,0:T(8,128)(2,1)}), bf16[96,3200]{1,0:T(8,128)(2,1)}) %all-reduce.6.cloned.1.call-update) | async-done | bytes 614416 | tf_op jit(solution)/shard_map/psum | solution.py:423
  931.8 113.0 %reduce-scatter.8.cloned.1.call-done = bf16[2,256,768]{2,1,0:T(8,128)(2,1)} async-done(((bf16[2,2048,768]{2,1,0:T(8,128)(2,1)}), bf16[2,256,768]{2,1,0:T(8,128)(2,1)}) %reduce-scatter.8.cloned.1.call-update) | async-done | bytes 786448 | tf_op jit(solution)/shard_map/reduce_scatter | solution.py:358
  1047.2 208.1 %reduce-scatter.6.cloned.1.call-done = bf16[2,96,4096]{2,1,0:T(8,128)(2,1)} async-done(((bf16[2,768,4096]{2,1,0:T(8,128)(2,1)}), bf16[2,96,4096]{2,1,0:T(8,128)(2,1)}) %reduce-scatter.6.cloned.1.call-update) | async-done | bytes 1572880 | tf_op jit(solution)/shard_map/reduce_scatter | solution.py:361
  (341 shorter events, 135.0 us)
Async XLA Ops:
  7.2 11.8 copy-start.32
  7.2 87.3 %all-gather.4.cloned.1.call-start = ((), (), s32[]{:S(2)}) async-start(), calls=%async_computation.7 | async-start | bytes 5529600 | tf_op jit(solution)/shard_map/all_gather | solution.py:175
  13.3 258.0 %all-gather.6.cloned.1.call-start = ((), (), s32[]{:S(2)}) async-start(), calls=%async_computation.8 | async-start | bytes 14155776 | tf_op jit(solution)/shard_map/all_gather | solution.py:187
  14.0 356.9 %all-gather.8.cloned.1.call-start = ((), (), s32[]{:S(2)}) async-start(), calls=%async_computation.9 | async-start | bytes 7077888 | tf_op jit(solution)/shard_map/all_gather | solution.py:188
  14.8 20.1 %copy-start.3 = (bf16[1,1024,768]{2,1,0:T(8,128)(2,1)S(1)}, bf16[1,1024,768]{2,1,0:T(8,128)(2,1)}, u32[]{:S(2)}) copy-start(bf16[1,1024,768]{2,1,0:T(8,128)(2,1)} %param.27) | copy-start | bytes 4718596
  20.0 76.5 %copy-start.82 = (f32[1024]{0:T(1024)}, f32[1024]{0:T(1024)S(1)}, u32[]{:S(2)}) copy-start(f32[1024]{0:T(1024)S(1)} %get-tuple-element.219) | copy-start | bytes 12292
  41.6 54.9 %copy-start.33 = (bf16[1,1024,768]{2,1,0:T(8,128)(2,1)S(1)}, bf16[1,1024,768]{2,1,0:T(8,128)(2,1)}, u32[]{:S(2)}) copy-start(bf16[1,1024,768]{2,1,0:T(8,128)(2,1)} %param.14) | copy-start | bytes 4718596
  52.5 107.1 %copy-start.12 = (pred[512,1024]{1,0:T(8,128)(4,1)}, pred[512,1024]{1,0:T(8,128)(4,1)S(1)}, u32[]{:S(2)}) copy-start(pred[512,1024]{1,0:T(8,128)(4,1)S(1)} %get-tuple-element.215) | copy-start | bytes 1572868
  52.5 129.8 %copy-start.30 = (pred[512,1024]{1,0:T(8,128)(4,1)}, pred[512,1024]{1,0:T(8,128)(4,1)S(1)}, u32[]{:S(2)}) copy-start(pred[512,1024]{1,0:T(8,128)(4,1)S(1)} %get-tuple-element.214) | copy-start | bytes 1572868
  112.8 69.5 %copy-start.10 = (bf16[1024,768]{0,1:T(8,128)(2,1)}, bf16[1024,768]{0,1:T(8,128)(2,1)S(1)}, u32[]{:S(2)}) copy-start(bf16[1024,768]{0,1:T(8,128)(2,1)S(1)} %copy.288) | copy-start | bytes 4718596
  121.0 11.4 copy-start.14
  121.0 11.4 copy-start.17
  121.0 11.4 copy-start.24
  121.0 11.4 copy-start.27
  132.4 27.2 %slice-start = ((s8[25165824]{0:T(1024)(128)(4,1)}), s8[4194304]{0:T(1024)(128)(4,1)S(1)}, s32[]{:S(2)}) async-start(s8[25165824]{0:T(1024)(128)(4,1)} %bitcast.171), calls=%async_computation.14 | async-start | bytes 8388608
  132.4 27.2 %slice-start.1 = ((s8[25165824]{0:T(1024)(128)(4,1)}), s8[4194304]{0:T(1024)(128)(4,1)S(1)}, s32[]{:S(2)}) async-start(s8[25165824]{0:T(1024)(128)(4,1)} %bitcast.171), calls=%async_computation.15 | async-start | bytes 8388608
  132.4 27.2 %slice-start.2 = ((s8[25165824]{0:T(1024)(128)(4,1)}), s8[4194304]{0:T(1024)(128)(4,1)S(1)}, s32[]{:S(2)}) async-start(s8[25165824]{0:T(1024)(128)(4,1)} %bitcast.171), calls=%async_computation.16 | async-start | bytes 8388608
  132.4 27.2 %slice-start.3 = ((s8[25165824]{0:T(1024)(128)(4,1)}), s8[4194304]{0:T(1024)(128)(4,1)S(1)}, s32[]{:S(2)}) async-start(s8[25165824]{0:T(1024)(128)(4,1)} %bitcast.171), calls=%async_computation.17 | async-start | bytes 8388608
  146.9 12.8 %slice-start.4 = ((s8[25165824]{0:T(1024)(128)(4,1)}), s8[4194304]{0:T(1024)(128)(4,1)S(1)}, s32[]{:S(2)}) async-start(s8[25165824]{0:T(1024)(128)(4,1)} %bitcast.171), calls=%async_computation.18 | async-start | bytes 8388608
  146.9 12.8 %slice-start.5 = ((s8[25165824]{0:T(1024)(128)(4,1)}), s8[4194304]{0:T(1024)(128)(4,1)S(1)}, s32[]{:S(2)}) async-start(s8[25165824]{0:T(1024)(128)(4,1)} %bitcast.171), calls=%async_computation.19 | async-start | bytes 8388608
  146.9 12.8 %copy-start.57 = (f32[12,512]{1,0:T(8,128)S(1)}, f32[12,512]{1,0:T(8,128)}, u32[]{:S(2)}) copy-start(f32[12,512]{1,0:T(8,128)} %get-tuple-element.224) | copy-start | bytes 73732
  168.2 16.2 %copy-start = (f32[12,512,1024]{2,1,0:T(8,128)S(1)}, f32[12,512,1024]{2,1,0:T(8,128)}, u32[]{:S(2)}) copy-start(f32[12,512,1024]{2,1,0:T(8,128)} %get-tuple-element.227) | copy-start | bytes 75497472
  168.2 16.2 %copy-start.59 = (f32[12,512]{1,0:T(8,128)S(1)}, f32[12,512]{1,0:T(8,128)}, u32[]{:S(2)}) copy-start(f32[12,512]{1,0:T(8,128)} %get-tuple-element.226) | copy-start | bytes 73732
  199.4 20.7 %copy-start.1 = (bf16[1024,768]{1,0:T(8,128)(2,1)}, bf16[1024,768]{1,0:T(8,128)(2,1)S(1)}, u32[]{:S(2)}) copy-start(bf16[1024,768]{1,0:T(8,128)(2,1)S(1)} %get-tuple-element.188) | copy-start | bytes 4718596
  211.1 41.9 %all-to-all-start = ((bf16[4,512,768]{2,1,0:T(8,128)(2,1)}), bf16[4,512,768]{2,1,0:T(8,128)(2,1)}, u32[]{:S(2)}, u32[]{:S(2)}) async-start(bf16[4,512,768]{2,1,0:T(8,128)(2,1)} %bitcast.180), calls=%async_computation | async-start | bytes 6291456 | tf_op jit(solution)/shard_map/all_to_all | solution.py:249
  253.0 42.5 %all-to-all-start.2 = ((bf16[4,512,768]{2,1,0:T(8,128)(2,1)}), bf16[4,512,768]{2,1,0:T(8,128)(2,1)S(1)}, u32[]{:S(2)}, u32[]{:S(2)}) async-start(bf16[4,512,768]{2,1,0:T(8,128)(2,1)} %bitcast.181), calls=%async_computation.2 | async-start | bytes 6291456 | tf_op jit(solution)/shard_map/all_to_all | solution.py:324
  295.5 99.9 %copy-start.39 = (bf16[4,512,768]{2,1,0:T(8,128)(2,1)}, bf16[4,512,768]{2,1,0:T(8,128)(2,1)S(1)}, u32[]{:S(2)}) copy-start(bf16[4,512,768]{2,1,0:T(8,128)(2,1)S(1)} %all-to-all-done.2) | copy-start | bytes 9437188
  417.0 9.9 copy-start.58
  417.0 9.9 copy-start.62
  417.0 9.9 copy-start.60
  417.0 9.9 copy-start.64
  417.0 42.4 %all-to-all-start.3 = ((bf16[4,512,768]{2,1,0:T(8,128)(2,1)}), bf16[4,512,768]{2,1,0:T(8,128)(2,1)}, u32[]{:S(2)}, u32[]{:S(2)}) async-start(bf16[4,512,768]{2,1,0:T(8,128)(2,1)} %bitcast.177), calls=%async_computation.3 | async-start | bytes 6291456 | tf_op jit(solution)/shard_map/all_to_all | solution.py:342
  459.4 44.1 %all-to-all-start.1 = ((bf16[4,512,768]{2,1,0:T(8,128)(2,1)}), bf16[4,512,768]{2,1,0:T(8,128)(2,1)}, u32[]{:S(2)}, u32[]{:S(2)}) async-start(bf16[4,512,768]{2,1,0:T(8,128)(2,1)} %bitcast.26), calls=%async_computation.1 | async-start | bytes 6291456 | tf_op jit(solution)/shard_map/all_to_all | solution.py:263
  465.2 422.6 %reduce-scatter.4.cloned.1.call-start = ((), (), s32[]{:S(2)}) async-start(), calls=%async_computation.10 | async-start | bytes 5529600 | tf_op jit(solution)/shard_map/reduce_scatter | solution.py:422
  532.3 49.2 %copy-start.54 = (s32[1,1024,2]{1,2,0:T(2,128)S(1)}, s32[1,1024,2]{1,2,0:T(2,128)}, u32[]{:S(2)}) copy-start(s32[1,1024,2]{1,2,0:T(2,128)} %param.16) | copy-start | bytes 24580
  532.3 49.2 %copy-start.88 = (s32[2]{0:T(128)S(1)}, s32[2]{0:T(128)}, u32[]{:S(2)}) copy-start(s32[2]{0:T(128)} %iota_add_fusion.1) | copy-start | bytes 28
  532.3 49.6 %copy-start.2 = (bf16[1024,768]{1,0:T(8,128)(2,1)S(1)}, bf16[1024,768]{1,0:T(8,128)(2,1)}, u32[]{:S(2)}) copy-start(bf16[1024,768]{1,0:T(8,128)(2,1)} %copy-done.1) | copy-start | bytes 4718596
  583.1 21.2 %copy-start.49 = (f32[1024,12]{0,1:T(8,128)}, f32[1024,12]{0,1:T(8,128)S(1)}, u32[]{:S(2)}) copy-start(f32[1024,12]{0,1:T(8,128)S(1)} %select_reduce_fusion) | copy-start | bytes 147460
  623.2 31.8 %copy-start.41 = (bf16[512,768]{0,1:T(8,128)(2,1)}, bf16[512,768]{0,1:T(8,128)(2,1)S(1)}, u32[]{:S(2)}) copy-start(bf16[512,768]{0,1:T(8,128)(2,1)S(1)} %get-tuple-element.204) | copy-start | bytes 2359300
  624.2 13.1 %copy-start.11 = (bf16[1024,768]{0,1:T(8,128)(2,1)S(1)}, bf16[1024,768]{0,1:T(8,128)(2,1)}, u32[]{:S(2)}) copy-start(bf16[1024,768]{0,1:T(8,128)(2,1)} %copy-done.10) | copy-start | bytes 4718596
  637.3 17.7 %copy-start.31 = (pred[512,1024]{1,0:T(8,128)(4,1)S(1)}, pred[512,1024]{1,0:T(8,128)(4,1)}, u32[]{:S(2)}) copy-start(pred[512,1024]{1,0:T(8,128)(4,1)} %copy-done.30) | copy-start | bytes 1572868
  676.6 41.7 %copy-start.25 = (bf16[1024,12,32]{0,2,1:T(8,128)(2,1)S(1)}, bf16[1024,12,32]{0,2,1:T(8,128)(2,1)}, u32[]{:S(2)}) copy-start(bf16[1024,12,32]{0,2,1:T(8,128)(2,1)} %copy-done.24) | copy-start | bytes 2359300
  676.6 41.7 %copy-start.28 = (bf16[1024,12,32]{0,2,1:T(8,128)(2,1)S(1)}, bf16[1024,12,32]{0,2,1:T(8,128)(2,1)}, u32[]{:S(2)}) copy-start(bf16[1024,12,32]{0,2,1:T(8,128)(2,1)} %copy-done.27) | copy-start | bytes 2359300
  737.6 13.3 %copy-start.26 = (bf16[1024,12,32]{0,2,1:T(8,128)(2,1)S(1)}, bf16[1024,12,32]{0,2,1:T(8,128)(2,1)}, u32[]{:S(2)}) copy-start(bf16[1024,12,32]{0,2,1:T(8,128)(2,1)} %copy-done.24) | copy-start | bytes 2359300
  737.6 13.3 %copy-start.29 = (bf16[1024,12,32]{0,2,1:T(8,128)(2,1)S(1)}, bf16[1024,12,32]{0,2,1:T(8,128)(2,1)}, u32[]{:S(2)}) copy-start(bf16[1024,12,32]{0,2,1:T(8,128)(2,1)} %copy-done.27) | copy-start | bytes 2359300
  789.2 133.7 %all-reduce.6.cloned.1.call-start = ((), (), s32[]{:S(2)}) async-start(), calls=%async_computation.11 | async-start | bytes 1228800 | tf_op jit(solution)/shard_map/psum | solution.py:423
  887.8 157.0 %reduce-scatter.8.cloned.1.call-start = ((), (), s32[]{:S(2)}) async-start(), calls=%async_computation.13 | async-start | bytes 7077888 | tf_op jit(solution)/shard_map/reduce_scatter | solution.py:358
  888.4 366.9 %reduce-scatter.6.cloned.1.call-start = ((), (), s32[]{:S(2)}) async-start(), calls=%async_computation.12 | async-start | bytes 14155776 | tf_op jit(solution)/shard_map/reduce_scatter | solution.py:361
  (60 other events, 255.8 us)
Sparse Core Ops, SparseCore 0:
  13.4 81.0 all-gather.3
  96.7 174.5 all-gather.5
  273.5 97.3 all-gather.7
  789.3 98.3 reduce-scatter.3
  890.1 32.8 all-reduce.5
  926.8 117.9 reduce-scatter.7
  1048.8 206.4 reduce-scatter.5

commit v2 on v1

--- a/solution.py
+++ b/solution.py
@@ -1,6 +1,10 @@
+import functools
+
 import jax
 import jax.numpy as jnp
 from jax import lax
+from jax.experimental import pallas as pl
+from jax.experimental.pallas import tpu as pltpu
 from jax.sharding import PartitionSpec as P
 
 HEADS = 12
@@ -140,6 +144,482 @@
             * score_scale
         )
     return (jnp.concatenate(query_grads, 0), grad_key, grad_value)
+
+
+MESH = pl.DeviceIdType.MESH
+
+
+def dp_grid(dp_count):
+    outer = 4 if dp_count % 4 == 0 else 1
+    return outer, dp_count // outer
+
+
+def place():
+    me, mine = lax.axis_index("dp"), lax.axis_index("expert")
+    return me, mine
+
+
+def greet(peers):
+    barrier = pltpu.get_barrier_semaphore()
+    for peer in peers:
+        pl.semaphore_signal(barrier, inc=1, device_id=peer, device_id_type=MESH)
+    pl.semaphore_wait(barrier, len(peers))
+
+
+def small_gather_kernel(dp_count, shard_ref, full_ref, send_sem, pass_sem, recv_sem, mate_sem, own_sem):
+    outer_count, inner_count = dp_grid(dp_count)
+    me, mine = place()
+    outer, inner = me // inner_count, me % inner_count
+    rows, columns = shard_ref.shape
+    half = columns // 2
+    side = pl.multiple_of((mine % 2) * half, 128)
+    mate = mine + 1 - 2 * (mine % 2)
+    outer_peers = [lax.rem(outer + k, outer_count) for k in range(1, outer_count)]
+    inner_peers = [lax.rem(inner + k, inner_count) for k in range(1, inner_count)]
+    greet(
+        [(peer * inner_count + inner, mine) for peer in outer_peers]
+        + [(outer * inner_count + peer, mine) for peer in inner_peers]
+        + [(me, mate)]
+    )
+
+    def spot(chunk):
+        return full_ref.at[pl.ds(pl.multiple_of(chunk * rows, 8), rows), pl.ds(side, half)]
+
+    sent = []
+
+    def send(source, chunk, device, send_at, recv_at):
+        copy = pltpu.make_async_remote_copy(
+            src_ref=source,
+            dst_ref=spot(chunk),
+            send_sem=send_at,
+            recv_sem=recv_at,
+            device_id=device,
+            device_id_type=MESH,
+        )
+        copy.start()
+        sent.append(copy)
+
+    def arrived(chunk):
+        pltpu.make_async_copy(spot(chunk), spot(chunk), recv_sem.at[chunk]).wait()
+
+    own_half = shard_ref.at[:, pl.ds(side, half)]
+    for k, peer in enumerate(outer_peers):
+        send(own_half, me, (peer * inner_count + inner, mine), send_sem.at[0, k], recv_sem.at[me])
+    for k, peer in enumerate(inner_peers):
+        send(own_half, me, (outer * inner_count + peer, mine), send_sem.at[1, k], recv_sem.at[me])
+    own = pltpu.make_async_copy(
+        shard_ref, full_ref.at[pl.ds(pl.multiple_of(me * rows, 8), rows), :], own_sem
+    )
+    own.start()
+    chunks = []
+    for k, peer in enumerate(outer_peers):
+        chunk = peer * inner_count + inner
+        arrived(chunk)
+        for j, other in enumerate(inner_peers):
+            send(spot(chunk), chunk, (outer * inner_count + other, mine), send_sem.at[2 + k, j], recv_sem.at[chunk])
+        send(spot(chunk), chunk, (me, mate), pass_sem.at[len(chunks)], mate_sem.at[chunk])
+        chunks.append(chunk)
+    for other in inner_peers:
+        for peer in [outer] + outer_peers:
+            chunk = peer * inner_count + other
+            arrived(chunk)
+            send(spot(chunk), chunk, (me, mate), pass_sem.at[len(chunks)], mate_sem.at[chunk])
+            chunks.append(chunk)
+    own.wait()
+    for chunk in chunks:
+        there = full_ref.at[
+            pl.ds(pl.multiple_of(chunk * rows, 8), rows), pl.ds(pl.multiple_of(half - side, 128), half)
+        ]
+        pltpu.make_async_copy(there, there, mate_sem.at[chunk]).wait()
+    for copy in sent:
+        copy.wait_send()
+
+
+def small_gather(shard, dp_count, collective):
+    outer_count, inner_count = dp_grid(dp_count)
+    rows, columns = shard.shape
+    lanes = max(outer_count, inner_count)
+    return pl.pallas_call(
+        functools.partial(small_gather_kernel, dp_count),
+        out_shape=jax.ShapeDtypeStruct((dp_count * rows, columns), shard.dtype),
+        in_specs=[pl.BlockSpec(memory_space=pl.ANY)],
+        out_specs=pl.BlockSpec(memory_space=pl.ANY),
+        scratch_shapes=[
+            pltpu.SemaphoreType.DMA((outer_count + 1, lanes)),
+            pltpu.SemaphoreType.DMA((dp_count,)),
+            pltpu.SemaphoreType.DMA((dp_count,)),
+            pltpu.SemaphoreType.DMA((dp_count,)),
+            pltpu.SemaphoreType.DMA,
+        ],
+        compiler_params=pltpu.CompilerParams(collective_id=collective, has_side_effects=True),
+        name="small_gather",
+    )(shard)
+
+
+def expert_gather_kernel(dp_count, tensor_count, cuts, crossed, owner_count, trade_count, *refs):
+    given = tensor_count + trade_count
+    shards, outgoing = refs[:tensor_count], refs[tensor_count:given]
+    fulls, incoming = refs[given : given + tensor_count], refs[given + tensor_count : 2 * given]
+    send_sem, recv_sem, own_sem, trade_send, trade_recv = refs[2 * given :]
+    outer_count, inner_count = dp_grid(dp_count)
+    me, mine = place()
+    outer, inner = me // inner_count, me % inner_count
+    below, above = lax.rem(outer + outer_count - 1, outer_count), lax.rem(outer + 1, outer_count)
+    inner_peers = [lax.rem(inner + k, inner_count) for k in range(1, inner_count)]
+    greet(
+        [(peer * inner_count + inner, mine) for peer in (below, above)]
+        + [(outer * inner_count + peer, mine) for peer in inner_peers]
+        + [(me, lax.rem(mine + k, owner_count)) for k in range(1, owner_count) if trade_count]
+    )
+    trades = []
+    for t in range(trade_count):
+        for k in range(1, owner_count):
+            peer = lax.rem(mine + k, owner_count)
+            trade = pltpu.make_async_remote_copy(
+                src_ref=outgoing[t].at[peer],
+                dst_ref=incoming[t].at[mine],
+                send_sem=trade_send.at[t, k],
+                recv_sem=trade_recv.at[t, mine],
+                device_id=(me, peer),
+                device_id_type=MESH,
+            )
+            trade.start()
+            trades.append(trade)
+        keep = pltpu.make_async_copy(
+            outgoing[t].at[mine], incoming[t].at[mine], trade_send.at[t, 0]
+        )
+        keep.start()
+    pieces = [
+        (t, e, c) for t in range(tensor_count) for e in range(shards[t].shape[0]) for c in range(cuts[t])
+    ]
+
+    def spot(p, chunk):
+        t, e, c = pieces[p]
+        rows = shards[t].shape[1]
+        part = rows // cuts[t]
+        return fulls[t].at[e, pl.ds(pl.multiple_of(chunk * rows + c * part, 8), part), :]
+
+    def copy_of(p, source, chunk, device, send_at):
+        return pltpu.make_async_remote_copy(
+            src_ref=source,
+            dst_ref=spot(p, chunk),
+            send_sem=send_at,
+            recv_sem=recv_sem.at[p, chunk],
+            device_id=device,
+            device_id_type=MESH,
+        )
+
+    def source_of(p):
+        t, e, c = pieces[p]
+        part = shards[t].shape[1] // cuts[t]
+        return shards[t].at[e, pl.ds(c * part, part), :]
+
+    def inner_sends(p, source, chunk):
+        return [
+            copy_of(p, source, chunk, (outer * inner_count + peer, mine), send_sem.at[p, 0, j, chunk])
+            for j, peer in enumerate(inner_peers)
+        ]
+
+    def up(p, source, chunk):
+        return copy_of(p, source, chunk, (above * inner_count + inner, mine), send_sem.at[p, 1, 0, chunk])
+
+    def down(p, source, chunk):
+        return copy_of(p, source, chunk, (below * inner_count + inner, mine), send_sem.at[p, 2, 0, chunk])
+
+    def arrived(p, chunk):
+        pltpu.make_async_copy(spot(p, chunk), spot(p, chunk), recv_sem.at[p, chunk]).wait()
+
+    can_up, can_down = outer < outer_count - 1, outer > 0
+    every = range(len(pieces))
+    own = []
+    for p in every:
+        for copy in inner_sends(p, source_of(p), me):
+            copy.start()
+        pl.when(can_up)(lambda p=p: up(p, source_of(p), me).start())
+        pl.when(can_down)(lambda p=p: down(p, source_of(p), me).start())
+        copy = pltpu.make_async_copy(source_of(p), spot(p, me), own_sem.at[p])
+        copy.start()
+        own.append(copy)
+
+    def passing(p, chunk, upward):
+        arrived(p, chunk)
+        if upward:
+            pl.when(can_up)(lambda: up(p, spot(p, chunk), chunk).start())
+        else:
+            pl.when(can_down)(lambda: down(p, spot(p, chunk), chunk).start())
+
+    for p in every:
+        if p in crossed:
+            for peer in inner_peers:
+                chunk = outer * inner_count + peer
+                arrived(p, chunk)
+                pl.when(can_up)(lambda p=p, chunk=chunk: up(p, spot(p, chunk), chunk).start())
+                pl.when(can_down)(lambda p=p, chunk=chunk: down(p, spot(p, chunk), chunk).start())
+    for step in range(1, outer_count):
+        low, high = outer - step, outer + step
+        for p in every:
+            for upward, there, source in ((True, low >= 0, low), (False, high < outer_count, high)):
+
+                def relay(p=p, upward=upward, source=source):
+                    chunk = source * inner_count + inner
+                    passing(p, chunk, upward)
+                    if p in crossed:
+                        for peer in inner_peers:
+                            passing(p, source * inner_count + peer, upward)
+                    else:
+                        for copy in inner_sends(p, spot(p, chunk), chunk):
+                            copy.start()
+
+                pl.when(there)(relay)
+    for t in range(trade_count):
+        pltpu.make_async_copy(
+            outgoing[t].at[mine], incoming[t].at[mine], trade_send.at[t, 0]
+        ).wait()
+        for k in range(1, owner_count):
+            there = incoming[t].at[lax.rem(mine + k, owner_count)]
+            pltpu.make_async_copy(
+                there, there, trade_recv.at[t, lax.rem(mine + k, owner_count)]
+            ).wait()
+    for trade in trades:
+        trade.wait_send()
+    for p in every:
+        own[p].wait()
+        if p not in crossed:
+            for peer in inner_peers:
+                for plane in range(outer_count):
+                    arrived(p, plane * inner_count + peer)
+        for copy in inner_sends(p, source_of(p), me):
+            copy.wait_send()
+        if p not in crossed:
+            for k in range(1, outer_count):
+                chunk = lax.rem(outer + k, outer_count) * inner_count + inner
+                for copy in inner_sends(p, spot(p, chunk), chunk):
+                    copy.wait_send()
+        columns = range(inner_count) if p in crossed else [inner]
+        for plane in range(outer_count):
+            for column in columns:
+                chunk = plane * inner_count + column
+                pl.when(can_up & (outer >= plane))(lambda p=p, chunk=chunk: up(p, spot(p, chunk), chunk).wait_send())
+                pl.when(can_down & (outer <= plane))(lambda p=p, chunk=chunk: down(p, spot(p, chunk), chunk).wait_send())
+
+
+def expert_gather(shards, dp_count, collective, cuts=None, crossed=(), owner_count=1, trades=()):
+    outer_count, inner_count = dp_grid(dp_count)
+    cuts = cuts or [1] * len(shards)
+    piece_count = sum(shard.shape[0] * cut for shard, cut in zip(shards, cuts))
+    anywhere = pl.BlockSpec(memory_space=pl.ANY)
+    given = len(shards) + len(trades)
+    return pl.pallas_call(
+        functools.partial(
+            expert_gather_kernel, dp_count, len(shards), cuts, crossed, owner_count, len(trades)
+        ),
+        out_shape=[
+            jax.ShapeDtypeStruct((s.shape[0], dp_count * s.shape[1], s.shape[2]), s.dtype)
+            for s in shards
+        ]
+        + [jax.ShapeDtypeStruct(t.shape, t.dtype) for t in trades],
+        in_specs=[anywhere] * given,
+        out_specs=[anywhere] * given,
+        scratch_shapes=[
+            pltpu.SemaphoreType.DMA((piece_count, 3, max(1, inner_count - 1), dp_count)),
+            pltpu.SemaphoreType.DMA((piece_count, dp_count)),
+            pltpu.SemaphoreType.DMA((piece_count,)),
+            pltpu.SemaphoreType.DMA((max(1, len(trades)), owner_count)),
+            pltpu.SemaphoreType.DMA((max(1, len(trades)), owner_count)),
+        ],
+        compiler_params=pltpu.CompilerParams(collective_id=collective, has_side_effects=True),
+        name="expert_gather",
+    )(*shards, *trades)
+
+
+def add_into(target, source, target_at, source_at):
+    rows = target.shape[-2]
+    step = 16
+
+    def body(i, carry):
+        here = pl.ds(pl.multiple_of(i * step, step), step)
+        target[target_at + (here, slice(None))] = (
+            target[target_at + (here, slice(None))].astype(jnp.float32)
+            + source(here).astype(jnp.float32)
+        ).astype(target.dtype)
+        return carry
+
+    lax.fori_loop(0, rows // step, body, 0)
+
+
+def final_reduce_kernel(
+    part_ref, small_ref, part_out, small_out,
+    swap, part_in, part_low, part_high, small_in, small_low, small_high, final_low, final_in,
+    swap_send, swap_recv, in_send, in_recv, line_send, line_recv, last_send, last_recv,
+):
+    outer_count, inner_count = 4, 2
+    me, mine = place()
+    outer, inner = me // inner_count, me % inner_count
+    side = mine % 2
+    mate, across = mine + 1 - 2 * side, lax.rem(mine + 2, 4)
+    beside = me + 1 - 2 * inner
+    half_rows = small_ref.shape[1] // 2
+    part_rows = part_ref.shape[1]
+
+    def remote(source, target, device, send_at, recv_at):
+        return pltpu.make_async_remote_copy(
+            src_ref=source,
+            dst_ref=target,
+            send_sem=send_at,
+            recv_sem=recv_at,
+            device_id=device,
+            device_id_type=MESH,
+        )
+
+    barrier = pltpu.get_barrier_semaphore()
+    low_peer = lax.rem(outer + outer_count - 1, outer_count) * inner_count + inner
+    high_peer = lax.rem(outer + 1, outer_count) * inner_count + inner
+    for device in ((me, mate), (me, across), (beside, mine), (low_peer, mine), (high_peer, mine)):
+        pl.semaphore_signal(barrier, inc=1, device_id=device, device_id_type=MESH)
+    pl.semaphore_wait(barrier, 5)
+
+    mate_rows = pl.ds(pl.multiple_of((1 - side) * half_rows, 16), half_rows)
+    own_rows = pl.ds(pl.multiple_of(side * half_rows, 16), half_rows)
+
+    def swap_copy(chunk):
+        return remote(
+            small_ref.at[chunk, mate_rows, :], swap.at[chunk], (me, mate), swap_send.at[chunk], swap_recv.at[chunk]
+        )
+
+    def inner_copy(p, plane):
+        if p == 0:
+            source = part_ref.at[plane * inner_count + 1 - inner]
+            target = part_in.at[plane]
+        else:
+            source = swap.at[plane * inner_count + 1 - inner]
+            target = small_in.at[plane]
+        return remote(source, target, (beside, mine), in_send.at[p, plane], in_recv.at[p, plane])
+
+    ins, lows, highs = (part_in, small_in), (part_low, small_low), (part_high, small_high)
+
+    def line_copy(p, plane, upward, device_plane):
+        target = (lows if upward else highs)[p].at[plane]
+        way = 0 if upward else 1
+        return remote(
+            ins[p].at[plane],
+            target,
+            (device_plane * inner_count + inner, mine),
+            line_send.at[p, way, plane],
+            line_recv.at[p, way, plane],
+        )
+
+    def at_plane(o):
+        order = sorted(range(outer_count), key=lambda t: (-abs(t - o), t))
+        for plane in order:
+            inner_copy(0, plane).start()
+        for plane in order:
+            for column in range(inner_count):
+                swap_copy(plane * inner_count + column).start()
+        for plane in order:
+            for column in range(inner_count):
+                chunk = plane * inner_count + column
+                swap_copy(chunk).wait_recv()
+                add_into(swap, lambda here, chunk=chunk: small_ref[chunk, pl.ds(side * half_rows + here.start, here.size), :], (chunk,), None)
+            inner_copy(1, plane).start()
+        for plane in order:
+            for p in (0, 1):
+                inner_copy(p, plane).wait_recv()
+                if p == 0:
+                    add_into(ins[p], lambda here, plane=plane: part_ref[plane * inner_count + inner, here, :], (plane,), None)
+                else:
+                    add_into(ins[p], lambda here, plane=plane: swap[plane * inner_count + inner, here, :], (plane,), None)
+                if plane > o:
+                    if o > 0:
+                        line_copy(p, plane, True, o + 1).wait_recv()
+                        add_into(ins[p], lambda here, p=p, plane=plane: lows[p][plane, here, :], (plane,), None)
+                    line_copy(p, plane, True, o + 1).start()
+                if plane < o:
+                    if o < outer_count - 1:
+                        line_copy(p, plane, False, o - 1).wait_recv()
+                        add_into(ins[p], lambda here, p=p, plane=plane: highs[p][plane, here, :], (plane,), None)
+                    line_copy(p, plane, False, o - 1).start()
+                if plane == o:
+                    if o > 0:
+                        line_copy(p, plane, True, o).wait_recv()
+                    if o < outer_count - 1:
+                        line_copy(p, plane, False, o).wait_recv()
+                    target = part_out if p == 0 else final_low
+                    rows = target.shape[0]
+
+                    def body(i, carry, p=p, target=target):
+                        here = pl.ds(pl.multiple_of(i * 16, 16), 16)
+                        total = ins[p][o, here, :].astype(jnp.float32)
+                        if o > 0:
+                            total = total + lows[p][o, here, :].astype(jnp.float32)
+                        if o < outer_count - 1:
+                            total = total + highs[p][o, here, :].astype(jnp.float32)
+                        target[here, :] = total.astype(target.dtype)
+                        return carry
+
+                    lax.fori_loop(0, rows // 16, body, 0)
+        for plane in range(outer_count):
+            for p in (0, 1):
+                inner_copy(p, plane).wait_send()
+                if plane > o:
+                    line_copy(p, plane, True, o + 1).wait_send()
+                if plane < o:
+                    line_copy(p, plane, False, o - 1).wait_send()
+            for column in range(inner_count):
+                swap_copy(plane * inner_count + column).wait_send()
+
+    for o in range(outer_count):
+        pl.when(outer == o)(functools.partial(at_plane, o))
+    across_copy = remote(final_low, final_in, (me, across), last_send.at[0], last_recv.at[0])
+    across_copy.start()
+    across_copy.wait()
+
+    def total_body(i, carry):
+        here = pl.ds(pl.multiple_of(i * 16, 16), 16)
+        there = pl.ds(pl.multiple_of(side * half_rows + i * 16, 16), 16)
+        small_out[there, :] = final_low[here, :].astype(jnp.float32) + final_in[here, :].astype(jnp.float32)
+        return carry
+
+    lax.fori_loop(0, half_rows // 16, total_body, 0)
+    mate_copy = remote(
+        small_out.at[own_rows, :], small_out.at[own_rows, :], (me, mate), last_send.at[1], last_recv.at[1]
+    )
+    mate_copy.start()
+    mate_copy.wait()
+
+
+def final_reduce(part, small, collective):
+    chunk_count, part_rows, part_columns = part.shape
+    _, small_rows, small_columns = small.shape
+    low = jnp.bfloat16
+    in_vmem = pl.BlockSpec(memory_space=pltpu.VMEM)
+    half = small_rows // 2
+    return pl.pallas_call(
+        final_reduce_kernel,
+        out_shape=[
+            jax.ShapeDtypeStruct((part_rows, part_columns), jnp.float32),
+            jax.ShapeDtypeStruct((small_rows, small_columns), jnp.float32),
+        ],
+        in_specs=[in_vmem] * 2,
+        out_specs=[in_vmem] * 2,
+        scratch_shapes=[pltpu.VMEM((chunk_count, half, small_columns), low)]
+        + [pltpu.VMEM((4, part_rows, part_columns), low)] * 3
+        + [pltpu.VMEM((4, half, small_columns), low)] * 3
+        + [pltpu.VMEM((half, small_columns), low)] * 2
+        + [
+            pltpu.SemaphoreType.DMA((chunk_count,)),
+            pltpu.SemaphoreType.DMA((chunk_count,)),
+            pltpu.SemaphoreType.DMA((2, 4)),
+            pltpu.SemaphoreType.DMA((2, 4)),
+            pltpu.SemaphoreType.DMA((2, 2, 4)),
+            pltpu.SemaphoreType.DMA((2, 2, 4)),
+            pltpu.SemaphoreType.DMA((2,)),
+            pltpu.SemaphoreType.DMA((2,)),
+        ],
+        compiler_params=pltpu.CompilerParams(
+            collective_id=collective, has_side_effects=True, vmem_limit_bytes=58 * 2**20
+        ),
+        name="final_reduce",
+    )(part, small)
 
 
 def shards(
@@ -168,11 +648,17 @@
     width_out = w_out.shape[1]
     small_parts = [w_router, w_const, v_const, gain_attn[:, None], gain_ffn[:, None]]
     small_width = sum(part.shape[1] for part in small_parts)
-    pad_width = -(width_qkv + width_out + small_width) % 128
+    pad_width = -(width_qkv + width_out + small_width) % 256
     packed = jnp.concatenate(
         [w_qkv, w_out] + small_parts + [jnp.zeros((w_qkv.shape[0], pad_width), jnp.bfloat16)], 1
     )
-    packed_full = lax.all_gather(packed, "dp", axis=0, tiled=True)
+    dp_count = lax.axis_size("dp")
+    owner_count = lax.axis_size("expert")
+    own_links = dp_count == 8 and owner_count == 4
+    if own_links:
+        packed_full = small_gather(packed, dp_count, 1)
+    else:
+        packed_full = lax.all_gather(packed, "dp", axis=0, tiled=True)
     qkv_full = packed_full[:, :width_qkv]
     out_full = packed_full[:, width_qkv : width_qkv + width_out]
     small_full = packed_full[:, width_qkv + width_out :]
@@ -183,14 +669,10 @@
     vector_full = small_full[:, first : first + v_const.shape[1]]
     first = first + v_const.shape[1]
     gain_one, gain_two = small_full[:, first], small_full[:, first + 1]
-    gate_up_full, down_full = (
-        lax.all_gather(w_gate_up, "dp", axis=1, tiled=True),
-        lax.all_gather(w_down, "dp", axis=1, tiled=True),
-    )
+    gate_up_full = lax.all_gather(w_gate_up, "dp", axis=1, tiled=True)
     local_count = gate_up_full.shape[0]
-    owner_count = lax.axis_size("expert")
     expert_count = owner_count * local_count
-    hidden_count = down_full.shape[1]
+    hidden_count = w_down.shape[1] * dp_count
     const_count = vector_full.shape[1]
     gain_first = gain_one.astype(jnp.float32)
     gain_second = gain_two.astype(jnp.float32)
@@ -246,9 +728,24 @@
     zero_row = jnp.zeros((1, model_width), jnp.bfloat16)
     padded_in = jnp.concatenate([normed_low, zero_row], 0)
     send_rows = padded_in[slot_pair // 2].reshape(owner_count, local_count * CAP, model_width)
-    arrived = lax.all_to_all(send_rows, "expert", split_axis=0, concat_axis=0, tiled=True).reshape(
-        owner_count, local_count, CAP, model_width
-    )
+    grad_final = out_grad.reshape(row_count, model_width).astype(jnp.float32)
+    pair_grads = (
+        (gate_weights[:, :, None] * grad_final[:, None, :])
+        .reshape(pair_count, model_width)
+        .astype(jnp.bfloat16)
+    )
+    padded_grad = jnp.concatenate([pair_grads, zero_row], 0)
+    send_grads = padded_grad[slot_pair].reshape(owner_count, local_count * CAP, model_width)
+    if own_links:
+        down_full, arrived, arrived_grad = expert_gather(
+            [w_down], dp_count, 2, owner_count=owner_count, trades=[send_rows, send_grads]
+        )
+    else:
+        down_full = lax.all_gather(w_down, "dp", axis=1, tiled=True)
+        arrived = lax.all_to_all(send_rows, "expert", split_axis=0, concat_axis=0, tiled=True)
+        arrived_grad = lax.all_to_all(send_grads, "expert", split_axis=0, concat_axis=0, tiled=True)
+    arrived = arrived.reshape(owner_count, local_count, CAP, model_width)
+    arrived_grad = arrived_grad.reshape(owner_count, local_count, CAP, model_width)
     gate_up = jnp.einsum(
         "secd,edf->secf", arrived, gate_up_full, preferred_element_type=jnp.float32
     )
@@ -288,7 +785,6 @@
         + jnp.sum(const_weight[:, :, None] * const_val, 1)
     )
     output = (middle + expert_mix).astype(jnp.bfloat16).reshape(tokens.shape)
-    grad_final = out_grad.reshape(row_count, model_width).astype(jnp.float32)
     dot_copy = jnp.sum(grad_final * normed_back, -1)
     dot_const = jnp.sum(grad_final[:, None, :] * const_val, -1)
     grad_gates = (
@@ -314,16 +810,6 @@
         + jnp.sum(grad_const_val * mixing[..., 0:1], 1)
     )
     grad_vector = jnp.dot(grad_final.T, const_weight * mixing[..., 1], precision=highest)
-    pair_grads = (
-        (gate_weights[:, :, None] * grad_final[:, None, :])
-        .reshape(pair_count, model_width)
-        .astype(jnp.bfloat16)
-    )
-    padded_grad = jnp.concatenate([pair_grads, zero_row], 0)
-    send_grads = padded_grad[slot_pair].reshape(owner_count, local_count * CAP, model_width)
-    arrived_grad = lax.all_to_all(
-        send_grads, "expert", split_axis=0, concat_axis=0, tiled=True
-    ).reshape(owner_count, local_count, CAP, model_width)
     grad_down = jnp.einsum(
         "secf,secd->efd", activated, arrived_grad, preferred_element_type=jnp.float32
     )
@@ -358,9 +844,13 @@
     grad_expert_down = lax.psum_scatter(
         grad_down, "dp", scatter_dimension=1, tiled=True
     ).astype(jnp.float32)
-    grad_expert_gu = lax.psum_scatter(
-        grad_expert_gu, "dp", scatter_dimension=1, tiled=True
-    ).astype(jnp.float32)
+    linked = local_count - 1 if own_links else local_count
+    gu_parts = [
+        lax.psum_scatter(grad_expert_gu[e], "dp", scatter_dimension=0, tiled=True).astype(
+            jnp.float32
+        )
+        for e in range(linked)
+    ]
     grad_middle, grad_gain_two = normalize_back(middle, scale_two, gain_second, grad_normed)
     grad_middle = grad_middle + grad_final
     grad_branch = grad_middle.astype(jnp.bfloat16)
@@ -419,8 +909,17 @@
         + [jnp.zeros((model_width, pad_width), jnp.bfloat16)],
         1,
     )
-    packed_part = lax.psum_scatter(packed_grads, "dp", scatter_dimension=0, tiled=True)
-    packed_part = lax.psum(packed_part, "expert").astype(jnp.float32)
+    if own_links:
+        gu_part, packed_part = final_reduce(
+            grad_expert_gu[linked].reshape(dp_count, model_width // dp_count, 2 * hidden_count),
+            packed_grads.reshape(dp_count, model_width // dp_count, packed_grads.shape[1]),
+            3,
+        )
+        gu_parts = gu_parts + [gu_part]
+    else:
+        packed_part = lax.psum_scatter(packed_grads, "dp", scatter_dimension=0, tiled=True)
+        packed_part = lax.psum(packed_part, "expert").astype(jnp.float32)
+    grad_expert_gu = jnp.stack(gu_parts)
     part_qkv = packed_part[:, :width_qkv]
     part_out = packed_part[:, width_qkv : width_qkv + width_out]
     small_part = packed_part[:, width_qkv + width_out :]

time: 1270 us -> 1020 us (0.80)
  waiting for transfers between devices: 617 us -> 22.5 us
  Pallas kernels: 0 us -> 317 us
  local copies, waits for them, and re-layouts: 148 us -> 165 us
    pallas_call x0 -> x3, Pallas kernels: none -> 317 us  [the longest x1 159 us: final_reduce(): pl.pallas_call(final_reduce_kernel, out_shape=[jax.ShapeDtypeStruct((part...]
    reduce_scatter x2 -> x1, waiting for transfers between devices: 307 us -> 0.01 us  [shards(): lax.psum_scatter(grad_expert_gu[e], 'dp', scatter_dimension=0, tiled=True)]
    all_gather x3 -> x1, waiting for transfers between devices: 131 us -> 0.02 us  [shards(): gate_up_full = lax.all_gather(w_gate_up, 'dp', axis=1, tiled=True)]
    reduce_scatter x1, waiting for transfers between devices: 113 us -> 0.01 us  [shards(): lax.psum_scatter(grad_down, 'dp', scatter_dimension=1, tiled=True)]
    psum x1 -> x0, waiting for transfers between devices: 29 us -> none  [shards(): packed_part = lax.psum(packed_part, 'expert').astype(jnp.float32)]
    all_to_all x2 -> x0, waiting for transfers between devices: 15.1 us -> none  [the longest x1 15.1 us: shards(): lax.all_to_all(send_rows, 'expert', split_axis=0, concat_axis=0, tiled=True)]
  transfers between devices with their start and end apart: 11 -> 5, of which waited for: 9 -> 2; matrix products, arithmetic and copies ran while one was open for 21% -> 43% of each run, Pallas kernels for 0% -> 32%
where the time goes in v2:
time: 1020 us; the launch traced here: 1010 us
  Pallas kernels  317 us (31%)
  matrix products  298 us (29%)
  other arithmetic  176 us (17%)
  local copies, waits for them, and re-layouts  165 us (16%)
  waiting for transfers between devices  22.5 us (2%)
  between operations  15.7 us (2%)
  starting transfers between devices  10.5 us (1%)
    pallas_call x1, Pallas kernels, final_reduce(): pl.pallas_call(final_reduce_kernel, out_shape=[jax.ShapeDtypeStruct((part...  159 us
    pallas_call x1, Pallas kernels, expert_gather(): pl.pallas_call(functools.partial(expert_gather_kernel, dp_count, len(shar...  97.9 us
    pallas_call x1, Pallas kernels, small_gather(): pl.pallas_call(functools.partial(small_gather_kernel, dp_count), out_shap...  60 us
    reduce_sum x1, other arithmetic, shards(): grad_mix_first = jnp.sum(grad_const_val * normed_back[:, None, :], -1)  47.9 us
    convert_element_type x1, other arithmetic, attend_backward(): grad_scores = (probs_full * (grad_probs - inner_sum)).astype(jnp.bfloat16)  43.8 us
    dot_general x2, matrix products, attend_backward(): jnp.einsum('qhd,khd->hqk', rows_grad, value_seq, preferred_element_type=j...  35.7 us
    reduce_sum x2, other arithmetic, attend_forward(): row_total = jnp.sum(shifted, -1, keepdims=True)  26.3 us
    dot_general x2, matrix products, attend_backward(): jnp.einsum('hqk,qhd->khd', prob_low, rows_grad, preferred_element_type=jn...  25.9 us
  transfers between devices with their start and end apart: 5, of which 2 were waited for; matrix products, arithmetic and copies ran while one was open for 43% of the time, Pallas kernels for 32%

profile of v2, /device:TPU:19, one launch (start us, length us, event | category | flops | bytes accessed | tf_op | source)
XLA Modules:
  0.0 1005.2 jit_solution(16086643693898776143)
XLA Ops:
  12.3 60.0 %small_gather.1 = bf16[768,3328]{1,0:T(8,128)(2,1)} custom-call(bf16[96,3328]{1,0:T(8,128)(2,1)} %concatenate.64.shard_ref), custom_call_target="tpu_custom_call" | custom-call | tf_op jit(solution)/shard_map/small_gather/pallas_call | solution.py:242
  75.2 6.0 fusion.46
  88.7 4.1 copy.250
  94.5 4.2 subtract_convert_fusion.2
  98.8 11.6 %fusion.25 = (f32[12,512]{1,0:T(8,128)S(1)}, f32[12,512,1024]{2,1,0:T(8,128)}) fusion(pred[512,1024]{1,0:T(8,128)(4,1)S(1)} %get-tuple-element.215, bf16[1024,12,32]{0,2,1:T(8,128)(2,1)S(1)} %get-tuple-element.199, bf16[1024,12,32]{0,2,1:T(8,128)(2,1)S(1)} %get-tuple-element.198, bf16[1024,12,32]{0,2,1:T(8,128)(2,1)S(1)} %get-tuple-element.208, ...), kind=kOutput, calls=%fused_computation.49 | convolution fusion | flops 828893184 | bytes 28860416 | tf_op jit(solution)/shard_map/while/body/eval_jaxpr/qhd,khd->hqk/dot_general | solution.py:80
  110.5 10.8 %fusion.24 = (f32[12,512]{1,0:T(8,128)S(1)}, f32[12,512,1024]{2,1,0:T(8,128)}) fusion(pred[512,1024]{1,0:T(8,128)(4,1)S(1)} %get-tuple-element.214, bf16[1024,12,32]{0,2,1:T(8,128)(2,1)S(1)} %get-tuple-element.199, bf16[1024,12,32]{0,2,1:T(8,128)(2,1)S(1)} %get-tuple-element.198, bf16[1024,12,32]{0,2,1:T(8,128)(2,1)S(1)} %get-tuple-element.209, ...), kind=kOutput, calls=%fused_computation.48 | convolution fusion | flops 828893184 | bytes 28860416 | tf_op jit(solution)/shard_map/while/body/eval_jaxpr/qhd,khd->hqk/dot_general | solution.py:80
  121.3 13.2 %fusion.1 = f32[12,512]{1,0:T(8,128)S(1)} fusion(f32[12,512]{1,0:T(8,128)S(1)} %get-tuple-element.224, f32[12,512,1024]{2,1,0:T(8,128)} %get-tuple-element.225, pred[512,1024]{1,0:T(8,128)(4,1)S(1)} %get-tuple-element.215), kind=kLoop, calls=%fused_computation.19 | loop fusion | flops 25159680 | bytes 25739264 | tf_op jit(solution)/shard_map/while/body/eval_jaxpr/reduce_sum | solution.py:103
  134.5 13.2 %fusion = f32[12,512]{1,0:T(8,128)S(1)} fusion(f32[12,512]{1,0:T(8,128)S(1)} %get-tuple-element.226, f32[12,512,1024]{2,1,0:T(8,128)} %get-tuple-element.227, pred[512,1024]{1,0:T(8,128)(4,1)S(1)} %get-tuple-element.214), kind=kLoop, calls=%fused_computation.18 | loop fusion | flops 25159680 | bytes 25739264 | tf_op jit(solution)/shard_map/while/body/eval_jaxpr/reduce_sum | solution.py:103
  147.8 7.8 fusion.64
  155.6 12.3 %fusion.63 = bf16[512,12,64]{0,2,1:T(8,128)(2,1)S(1)} fusion(bf16[1024,12,64]{0,2,1:T(8,128)(2,1)S(1)} %bitcast.187, f32[12,512]{1,0:T(8,128)S(1)} %fusion, f32[12,512]{1,0:T(8,128)S(1)} %get-tuple-element.226, f32[12,512,1024]{2,1,0:T(8,128)} %get-tuple-element.227, pred[512,1024]{1,0:T(8,128)(4,1)S(1)} %get-tuple-element.214), kind=kOutput, calls=%fused_computation.134 | convolution fusion | flops 837156864 | bytes 28098560 | tf_op jit(solution)/shard_map/while/body/eval_jaxpr/hqk,khd->qhd/dot_general | solution.py:106
  191.4 4.7 mul.650
  196.1 8.5 mul.651
  214.2 8.1 scatter_custom_fusion
  222.3 12.6 %gather_fusion.1 = bf16[2048,768]{1,0:T(8,128)(2,1)} fusion(bf16[2049,768]{1,0:T(8,128)(2,1)} %concatenate.69, s32[2048]{0:T(1024)S(1)} %get-tuple-element.212), kind=kCustom, calls=%fused_computation.1 | custom fusion | bytes 6299648 | tf_op jit(solution)/shard_map/gather | solution.py:738
  234.9 9.4 gather_fusion
  244.3 97.9 %expert_gather.1 = (bf16[2,2048,768]{2,1,0:T(8,128)(2,1)}, bf16[4,512,768]{2,1,0:T(8,128)(2,1)}, bf16[4,512,768]{2,1,0:T(8,128)(2,1)}) custom-call(bf16[2,256,768]{2,1,0:T(8,128)(2,1)} %refs_0_.1, bf16[4,512,768]{2,1,0:T(8,128)(2,1)} %bitcast.196, bf16[4,512,768]{2,1,0:T(8,128)(2,1)} %bitcast.195), custom_call_target="tpu_custom_call" | custom-call | tf_op jit(solution)/shard_map/expert_gather/pallas_call | solution.py:412
  342.2 24.3 %convolution_bitcast_fusion = f32[4,2,256,4096]{3,2,0,1:T(8,128)} fusion(bf16[2,768,4096]{2,1,0:T(8,128)(2,1)} %all-gather.2.cloned.1.call-done, bf16[4,2,256,768]{3,2,1,0:T(8,128)(2,1)} %bitcast.230), kind=kOutput, calls=%fused_computation.34 | convolution fusion | flops 12884901888 | bytes 49283072 | tf_op jit(solution)/shard_map/secd,edf->secf/dot_general | solution.py:749
  366.5 24.4 %fusion.6 = (bf16[4,2,256,2048]{3,2,0,1:T(8,128)(2,1)}, bf16[4,2,256,2048]{3,2,0,1:T(8,128)(2,1)}, bf16[4,2,256,2048]{3,2,0,1:T(8,128)(2,1)}) fusion(f32[4,2,256,4096]{3,2,0,1:T(8,128)} %convolution_bitcast_fusion, bf16[4,2,256,768]{3,2,1,0:T(8,128)(2,1)S(1)} %bitcast.233, bf16[2,2048,768]{2,1,0:T(8,128)(2,1)} %get-tuple-element.71), kind=kOutput, calls=%fused_computation.27 | convolution fusion | flops 6505365504 | bytes 68157440 | tf_op jit(solution)/shard_map/secd,efd->secf/dot_general | solution.py:816
  391.0 19.9 %convert_bitcast_fusion = bf16[4,2,256,768]{3,2,0,1:T(8,128)(2,1)S(1)} fusion(bf16[2,768,4096]{2,1,0:T(8,128)(2,1)} %all-gather.2.cloned.1.call-done, bf16[4,2,256,2048]{3,2,0,1:T(8,128)(2,1)} %get-tuple-element.188, bf16[4,2,256,2048]{3,2,0,1:T(8,128)(2,1)} %get-tuple-element.187), kind=kOutput, calls=%fused_computation.92 | convolution fusion | flops 12920029184 | bytes 32505856 | tf_op jit(solution)/shard_map/secf,edf->secd/dot_general | solution.py:825
  412.8 4.4 all-to-all-start.1
  420.5 10.9 %convert_bitcast_fusion.1 = bf16[4,2,256,768]{3,2,0,1:T(8,128)(2,1)S(1)} fusion(bf16[4,2,256,2048]{3,2,0,1:T(8,128)(2,1)} %get-tuple-element.189, bf16[2,2048,768]{2,1,0:T(8,128)(2,1)} %get-tuple-element.71), kind=kOutput, calls=%fused_computation.96 | convolution fusion | flops 6444023808 | bytes 17825792 | tf_op jit(solution)/shard_map/secf,efd->secd/dot_general | solution.py:757
  433.3 20.0 %all-to-all-done.1 = bf16[4,512,768]{2,1,0:T(8,128)(2,1)S(1)} async-done(((bf16[4,512,768]{2,1,0:T(8,128)(2,1)}), bf16[4,512,768]{2,1,0:T(8,128)(2,1)S(1)}, u32[]{:S(2)}, u32[]{:S(2)}) %all-to-all-start.1) | async-done | bytes 3145760 | tf_op jit(solution)/shard_map/all_to_all | solution.py:828
  455.2 5.6 all-to-all-start
  460.7 12.6 %bitcast_convert_fusion.1 = bf16[2,2048,768]{2,1,0:T(8,128)(2,1)} fusion(bf16[4,2,256,2048]{3,2,0,1:T(8,128)(2,1)} %get-tuple-element.189, bf16[4,2,256,768]{3,2,1,0:T(8,128)(2,1)} %bitcast.232), kind=kOutput, calls=%fused_computation.37 | convolution fusion | flops 6445596672 | bytes 17825792 | tf_op jit(solution)/shard_map/secf,secd->efd/dot_general | solution.py:813
  473.4 19.7 %bitcast_convert_fusion = bf16[2,768,4096]{2,1,0:T(8,128)(2,1)} fusion(bf16[4,2,256,768]{3,2,1,0:T(8,128)(2,1)S(1)} %bitcast.231, bf16[4,2,256,2048]{3,2,0,1:T(8,128)(2,1)} %get-tuple-element.188, bf16[4,2,256,2048]{3,2,0,1:T(8,128)(2,1)} %get-tuple-element.187), kind=kOutput, calls=%fused_computation.5 | convolution fusion | flops 12924747776 | bytes 32505856 | tf_op jit(solution)/shard_map/secd,secf->edf/dot_general | solution.py:822
  500.8 9.4 gather_fusion.3
  510.2 12.6 %gather_fusion.2 = bf16[2048,768]{1,0:T(8,128)(2,1)} fusion(bf16[2049,768]{1,0:T(8,128)(2,1)} %concatenate.70, s32[2048]{0:T(1024)S(1)} %broadcast_clamp_fusion), kind=kCustom, calls=%fused_computation.2 | custom fusion | bytes 6299648 | tf_op jit(solution)/shard_map/gather | solution.py:768
  522.9 8.0 reshape.781
  530.9 47.9 %fusion.26 = (f32[1024,2]{1,0:T(8,128)}, f32[1024,2]{1,0:T(8,128)}, f32[1024,768]{1,0:T(8,128)}, f32[1024,768]{1,0:T(8,128)}, f32[1024,2]{1,0:T(8,128)}, /*index=5*/f32[1024,768]{1,0:T(8,128)}, f32[1024,2]{1,0:T(8,128)}) fusion(f32[1024,768]{1,0:T(8,128)} %convert_element_type.274, f32[1024,2]{1,0:T(8,128)} %copy.260, f32[1024,768]{1,0:T(8,128)S(1)} %copy-done.7, ...), kind=kLoop, calls=%fused_computation.56 | loop fusion | flops 25944064 | bytes 22091776 | tf_op jit(solution)/shard_map/reduce_sum | solution.py:802
  584.3 4.1 fusion.81
  588.4 4.9 reshape.782
  593.3 12.0 %reduce_sum.282 = f32[1024,768]{1,0:T(8,128)} reduce(f32[1024,2,768]{2,1,0:T(2,128)} %reshape.782, f32[]{:T(128)} %constant.151.clone.1), dimensions={1}, to_apply=%region_28.29 | reduce | flops 786432 | bytes 9437188 | tf_op jit(solution)/shard_map/reduce_sum | solution.py:836
  605.3 7.8 add_add_fusion
  613.1 10.6 %slice_bitcast_fusion = (bf16[768,4096]{1,0:T(8,128)(2,1)}, bf16[1,768,4096]{2,1,0:T(8,128)(2,1)}) fusion(bf16[2,768,4096]{2,1,0:T(8,128)(2,1)} %bitcast_convert_fusion), kind=kLoop, calls=%fused_computation.63 | loop fusion | bytes 25165824 | tf_op jit(solution)/shard_map/squeeze | solution.py:849
  630.1 5.8 subtract_add_fusion
  642.1 17.7 %multiply_reduce_fusion.1 = (f32[12,512]{1,0:T(8,128)S(1)}, f32[12,512,1024]{2,1,0:T(8,128)}) fusion(f32[12,512]{1,0:T(8,128)S(1)} %log_add_fusion.1, f32[12,512,1024]{2,1,0:T(8,128)} %get-tuple-element.227, pred[512,1024]{1,0:T(8,128)(4,1)} %copy-done.24, bf16[512,12,64]{0,2,1:T(8,128)(2,1)} %bitcast.200, bf16[1024,12,64]{0,2,1:T(8,128)(2,1)S(1)} %bitcast.188), kind=kOutput, calls=%fused_computation.10 | convolution fusion | flops 836757504 | bytes 53264384 | tf_op jit(solution)/shard_map/while/body/eval_jaxpr/qhd,khd->hqk/dot_general | solution.py:127
  659.8 17.9 %multiply_reduce_fusion = (f32[12,512]{1,0:T(8,128)S(1)}, f32[12,512,1024]{2,1,0:T(8,128)}) fusion(f32[12,512]{1,0:T(8,128)S(1)} %log_add_fusion, f32[12,512,1024]{2,1,0:T(8,128)} %get-tuple-element.225, pred[512,1024]{1,0:T(8,128)(4,1)} %copy-done.10, bf16[512,12,64]{0,2,1:T(8,128)(2,1)} %bitcast.202, bf16[1024,12,64]{0,2,1:T(8,128)(2,1)S(1)} %bitcast.189), kind=kOutput, calls=%fused_computation.7 | convolution fusion | flops 836757504 | bytes 53264384 | tf_op jit(solution)/shard_map/while/body/eval_jaxpr/qhd,khd->hqk/dot_general | solution.py:127
  677.8 43.8 %multiply_convert_fusion = (bf16[12,512,1024]{2,1,0:T(8,128)(2,1)}, bf16[12,512,1024]{2,1,0:T(8,128)(2,1)}) fusion(f32[12,512,1024]{2,1,0:T(8,128)} %get-tuple-element.231, f32[12,512]{1,0:T(8,128)S(1)} %get-tuple-element.230, f32[12,512]{1,0:T(8,128)S(1)} %log_add_fusion, f32[12,512,1024]{2,1,0:T(8,128)} %get-tuple-element.225, ...), kind=kLoop, calls=%fused_computation.6 | loop fusion | flops 75497472 | bytes 126976000 | tf_op jit(solution)/shard_map/while/body/eval_jaxpr/convert_element_type | solution.py:134
  725.7 7.1 fusion.128
  732.9 8.6 multiply_bitcast_fusion.2
  741.4 8.5 multiply_bitcast_fusion.1
  750.0 7.4 multiply_bitcast_fusion
  761.2 12.3 %fusion.11 = f32[12,64,1024]{2,1,0:T(8,128)S(1)} fusion(bf16[512,12,64]{0,2,1:T(8,128)(2,1)S(1)} %bitcast.203, f32[12,512]{1,0:T(8,128)S(1)} %log_add_fusion, f32[12,512,1024]{2,1,0:T(8,128)} %get-tuple-element.225, pred[512,1024]{1,0:T(8,128)(4,1)S(1)} %copy-done.11), kind=kOutput, calls=%fused_computation.35 | convolution fusion | flops 830472192 | bytes 29646848 | tf_op jit(solution)/shard_map/while/body/eval_jaxpr/hqk,qhd->khd/dot_general | solution.py:130
  773.6 13.6 %add_convert_fusion = bf16[12,64,1024]{2,1,0:T(8,128)(2,1)} fusion(f32[12,64,1024]{2,1,0:T(8,128)S(1)} %fusion.11, bf16[512,12,64]{0,2,1:T(8,128)(2,1)S(1)} %bitcast.201, f32[12,512]{1,0:T(8,128)S(1)} %log_add_fusion.1, f32[12,512,1024]{2,1,0:T(8,128)} %get-tuple-element.227, pred[512,1024]{1,0:T(8,128)(4,1)S(1)} %copy-done.25), kind=kOutput, calls=%fused_computation.88 | convolution fusion | flops 832045056 | bytes 31219712 | tf_op jit(solution)/shard_map/while/body/eval_jaxpr/hqk,qhd->khd/dot_general | solution.py:130
  787.2 7.5 fusion.42
  799.8 9.3 convolution_convert_fusion
  809.1 9.5 concatenate.82.small_ref
  818.7 159.4 %final_reduce.1 = (f32[96,4096]{1,0:T(8,128)}, f32[96,3328]{1,0:T(8,128)}) custom-call(bf16[8,96,4096]{2,1,0:T(8,128)(2,1)} %bitcast.185, bf16[8,96,3328]{2,1,0:T(8,128)(2,1)} %concatenate.82.small_ref), custom_call_target="tpu_custom_call" | custom-call | tf_op jit(solution)/shard_map/final_reduce/pallas_call | solution.py:596
  (327 shorter events, 117.7 us)
Async XLA Ops:
  7.2 335.0 %all-gather.2.cloned.1.call-start = ((), (), s32[]{:S(2)}) async-start(), calls=%async_computation.4 | async-start | bytes 14155776 | tf_op jit(solution)/shard_map/all_gather | solution.py:672
  12.3 61.9 %copy-start.26 = (bf16[1,1024,768]{2,1,0:T(8,128)(2,1)S(1)}, bf16[1,1024,768]{2,1,0:T(8,128)(2,1)}, u32[]{:S(2)}) copy-start(bf16[1,1024,768]{2,1,0:T(8,128)(2,1)} %param.14) | copy-start | bytes 4718596
  88.7 66.9 %copy-start.8 = (bf16[1024,768]{0,1:T(8,128)(2,1)}, bf16[1024,768]{0,1:T(8,128)(2,1)S(1)}, u32[]{:S(2)}) copy-start(bf16[1024,768]{0,1:T(8,128)(2,1)S(1)} %copy.249) | copy-start | bytes 4718596
  94.5 53.2 %copy-start.10 = (pred[512,1024]{1,0:T(8,128)(4,1)}, pred[512,1024]{1,0:T(8,128)(4,1)S(1)}, u32[]{:S(2)}) copy-start(pred[512,1024]{1,0:T(8,128)(4,1)S(1)} %get-tuple-element.215) | copy-start | bytes 1572868
  94.5 61.1 %copy-start.24 = (pred[512,1024]{1,0:T(8,128)(4,1)}, pred[512,1024]{1,0:T(8,128)(4,1)S(1)}, u32[]{:S(2)}) copy-start(pred[512,1024]{1,0:T(8,128)(4,1)S(1)} %get-tuple-element.214) | copy-start | bytes 1572868
  98.7 11.7 %copy-start.12 = (bf16[1024,12,32]{0,2,1:T(8,128)(2,1)}, bf16[1024,12,32]{0,2,1:T(8,128)(2,1)S(1)}, u32[]{:S(2)}) copy-start(bf16[1024,12,32]{0,2,1:T(8,128)(2,1)S(1)} %get-tuple-element.208) | copy-start | bytes 2359300
  98.8 11.7 %copy-start.14 = (bf16[1024,12,32]{0,2,1:T(8,128)(2,1)}, bf16[1024,12,32]{0,2,1:T(8,128)(2,1)S(1)}, u32[]{:S(2)}) copy-start(bf16[1024,12,32]{0,2,1:T(8,128)(2,1)S(1)} %get-tuple-element.209) | copy-start | bytes 2359300
  98.8 11.7 %copy-start.20 = (bf16[1024,12,32]{0,2,1:T(8,128)(2,1)}, bf16[1024,12,32]{0,2,1:T(8,128)(2,1)S(1)}, u32[]{:S(2)}) copy-start(bf16[1024,12,32]{0,2,1:T(8,128)(2,1)S(1)} %get-tuple-element.198) | copy-start | bytes 2359300
  98.8 11.7 %copy-start.22 = (bf16[1024,12,32]{0,2,1:T(8,128)(2,1)}, bf16[1024,12,32]{0,2,1:T(8,128)(2,1)S(1)}, u32[]{:S(2)}) copy-start(bf16[1024,12,32]{0,2,1:T(8,128)(2,1)S(1)} %get-tuple-element.199) | copy-start | bytes 2359300
  110.4 37.3 %copy-start.49 = (f32[12,512]{1,0:T(8,128)}, f32[12,512]{1,0:T(8,128)S(1)}, u32[]{:S(2)}) copy-start(f32[12,512]{1,0:T(8,128)S(1)} %get-tuple-element.224) | copy-start | bytes 73732
  121.3 34.3 %copy-start.52 = (f32[12,512]{1,0:T(8,128)}, f32[12,512]{1,0:T(8,128)S(1)}, u32[]{:S(2)}) copy-start(f32[12,512]{1,0:T(8,128)S(1)} %get-tuple-element.226) | copy-start | bytes 73732
  121.3 26.4 %slice-start = ((s8[25165824]{0:T(1024)(128)(4,1)}), s8[4194304]{0:T(1024)(128)(4,1)S(1)}, s32[]{:S(2)}) async-start(s8[25165824]{0:T(1024)(128)(4,1)} %bitcast.183), calls=%async_computation.7 | async-start | bytes 8388608
  121.3 26.4 %slice-start.1 = ((s8[25165824]{0:T(1024)(128)(4,1)}), s8[4194304]{0:T(1024)(128)(4,1)S(1)}, s32[]{:S(2)}) async-start(s8[25165824]{0:T(1024)(128)(4,1)} %bitcast.183), calls=%async_computation.8 | async-start | bytes 8388608
  121.3 26.4 %slice-start.2 = ((s8[25165824]{0:T(1024)(128)(4,1)}), s8[4194304]{0:T(1024)(128)(4,1)S(1)}, s32[]{:S(2)}) async-start(s8[25165824]{0:T(1024)(128)(4,1)} %bitcast.183), calls=%async_computation.9 | async-start | bytes 8388608
  134.5 13.2 %copy-start.56 = (f32[12,512]{1,0:T(8,128)}, f32[12,512]{1,0:T(8,128)S(1)}, u32[]{:S(2)}) copy-start(f32[12,512]{1,0:T(8,128)S(1)} %fusion.1) | copy-start | bytes 73732
  134.5 13.3 %slice-start.3 = ((s8[25165824]{0:T(1024)(128)(4,1)}), s8[4194304]{0:T(1024)(128)(4,1)S(1)}, s32[]{:S(2)}) async-start(s8[25165824]{0:T(1024)(128)(4,1)} %bitcast.183), calls=%async_computation.10 | async-start | bytes 8388608
  134.5 13.3 %slice-start.4 = ((s8[25165824]{0:T(1024)(128)(4,1)}), s8[4194304]{0:T(1024)(128)(4,1)S(1)}, s32[]{:S(2)}) async-start(s8[25165824]{0:T(1024)(128)(4,1)} %bitcast.183), calls=%async_computation.11 | async-start | bytes 8388608
  134.5 13.3 %slice-start.5 = ((s8[25165824]{0:T(1024)(128)(4,1)}), s8[4194304]{0:T(1024)(128)(4,1)S(1)}, s32[]{:S(2)}) async-start(s8[25165824]{0:T(1024)(128)(4,1)} %bitcast.183), calls=%async_computation.12 | async-start | bytes 8388608
  147.7 7.9 copy-start.54
  175.1 31.1 %copy-start = (bf16[1024,768]{1,0:T(8,128)(2,1)}, bf16[1024,768]{1,0:T(8,128)(2,1)S(1)}, u32[]{:S(2)}) copy-start(bf16[1024,768]{1,0:T(8,128)(2,1)S(1)} %get-tuple-element.186) | copy-start | bytes 4718596
  196.1 10.1 %copy-start.66 = (bf16[1,1024,12]{1,2,0:T(8,128)(2,1)S(1)}, bf16[1,1024,12]{1,2,0:T(8,128)(2,1)}, u32[]{:S(2)}) copy-start(bf16[1,1024,12]{1,2,0:T(8,128)(2,1)} %param.15) | copy-start | bytes 73732
  342.2 24.3 %copy-start.86 = (bf16[4,512,768]{2,1,0:T(8,128)(2,1)S(1)}, bf16[4,512,768]{2,1,0:T(8,128)(2,1)}, u32[]{:S(2)}) copy-start(bf16[4,512,768]{2,1,0:T(8,128)(2,1)} %get-tuple-element.73) | copy-start | bytes 9437188
  412.8 40.5 %all-to-all-start.1 = ((bf16[4,512,768]{2,1,0:T(8,128)(2,1)}), bf16[4,512,768]{2,1,0:T(8,128)(2,1)S(1)}, u32[]{:S(2)}, u32[]{:S(2)}) async-start(bf16[4,512,768]{2,1,0:T(8,128)(2,1)} %bitcast.191), calls=%async_computation.1 | async-start | bytes 6291456 | tf_op jit(solution)/shard_map/all_to_all | solution.py:828
  455.2 41.7 %all-to-all-start = ((bf16[4,512,768]{2,1,0:T(8,128)(2,1)}), bf16[4,512,768]{2,1,0:T(8,128)(2,1)}, u32[]{:S(2)}, u32[]{:S(2)}) async-start(bf16[4,512,768]{2,1,0:T(8,128)(2,1)} %bitcast.192), calls=%async_computation | async-start | bytes 6291456 | tf_op jit(solution)/shard_map/all_to_all | solution.py:760
  460.7 12.7 %copy-start.85 = (bf16[4,512,768]{2,1,0:T(8,128)(2,1)S(1)}, bf16[4,512,768]{2,1,0:T(8,128)(2,1)}, u32[]{:S(2)}) copy-start(bf16[4,512,768]{2,1,0:T(8,128)(2,1)} %get-tuple-element.72) | copy-start | bytes 9437188
  460.7 531.6 %reduce-scatter.3.cloned.1.call-start = ((), (), s32[]{:S(2)}) async-start(), calls=%async_computation.5 | async-start | bytes 7077888 | tf_op jit(solution)/shard_map/reduce_scatter | solution.py:849
  522.9 8.0 copy-start.7
  522.9 8.0 copy-start.71
  530.8 53.2 %copy-start.48 = (f32[1024,2]{0,1:T(2,128)S(1)}, f32[1024,2]{0,1:T(2,128)}, u32[]{:S(2)}) copy-start(f32[1024,2]{0,1:T(2,128)} %copy-done.47) | copy-start | bytes 24580
  530.8 53.2 %copy-start.59 = (f32[1024]{0:T(1024)S(1)}, f32[1024]{0:T(1024)}, u32[]{:S(2)}) copy-start(f32[1024]{0:T(1024)} %copy-done.58) | copy-start | bytes 12292
  530.8 53.2 %copy-start.61 = (f32[1024]{0:T(1024)S(1)}, f32[1024]{0:T(1024)}, u32[]{:S(2)}) copy-start(f32[1024]{0:T(1024)} %copy-done.60) | copy-start | bytes 12292
  530.9 53.2 %copy-start.79 = (f32[1024]{0:T(1024)S(1)}, f32[1024]{0:T(1024)}, u32[]{:S(2)}) copy-start(f32[1024]{0:T(1024)} %get-tuple-element.185) | copy-start | bytes 12292
  578.7 9.6 copy-start.19
  584.3 137.3 %copy-start.41 = (f32[1024,12]{0,1:T(8,128)}, f32[1024,12]{0,1:T(8,128)S(1)}, u32[]{:S(2)}) copy-start(f32[1024,12]{0,1:T(8,128)S(1)} %select_reduce_fusion) | copy-start | bytes 147460
  593.3 12.0 %copy-start.3 = (bf16[1,1024,768]{2,1,0:T(8,128)(2,1)S(1)}, bf16[1,1024,768]{2,1,0:T(8,128)(2,1)}, u32[]{:S(2)}) copy-start(bf16[1,1024,768]{2,1,0:T(8,128)(2,1)} %param.27) | copy-start | bytes 4718596
  623.7 372.2 %reduce-scatter.5.cloned.1.call-start = ((), (), s32[]{:S(2)}) async-start(), calls=%async_computation.6 | async-start | bytes 7077888 | tf_op jit(solution)/shard_map/reduce_scatter | solution.py:844
  750.0 7.5 copy-start.38
  750.0 7.5 copy-start.40
  761.1 12.4 %copy-start.25 = (pred[512,1024]{1,0:T(8,128)(4,1)S(1)}, pred[512,1024]{1,0:T(8,128)(4,1)}, u32[]{:S(2)}) copy-start(pred[512,1024]{1,0:T(8,128)(4,1)} %copy-done.24) | copy-start | bytes 1572868
  761.2 12.4 %copy-start.31 = (bf16[512,768]{0,1:T(8,128)(2,1)S(1)}, bf16[512,768]{0,1:T(8,128)(2,1)}, u32[]{:S(2)}) copy-start(bf16[512,768]{0,1:T(8,128)(2,1)} %get-tuple-element.204) | copy-start | bytes 2359300
  761.2 26.0 %slice-start.6 = ((s8[5111808]{0:T(1024)(128)(4,1)}), s8[4194304]{0:T(1024)(128)(4,1)S(1)}, s32[]{:S(2)}) async-start(s8[5111808]{0:T(1024)(128)(4,1)} %bitcast.197), calls=%async_computation.13 | async-start | bytes 8388608
  773.5 13.6 %slice-start.7 = ((s8[5111808]{0:T(1024)(128)(4,1)}), s8[917504]{0:T(1024)(128)(4,1)S(1)}, s32[]{:S(2)}) async-start(s8[5111808]{0:T(1024)(128)(4,1)} %bitcast.197), calls=%async_computation.14 | async-start | bytes 1835008
  773.6 13.6 %copy-start.28 = (bf16[1,1024,768]{2,1,0:T(8,128)(2,1)S(1)}, bf16[1,1024,768]{2,1,0:T(8,128)(2,1)}, u32[]{:S(2)}) copy-start(bf16[1,1024,768]{2,1,0:T(8,128)(2,1)} %param.14) | copy-start | bytes 4718596
  773.6 13.6 %copy-start.73 = (f32[768]{0:T(1024)S(1)}, f32[768]{0:T(1024)}, u32[]{:S(2)}) copy-start(f32[768]{0:T(1024)} %copy-done.72) | copy-start | bytes 9220
  773.6 13.6 %copy-start.76 = (f32[1024]{0:T(1024)S(1)}, f32[1024]{0:T(1024)}, u32[]{:S(2)}) copy-start(f32[1024]{0:T(1024)} %copy-done.75) | copy-start | bytes 12292
  787.2 8.6 copy-start.17
  818.7 169.4 %copy-start.42 = (f32[1024,12]{0,1:T(8,128)S(1)}, f32[1024,12]{0,1:T(8,128)}, u32[]{:S(2)}) copy-start(f32[1024,12]{0,1:T(8,128)} %copy-done.41) | copy-start | bytes 147460
  818.7 170.0 %copy-start.74 = (f32[1024]{0:T(1024)S(1)}, f32[1024]{0:T(1024)}, u32[]{:S(2)}) copy-start(f32[1024]{0:T(1024)} %get-tuple-element.218) | copy-start | bytes 12292
  (53 other events, 183.3 us)
Sparse Core Ops, SparseCore 0:
  10.3 195.4 all-gather.1
  623.8 118.8 reduce-scatter.2
  746.3 130.8 reduce-scatter.4

commit v3 on v2

v3 whole, which is shorter than its diff:
```python
import functools

import jax
import jax.numpy as jnp
import numpy as np
from jax import lax
from jax.experimental import pallas as pl
from jax.experimental.pallas import tpu as pltpu
from jax.sharding import PartitionSpec as P

HEADS = 12
BLOCK = 256
CAP = 256
GROUP = 256
MESH = pl.DeviceIdType.MESH
epsilon = 1e-06


def rotary_lanes(length, head_dim):
    half_dim = head_dim // 2
    frequency = (10000.0 ** (-np.arange(half_dim, dtype=np.float32) / half_dim)).astype(np.float32)
    angles = (np.arange(length, dtype=np.float32)[:, None] * frequency[None, :]).astype(np.float64)
    cosine = np.cos(angles).astype(np.float32)
    sine = np.sin(angles).astype(np.float32)
    return (
        np.concatenate([cosine] * 4, 1),
        np.concatenate([-sine, sine, -sine, sine], 1),
    )


def nt(left, right):
    return lax.dot_general(left, right, (((1,), (1,)), ((), ())), preferred_element_type=jnp.float32)


def tn(left, right):
    return lax.dot_general(left, right, (((0,), (0,)), ((), ())), preferred_element_type=jnp.float32)


def nn(left, right):
    return jnp.dot(left, right, preferred_element_type=jnp.float32)


def lane_ids(shape):
    return lax.broadcasted_iota(jnp.int32, shape, len(shape) - 1)


def turn(values, cosine, sine):
    lanes = lane_ids(values.shape)
    ahead, behind = pltpu.roll(values, 96, 1), pltpu.roll(values, 32, 1)
    return values * cosine + jnp.where(lanes % 64 < 32, ahead, behind) * sine


def key_span(i):
    return max(0, i - 2) * BLOCK, (i + 1) * BLOCK


def mask_of(docs_column, docs_row, i):
    low, high = key_span(i)
    return docs_column[low:high, :] == docs_row[:, i * BLOCK : (i + 1) * BLOCK]


def attention_forward_kernel(
    tokens_ref, wq_ref, wk_ref, wv_ref, wo_ref, small_ref, docs_row_ref, docs_column_ref,
    cosine_ref, sine_ref, routes_ref, resid_ref,
    normed_ref, q_ref, k_ref, v_ref, attended_ref, middle_ref, normed_two_ref, aux_ref,
    branch_ref,
):
    step = pl.program_id(0)
    rows = tokens_ref.shape[0]

    @pl.when(step == 0)
    def _():
        inputs = tokens_ref[...].astype(jnp.float32)
        gains = jnp.transpose(small_ref[:, :128].astype(jnp.float32))[18:19, :]
        scale = lax.rsqrt(jnp.mean(inputs * inputs, -1, keepdims=True) + epsilon)
        normed_ref[...] = (inputs * scale * gains).astype(jnp.bfloat16)
        branch_ref[...] = jnp.zeros_like(branch_ref)

    normed = normed_ref[...]
    cosine, sine = cosine_ref[...], sine_ref[...]
    for w_ref, out_ref, turned in ((wq_ref, q_ref, True), (wk_ref, k_ref, True), (wv_ref, v_ref, False)):
        projected = nn(normed, w_ref[...])
        for half in range(2):
            part = projected[:, half * 128 : half * 128 + 128]
            if turned:
                part = turn(part, cosine, sine)
            out_ref[:, half * 128 : half * 128 + 128] = part.astype(jnp.bfloat16)

    docs_row, docs_column = docs_row_ref[...], docs_column_ref[...]
    for i in range(rows // BLOCK):
        low, high = key_span(i)
        here = slice(i * BLOCK, (i + 1) * BLOCK)
        allowed = mask_of(docs_column, docs_row, i)
        for pair in range(2):
            lanes = slice(pair * 128, pair * 128 + 128)
            queries = q_ref[here, lanes] * jnp.asarray(0.125, jnp.bfloat16)
            keys, values = k_ref[low:high, lanes], v_ref[low:high, lanes]
            left = lane_ids(queries.shape) < 64
            outs = []
            for head in range(2):
                own = left if head == 0 else jnp.logical_not(left)
                scores = nt(keys, jnp.where(own, queries, jnp.zeros_like(queries)))
                scores = jnp.where(allowed, scores, -1e30)
                shifted = jnp.exp(scores - jnp.max(scores, 0, keepdims=True))
                probs = shifted * (1.0 / jnp.sum(shifted, 0, keepdims=True))
                outs.append(tn(probs.astype(jnp.bfloat16), values))
            attended_ref[here, lanes] = jnp.where(left, outs[0], outs[1]).astype(jnp.bfloat16)
    branch_ref[...] += nn(attended_ref[...], wo_ref[...])

    @pl.when(step == pl.num_programs(0) - 1)
    def _():
        small = small_ref[:, :128]
        gains = jnp.transpose(small.astype(jnp.float32))[19:20, :]
        middle = tokens_ref[...].astype(jnp.float32) + branch_ref[...]
        middle_ref[...] = middle
        scale = lax.rsqrt(jnp.mean(middle * middle, -1, keepdims=True) + epsilon)
        normed_two = (middle * scale * gains).astype(jnp.bfloat16)
        normed_two_ref[...] = normed_two
        logits = nn(normed_two, small) + resid_ref[...].astype(jnp.float32)
        lanes = lane_ids(logits.shape)

        def lane(at):
            return jnp.sum(jnp.where(lanes == at, logits, 0.0), -1, keepdims=True)

        def two(first, second):
            peak = jnp.maximum(first, second)
            first, second = jnp.exp(first - peak), jnp.exp(second - peak)
            return first / (first + second), second / (first + second)

        columns = list(two(lane(routes_ref[:, 0:1]), lane(routes_ref[:, 1:2])))
        columns += list(two(lane(12), lane(13))) + list(two(lane(14), lane(15)))
        columns.append(scale)
        aux = jnp.zeros_like(logits)
        for at, column in enumerate(columns):
            aux = jnp.where(lanes == at, column, aux)
        aux_ref[...] = aux


def attention_forward(tokens, packed, docs_row, docs_column, cosine, sine, routes, resid):
    rows, width = tokens.shape
    groups = width // GROUP
    low = jnp.bfloat16
    whole = lambda shape: pl.BlockSpec(shape, lambda j: (0, 0))
    column = lambda at: pl.BlockSpec((width, GROUP), lambda j: (0, at + j))
    out_column = pl.BlockSpec((rows, GROUP), lambda j: (0, j))
    full = jax.ShapeDtypeStruct((rows, width), low)
    return pl.pallas_call(
        attention_forward_kernel,
        grid=(groups,),
        out_shape=[full] * 5
        + [
            jax.ShapeDtypeStruct((rows, width), jnp.float32),
            full,
            jax.ShapeDtypeStruct((rows, 128), jnp.float32),
        ],
        in_specs=[
            whole((rows, width)),
            column(0),
            column(groups),
            column(2 * groups),
            pl.BlockSpec((GROUP, width), lambda j: (j, 3)),
            pl.BlockSpec((width, 256), lambda j: (0, 12)),
            whole((1, rows)),
            whole((rows, 1)),
            whole((rows, 128)),
            whole((rows, 128)),
            whole((rows, 2)),
            whole((rows, 128)),
        ],
        out_specs=[whole((rows, width))]
        + [out_column] * 4
        + [whole((rows, width)), whole((rows, width)), whole((rows, 128))],
        scratch_shapes=[pltpu.VMEM((rows, width), jnp.float32)],
        compiler_params=pltpu.CompilerParams(
            dimension_semantics=("arbitrary",), vmem_limit_bytes=56 * 2**20
        ),
        cost_estimate=pl.CostEstimate(
            flops=2 * rows * width * 4 * width + 8 * rows * rows * width // 2,
            bytes_accessed=24 * rows * width,
            transcendentals=rows * rows * HEADS // 2,
        ),
        name="attention_forward",
    )(tokens, packed, packed, packed, packed, packed, docs_row, docs_column, cosine, sine, routes, resid)


def attention_backward_kernel(
    grad_middle_ref, q_ref, k_ref, v_ref, attended_ref, normed_ref, tokens_ref,
    wq_ref, wk_ref, wv_ref, wo_ref, small_ref, docs_row_ref, docs_column_ref,
    cosine_ref, sine_ref, small_grad_ref,
    token_grad_ref, gq_ref, gk_ref, gv_ref, go_ref, small_out_ref,
    branch_ref, back_ref, turned_ref, key_acc, value_acc, query_acc,
):
    step = pl.program_id(0)
    rows, width = tokens_ref.shape

    @pl.when(step == 0)
    def _():
        branch_ref[...] = grad_middle_ref[...].astype(jnp.bfloat16)
        back_ref[...] = jnp.zeros_like(back_ref)

    grad_branch = branch_ref[...]
    grad_attended = nt(grad_branch, wo_ref[...]).astype(jnp.bfloat16)
    go_ref[...] = tn(attended_ref[...], grad_branch).astype(jnp.bfloat16)
    cosine, sine = cosine_ref[...], sine_ref[...]
    docs_row, docs_column = docs_row_ref[...], docs_column_ref[...]
    for pair in range(2):
        lanes = slice(pair * 128, pair * 128 + 128)
        key_acc[...] = jnp.zeros_like(key_acc)
        value_acc[...] = jnp.zeros_like(value_acc)
        for i in range(rows // BLOCK):
            low, high = key_span(i)
            here = slice(i * BLOCK, (i + 1) * BLOCK)
            allowed = mask_of(docs_column, docs_row, i)
            queries = q_ref[here, lanes] * jnp.asarray(0.125, jnp.bfloat16)
            grads = grad_attended[here, lanes]
            keys, values = k_ref[low:high, lanes], v_ref[low:high, lanes]
            left = lane_ids(queries.shape) < 64
            query_grads = []
            key_grad, value_grad = None, None
            for head in range(2):
                own = left if head == 0 else jnp.logical_not(left)
                own_queries = jnp.where(own, queries, jnp.zeros_like(queries))
                own_grads = jnp.where(own, grads, jnp.zeros_like(grads))
                scores = jnp.where(allowed, nt(keys, own_queries), -1e30)
                shifted = jnp.exp(scores - jnp.max(scores, 0, keepdims=True))
                probs = shifted * (1.0 / jnp.sum(shifted, 0, keepdims=True))
                grad_probs = nt(values, own_grads)
                inner = jnp.sum(probs * grad_probs, 0, keepdims=True)
                grad_scores = (probs * (grad_probs - inner)).astype(jnp.bfloat16)
                part_value = nn(probs.astype(jnp.bfloat16), own_grads)
                part_key = nn(grad_scores, own_queries)
                value_grad = part_value if head == 0 else value_grad + part_value
                key_grad = part_key if head == 0 else key_grad + part_key
                query_grads.append(tn(grad_scores, keys))
            value_acc[low:high, :] += value_grad
            key_acc[low:high, :] += key_grad
            query_acc[here, :] = jnp.where(left, query_grads[0], query_grads[1]) * 0.125
        turned_ref[0, :, lanes] = turn(query_acc[...], cosine, -sine).astype(jnp.bfloat16)
        turned_ref[1, :, lanes] = turn(key_acc[...], cosine, -sine).astype(jnp.bfloat16)
        turned_ref[2, :, lanes] = value_acc[...].astype(jnp.bfloat16)
    normed = normed_ref[...]
    for at, (w_ref, out_ref) in enumerate(((wq_ref, gq_ref), (wk_ref, gk_ref), (wv_ref, gv_ref))):
        turned = turned_ref[at]
        out_ref[...] = tn(normed, turned).astype(jnp.bfloat16)
        back_ref[...] += nt(turned, w_ref[...])

    @pl.when(step == pl.num_programs(0) - 1)
    def _():
        gains = jnp.transpose(small_ref[:, :128].astype(jnp.float32))[18:19, :]
        inputs = tokens_ref[...].astype(jnp.float32)
        grads = back_ref[...]
        scale = lax.rsqrt(jnp.mean(inputs * inputs, -1, keepdims=True) + epsilon)
        weighted = grads * gains
        mean = jnp.mean(weighted * inputs, -1, keepdims=True)
        grad_inputs = scale * weighted - inputs * (scale * scale * scale * mean)
        token_grad_ref[...] = (grad_inputs + grad_middle_ref[...]).astype(jnp.bfloat16)
        gain_grad = jnp.sum(grads * inputs * scale, 0, keepdims=True)
        column = jnp.transpose(jnp.broadcast_to(gain_grad, (128, width)))
        small_grad = small_grad_ref[...]
        small_grad = jnp.where(lane_ids(small_grad.shape) == 18, column, small_grad)
        small_out_ref[:, :128] = small_grad.astype(jnp.bfloat16)
        small_out_ref[:, 128:] = jnp.zeros((width, 128), jnp.bfloat16)


def attention_backward(
    grad_middle, queries, keys, values, attended, normed, tokens, packed, docs_row, docs_column,
    cosine, sine, small_grad,
):
    rows, width = tokens.shape
    groups = width // GROUP
    low = jnp.bfloat16
    whole = lambda shape: pl.BlockSpec(shape, lambda j: (0, 0))
    column = lambda at: pl.BlockSpec((width, GROUP), lambda j: (0, at + j))
    by_group = pl.BlockSpec((rows, GROUP), lambda j: (0, j))
    weight = jax.ShapeDtypeStruct((width, width), low)
    return pl.pallas_call(
        attention_backward_kernel,
        grid=(groups,),
        out_shape=[jax.ShapeDtypeStruct((rows, width), low)]
        + [weight] * 4
        + [jax.ShapeDtypeStruct((width, 256), low)],
        in_specs=[
            whole((rows, width)),
            by_group,
            by_group,
            by_group,
            by_group,
            whole((rows, width)),
            whole((rows, width)),
            column(0),
            column(groups),
            column(2 * groups),
            pl.BlockSpec((GROUP, width), lambda j: (j, 3)),
            pl.BlockSpec((width, 256), lambda j: (0, 12)),
            whole((1, rows)),
            whole((rows, 1)),
            whole((rows, 128)),
            whole((rows, 128)),
            whole((width, 128)),
        ],
        out_specs=[
            whole((rows, width)),
            column(0),
            column(0),
            column(0),
            pl.BlockSpec((GROUP, width), lambda j: (j, 0)),
            whole((width, 256)),
        ],
        scratch_shapes=[
            pltpu.VMEM((rows, width), low),
            pltpu.VMEM((rows, width), jnp.float32),
            pltpu.VMEM((3, rows, GROUP), low),
            pltpu.VMEM((rows, 128), jnp.float32),
            pltpu.VMEM((rows, 128), jnp.float32),
            pltpu.VMEM((rows, 128), jnp.float32),
        ],
        compiler_params=pltpu.CompilerParams(
            dimension_semantics=("arbitrary",), vmem_limit_bytes=56 * 2**20
        ),
        cost_estimate=pl.CostEstimate(
            flops=4 * rows * width * 4 * width + 20 * rows * rows * width // 2,
            bytes_accessed=32 * rows * width,
            transcendentals=rows * rows * HEADS // 2,
        ),
        name="attention_backward",
    )(
        grad_middle, queries, keys, values, attended, normed, tokens, packed, packed, packed,
        packed, packed, docs_row, docs_column, cosine, sine, small_grad,
    )


def routing_kernel(expert_count, routes_ref, columns_ref, rows_ref):
    rows = routes_ref.shape[0]
    lanes = lane_ids((rows, 128))
    first = (lanes == routes_ref[:, 0:1]).astype(jnp.float32)
    second = (lanes == routes_ref[:, 1:2]).astype(jnp.float32)
    down = lax.broadcasted_iota(jnp.int32, (rows, rows), 0)
    lower = (down > lane_ids((rows, rows))).astype(jnp.bfloat16)
    before_first = nn(lower, first.astype(jnp.bfloat16))
    before_second = nn(lower, second.astype(jnp.bfloat16)) + jnp.sum(first, 0, keepdims=True)
    spots = []
    for picked, before, at in ((first, before_first, 0), (second, before_second, 1)):
        rank = jnp.sum(picked * before, -1, keepdims=True)
        route = routes_ref[:, at : at + 1]
        spot = route.astype(jnp.float32) * CAP + rank
        spots.append(jnp.where(route < expert_count, spot, jnp.full_like(spot, 2.0 * expert_count * CAP)))
    both = jnp.where(lanes == 0, spots[0], jnp.where(lanes == 1, spots[1], 0.0))
    columns_ref[...] = both.astype(jnp.int32)
    rows_ref[...] = jnp.transpose(both)[0:8, :].astype(jnp.int32)


def routing(routes, expert_count):
    rows = routes.shape[0]
    return pl.pallas_call(
        functools.partial(routing_kernel, expert_count),
        out_shape=[
            jax.ShapeDtypeStruct((rows, 128), jnp.int32),
            jax.ShapeDtypeStruct((8, rows), jnp.int32),
        ],
        compiler_params=pltpu.CompilerParams(vmem_limit_bytes=40 * 2**20),
        name="routing",
    )(routes)


def dispatch_kernel(spots_ref, aux_ref, normed_ref, cot_ref, rows_ref, grads_ref, gates_ref):
    step = pl.program_id(0)

    @pl.when(step == 0)
    def _():
        gates_ref[...] = jnp.transpose(aux_ref[...])[0:8, :]

    shape = (rows_ref.shape[0], normed_ref.shape[0])
    slots = step * rows_ref.shape[0] + lax.broadcasted_iota(jnp.int32, shape, 0)
    first, second = slots == spots_ref[0:1, :], slots == spots_ref[1:2, :]
    gates = jnp.sum(
        jnp.where(first, gates_ref[0:1, :], jnp.where(second, gates_ref[1:2, :], 0.0)), -1, keepdims=True
    )
    chosen = jnp.where(first | second, 1.0, 0.0).astype(jnp.bfloat16)
    rows_ref[...] = nn(chosen, normed_ref[...]).astype(jnp.bfloat16)
    grads_ref[...] = (nn(chosen, cot_ref[...]) * gates).astype(jnp.bfloat16)


def dispatch(spots, aux, normed, cot, slot_count):
    rows, width = normed.shape
    whole = lambda shape: pl.BlockSpec(shape, lambda j: (0, 0))
    block = pl.BlockSpec((CAP, width), lambda j: (j, 0))
    return pl.pallas_call(
        dispatch_kernel,
        grid=(slot_count // CAP,),
        out_shape=[jax.ShapeDtypeStruct((slot_count, width), jnp.bfloat16)] * 2,
        in_specs=[whole((8, rows)), whole((rows, 128)), whole((rows, width)), whole((rows, width))],
        out_specs=[block, block],
        scratch_shapes=[pltpu.VMEM((8, rows), jnp.float32)],
        compiler_params=pltpu.CompilerParams(
            dimension_semantics=("arbitrary",), vmem_limit_bytes=40 * 2**20
        ),
        cost_estimate=pl.CostEstimate(
            flops=4 * slot_count * rows * width,
            bytes_accessed=4 * (rows + slot_count) * width,
            transcendentals=0,
        ),
        name="dispatch",
    )(spots, aux, normed, cot)


def halves(values):
    high = values.astype(jnp.bfloat16)
    return high, (values - high.astype(jnp.float32)).astype(jnp.bfloat16)


def combine_kernel(
    expert_count, returned_ref, spots_ref, routes_ref, aux_ref, normed_ref, middle_ref, cot_ref, small_ref,
    output_ref, logit_ref, grad_ref, small_grad_ref, vectors_ref,
):
    step = pl.program_id(0)

    @pl.when(step == 0)
    def _():
        vectors_ref[...] = jnp.transpose(small_ref[:, :128].astype(jnp.float32))[16:24, :]
        small_grad_ref[...] = jnp.zeros_like(small_grad_ref)

    rows = normed_ref.shape[0]
    slots = lane_ids((rows, returned_ref.shape[0]))
    returned = returned_ref[...]
    normed_low, cot_low = normed_ref[...], cot_ref[...]
    normed, cot = normed_low.astype(jnp.float32), cot_low.astype(jnp.float32)
    total = lambda values: jnp.sum(values, -1, keepdims=True)
    picks, inner = [], []
    for s in range(2):
        chosen = jnp.where(slots == spots_ref[:, s : s + 1], 1.0, 0.0).astype(jnp.bfloat16)
        pick = nn(chosen, returned)
        picks.append(pick)
        inner.append(total(pick * cot))
    gates = [aux_ref[:, s : s + 1] for s in range(2)]
    routes = [routes_ref[:, s : s + 1] for s in range(2)]
    dot_copy = total(cot * normed)

    def weight_of(route):
        return sum(jnp.where(routes[s] == route, gates[s], 0.0) for s in range(2))

    copy_weight = weight_of(expert_count + 1)
    mix = gates[0] * picks[0] + gates[1] * picks[1]
    pass_weight = copy_weight
    gate_grads = [
        inner[s] + jnp.where(routes[s] == expert_count + 1, dot_copy, 0.0) for s in range(2)
    ]
    lanes = lane_ids((rows, 128))
    spread = jnp.zeros((rows, 128), jnp.float32)
    for k in range(2):
        vector = vectors_ref[k : k + 1, :]
        keep, blend = aux_ref[:, 2 + 2 * k : 3 + 2 * k], aux_ref[:, 3 + 2 * k : 4 + 2 * k]
        weight = weight_of(expert_count + 2 + k)
        dot_vector = total(cot * vector)
        pass_weight = pass_weight + weight * keep
        mix = mix + (weight * blend) * vector
        value = keep * dot_copy + blend * dot_vector
        for s in range(2):
            gate_grads[s] = gate_grads[s] + jnp.where(routes[s] == expert_count + 2 + k, value, 0.0)
        term = keep * blend * (weight * dot_copy - weight * dot_vector)
        spread = jnp.where(lanes == 12 + 2 * k, term, spread)
        spread = jnp.where(lanes == 13 + 2 * k, -term, spread)
        spread = jnp.where(lanes == 16 + k, weight * blend, spread)
    mix = mix + pass_weight * normed
    output_ref[...] = (middle_ref[...] + mix).astype(jnp.bfloat16)
    mean = gates[0] * gate_grads[0] + gates[1] * gate_grads[1]
    for s in range(2):
        spread = jnp.where(lanes == routes[s], gates[s] * (gate_grads[s] - mean), spread)
    logit_ref[...] = spread[:, : logit_ref.shape[1]].astype(jnp.bfloat16)
    logits = jnp.where(lanes < 16, spread, 0.0)
    high, low = halves(logits)
    small = small_ref[:, :128]
    grad_ref[...] = pass_weight * cot + nt(high, small) + nt(low, small)
    vector_high, vector_low = halves(spread - logits)
    small_grad_ref[...] += (
        tn(normed_low, high) + tn(normed_low, low) + tn(cot_low, vector_high) + tn(cot_low, vector_low)
    )


def combine(returned, spots, routes, aux, normed, middle, cot, packed, choice_count, expert_count):
    rows, width = normed.shape
    slot_count = returned.shape[0]
    size = 256
    block = lambda columns: pl.BlockSpec((size, columns), lambda j: (j, 0))
    whole = lambda shape: pl.BlockSpec(shape, lambda j: (0, 0))
    return pl.pallas_call(
        functools.partial(combine_kernel, expert_count),
        grid=(rows // size,),
        out_shape=[
            jax.ShapeDtypeStruct((rows, width), jnp.bfloat16),
            jax.ShapeDtypeStruct((rows, choice_count), jnp.bfloat16),
            jax.ShapeDtypeStruct((rows, width), jnp.float32),
            jax.ShapeDtypeStruct((width, 128), jnp.float32),
        ],
        in_specs=[
            whole((slot_count, width)),
            block(128),
            block(2),
            block(128),
            block(width),
            block(width),
            block(width),
            pl.BlockSpec((width, 256), lambda j: (0, 12)),
        ],
        out_specs=[block(width), block(choice_count), block(width), whole((width, 128))],
        scratch_shapes=[pltpu.VMEM((8, width), jnp.float32)],
        compiler_params=pltpu.CompilerParams(
            dimension_semantics=("arbitrary",), vmem_limit_bytes=48 * 2**20
        ),
        cost_estimate=pl.CostEstimate(
            flops=4 * slot_count * rows * width,
            bytes_accessed=16 * rows * width + 2 * slot_count * width,
            transcendentals=0,
        ),
        name="combine",
    )(returned, spots, routes, aux, normed, middle, cot, packed)


def combine_back_kernel(
    back_ref, spots_ref, aux_ref, middle_ref, cot_ref, grad_ref, small_ref, small_grad_ref,
    grad_middle_ref, small_out_ref, gain_ref,
):
    step = pl.program_id(0)

    @pl.when(step == 0)
    def _():
        gain_ref[0:8, :] = jnp.transpose(small_ref[:, :128].astype(jnp.float32))[16:24, :]
        gain_ref[8:16, :] = jnp.zeros((8, gain_ref.shape[1]), jnp.float32)

    rows, width = middle_ref.shape
    slots = lane_ids((rows, back_ref.shape[0]))
    chosen = jnp.where(
        (slots == spots_ref[:, 0:1]) | (slots == spots_ref[:, 1:2]), 1.0, 0.0
    ).astype(jnp.bfloat16)
    grads = grad_ref[...] + nn(chosen, back_ref[...])
    middle, scale = middle_ref[...], aux_ref[:, 6:7]
    gain_ref[8:9, :] += jnp.sum(grads * middle * scale, 0, keepdims=True)
    weighted = grads * gain_ref[3:4, :]
    mean = jnp.mean(weighted * middle, -1, keepdims=True)
    grad_middle_ref[...] = (
        cot_ref[...].astype(jnp.float32) + scale * weighted - middle * (scale * scale * scale * mean)
    )

    @pl.when(step == pl.num_programs(0) - 1)
    def _():
        column = jnp.transpose(jnp.broadcast_to(gain_ref[8:9, :], (128, width)))
        small_grad = small_grad_ref[...]
        small_out_ref[...] = jnp.where(lane_ids(small_grad.shape) == 19, column, small_grad)


def combine_back(back, spots, aux, middle, cot, grad, packed, small_grad):
    rows, width = middle.shape
    slot_count = back.shape[0]
    size = 256
    block = lambda columns: pl.BlockSpec((size, columns), lambda j: (j, 0))
    whole = lambda shape: pl.BlockSpec(shape, lambda j: (0, 0))
    return pl.pallas_call(
        combine_back_kernel,
        grid=(rows // size,),
        out_shape=[
            jax.ShapeDtypeStruct((rows, width), jnp.float32),
            jax.ShapeDtypeStruct((width, 128), jnp.float32),
        ],
        in_specs=[
            whole((slot_count, width)),
            block(128),
            block(128),
            block(width),
            block(width),
            block(width),
            pl.BlockSpec((width, 256), lambda j: (0, 12)),
            whole((width, 128)),
        ],
        out_specs=[block(width), whole((width, 128))],
        scratch_shapes=[pltpu.VMEM((16, width), jnp.float32)],
        compiler_params=pltpu.CompilerParams(
            dimension_semantics=("arbitrary",), vmem_limit_bytes=48 * 2**20
        ),
        cost_estimate=pl.CostEstimate(
            flops=2 * slot_count * rows * width,
            bytes_accessed=14 * rows * width + 2 * slot_count * width,
            transcendentals=0,
        ),
        name="combine_back",
    )(back, spots, aux, middle, cot, grad, packed, small_grad)


def dp_grid(dp_count):
    outer = 4 if dp_count % 4 == 0 else 1
    return outer, dp_count // outer


def place():
    me, mine = lax.axis_index("dp"), lax.axis_index("expert")
    return me, mine


def greet(peers):
    barrier = pltpu.get_barrier_semaphore()
    for peer in peers:
        pl.semaphore_signal(barrier, inc=1, device_id=peer, device_id_type=MESH)
    pl.semaphore_wait(barrier, len(peers))


def small_gather_kernel(dp_count, shard_ref, full_ref, send_sem, pass_sem, recv_sem, mate_sem, own_sem):
    outer_count, inner_count = dp_grid(dp_count)
    me, mine = place()
    outer, inner = me // inner_count, me % inner_count
    rows, columns = shard_ref.shape
    half = columns // 2
    side = pl.multiple_of((mine % 2) * half, 128)
    mate = mine + 1 - 2 * (mine % 2)
    outer_peers = [lax.rem(outer + k, outer_count) for k in range(1, outer_count)]
    inner_peers = [lax.rem(inner + k, inner_count) for k in range(1, inner_count)]
    greet(
        [(peer * inner_count + inner, mine) for peer in outer_peers]
        + [(outer * inner_count + peer, mine) for peer in inner_peers]
        + [(me, mate)]
    )

    def spot(chunk):
        return full_ref.at[pl.ds(pl.multiple_of(chunk * rows, 8), rows), pl.ds(side, half)]

    sent = []

    def send(source, chunk, device, send_at, recv_at):
        copy = pltpu.make_async_remote_copy(
            src_ref=source,
            dst_ref=spot(chunk),
            send_sem=send_at,
            recv_sem=recv_at,
            device_id=device,
            device_id_type=MESH,
        )
        copy.start()
        sent.append(copy)

    def arrived(chunk):
        pltpu.make_async_copy(spot(chunk), spot(chunk), recv_sem.at[chunk]).wait()

    own_half = shard_ref.at[:, pl.ds(side, half)]
    for k, peer in enumerate(outer_peers):
        send(own_half, me, (peer * inner_count + inner, mine), send_sem.at[0, k], recv_sem.at[me])
    for k, peer in enumerate(inner_peers):
        send(own_half, me, (outer * inner_count + peer, mine), send_sem.at[1, k], recv_sem.at[me])
    own = pltpu.make_async_copy(
        shard_ref, full_ref.at[pl.ds(pl.multiple_of(me * rows, 8), rows), :], own_sem
    )
    own.start()
    chunks = []
    for k, peer in enumerate(outer_peers):
        chunk = peer * inner_count + inner
        arrived(chunk)
        for j, other in enumerate(inner_peers):
            send(spot(chunk), chunk, (outer * inner_count + other, mine), send_sem.at[2 + k, j], recv_sem.at[chunk])
        send(spot(chunk), chunk, (me, mate), pass_sem.at[len(chunks)], mate_sem.at[chunk])
        chunks.append(chunk)
    for other in inner_peers:
        for peer in [outer] + outer_peers:
            chunk = peer * inner_count + other
            arrived(chunk)
            send(spot(chunk), chunk, (me, mate), pass_sem.at[len(chunks)], mate_sem.at[chunk])
            chunks.append(chunk)
    own.wait()
    for chunk in chunks:
        there = full_ref.at[
            pl.ds(pl.multiple_of(chunk * rows, 8), rows), pl.ds(pl.multiple_of(half - side, 128), half)
        ]
        pltpu.make_async_copy(there, there, mate_sem.at[chunk]).wait()
    for copy in sent:
        copy.wait_send()


def small_gather(shard, dp_count, collective):
    outer_count, inner_count = dp_grid(dp_count)
    rows, columns = shard.shape
    lanes = max(outer_count, inner_count)
    return pl.pallas_call(
        functools.partial(small_gather_kernel, dp_count),
        out_shape=jax.ShapeDtypeStruct((dp_count * rows, columns), shard.dtype),
        in_specs=[pl.BlockSpec(memory_space=pl.ANY)],
        out_specs=pl.BlockSpec(memory_space=pl.ANY),
        scratch_shapes=[
            pltpu.SemaphoreType.DMA((outer_count + 1, lanes)),
            pltpu.SemaphoreType.DMA((dp_count,)),
            pltpu.SemaphoreType.DMA((dp_count,)),
            pltpu.SemaphoreType.DMA((dp_count,)),
            pltpu.SemaphoreType.DMA,
        ],
        compiler_params=pltpu.CompilerParams(collective_id=collective, has_side_effects=True),
        name="small_gather",
    )(shard)


def expert_gather_kernel(dp_count, tensor_count, cuts, crossed, owner_count, trade_count, *refs):
    given = tensor_count + trade_count
    shards, outgoing = refs[:tensor_count], refs[tensor_count:given]
    fulls, incoming = refs[given : given + tensor_count], refs[given + tensor_count : 2 * given]
    send_sem, recv_sem, own_sem, trade_send, trade_recv = refs[2 * given :]
    outer_count, inner_count = dp_grid(dp_count)
    me, mine = place()
    outer, inner = me // inner_count, me % inner_count
    below, above = lax.rem(outer + outer_count - 1, outer_count), lax.rem(outer + 1, outer_count)
    inner_peers = [lax.rem(inner + k, inner_count) for k in range(1, inner_count)]
    greet(
        [(peer * inner_count + inner, mine) for peer in (below, above)]
        + [(outer * inner_count + peer, mine) for peer in inner_peers]
        + [(me, lax.rem(mine + k, owner_count)) for k in range(1, owner_count) if trade_count]
    )
    trades = []
    for t in range(trade_count):
        for k in range(1, owner_count):
            peer = lax.rem(mine + k, owner_count)
            trade = pltpu.make_async_remote_copy(
                src_ref=outgoing[t].at[peer],
                dst_ref=incoming[t].at[mine],
                send_sem=trade_send.at[t, k],
                recv_sem=trade_recv.at[t, mine],
                device_id=(me, peer),
                device_id_type=MESH,
            )
            trade.start()
            trades.append(trade)
        keep = pltpu.make_async_copy(
            outgoing[t].at[mine], incoming[t].at[mine], trade_send.at[t, 0]
        )
        keep.start()
    pieces = [
        (t, e, c) for t in range(tensor_count) for e in range(shards[t].shape[0]) for c in range(cuts[t])
    ]

    def spot(p, chunk):
        t, e, c = pieces[p]
        rows = shards[t].shape[1]
        part = rows // cuts[t]
        return fulls[t].at[e, pl.ds(pl.multiple_of(chunk * rows + c * part, 8), part), :]

    def copy_of(p, source, chunk, device, send_at):
        return pltpu.make_async_remote_copy(
            src_ref=source,
            dst_ref=spot(p, chunk),
            send_sem=send_at,
            recv_sem=recv_sem.at[p, chunk],
            device_id=device,
            device_id_type=MESH,
        )

    def source_of(p):
        t, e, c = pieces[p]
        part = shards[t].shape[1] // cuts[t]
        return shards[t].at[e, pl.ds(c * part, part), :]

    def inner_sends(p, source, chunk):
        return [
            copy_of(p, source, chunk, (outer * inner_count + peer, mine), send_sem.at[p, 0, j, chunk])
            for j, peer in enumerate(inner_peers)
        ]

    def up(p, source, chunk):
        return copy_of(p, source, chunk, (above * inner_count + inner, mine), send_sem.at[p, 1, 0, chunk])

    def down(p, source, chunk):
        return copy_of(p, source, chunk, (below * inner_count + inner, mine), send_sem.at[p, 2, 0, chunk])

    def arrived(p, chunk):
        pltpu.make_async_copy(spot(p, chunk), spot(p, chunk), recv_sem.at[p, chunk]).wait()

    can_up, can_down = outer < outer_count - 1, outer > 0
    every = range(len(pieces))
    own = []
    for p in every:
        for copy in inner_sends(p, source_of(p), me):
            copy.start()
        pl.when(can_up)(lambda p=p: up(p, source_of(p), me).start())
        pl.when(can_down)(lambda p=p: down(p, source_of(p), me).start())
        copy = pltpu.make_async_copy(source_of(p), spot(p, me), own_sem.at[p])
        copy.start()
        own.append(copy)

    def passing(p, chunk, upward):
        arrived(p, chunk)
        if upward:
            pl.when(can_up)(lambda: up(p, spot(p, chunk), chunk).start())
        else:
            pl.when(can_down)(lambda: down(p, spot(p, chunk), chunk).start())

    for p in every:
        if p in crossed:
            for peer in inner_peers:
                chunk = outer * inner_count + peer
                arrived(p, chunk)
                pl.when(can_up)(lambda p=p, chunk=chunk: up(p, spot(p, chunk), chunk).start())
                pl.when(can_down)(lambda p=p, chunk=chunk: down(p, spot(p, chunk), chunk).start())
    for step in range(1, outer_count):
        low, high = outer - step, outer + step
        for p in every:
            for upward, there, source in ((True, low >= 0, low), (False, high < outer_count, high)):

                def relay(p=p, upward=upward, source=source):
                    chunk = source * inner_count + inner
                    passing(p, chunk, upward)
                    if p in crossed:
                        for peer in inner_peers:
                            passing(p, source * inner_count + peer, upward)
                    else:
                        for copy in inner_sends(p, spot(p, chunk), chunk):
                            copy.start()

                pl.when(there)(relay)
    for t in range(trade_count):
        pltpu.make_async_copy(
            outgoing[t].at[mine], incoming[t].at[mine], trade_send.at[t, 0]
        ).wait()
        for k in range(1, owner_count):
            there = incoming[t].at[lax.rem(mine + k, owner_count)]
            pltpu.make_async_copy(
                there, there, trade_recv.at[t, lax.rem(mine + k, owner_count)]
            ).wait()
    for trade in trades:
        trade.wait_send()
    for p in every:
        own[p].wait()
        if p not in crossed:
            for peer in inner_peers:
                for plane in range(outer_count):
                    arrived(p, plane * inner_count + peer)
        for copy in inner_sends(p, source_of(p), me):
            copy.wait_send()
        if p not in crossed:
            for k in range(1, outer_count):
                chunk = lax.rem(outer + k, outer_count) * inner_count + inner
                for copy in inner_sends(p, spot(p, chunk), chunk):
                    copy.wait_send()
        columns = range(inner_count) if p in crossed else [inner]
        for plane in range(outer_count):
            for column in columns:
                chunk = plane * inner_count + column
                pl.when(can_up & (outer >= plane))(lambda p=p, chunk=chunk: up(p, spot(p, chunk), chunk).wait_send())
                pl.when(can_down & (outer <= plane))(lambda p=p, chunk=chunk: down(p, spot(p, chunk), chunk).wait_send())


def expert_gather(shards, dp_count, collective, cuts=None, crossed=(), owner_count=1, trades=()):
    outer_count, inner_count = dp_grid(dp_count)
    cuts = cuts or [1] * len(shards)
    piece_count = sum(shard.shape[0] * cut for shard, cut in zip(shards, cuts))
    anywhere = pl.BlockSpec(memory_space=pl.ANY)
    given = len(shards) + len(trades)
    return pl.pallas_call(
        functools.partial(
            expert_gather_kernel, dp_count, len(shards), cuts, crossed, owner_count, len(trades)
        ),
        out_shape=[
            jax.ShapeDtypeStruct((s.shape[0], dp_count * s.shape[1], s.shape[2]), s.dtype)
            for s in shards
        ]
        + [jax.ShapeDtypeStruct(t.shape, t.dtype) for t in trades],
        in_specs=[anywhere] * given,
        out_specs=[anywhere] * given,
        scratch_shapes=[
            pltpu.SemaphoreType.DMA((piece_count, 3, max(1, inner_count - 1), dp_count)),
            pltpu.SemaphoreType.DMA((piece_count, dp_count)),
            pltpu.SemaphoreType.DMA((piece_count,)),
            pltpu.SemaphoreType.DMA((max(1, len(trades)), owner_count)),
            pltpu.SemaphoreType.DMA((max(1, len(trades)), owner_count)),
        ],
        compiler_params=pltpu.CompilerParams(collective_id=collective, has_side_effects=True),
        name="expert_gather",
    )(*shards, *trades)


def add_into(target, source, target_at):
    rows = target.shape[-2]
    step = 16

    def body(i, carry):
        here = pl.ds(pl.multiple_of(i * step, step), step)
        target[target_at + (here, slice(None))] = (
            target[target_at + (here, slice(None))].astype(jnp.float32)
            + source(here).astype(jnp.float32)
        ).astype(target.dtype)
        return carry

    lax.fori_loop(0, rows // step, body, 0)


def final_reduce_kernel(small_count, part_ref, *refs):
    small_refs, refs = refs[:small_count], refs[small_count:]
    (
    part_out, small_out, swap, part_in, part_low, part_high, small_in, small_low, small_high, final_low, final_in,
    swap_send, swap_recv, in_send, in_recv, line_send, line_recv, last_send, last_recv,
    ) = refs
    outer_count, inner_count = 4, 2
    me, mine = place()
    outer, inner = me // inner_count, me % inner_count
    side = mine % 2
    mate, across = mine + 1 - 2 * side, lax.rem(mine + 2, 4)
    beside = me + 1 - 2 * inner
    half_rows = small_refs[0].shape[1] // 2
    starts = [sum(ref.shape[2] for ref in small_refs[:n]) for n in range(small_count + 1)]

    def remote(source, target, device, send_at, recv_at):
        return pltpu.make_async_remote_copy(
            src_ref=source,
            dst_ref=target,
            send_sem=send_at,
            recv_sem=recv_at,
            device_id=device,
            device_id_type=MESH,
        )

    barrier = pltpu.get_barrier_semaphore()
    low_peer = lax.rem(outer + outer_count - 1, outer_count) * inner_count + inner
    high_peer = lax.rem(outer + 1, outer_count) * inner_count + inner
    for device in ((me, mate), (me, across), (beside, mine), (low_peer, mine), (high_peer, mine)):
        pl.semaphore_signal(barrier, inc=1, device_id=device, device_id_type=MESH)
    pl.semaphore_wait(barrier, 5)

    mate_rows = pl.ds(pl.multiple_of((1 - side) * half_rows, 16), half_rows)
    own_rows = pl.ds(pl.multiple_of(side * half_rows, 16), half_rows)

    def swap_copy(n):
        return remote(
            small_refs[n].at[:, mate_rows, :],
            swap.at[:, :, starts[n] : starts[n + 1]],
            (me, mate),
            swap_send.at[n],
            swap_recv.at[n],
        )

    def inner_copy(p, plane):
        if p == 0:
            source = part_ref.at[plane * inner_count + 1 - inner]
            target = part_in.at[plane]
        else:
            source = swap.at[plane * inner_count + 1 - inner]
            target = small_in.at[plane]
        return remote(source, target, (beside, mine), in_send.at[p, plane], in_recv.at[p, plane])

    ins, lows, highs = (part_in, small_in), (part_low, small_low), (part_high, small_high)

    def line_copy(p, plane, upward, device_plane):
        target = (lows if upward else highs)[p].at[plane]
        way = 0 if upward else 1
        return remote(
            ins[p].at[plane],
            target,
            (device_plane * inner_count + inner, mine),
            line_send.at[p, way, plane],
            line_recv.at[p, way, plane],
        )

    def add_own(chunk):
        def body(i, carry):
            here = pl.ds(pl.multiple_of(i * 16, 16), 16)
            there = pl.ds(pl.multiple_of(side * half_rows + i * 16, 16), 16)
            for n in range(small_count):
                columns = slice(starts[n], starts[n + 1])
                swap[chunk, here, columns] = (
                    swap[chunk, here, columns].astype(jnp.float32)
                    + small_refs[n][chunk, there, :].astype(jnp.float32)
                ).astype(swap.dtype)
            return carry

        lax.fori_loop(0, half_rows // 16, body, 0)

    def at_plane(o):
        order = sorted(range(outer_count), key=lambda t: (-abs(t - o), t))
        for plane in order:
            inner_copy(0, plane).start()
        for n in range(small_count):
            swap_copy(n).start()
        for n in range(small_count):
            swap_copy(n).wait_recv()
        for plane in order:
            for column in range(inner_count):
                add_own(plane * inner_count + column)
            inner_copy(1, plane).start()
        for plane in order:
            for p in (0, 1):
                inner_copy(p, plane).wait_recv()
                if p == 0:
                    add_into(ins[p], lambda here, plane=plane: part_ref[plane * inner_count + inner, here, :], (plane,))
                else:
                    add_into(ins[p], lambda here, plane=plane: swap[plane * inner_count + inner, here, :], (plane,))
                if plane > o:
                    if o > 0:
                        line_copy(p, plane, True, o + 1).wait_recv()
                        add_into(ins[p], lambda here, p=p, plane=plane: lows[p][plane, here, :], (plane,))
                    line_copy(p, plane, True, o + 1).start()
                if plane < o:
                    if o < outer_count - 1:
                        line_copy(p, plane, False, o - 1).wait_recv()
                        add_into(ins[p], lambda here, p=p, plane=plane: highs[p][plane, here, :], (plane,))
                    line_copy(p, plane, False, o - 1).start()
                if plane == o:
                    if o > 0:
                        line_copy(p, plane, True, o).wait_recv()
                    if o < outer_count - 1:
                        line_copy(p, plane, False, o).wait_recv()
                    target = part_out if p == 0 else final_low
                    rows = target.shape[0]

                    def body(i, carry, p=p, target=target):
                        here = pl.ds(pl.multiple_of(i * 16, 16), 16)
                        total = ins[p][o, here, :].astype(jnp.float32)
                        if o > 0:
                            total = total + lows[p][o, here, :].astype(jnp.float32)
                        if o < outer_count - 1:
                            total = total + highs[p][o, here, :].astype(jnp.float32)
                        target[here, :] = total.astype(target.dtype)
                        return carry

                    lax.fori_loop(0, rows // 16, body, 0)
        for plane in range(outer_count):
            for p in (0, 1):
                inner_copy(p, plane).wait_send()
                if plane > o:
                    line_copy(p, plane, True, o + 1).wait_send()
                if plane < o:
                    line_copy(p, plane, False, o - 1).wait_send()
        for n in range(small_count):
            swap_copy(n).wait_send()

    for o in range(outer_count):
        pl.when(outer == o)(functools.partial(at_plane, o))
    across_copy = remote(final_low, final_in, (me, across), last_send.at[0], last_recv.at[0])
    across_copy.start()
    across_copy.wait()

    def total_body(i, carry):
        here = pl.ds(pl.multiple_of(i * 16, 16), 16)
        there = pl.ds(pl.multiple_of(side * half_rows + i * 16, 16), 16)
        small_out[there, :] = final_low[here, :].astype(jnp.float32) + final_in[here, :].astype(jnp.float32)
        return carry

    lax.fori_loop(0, half_rows // 16, total_body, 0)
    mate_copy = remote(
        small_out.at[own_rows, :], small_out.at[own_rows, :], (me, mate), last_send.at[1], last_recv.at[1]
    )
    mate_copy.start()
    mate_copy.wait()


def final_reduce(part, smalls, collective):
    chunk_count, part_rows, part_columns = part.shape
    small_rows = smalls[0].shape[1]
    small_columns = sum(small.shape[2] for small in smalls)
    low = jnp.bfloat16
    in_vmem = pl.BlockSpec(memory_space=pltpu.VMEM)
    half = small_rows // 2
    return pl.pallas_call(
        functools.partial(final_reduce_kernel, len(smalls)),
        out_shape=[
            jax.ShapeDtypeStruct((part_rows, part_columns), jnp.float32),
            jax.ShapeDtypeStruct((small_rows, small_columns), jnp.float32),
        ],
        in_specs=[in_vmem] * (1 + len(smalls)),
        out_specs=[in_vmem] * 2,
        scratch_shapes=[pltpu.VMEM((chunk_count, half, small_columns), low)]
        + [pltpu.VMEM((4, part_rows, part_columns), low)] * 3
        + [pltpu.VMEM((4, half, small_columns), low)] * 3
        + [pltpu.VMEM((half, small_columns), low)] * 2
        + [
            pltpu.SemaphoreType.DMA((len(smalls),)),
            pltpu.SemaphoreType.DMA((len(smalls),)),
            pltpu.SemaphoreType.DMA((2, 4)),
            pltpu.SemaphoreType.DMA((2, 4)),
            pltpu.SemaphoreType.DMA((2, 2, 4)),
            pltpu.SemaphoreType.DMA((2, 2, 4)),
            pltpu.SemaphoreType.DMA((2,)),
            pltpu.SemaphoreType.DMA((2,)),
        ],
        compiler_params=pltpu.CompilerParams(
            collective_id=collective, has_side_effects=True, vmem_limit_bytes=58 * 2**20
        ),
        name="final_reduce",
    )(part, *smalls)


def shards(
    tokens,
    resid_logits,
    routes,
    doc_ids,
    w_qkv,
    w_out,
    gain_attn,
    gain_ffn,
    w_router,
    w_const,
    v_const,
    w_gate_up,
    w_down,
    out_grad,
):
    dp_count, owner_count = lax.axis_size("dp"), lax.axis_size("expert")
    own_links = dp_count == 8 and owner_count == 4
    seq_count, length, width = tokens.shape
    assert seq_count == 1
    rows = seq_count * length
    choice_count = resid_logits.shape[-1]
    local_count = w_gate_up.shape[0]
    expert_count = owner_count * local_count
    hidden_count = w_down.shape[1] * dp_count
    width_qkv, width_out = w_qkv.shape[1], w_out.shape[1]
    small_parts = [w_router, w_const, v_const, gain_attn[:, None], gain_ffn[:, None]]
    small_width = sum(part.shape[1] for part in small_parts)
    pad = jnp.zeros((w_qkv.shape[0], 256 - small_width), jnp.bfloat16)
    packed = jnp.concatenate([w_qkv, w_out] + small_parts + [pad], 1)
    inputs = tokens.reshape(rows, width)
    cot = out_grad.reshape(rows, width)
    route_rows = routes.reshape(rows, 2)
    spots, spot_rows = routing(route_rows, expert_count)
    cosine, sine = rotary_lanes(length, width // HEADS)
    docs_row, docs_column = doc_ids.reshape(1, rows), doc_ids.reshape(rows, 1)
    resid = jnp.pad(
        resid_logits.reshape(rows, choice_count).astype(jnp.float32), ((0, 0), (0, 128 - choice_count))
    )
    if own_links:
        packed_full = small_gather(packed, dp_count, 1)
    else:
        packed_full = lax.all_gather(packed, "dp", axis=0, tiled=True)
    gate_up_full = lax.all_gather(w_gate_up, "dp", axis=1, tiled=True)
    normed_one, queries, keys, values, attended, middle, normed_two, aux = attention_forward(
        inputs, packed_full, docs_row, docs_column, cosine, sine, route_rows, resid
    )
    send_rows, send_grads = dispatch(spot_rows, aux, normed_two, cot, expert_count * CAP)
    send_rows = send_rows.reshape(owner_count, local_count * CAP, width)
    send_grads = send_grads.reshape(owner_count, local_count * CAP, width)
    exchange = functools.partial(
        lax.all_to_all, axis_name="expert", split_axis=0, concat_axis=0, tiled=True
    )
    if own_links:
        down_full, arrived, arrived_grad = expert_gather(
            [w_down], dp_count, 2, owner_count=owner_count, trades=[send_rows, send_grads]
        )
    else:
        down_full = lax.all_gather(w_down, "dp", axis=1, tiled=True)
        arrived, arrived_grad = exchange(send_rows), exchange(send_grads)
    arrived = arrived.reshape(owner_count, local_count, CAP, width)
    arrived_grad = arrived_grad.reshape(owner_count, local_count, CAP, width)

    gate_up = jnp.einsum(
        "secd,edf->secf", arrived, gate_up_full, preferred_element_type=jnp.float32
    )
    gate_part = gate_up[..., :hidden_count]
    up_part = gate_up[..., hidden_count:]
    squashed = lax.logistic(gate_part)
    silu_gate = gate_part * squashed
    activated = (silu_gate * up_part).astype(jnp.bfloat16)
    grad_down = jnp.einsum(
        "secf,secd->efd", activated, arrived_grad, preferred_element_type=jnp.float32
    ).astype(jnp.bfloat16)
    activated, arrived_grad, grad_down = lax.optimization_barrier(
        (activated, arrived_grad, grad_down)
    )
    grad_expert_down = lax.psum_scatter(
        grad_down, "dp", scatter_dimension=1, tiled=True
    ).astype(jnp.float32)
    expert_out = jnp.einsum(
        "secf,efd->secd", activated, down_full, preferred_element_type=jnp.float32
    ).astype(jnp.bfloat16)
    returned = exchange(expert_out.reshape(owner_count, local_count * CAP, width))
    grad_act = jnp.einsum(
        "secd,efd->secf", arrived_grad, down_full, preferred_element_type=jnp.float32
    )
    grad_gate = grad_act * up_part * squashed * (1.0 + gate_part * (1.0 - squashed))
    grad_up = grad_act * silu_gate
    grad_gate_up = jnp.concatenate([grad_gate, grad_up], -1).astype(jnp.bfloat16)
    grad_rows = jnp.einsum(
        "secf,edf->secd", grad_gate_up, gate_up_full, preferred_element_type=jnp.float32
    ).astype(jnp.bfloat16)
    back = exchange(grad_rows.reshape(owner_count, local_count * CAP, width))
    gu_grads = [
        jnp.einsum(
            "scd,scf->df", arrived[:, e], grad_gate_up[:, e], preferred_element_type=jnp.float32
        ).astype(jnp.bfloat16)
        for e in range(local_count)
    ]
    returned, gu_grads = lax.optimization_barrier((returned, gu_grads))
    linked = local_count - 1 if own_links else local_count
    gu_parts = [
        lax.psum_scatter(gu_grads[e], "dp", scatter_dimension=0, tiled=True).astype(jnp.float32)
        for e in range(linked)
    ]

    output, logit_grad, grad_part, small_grad = combine(
        returned.reshape(expert_count * CAP, width), spots, route_rows, aux, normed_two, middle,
        cot, packed_full, choice_count, expert_count,
    )
    grad_middle, small_grad = combine_back(
        back.reshape(expert_count * CAP, width), spots, aux, middle, cot, grad_part, packed_full,
        small_grad,
    )
    token_grad, *weight_grads = attention_backward(
        grad_middle, queries, keys, values, attended, normed_one, inputs, packed_full, docs_row,
        docs_column, cosine, sine, small_grad,
    )
    if own_links:
        part_width = width // dp_count
        gu_part, packed_part = final_reduce(
            gu_grads[linked].reshape(dp_count, part_width, 2 * hidden_count),
            [grad.reshape(dp_count, part_width, grad.shape[1]) for grad in weight_grads],
            3,
        )
        gu_parts = gu_parts + [gu_part]
    else:
        packed_part = lax.psum_scatter(
            jnp.concatenate(weight_grads, 1), "dp", scatter_dimension=0, tiled=True
        )
        packed_part = lax.psum(packed_part, "expert").astype(jnp.float32)
    part_qkv = packed_part[:, :width_qkv]
    part_out = packed_part[:, width_qkv : width_qkv + width_out]
    small_part = packed_part[:, width_qkv + width_out :]
    return (
        output.reshape(tokens.shape),
        token_grad.reshape(tokens.shape),
        logit_grad.reshape(resid_logits.shape),
        part_qkv,
        part_out,
        small_part[:, 18],
        small_part[:, 19],
        small_part[:, 0:12],
        small_part[:, 12:16],
        small_part[:, 16:18],
        jnp.stack(gu_parts),
        grad_expert_down,
    )


def solution(mesh):
    placed = (
        P(("dp", "expert"), None, None),
        P(("dp", "expert"), None, None),
        P(("dp", "expert"), None, None),
        P(("dp", "expert"), None),
        P("dp", None),
        P("dp", None),
        P("dp"),
        P("dp"),
        P("dp", None),
        P("dp", None),
        P("dp", None),
        P("expert", "dp", None),
        P("expert", "dp", None),
        P(("dp", "expert"), None, None),
    )
    return jax.shard_map(
        shards,
        mesh=mesh,
        in_specs=placed,
        out_specs=(
            P(("dp", "expert"), None, None),
            P(("dp", "expert"), None, None),
            P(("dp", "expert"), None, None),
            P("dp", None),
            P("dp", None),
            P("dp"),
            P("dp"),
            P("dp", None),
            P("dp", None),
            P("dp", None),
            P("expert", "dp", None),
            P("expert", "dp", None),
        ),
        check_vma=False,
    )
```

time: 1020 us -> 705 us (0.69)
  matrix products: 298 us -> 115 us
  Pallas kernels: 317 us -> 487 us
  other arithmetic: 176 us -> 18.6 us
  local copies, waits for them, and re-layouts: 165 us -> 36.9 us
    dot_general x26 -> x2, matrix products: 206 us -> 27.4 us  [shards(): jnp.einsum('scd,scf->df', arrived[:, e], grad_gate_up[:, e], preferred_el...]
    pallas_call x1 -> x7, Pallas kernels: 159 us -> 296 us  [the longest x1 167 us: final_reduce(): pl.pallas_call(functools.partial(final_reduce_kernel, len(smalls)), out_s...]
    reduce_sum x15 -> x0, other arithmetic: 92.2 us -> none  [the longest x1 47.9 us: shards(): grad_mix_first = jnp.sum(grad_const_val * normed_back[:, None, :], -1)]
    gather x4 -> x0, local copies, waits for them, and re-layouts: 44 us -> none  [the longest x1 12.6 us: shards(): padded_out[destination].reshape(row_count, 2, model_width)]
    convert_element_type x8 -> x1, other arithmetic: 53.2 us -> 12.3 us  [shards(): activated = (silu_gate * up_part).astype(jnp.bfloat16)]
    pallas_call x1, Pallas kernels: 97.9 us -> 122 us  [expert_gather(): pl.pallas_call(functools.partial(expert_gather_kernel, dp_count, len(shar...]
    mul x8 -> x0, local copies, waits for them, and re-layouts: 18.3 us -> none  [the longest x2 13.2 us: shards(): gate_weights[:, :, None] * grad_final[:, None, :]]
    convert_element_type x7 -> x0, local copies, waits for them, and re-layouts: 17.5 us -> none  [the longest x1 7.97 us: shards(): padded_out[destination].reshape(row_count, 2, model_width)]
  transfers between devices with their start and end apart: 5 -> 5, of which waited for: 2 -> 1; matrix products, arithmetic and copies ran while one was open for 43% -> 16% of each run, Pallas kernels for 32% -> 70%
where the time goes in v3:
time: 705 us; the launch traced here: 700 us
  Pallas kernels  487 us (69%)
  matrix products  115 us (16%)
  local copies, waits for them, and re-layouts  36.9 us (5%)
  other arithmetic  18.6 us (3%)
  waiting for transfers between devices  18 us (3%)
  between operations  14.2 us (2%)
  starting transfers between devices  9.68 us (1%)
    pallas_call x1, Pallas kernels, final_reduce(): pl.pallas_call(functools.partial(final_reduce_kernel, len(smalls)), out_s...  167 us
    pallas_call x1, Pallas kernels, expert_gather(): pl.pallas_call(functools.partial(expert_gather_kernel, dp_count, len(shar...  122 us
    pallas_call x1, Pallas kernels, small_gather(): pl.pallas_call(functools.partial(small_gather_kernel, dp_count), out_shap...  68.4 us
    pallas_call x1, Pallas kernels, attention_backward(): pl.pallas_call(attention_backward_kernel, grid=(groups,), out_shape=[jax....  56 us
    pallas_call x1, Pallas kernels, attention_forward(): pl.pallas_call(attention_forward_kernel, grid=(groups,), out_shape=[full]...  33.2 us
    dot_general x2, matrix products, shards(): jnp.einsum('scd,scf->df', arrived[:, e], grad_gate_up[:, e], preferred_el...  27.4 us
    dot_general x1, matrix products, shards(): jnp.einsum('secd,edf->secf', arrived, gate_up_full, preferred_element_typ...  24.2 us
    dot_general x1, matrix products, shards(): jnp.einsum('secd,efd->secf', arrived_grad, down_full, preferred_element_t...  22.8 us
  transfers between devices with their start and end apart: 5, of which 1 were waited for; matrix products, arithmetic and copies ran while one was open for 16% of the time, Pallas kernels for 70%

profile of v3, /device:TPU:19, one launch (start us, length us, event | category | flops | bytes accessed | tf_op | source)
XLA Modules:
  0.0 699.6 jit_solution(9714314537000771)
XLA Ops:
  8.0 0.9 copy.46
  8.9 4.3 routing.1
  13.3 0.8 copy.47
  14.1 0.8 copy.48
  14.9 0.8 copy.49
  15.6 0.8 copy.50
  16.4 0.8 copy.51
  17.2 2.2 concatenate.7.shard_ref
  19.3 68.4 %small_gather.1.wq_ref.wk_ref.wv_ref.wo_ref.small_ref = bf16[768,3328]{1,0:T(8,128)(2,1)} custom-call(bf16[96,3328]{1,0:T(8,128)(2,1)} %concatenate.7.shard_ref), custom_call_target="tpu_custom_call" | custom-call | tf_op jit(solution)/shard_map/small_gather/pallas_call | solution.py:677
  87.8 1.0 copy.53.docs_column_ref
  89.0 0.8 pad_convert_fusion.resid_ref
  89.8 33.2 %attention_forward.1 = (bf16[1024,768]{1,0:T(8,128)(2,1)}, bf16[1024,768]{1,0:T(8,128)(2,1)}, bf16[1024,768]{1,0:T(8,128)(2,1)}, bf16[1024,768]{1,0:T(8,128)(2,1...) custom-call(bf16[1024,768]{1,0:T(8,128)(2,1)} %bitcast.119, ...), custom_call_target="tpu_custom_call" | custom-call | flops 8053063680 | bytes 18874368 | tf_op jit(solution)/shard_map/attention_forward/pallas_call | solution.py:147
  123.1 1.0 copy-done.6
  124.1 1.4 copy-done.11
  125.5 9.2 %dispatch.1 = (bf16[2048,768]{1,0:T(8,128)(2,1)S(1)}, bf16[2048,768]{1,0:T(8,128)(2,1)S(1)}) custom-call(s32[8,1024]{1,0:T(8,128)S(1)} %get-tuple-element.47.spots_ref, f32[1024,128]{1,0:T(8,128)S(1)} %copy-done.6, bf16[1024,768]{1,0:T(8,128)(2,1)S(1)} %copy-done.11, bf16[1024,768]{1,0:T(8,128)(2,1)S(1)} %bitcast.97), custom_call_target="tpu_custom_call" | custom-call | flops 6442450944 | bytes 9437184 | tf_op jit(solution)/shard_map/dispatch/pallas_call | solution.py:387
  134.7 1.6 copy-done
  136.4 1.6 copy-done.1
  138.0 122.1 %expert_gather.1 = (bf16[2,2048,768]{2,1,0:T(8,128)(2,1)}, bf16[4,512,768]{2,1,0:T(8,128)(2,1)}, bf16[4,512,768]{2,1,0:T(8,128)(2,1)}) custom-call(bf16[2,256,768]{2,1,0:T(8,128)(2,1)} %refs_0_.1, bf16[4,512,768]{2,1,0:T(8,128)(2,1)} %bitcast.92, bf16[4,512,768]{2,1,0:T(8,128)(2,1)} %bitcast.93), custom_call_target="tpu_custom_call" | custom-call | tf_op jit(solution)/shard_map/expert_gather/pallas_call | solution.py:847
  260.1 24.2 %convolution_bitcast_fusion = f32[4,2,256,4096]{3,2,0,1:T(8,128)} fusion(bf16[2,768,4096]{2,1,0:T(8,128)(2,1)} %all-gather.2.cloned.1.call-done, bf16[4,2,256,768]{3,2,1,0:T(8,128)(2,1)} %bitcast.114), kind=kOutput, calls=%fused_computation.15 | convolution fusion | flops 12884901888 | bytes 49283072 | tf_op jit(solution)/shard_map/secd,edf->secf/dot_general | solution.py:1142
  284.3 12.3 %multiply_convert_fusion = bf16[4,2,256,2048]{3,2,0,1:T(8,128)(2,1)S(1)} fusion(f32[4,2,256,4096]{3,2,0,1:T(8,128)} %convolution_bitcast_fusion), kind=kLoop, calls=%fused_computation.12 | loop fusion | flops 25165824 | bytes 41943040 | tf_op jit(solution)/shard_map/convert_element_type | solution.py:1149
  296.6 3.3 copy-done.13
  299.9 9.0 %bitcast_convert_fusion.2 = bf16[2,2048,768]{2,1,0:T(8,128)(2,1)} fusion(bf16[4,2,256,2048]{3,2,0,1:T(8,128)(2,1)S(1)} %multiply_convert_fusion, bf16[4,2,256,768]{3,2,1,0:T(8,128)(2,1)S(1)} %bitcast.118), kind=kOutput, calls=%fused_computation.20 | convolution fusion | flops 6445596672 | bytes 17825792 | tf_op jit(solution)/shard_map/secf,secd->efd/dot_general | solution.py:1150
  308.9 10.9 %convert_bitcast_fusion.1 = bf16[4,2,256,768]{3,2,0,1:T(8,128)(2,1)S(1)} fusion(bf16[4,2,256,2048]{3,2,0,1:T(8,128)(2,1)} %copy-done.13, bf16[2,2048,768]{2,1,0:T(8,128)(2,1)} %get-tuple-element.52), kind=kOutput, calls=%fused_computation.36 | convolution fusion | flops 6444023808 | bytes 17825792 | tf_op jit(solution)/shard_map/secf,efd->secd/dot_general | solution.py:1159
  319.8 1.9 copy.57
  321.7 5.0 all-to-all-start
  326.7 22.8 %fusion.4 = (bf16[4,2,256,2048]{3,2,0,1:T(8,128)(2,1)}, bf16[4,2,256,2048]{3,2,0,1:T(8,128)(2,1)}) fusion(f32[4,2,256,4096]{3,2,0,1:T(8,128)} %convolution_bitcast_fusion, bf16[4,2,256,768]{3,2,1,0:T(8,128)(2,1)} %bitcast.117, bf16[2,2048,768]{2,1,0:T(8,128)(2,1)} %get-tuple-element.52), kind=kOutput, calls=%fused_computation.11 | convolution fusion | flops 6496976896 | bytes 59768832 | tf_op jit(solution)/shard_map/secd,efd->secf/dot_general | solution.py:1163
  349.5 13.6 %bitcast_convert_fusion.1 = bf16[768,4096]{1,0:T(8,128)(2,1)} fusion(bf16[4,2,256,2048]{3,2,0,1:T(8,128)(2,1)} %get-tuple-element.109, bf16[4,2,256,2048]{3,2,0,1:T(8,128)(2,1)} %get-tuple-element.108, bf16[4,2,256,768]{3,2,1,0:T(8,128)(2,1)} %bitcast.115), kind=kOutput, calls=%fused_computation.19 | convolution fusion | flops 6462373888 | bytes 24641536 | tf_op jit(solution)/shard_map/scd,scf->df/dot_general | solution.py:1174
  363.1 13.7 %bitcast_convert_fusion = bf16[768,4096]{1,0:T(8,128)(2,1)} fusion(bf16[4,2,256,2048]{3,2,0,1:T(8,128)(2,1)} %get-tuple-element.109, bf16[4,2,256,2048]{3,2,0,1:T(8,128)(2,1)} %get-tuple-element.108, bf16[4,2,256,768]{3,2,1,0:T(8,128)(2,1)} %bitcast.116), kind=kOutput, calls=%fused_computation.18 | convolution fusion | flops 6462373888 | bytes 24641536 | tf_op jit(solution)/shard_map/scd,scf->df/dot_general | solution.py:1174
  376.9 21.0 %convert_bitcast_fusion = bf16[4,2,256,768]{3,2,0,1:T(8,128)(2,1)} fusion(bf16[2,768,4096]{2,1,0:T(8,128)(2,1)} %all-gather.2.cloned.1.call-done, bf16[4,2,256,2048]{3,2,0,1:T(8,128)(2,1)} %get-tuple-element.108, bf16[4,2,256,2048]{3,2,0,1:T(8,128)(2,1)} %get-tuple-element.109), kind=kOutput, calls=%fused_computation.35 | convolution fusion | flops 12920029184 | bytes 32505856 | tf_op jit(solution)/shard_map/secf,edf->secd/dot_general | solution.py:1169
  397.9 4.0 copy.62
  401.9 4.6 all-to-all-start.1
  406.6 1.4 copy-done.12
  408.0 16.8 %combine.1 = (bf16[1024,768]{1,0:T(8,128)(2,1)}, bf16[1024,12]{1,0:T(8,128)(2,1)S(1)}, f32[1024,768]{1,0:T(8,128)}, f32[768,128]{1,0:T(8,128)S(1)}) custom-call(bf16[2048,768]{1,0:T(8,128)(2,1)} %bitcast.28.returned_ref, s32[1024,128]{1,0:T(8,128)S(1)} %get-tuple-element.58.spots_ref, s32[1024,2]{1,0:T(8,128)S(1)} %bitcast.96, f32[1024,128]{1,0:T(8,128)S(1)} %copy-done.7, ...), custom_call_target="tpu_custom_call" | custom-call | flops 6442450944 | bytes 15728640 | tf_op jit(solution)/shard_map/combine/pallas_call | solution.py:485
  425.5 17.3 %all-to-all-done.1 = bf16[4,512,768]{2,1,0:T(8,128)(2,1)} async-done(((bf16[4,512,768]{2,1,0:T(8,128)(2,1)}), bf16[4,512,768]{2,1,0:T(8,128)(2,1)}, u32[]{:S(2)}, u32[]{:S(2)}) %all-to-all-start.1) | async-done | bytes 3145760 | tf_op jit(solution)/shard_map/all_to_all | solution.py:1172
  442.8 10.1 %combine_back.1 = (f32[1024,768]{1,0:T(8,128)}, f32[768,128]{1,0:T(8,128)S(1)}) custom-call(bf16[2048,768]{1,0:T(8,128)(2,1)} %bitcast.33.back_ref, s32[1024,128]{1,0:T(8,128)S(1)} %get-tuple-element.58.spots_ref, f32[1024,128]{1,0:T(8,128)S(1)} %copy-done.7, f32[1024,768]{1,0:T(8,128)} %get-tuple-element.59.middle_ref, bf16[1024,768]{1,0:T(8,128)(2,1)S(1)} %bitcast.99, ...), custom_call_target="tpu_custom_call" | custom-call | flops 3221225472 | bytes 14155776 | tf_op jit(solution)/shard_map/combine_back/pallas_call | solution.py:556
  452.9 0.8 copy-done.10
  453.6 56.0 %attention_backward.1 = (bf16[1024,768]{1,0:T(8,128)(2,1)}, bf16[768,768]{1,0:T(8,128)(2,1)}, bf16[768,768]{1,0:T(8,128)(2,1)}, bf16[768,768]{1,0:T(8,128)(2,1)}...) custom-call(f32[1024,768]{1,0:T(8,128)} %get-tuple-element.63.grad_middle_ref, ...), custom_call_target="tpu_custom_call" | custom-call | flops 17716740096 | bytes 25165824 | tf_op jit(solution)/shard_map/attention_backward/pallas_call | solution.py:276
  509.6 166.9 %final_reduce.1 = (f32[96,4096]{1,0:T(8,128)}, f32[96,3328]{1,0:T(8,128)}) custom-call(bf16[8,96,4096]{2,1,0:T(8,128)(2,1)} %bitcast.103, bf16[8,96,768]{2,1,0:T(8,128)(2,1)} %bitcast.105, bf16[8,96,768]{2,1,0:T(8,128)(2,1)} %bitcast.106, bf16[8,96,768]{2,1,0:T(8,128)(2,1)} %bitcast.107, bf16[8,96,768]{2,1,0:T(8,128)(2,1)} %bitcast.108, ...), custom_call_target="tpu_custom_call" | custom-call | tf_op jit(solution)/shard_map/final_reduce/pallas_call | solution.py:1050
  676.5 2.3 slice.51
  678.8 1.7 slice.52
  680.5 0.8 slice.55
  681.3 0.9 slice.56
  682.1 0.9 slice.57
  683.0 0.8 copy.64
  685.7 1.6 slice_reduce_fusion
  687.3 2.4 convert_element_type.44
  689.7 1.3 bitcast_convert_fusion.3
  691.0 1.9 pad_maximum_fusion.2
  (44 shorter events, 3.7 us)
Async XLA Ops:
  7.2 80.6 %copy-start.16 = (s32[1,1024]{1,0:T(1,128)S(1)}, s32[1,1024]{1,0:T(1,128)}, u32[]{:S(2)}) copy-start(s32[1,1024]{1,0:T(1,128)} %docs_row_ref.3) | copy-start | bytes 12292
  7.2 81.6 %copy-start.15 = (bf16[1,1024,12]{1,2,0:T(8,128)(2,1)S(1)}, bf16[1,1024,12]{1,2,0:T(8,128)(2,1)}, u32[]{:S(2)}) copy-start(bf16[1,1024,12]{1,2,0:T(8,128)(2,1)} %param.17) | copy-start | bytes 73732
  7.2 252.9 %all-gather.2.cloned.1.call-start = ((), (), s32[]{:S(2)}) async-start(), calls=%async_computation.4 | async-start | bytes 14155776 | tf_op jit(solution)/shard_map/all_gather | solution.py:1122
  7.9 679.4 %reduce-scatter.5.cloned.1.call-start = ((), (), s32[]{:S(2)}) async-start(), calls=%async_computation.6 | async-start | bytes 7077888 | tf_op jit(solution)/shard_map/reduce_scatter | solution.py:1156
  8.9 80.9 %copy-start.2 = (s32[1,1024,2]{2,1,0:T(8,128)}, s32[1,1024,2]{2,1,0:T(8,128)S(1)}, u32[]{:S(2)}) copy-start(s32[1,1024,2]{2,1,0:T(8,128)S(1)} %copy.46) | copy-start | bytes 24580
  89.8 33.2 %copy-start.4 = (bf16[1,1024,768]{2,1,0:T(8,128)(2,1)S(1)}, bf16[1,1024,768]{2,1,0:T(8,128)(2,1)}, u32[]{:S(2)}) copy-start(bf16[1,1024,768]{2,1,0:T(8,128)(2,1)} %param.29) | copy-start | bytes 4718596
  123.1 1.0 copy-start.6
  124.1 1.4 copy-start.11
  134.7 1.6 copy-start
  136.4 1.6 copy-start.1
  284.3 15.6 %copy-start.17 = (bf16[4,512,768]{2,1,0:T(8,128)(2,1)S(1)}, bf16[4,512,768]{2,1,0:T(8,128)(2,1)}, u32[]{:S(2)}) copy-start(bf16[4,512,768]{2,1,0:T(8,128)(2,1)} %get-tuple-element.54) | copy-start | bytes 9437188
  296.5 3.3 copy-start.13
  321.7 55.1 %all-to-all-start = ((bf16[4,512,768]{2,1,0:T(8,128)(2,1)}), bf16[4,512,768]{2,1,0:T(8,128)(2,1)}, u32[]{:S(2)}, u32[]{:S(2)}) async-start(bf16[4,512,768]{2,1,0:T(8,128)(2,1)} %bitcast.101), calls=%async_computation | async-start | bytes 6291456 | tf_op jit(solution)/shard_map/all_to_all | solution.py:1162
  326.7 363.0 %reduce-scatter.3.cloned.1.call-start = ((), (), s32[]{:S(2)}) async-start(), calls=%async_computation.5 | async-start | bytes 7077888 | tf_op jit(solution)/shard_map/reduce_scatter | solution.py:1182
  397.9 8.7 %copy-start.3 = (s32[1,1024,2]{2,1,0:T(8,128)S(1)}, s32[1,1024,2]{2,1,0:T(8,128)}, u32[]{:S(2)}) copy-start(s32[1,1024,2]{2,1,0:T(8,128)} %copy-done.2) | copy-start | bytes 24580
  397.9 8.7 %copy-start.5 = (bf16[1,1024,768]{2,1,0:T(8,128)(2,1)S(1)}, bf16[1,1024,768]{2,1,0:T(8,128)(2,1)}, u32[]{:S(2)}) copy-start(bf16[1,1024,768]{2,1,0:T(8,128)(2,1)} %param.29) | copy-start | bytes 4718596
  397.9 8.7 %copy-start.7 = (f32[1024,128]{1,0:T(8,128)S(1)}, f32[1024,128]{1,0:T(8,128)}, u32[]{:S(2)}) copy-start(f32[1024,128]{1,0:T(8,128)} %get-tuple-element.48.aux_ref) | copy-start | bytes 1572868
  401.9 40.9 %all-to-all-start.1 = ((bf16[4,512,768]{2,1,0:T(8,128)(2,1)}), bf16[4,512,768]{2,1,0:T(8,128)(2,1)}, u32[]{:S(2)}, u32[]{:S(2)}) async-start(bf16[4,512,768]{2,1,0:T(8,128)(2,1)} %bitcast.102), calls=%async_computation.1 | async-start | bytes 6291456 | tf_op jit(solution)/shard_map/all_to_all | solution.py:1172
  406.6 1.4 copy-start.12
  424.8 0.7 copy-start.8
  452.9 0.8 copy-start.10
  509.6 173.4 %copy-start.9 = (bf16[1024,12]{1,0:T(8,128)(2,1)S(1)}, bf16[1024,12]{1,0:T(8,128)(2,1)}, u32[]{:S(2)}) copy-start(bf16[1024,12]{1,0:T(8,128)(2,1)} %copy-done.8) | copy-start | bytes 73732
  676.5 14.5 %copy-start.14 = (f32[96,4096]{1,0:T(8,128)S(1)}, f32[96,4096]{1,0:T(8,128)}, u32[]{:S(2)}) copy-start(f32[96,4096]{1,0:T(8,128)} %get-tuple-element.80) | copy-start | bytes 4718596
Sparse Core Ops, SparseCore 0:
  10.2 231.8 all-gather.1
  309.0 129.0 reduce-scatter.4
  441.7 126.0 reduce-scatter.2

commit v4 on v3

--- a/solution.py
+++ b/solution.py
@@ -12,6 +12,7 @@
 BLOCK = 256
 CAP = 256
 GROUP = 256
+FF_BLOCK = 512
 MESH = pl.DeviceIdType.MESH
 epsilon = 1e-06
 
@@ -392,7 +393,7 @@
         out_specs=[block, block],
         scratch_shapes=[pltpu.VMEM((8, rows), jnp.float32)],
         compiler_params=pltpu.CompilerParams(
-            dimension_semantics=("arbitrary",), vmem_limit_bytes=40 * 2**20
+            dimension_semantics=("arbitrary",), vmem_limit_bytes=60 * 2**20
         ),
         cost_estimate=pl.CostEstimate(
             flops=4 * slot_count * rows * width,
@@ -409,28 +410,37 @@
 
 
 def combine_kernel(
-    expert_count, returned_ref, spots_ref, routes_ref, aux_ref, normed_ref, middle_ref, cot_ref, small_ref,
-    output_ref, logit_ref, grad_ref, small_grad_ref, vectors_ref,
+    expert_count, local_count, *refs
 ):
+    parts, refs = refs[:local_count], refs[local_count:]
+    (
+        spots_ref, routes_ref, aux_ref, normed_ref, middle_ref, cot_ref, small_ref,
+        output_ref, logit_ref, grad_middle_ref, small_out_ref, vectors_ref, small_grad_ref,
+    ) = refs
     step = pl.program_id(0)
 
     @pl.when(step == 0)
     def _():
-        vectors_ref[...] = jnp.transpose(small_ref[:, :128].astype(jnp.float32))[16:24, :]
+        vectors_ref[0:8, :] = jnp.transpose(small_ref[:, :128].astype(jnp.float32))[16:24, :]
+        vectors_ref[8:16, :] = jnp.zeros((8, vectors_ref.shape[1]), jnp.float32)
         small_grad_ref[...] = jnp.zeros_like(small_grad_ref)
 
-    rows = normed_ref.shape[0]
-    slots = lane_ids((rows, returned_ref.shape[0]))
-    returned = returned_ref[...]
+    rows, width = normed_ref.shape
     normed_low, cot_low = normed_ref[...], cot_ref[...]
     normed, cot = normed_low.astype(jnp.float32), cot_low.astype(jnp.float32)
     total = lambda values: jnp.sum(values, -1, keepdims=True)
-    picks, inner = [], []
-    for s in range(2):
-        chosen = jnp.where(slots == spots_ref[:, s : s + 1], 1.0, 0.0).astype(jnp.bfloat16)
-        pick = nn(chosen, returned)
-        picks.append(pick)
-        inner.append(total(pick * cot))
+    picks, back = [0.0, 0.0], 0.0
+    for e in range(local_count):
+        count = parts[e].shape[0] * CAP
+        slots = lane_ids((rows, count))
+        slots = slots // CAP * (local_count * CAP) + e * CAP + slots % CAP
+        hits = [slots == spots_ref[:, s : s + 1] for s in range(2)]
+        chosen = [jnp.where(hit, 1.0, 0.0).astype(jnp.bfloat16) for hit in hits]
+        returned = parts[e][:, 0].reshape(count, width)
+        for s in range(2):
+            picks[s] = picks[s] + nn(chosen[s], returned)
+        back = back + nn(chosen[0] + chosen[1], parts[e][:, 1].reshape(count, width))
+    inner = [total(pick * cot) for pick in picks]
     gates = [aux_ref[:, s : s + 1] for s in range(2)]
     routes = [routes_ref[:, s : s + 1] for s in range(2)]
     dot_copy = total(cot * normed)
@@ -461,7 +471,8 @@
         spread = jnp.where(lanes == 13 + 2 * k, -term, spread)
         spread = jnp.where(lanes == 16 + k, weight * blend, spread)
     mix = mix + pass_weight * normed
-    output_ref[...] = (middle_ref[...] + mix).astype(jnp.bfloat16)
+    middle, scale = middle_ref[...], aux_ref[:, 6:7]
+    output_ref[...] = (middle + mix).astype(jnp.bfloat16)
     mean = gates[0] * gate_grads[0] + gates[1] * gate_grads[1]
     for s in range(2):
         spread = jnp.where(lanes == routes[s], gates[s] * (gate_grads[s] - mean), spread)
@@ -469,21 +480,32 @@
     logits = jnp.where(lanes < 16, spread, 0.0)
     high, low = halves(logits)
     small = small_ref[:, :128]
-    grad_ref[...] = pass_weight * cot + nt(high, small) + nt(low, small)
     vector_high, vector_low = halves(spread - logits)
     small_grad_ref[...] += (
         tn(normed_low, high) + tn(normed_low, low) + tn(cot_low, vector_high) + tn(cot_low, vector_low)
     )
-
-
-def combine(returned, spots, routes, aux, normed, middle, cot, packed, choice_count, expert_count):
+    grads = back + pass_weight * cot + nt(high, small) + nt(low, small)
+    vectors_ref[8:9, :] += jnp.sum(grads * middle * scale, 0, keepdims=True)
+    weighted = grads * vectors_ref[3:4, :]
+    mean = jnp.mean(weighted * middle, -1, keepdims=True)
+    grad_middle_ref[...] = cot + scale * weighted - middle * (scale * scale * scale * mean)
+
+    @pl.when(step == pl.num_programs(0) - 1)
+    def _():
+        column = jnp.transpose(jnp.broadcast_to(vectors_ref[8:9, :], (128, width)))
+        small_grad = small_grad_ref[...]
+        small_out_ref[...] = jnp.where(lane_ids(small_grad.shape) == 19, column, small_grad)
+
+
+def combine(parts, spots, routes, aux, normed, middle, cot, packed, choice_count, expert_count):
     rows, width = normed.shape
-    slot_count = returned.shape[0]
+    local_count = len(parts)
+    slot_count = expert_count * CAP
     size = 256
     block = lambda columns: pl.BlockSpec((size, columns), lambda j: (j, 0))
-    whole = lambda shape: pl.BlockSpec(shape, lambda j: (0, 0))
+    whole = lambda shape: pl.BlockSpec(shape, lambda j: (0,) * len(shape))
     return pl.pallas_call(
-        functools.partial(combine_kernel, expert_count),
+        functools.partial(combine_kernel, expert_count, local_count),
         grid=(rows // size,),
         out_shape=[
             jax.ShapeDtypeStruct((rows, width), jnp.bfloat16),
@@ -491,8 +513,8 @@
             jax.ShapeDtypeStruct((rows, width), jnp.float32),
             jax.ShapeDtypeStruct((width, 128), jnp.float32),
         ],
-        in_specs=[
-            whole((slot_count, width)),
+        in_specs=[whole(part.shape) for part in parts]
+        + [
             block(128),
             block(2),
             block(128),
@@ -502,86 +524,159 @@
             pl.BlockSpec((width, 256), lambda j: (0, 12)),
         ],
         out_specs=[block(width), block(choice_count), block(width), whole((width, 128))],
-        scratch_shapes=[pltpu.VMEM((8, width), jnp.float32)],
+        scratch_shapes=[pltpu.VMEM((16, width), jnp.float32), pltpu.VMEM((width, 128), jnp.float32)],
         compiler_params=pltpu.CompilerParams(
-            dimension_semantics=("arbitrary",), vmem_limit_bytes=48 * 2**20
+            dimension_semantics=("arbitrary",), vmem_limit_bytes=56 * 2**20
         ),
         cost_estimate=pl.CostEstimate(
-            flops=4 * slot_count * rows * width,
-            bytes_accessed=16 * rows * width + 2 * slot_count * width,
+            flops=6 * slot_count * rows * width,
+            bytes_accessed=14 * rows * width + 4 * slot_count * width,
             transcendentals=0,
         ),
         name="combine",
-    )(returned, spots, routes, aux, normed, middle, cot, packed)
-
-
-def combine_back_kernel(
-    back_ref, spots_ref, aux_ref, middle_ref, cot_ref, grad_ref, small_ref, small_grad_ref,
-    grad_middle_ref, small_out_ref, gain_ref,
-):
+    )(*parts, spots, routes, aux, normed, middle, cot, packed)
+
+
+def experts_kernel(linked, *refs):
+    if linked:
+        (
+            rows_ref, grads_ref, w_gate_ref, w_up_ref, w_down_ref, before_ref,
+            grad_gu_ref, grad_down_ref, first_in, second_in,
+            turned_ref, out_ref, back_ref, both_ref, send_sem, recv_sem,
+        ) = refs
+    else:
+        (
+            rows_ref, grads_ref, w_gate_ref, w_up_ref, w_down_ref, grad_gu_ref, grad_down_ref,
+            both_ref, turned_ref, out_ref, back_ref,
+        ) = refs
     step = pl.program_id(0)
+    width = rows_ref.shape[-1]
+    rows = rows_ref[...].reshape(-1, width)
+    grads = grads_ref[...].reshape(-1, width)
+
+    if linked:
+        me, mine = place()
+        owner_count = both_ref.shape[0]
+        peers = [lax.rem(mine + k, owner_count) for k in range(1, owner_count)]
+
+        def trade(n, source, target, k, peer):
+            return pltpu.make_async_remote_copy(
+                src_ref=source.at[peer],
+                dst_ref=target.at[mine],
+                send_sem=send_sem.at[n, k],
+                recv_sem=recv_sem.at[n, mine],
+                device_id=(me, peer),
+                device_id_type=MESH,
+            )
+
+        def keep(n, source, target):
+            return pltpu.make_async_copy(source.at[mine], target.at[mine], send_sem.at[n, 0])
+
+        def trade_start(n, source, target):
+            for k, peer in enumerate(peers):
+                trade(n, source, target, k + 1, peer).start()
+            keep(n, source, target).start()
+
+        def trade_finish(n, source, target):
+            keep(n, source, target).wait()
+            for k, peer in enumerate(peers):
+                pltpu.make_async_copy(target.at[peer], target.at[peer], recv_sem.at[n, peer]).wait()
+                trade(n, source, target, k + 1, peer).wait_send()
+
+        @pl.when(step == 0)
+        def _():
+            greet([(me, peer) for peer in peers])
+            trade_start(0, before_ref, first_in)
 
     @pl.when(step == 0)
     def _():
-        gain_ref[0:8, :] = jnp.transpose(small_ref[:, :128].astype(jnp.float32))[16:24, :]
-        gain_ref[8:16, :] = jnp.zeros((8, gain_ref.shape[1]), jnp.float32)
-
-    rows, width = middle_ref.shape
-    slots = lane_ids((rows, back_ref.shape[0]))
-    chosen = jnp.where(
-        (slots == spots_ref[:, 0:1]) | (slots == spots_ref[:, 1:2]), 1.0, 0.0
-    ).astype(jnp.bfloat16)
-    grads = grad_ref[...] + nn(chosen, back_ref[...])
-    middle, scale = middle_ref[...], aux_ref[:, 6:7]
-    gain_ref[8:9, :] += jnp.sum(grads * middle * scale, 0, keepdims=True)
-    weighted = grads * gain_ref[3:4, :]
-    mean = jnp.mean(weighted * middle, -1, keepdims=True)
-    grad_middle_ref[...] = (
-        cot_ref[...].astype(jnp.float32) + scale * weighted - middle * (scale * scale * scale * mean)
-    )
+        turned_ref[...] = jnp.transpose(rows)
+        out_ref[...] = jnp.zeros_like(out_ref)
+        back_ref[...] = jnp.zeros_like(back_ref)
+
+    w_gate, w_up, w_down = w_gate_ref[...], w_up_ref[...], w_down_ref[0]
+    gate, up = nn(rows, w_gate), nn(rows, w_up)
+    squashed = 1.0 / (1.0 + jnp.exp(-gate))
+    silu = gate * squashed
+    activated = (silu * up).astype(jnp.bfloat16)
+    grad_act = nt(grads, w_down)
+    grad_gate = (grad_act * up * (squashed * (1.0 + gate * (1.0 - squashed)))).astype(jnp.bfloat16)
+    grad_up = (grad_act * silu).astype(jnp.bfloat16)
+    out_ref[...] += nn(activated, w_down)
+    grad_down_ref[...] = tn(activated, grads).astype(jnp.bfloat16)
+    back_ref[...] += nt(grad_gate, w_gate) + nt(grad_up, w_up)
+    grad_gu_ref[0] = nn(turned_ref[...], grad_gate).astype(jnp.bfloat16)
+    grad_gu_ref[1] = nn(turned_ref[...], grad_up).astype(jnp.bfloat16)
 
     @pl.when(step == pl.num_programs(0) - 1)
     def _():
-        column = jnp.transpose(jnp.broadcast_to(gain_ref[8:9, :], (128, width)))
-        small_grad = small_grad_ref[...]
-        small_out_ref[...] = jnp.where(lane_ids(small_grad.shape) == 19, column, small_grad)
-
-
-def combine_back(back, spots, aux, middle, cot, grad, packed, small_grad):
-    rows, width = middle.shape
-    slot_count = back.shape[0]
-    size = 256
-    block = lambda columns: pl.BlockSpec((size, columns), lambda j: (j, 0))
-    whole = lambda shape: pl.BlockSpec(shape, lambda j: (0, 0))
+        shape = (both_ref.shape[0],) + both_ref.shape[2:]
+        both_ref[:, 0] = out_ref[...].astype(jnp.bfloat16).reshape(shape)
+        both_ref[:, 1] = back_ref[...].astype(jnp.bfloat16).reshape(shape)
+        if linked:
+            trade_start(1, both_ref, second_in)
+            trade_finish(0, before_ref, first_in)
+            trade_finish(1, both_ref, second_in)
+
+
+def experts(arrived, arrived_grad, gate_up, down, at, before=None, collective=None):
+    owners, _, cap, width = arrived.shape
+    hidden = down.shape[1]
+    count = owners * cap
+    block = FF_BLOCK if count <= 1024 else FF_BLOCK // 4
+    steps = hidden // block
+    linked = before is not None
+    pairs = pl.BlockSpec(
+        (owners, 1, cap, width), lambda j: (0, at, 0, 0), pipeline_mode=pl.Buffered(1)
+    )
+    anywhere = pl.BlockSpec(memory_space=pl.ANY)
+    both = jax.ShapeDtypeStruct((owners, 2, cap, width), jnp.bfloat16)
+    links = {"collective_id": collective, "has_side_effects": True} if linked else {}
     return pl.pallas_call(
-        combine_back_kernel,
-        grid=(rows // size,),
+        functools.partial(experts_kernel, linked),
+        grid=(steps,),
         out_shape=[
-            jax.ShapeDtypeStruct((rows, width), jnp.float32),
-            jax.ShapeDtypeStruct((width, 128), jnp.float32),
-        ],
+            jax.ShapeDtypeStruct((2, width, hidden), jnp.bfloat16),
+            jax.ShapeDtypeStruct((hidden, width), jnp.bfloat16),
+        ]
+        + [both] * (2 if linked else 1),
         in_specs=[
-            whole((slot_count, width)),
-            block(128),
-            block(128),
-            block(width),
-            block(width),
-            block(width),
-            pl.BlockSpec((width, 256), lambda j: (0, 12)),
-            whole((width, 128)),
-        ],
-        out_specs=[block(width), whole((width, 128))],
-        scratch_shapes=[pltpu.VMEM((16, width), jnp.float32)],
+            pairs,
+            pairs,
+            pl.BlockSpec((width, block), lambda j: (0, j)),
+            pl.BlockSpec((width, block), lambda j: (0, steps + j)),
+            pl.BlockSpec((1, block, width), lambda j: (at, j, 0)),
+        ]
+        + [anywhere] * linked,
+        out_specs=[
+            pl.BlockSpec((2, width, block), lambda j: (0, 0, j)),
+            pl.BlockSpec((block, width), lambda j: (j, 0)),
+        ]
+        + ([anywhere] * 2 if linked else [pl.BlockSpec(both.shape, lambda j: (0, 0, 0, 0))]),
+        scratch_shapes=[
+            pltpu.VMEM((width, count), jnp.bfloat16),
+            pltpu.VMEM((count, width), jnp.float32),
+            pltpu.VMEM((count, width), jnp.float32),
+        ]
+        + (
+            [
+                pltpu.VMEM(both.shape, jnp.bfloat16),
+                pltpu.SemaphoreType.DMA((2, owners)),
+                pltpu.SemaphoreType.DMA((2, owners)),
+            ]
+            if linked
+            else []
+        ),
         compiler_params=pltpu.CompilerParams(
-            dimension_semantics=("arbitrary",), vmem_limit_bytes=48 * 2**20
+            dimension_semantics=("arbitrary",), vmem_limit_bytes=58 * 2**20, **links
         ),
         cost_estimate=pl.CostEstimate(
-            flops=2 * slot_count * rows * width,
-            bytes_accessed=14 * rows * width + 2 * slot_count * width,
-            transcendentals=0,
+            flops=18 * count * width * hidden,
+            bytes_accessed=12 * width * hidden + 8 * count * width,
+            transcendentals=count * hidden,
         ),
-        name="combine_back",
-    )(back, spots, aux, middle, cot, grad, packed, small_grad)
+        name="experts",
+    )(arrived, arrived_grad, gate_up, gate_up, down, *([before] if linked else []))
 
 
 def dp_grid(dp_count):
@@ -867,26 +962,20 @@
     )(*shards, *trades)
 
 
-def add_into(target, source, target_at):
-    rows = target.shape[-2]
-    step = 16
-
-    def body(i, carry):
-        here = pl.ds(pl.multiple_of(i * step, step), step)
-        target[target_at + (here, slice(None))] = (
-            target[target_at + (here, slice(None))].astype(jnp.float32)
-            + source(here).astype(jnp.float32)
-        ).astype(target.dtype)
+def by_rows(count, body):
+    def step(i, carry):
+        body(i * 16)
         return carry
 
-    lax.fori_loop(0, rows // step, body, 0)
+    lax.fori_loop(0, count // 16, step, 0)
 
 
 def final_reduce_kernel(small_count, part_ref, *refs):
     small_refs, refs = refs[:small_count], refs[small_count:]
     (
-    part_out, small_out, swap, part_in, part_low, part_high, small_in, small_low, small_high, final_low, final_in,
-    swap_send, swap_recv, in_send, in_recv, line_send, line_recv, last_send, last_recv,
+        part_out, small_out, swap, part_in, part_low, part_high, small_in, small_low, small_high,
+        final_low, final_in,
+        swap_send, swap_recv, in_send, in_recv, line_send, line_recv, last_send, last_recv,
     ) = refs
     outer_count, inner_count = 4, 2
     me, mine = place()
@@ -895,6 +984,7 @@
     mate, across = mine + 1 - 2 * side, lax.rem(mine + 2, 4)
     beside = me + 1 - 2 * inner
     half_rows = small_refs[0].shape[1] // 2
+    part_rows = part_ref.shape[2]
     starts = [sum(ref.shape[2] for ref in small_refs[:n]) for n in range(small_count + 1)]
 
     def remote(source, target, device, send_at, recv_at):
@@ -926,113 +1016,146 @@
             swap_recv.at[n],
         )
 
-    def inner_copy(p, plane):
-        if p == 0:
-            source = part_ref.at[plane * inner_count + 1 - inner]
-            target = part_in.at[plane]
-        else:
-            source = swap.at[plane * inner_count + 1 - inner]
-            target = small_in.at[plane]
-        return remote(source, target, (beside, mine), in_send.at[p, plane], in_recv.at[p, plane])
-
-    ins, lows, highs = (part_in, small_in), (part_low, small_low), (part_high, small_high)
-
-    def line_copy(p, plane, upward, device_plane):
-        target = (lows if upward else highs)[p].at[plane]
+    def inner_copy(plane):
+        return remote(
+            swap.at[plane * inner_count + 1 - inner],
+            small_in.at[plane],
+            (beside, mine),
+            in_send.at[plane],
+            in_recv.at[plane],
+        )
+
+    def line_copy(p, plane, upward, device_plane, source):
+        target = ((part_low, small_low), (part_high, small_high))[0 if upward else 1][p].at[plane]
         way = 0 if upward else 1
         return remote(
-            ins[p].at[plane],
+            source,
             target,
             (device_plane * inner_count + inner, mine),
             line_send.at[p, way, plane],
             line_recv.at[p, way, plane],
         )
 
+    def wide(values):
+        return values.astype(jnp.float32)
+
     def add_own(chunk):
-        def body(i, carry):
-            here = pl.ds(pl.multiple_of(i * 16, 16), 16)
-            there = pl.ds(pl.multiple_of(side * half_rows + i * 16, 16), 16)
+        def body(at):
+            here = pl.ds(pl.multiple_of(at, 16), 16)
+            there = pl.ds(pl.multiple_of(side * half_rows + at, 16), 16)
             for n in range(small_count):
                 columns = slice(starts[n], starts[n + 1])
                 swap[chunk, here, columns] = (
-                    swap[chunk, here, columns].astype(jnp.float32)
-                    + small_refs[n][chunk, there, :].astype(jnp.float32)
+                    wide(swap[chunk, here, columns]) + wide(small_refs[n][chunk, there, :])
                 ).astype(swap.dtype)
-            return carry
-
-        lax.fori_loop(0, half_rows // 16, body, 0)
+
+        by_rows(half_rows, body)
 
     def at_plane(o):
         order = sorted(range(outer_count), key=lambda t: (-abs(t - o), t))
-        for plane in order:
-            inner_copy(0, plane).start()
+
+        def arrive(p, plane, upward):
+            line_copy(p, plane, upward, o, part_in.at[0] if p == 0 else small_in.at[0]).wait_recv()
+
+        def held(plane):
+            relayed = (plane > o > 0) or (plane < o < outer_count - 1)
+            return part_in.at[plane] if relayed else part_ref.at[:, plane]
+
+        def line_start(p, plane):
+            source = held(plane) if p == 0 else small_in.at[plane]
+            return line_copy(p, plane, plane > o, o + 1 if plane > o else o - 1, source)
+
         for n in range(small_count):
             swap_copy(n).start()
+        for plane in order:
+            if (plane > o and o == 0) or (plane < o and o == outer_count - 1):
+                line_start(0, plane).start()
         for n in range(small_count):
             swap_copy(n).wait_recv()
         for plane in order:
             for column in range(inner_count):
                 add_own(plane * inner_count + column)
-            inner_copy(1, plane).start()
+            inner_copy(plane).start()
         for plane in order:
-            for p in (0, 1):
-                inner_copy(p, plane).wait_recv()
-                if p == 0:
-                    add_into(ins[p], lambda here, plane=plane: part_ref[plane * inner_count + inner, here, :], (plane,))
-                else:
-                    add_into(ins[p], lambda here, plane=plane: swap[plane * inner_count + inner, here, :], (plane,))
-                if plane > o:
+            upward = plane > o
+            if plane != o and 0 < o < outer_count - 1:
+                arrive(0, plane, upward)
+                lines = part_low if upward else part_high
+
+                def relay(at, plane=plane, lines=lines):
+                    here = pl.ds(pl.multiple_of(at, 16), 16)
+                    part_in[plane, :, here, :] = (
+                        wide(part_ref[:, plane, here, :]) + wide(lines[plane, :, here, :])
+                    ).astype(part_in.dtype)
+
+                by_rows(part_rows, relay)
+                line_start(0, plane).start()
+            inner_copy(plane).wait_recv()
+            relayed = plane != o and 0 < o < outer_count - 1
+            lines = small_low if upward else small_high
+            if relayed:
+                arrive(1, plane, upward)
+
+            def gather(at, plane=plane, lines=lines, relayed=relayed):
+                here = pl.ds(pl.multiple_of(at, 16), 16)
+                total = wide(small_in[plane, here, :]) + wide(swap[plane * inner_count + inner, here, :])
+                if relayed:
+                    total = total + wide(lines[plane, here, :])
+                small_in[plane, here, :] = total.astype(small_in.dtype)
+
+            by_rows(half_rows, gather)
+            if plane != o:
+                line_start(1, plane).start()
+        for p in (1, 0):
+            if o > 0:
+                arrive(p, o, True)
+            if o < outer_count - 1:
+                arrive(p, o, False)
+            if p == 1:
+
+                def finish_small(at):
+                    here = pl.ds(pl.multiple_of(at, 16), 16)
+                    total = wide(small_in[o, here, :])
                     if o > 0:
-                        line_copy(p, plane, True, o + 1).wait_recv()
-                        add_into(ins[p], lambda here, p=p, plane=plane: lows[p][plane, here, :], (plane,))
-                    line_copy(p, plane, True, o + 1).start()
-                if plane < o:
+                        total = total + wide(small_low[o, here, :])
                     if o < outer_count - 1:
-                        line_copy(p, plane, False, o - 1).wait_recv()
-                        add_into(ins[p], lambda here, p=p, plane=plane: highs[p][plane, here, :], (plane,))
-                    line_copy(p, plane, False, o - 1).start()
-                if plane == o:
-                    if o > 0:
-                        line_copy(p, plane, True, o).wait_recv()
-                    if o < outer_count - 1:
-                        line_copy(p, plane, False, o).wait_recv()
-                    target = part_out if p == 0 else final_low
-                    rows = target.shape[0]
-
-                    def body(i, carry, p=p, target=target):
-                        here = pl.ds(pl.multiple_of(i * 16, 16), 16)
-                        total = ins[p][o, here, :].astype(jnp.float32)
+                        total = total + wide(small_high[o, here, :])
+                    final_low[here, :] = total.astype(final_low.dtype)
+
+                by_rows(half_rows, finish_small)
+                remote(final_low, final_in, (me, across), last_send.at[0], last_recv.at[0]).start()
+            else:
+
+                def finish_part(at):
+                    here = pl.ds(pl.multiple_of(at, 16), 16)
+                    for side_at in range(2):
+                        total = wide(part_ref[side_at, o, here, :])
                         if o > 0:
-                            total = total + lows[p][o, here, :].astype(jnp.float32)
+                            total = total + wide(part_low[o, side_at, here, :])
                         if o < outer_count - 1:
-                            total = total + highs[p][o, here, :].astype(jnp.float32)
-                        target[here, :] = total.astype(target.dtype)
-                        return carry
-
-                    lax.fori_loop(0, rows // 16, body, 0)
+                            total = total + wide(part_high[o, side_at, here, :])
+                        size = total.shape[1]
+                        part_out[here, side_at * size : (side_at + 1) * size] = total
+
+                by_rows(part_rows, finish_part)
         for plane in range(outer_count):
-            for p in (0, 1):
-                inner_copy(p, plane).wait_send()
-                if plane > o:
-                    line_copy(p, plane, True, o + 1).wait_send()
-                if plane < o:
-                    line_copy(p, plane, False, o - 1).wait_send()
+            inner_copy(plane).wait_send()
+            if plane != o:
+                line_start(0, plane).wait_send()
+                line_start(1, plane).wait_send()
         for n in range(small_count):
             swap_copy(n).wait_send()
 
     for o in range(outer_count):
         pl.when(outer == o)(functools.partial(at_plane, o))
-    across_copy = remote(final_low, final_in, (me, across), last_send.at[0], last_recv.at[0])
-    across_copy.start()
-    across_copy.wait()
-
-    def total_body(i, carry):
-        here = pl.ds(pl.multiple_of(i * 16, 16), 16)
-        there = pl.ds(pl.multiple_of(side * half_rows + i * 16, 16), 16)
-        small_out[there, :] = final_low[here, :].astype(jnp.float32) + final_in[here, :].astype(jnp.float32)
-        return carry
-
-    lax.fori_loop(0, half_rows // 16, total_body, 0)
+    remote(final_low, final_in, (me, across), last_send.at[0], last_recv.at[0]).wait()
+
+    def total_body(at):
+        here = pl.ds(pl.multiple_of(at, 16), 16)
+        there = pl.ds(pl.multiple_of(side * half_rows + at, 16), 16)
+        small_out[there, :] = wide(final_low[here, :]) + wide(final_in[here, :])
+
+    by_rows(half_rows, total_body)
     mate_copy = remote(
         small_out.at[own_rows, :], small_out.at[own_rows, :], (me, mate), last_send.at[1], last_recv.at[1]
     )
@@ -1041,8 +1164,8 @@
 
 
 def final_reduce(part, smalls, collective):
-    chunk_count, part_rows, part_columns = part.shape
-    small_rows = smalls[0].shape[1]
+    sides, planes, part_rows, part_columns = part.shape
+    chunk_count, small_rows, _ = smalls[0].shape
     small_columns = sum(small.shape[2] for small in smalls)
     low = jnp.bfloat16
     in_vmem = pl.BlockSpec(memory_space=pltpu.VMEM)
@@ -1050,22 +1173,22 @@
     return pl.pallas_call(
         functools.partial(final_reduce_kernel, len(smalls)),
         out_shape=[
-            jax.ShapeDtypeStruct((part_rows, part_columns), jnp.float32),
+            jax.ShapeDtypeStruct((part_rows, sides * part_columns), jnp.float32),
             jax.ShapeDtypeStruct((small_rows, small_columns), jnp.float32),
         ],
         in_specs=[in_vmem] * (1 + len(smalls)),
         out_specs=[in_vmem] * 2,
         scratch_shapes=[pltpu.VMEM((chunk_count, half, small_columns), low)]
-        + [pltpu.VMEM((4, part_rows, part_columns), low)] * 3
-        + [pltpu.VMEM((4, half, small_columns), low)] * 3
+        + [pltpu.VMEM((planes, sides, part_rows, part_columns), low)] * 3
+        + [pltpu.VMEM((planes, half, small_columns), low)] * 3
         + [pltpu.VMEM((half, small_columns), low)] * 2
         + [
             pltpu.SemaphoreType.DMA((len(smalls),)),
             pltpu.SemaphoreType.DMA((len(smalls),)),
-            pltpu.SemaphoreType.DMA((2, 4)),
-            pltpu.SemaphoreType.DMA((2, 4)),
-            pltpu.SemaphoreType.DMA((2, 2, 4)),
-            pltpu.SemaphoreType.DMA((2, 2, 4)),
+            pltpu.SemaphoreType.DMA((planes,)),
+            pltpu.SemaphoreType.DMA((planes,)),
+            pltpu.SemaphoreType.DMA((2, 2, planes)),
+            pltpu.SemaphoreType.DMA((2, 2, planes)),
             pltpu.SemaphoreType.DMA((2,)),
             pltpu.SemaphoreType.DMA((2,)),
         ],
@@ -1119,7 +1242,9 @@
         packed_full = small_gather(packed, dp_count, 1)
     else:
         packed_full = lax.all_gather(packed, "dp", axis=0, tiled=True)
-    gate_up_full = lax.all_gather(w_gate_up, "dp", axis=1, tiled=True)
+    gate_up_full = [
+        lax.all_gather(w_gate_up[e], "dp", axis=0, tiled=True) for e in range(local_count)
+    ]
     normed_one, queries, keys, values, attended, middle, normed_two, aux = attention_forward(
         inputs, packed_full, docs_row, docs_column, cosine, sine, route_rows, resid
     )
@@ -1139,57 +1264,37 @@
     arrived = arrived.reshape(owner_count, local_count, CAP, width)
     arrived_grad = arrived_grad.reshape(owner_count, local_count, CAP, width)
 
-    gate_up = jnp.einsum(
-        "secd,edf->secf", arrived, gate_up_full, preferred_element_type=jnp.float32
-    )
-    gate_part = gate_up[..., :hidden_count]
-    up_part = gate_up[..., hidden_count:]
-    squashed = lax.logistic(gate_part)
-    silu_gate = gate_part * squashed
-    activated = (silu_gate * up_part).astype(jnp.bfloat16)
-    grad_down = jnp.einsum(
-        "secf,secd->efd", activated, arrived_grad, preferred_element_type=jnp.float32
-    ).astype(jnp.bfloat16)
-    activated, arrived_grad, grad_down = lax.optimization_barrier(
-        (activated, arrived_grad, grad_down)
-    )
-    grad_expert_down = lax.psum_scatter(
-        grad_down, "dp", scatter_dimension=1, tiled=True
-    ).astype(jnp.float32)
-    expert_out = jnp.einsum(
-        "secf,efd->secd", activated, down_full, preferred_element_type=jnp.float32
-    ).astype(jnp.bfloat16)
-    returned = exchange(expert_out.reshape(owner_count, local_count * CAP, width))
-    grad_act = jnp.einsum(
-        "secd,efd->secf", arrived_grad, down_full, preferred_element_type=jnp.float32
-    )
-    grad_gate = grad_act * up_part * squashed * (1.0 + gate_part * (1.0 - squashed))
-    grad_up = grad_act * silu_gate
-    grad_gate_up = jnp.concatenate([grad_gate, grad_up], -1).astype(jnp.bfloat16)
-    grad_rows = jnp.einsum(
-        "secf,edf->secd", grad_gate_up, gate_up_full, preferred_element_type=jnp.float32
-    ).astype(jnp.bfloat16)
-    back = exchange(grad_rows.reshape(owner_count, local_count * CAP, width))
-    gu_grads = [
-        jnp.einsum(
-            "scd,scf->df", arrived[:, e], grad_gate_up[:, e], preferred_element_type=jnp.float32
-        ).astype(jnp.bfloat16)
-        for e in range(local_count)
-    ]
-    returned, gu_grads = lax.optimization_barrier((returned, gu_grads))
-    linked = local_count - 1 if own_links else local_count
-    gu_parts = [
-        lax.psum_scatter(gu_grads[e], "dp", scatter_dimension=0, tiled=True).astype(jnp.float32)
-        for e in range(linked)
-    ]
-
-    output, logit_grad, grad_part, small_grad = combine(
-        returned.reshape(expert_count * CAP, width), spots, route_rows, aux, normed_two, middle,
-        cot, packed_full, choice_count, expert_count,
-    )
-    grad_middle, small_grad = combine_back(
-        back.reshape(expert_count * CAP, width), spots, aux, middle, cot, grad_part, packed_full,
-        small_grad,
+    parts, gu_parts, down_parts = [], [], []
+    for e in range(local_count):
+        if own_links and e == local_count - 1:
+            grad_gu, grad_down, *parts = experts(
+                arrived, arrived_grad, gate_up_full[e], down_full, e, both, 4
+            )
+        else:
+            grad_gu, grad_down, both = experts(
+                arrived, arrived_grad, gate_up_full[e], down_full, e
+            )
+            if not own_links:
+                parts.append(exchange(both))
+        down_parts.append(lax.psum_scatter(grad_down, "dp", scatter_dimension=0, tiled=True))
+        if own_links and e == local_count - 1:
+            inner = lax.axis_index("dp") % 2
+            grad_gu = grad_gu.reshape(2, dp_count // 2, 2, width // dp_count, hidden_count)
+            theirs = lax.ppermute(
+                lax.dynamic_index_in_dim(grad_gu, 1 - inner, 2, False),
+                "dp",
+                [(i, i + 1 - 2 * (i % 2)) for i in range(dp_count)],
+            )
+        else:
+            gu_part = lax.psum_scatter(grad_gu, "dp", scatter_dimension=1, tiled=True)
+            gu_parts.append(
+                jnp.concatenate([gu_part[0], gu_part[1]], -1).astype(jnp.float32)
+            )
+
+    if own_links:
+        parts, down_parts[0] = lax.optimization_barrier((parts, down_parts[0]))
+    output, logit_grad, grad_middle, small_grad = combine(
+        parts, spots, route_rows, aux, normed_two, middle, cot, packed_full, choice_count, expert_count
     )
     token_grad, *weight_grads = attention_backward(
         grad_middle, queries, keys, values, attended, normed_one, inputs, packed_full, docs_row,
@@ -1197,8 +1302,13 @@
     )
     if own_links:
         part_width = width // dp_count
+        theirs, weight_grads = lax.optimization_barrier((theirs, weight_grads))
+        linked = (
+            lax.dynamic_index_in_dim(grad_gu, inner, 2, False).astype(jnp.float32)
+            + theirs.astype(jnp.float32)
+        ).astype(jnp.bfloat16)
         gu_part, packed_part = final_reduce(
-            gu_grads[linked].reshape(dp_count, part_width, 2 * hidden_count),
+            linked,
             [grad.reshape(dp_count, part_width, grad.shape[1]) for grad in weight_grads],
             3,
         )
@@ -1223,7 +1333,7 @@
         small_part[:, 12:16],
         small_part[:, 16:18],
         jnp.stack(gu_parts),
-        grad_expert_down,
+        jnp.stack(down_parts).astype(jnp.float32),
     )
 
 

time: 705 us -> 697 us (0.989)
  Pallas kernels: 487 us -> 628 us
  matrix products: 115 us -> 0 us
  local copies, waits for them, and re-layouts: 36.9 us -> 23.2 us
  starting transfers between devices: 9.68 us -> 0.23 us
  other arithmetic: 18.6 us -> 10.3 us
    dot_general x7 -> x0, matrix products: 115 us -> none  [the longest x2 27.4 us: shards(): jnp.einsum('scd,scf->df', arrived[:, e], grad_gate_up[:, e], preferred_el...]
    pallas_call x2 -> x3, Pallas kernels: 26.9 us -> 135 us  [the longest x2 114 us: experts(): pl.pallas_call(functools.partial(experts_kernel, linked), grid=(steps,),...]
    pallas_call x1, Pallas kernels: 122 us -> 143 us  [expert_gather(): pl.pallas_call(functools.partial(expert_gather_kernel, dp_count, len(shar...]
    all_to_all x2 -> x0, waiting for transfers between devices: 17.3 us -> none  [the longest x1 17.3 us: shards(): back = exchange(grad_rows.reshape(owner_count, local_count * CAP, width))]
    pallas_call x1, Pallas kernels: 167 us -> 183 us  [final_reduce(): pl.pallas_call(functools.partial(final_reduce_kernel, len(smalls)), out_s...]
    ppermute x0 -> x1, waiting for transfers between devices: none -> 13.5 us  [shards(): lax.ppermute(lax.dynamic_index_in_dim(grad_gu, 1 - inner, 2, False), 'dp'...]
    unnamed x45, local copies, waits for them, and re-layouts: 18.1 us -> 5 us
    all_to_all x2 -> x0, starting transfers between devices: 9.6 us -> none  [the longest x1 4.96 us: shards(): exchange(expert_out.reshape(owner_count, local_count * CAP, width))]
  transfers between devices with their start and end apart: 5 -> 6, of which waited for: 1 -> 1; matrix products, arithmetic and copies ran while one was open for 16% -> 4% of each run, Pallas kernels for 70% -> 91%
where the time goes in v4:
time: 697 us; the launch traced here: 691 us
  Pallas kernels  628 us (90%)
  local copies, waits for them, and re-layouts  23.2 us (3%)
  waiting for transfers between devices  14.9 us (2%)
  between operations  14.5 us (2%)
  other arithmetic  10.3 us (1%)
    pallas_call x1, Pallas kernels, final_reduce(): pl.pallas_call(functools.partial(final_reduce_kernel, len(smalls)), out_s...  183 us
    pallas_call x1, Pallas kernels, expert_gather(): pl.pallas_call(functools.partial(expert_gather_kernel, dp_count, len(shar...  143 us
    pallas_call x2, Pallas kernels, experts(): pl.pallas_call(functools.partial(experts_kernel, linked), grid=(steps,),...  114 us
    pallas_call x1, Pallas kernels, small_gather(): pl.pallas_call(functools.partial(small_gather_kernel, dp_count), out_shap...  60.6 us
    pallas_call x1, Pallas kernels, attention_backward(): pl.pallas_call(attention_backward_kernel, grid=(groups,), out_shape=[jax....  56.4 us
    pallas_call x1, Pallas kernels, attention_forward(): pl.pallas_call(attention_forward_kernel, grid=(groups,), out_shape=[full]...  33.4 us
    pallas_call x1, Pallas kernels, combine(): pl.pallas_call(functools.partial(combine_kernel, expert_count, local_coun...  21.3 us
  transfers between devices with their start and end apart: 6, of which 1 were waited for; matrix products, arithmetic and copies ran while one was open for 4% of the time, Pallas kernels for 91%

profile of v4, /device:TPU:19, one launch (start us, length us, event | category | flops | bytes accessed | tf_op | source)
XLA Modules:
  0.0 690.9 jit_solution(15192626909240940617)
XLA Ops:
  7.3 0.0 all-gather.7.cloned.1.call-start
  7.3 2.7 fusion.1
  10.0 0.0 all-gather.5.cloned.1.call-start
  10.1 0.7 all-gather.5.cloned.1.call-update
  10.8 0.0 reduce-scatter.4.cloned.1.call-start
  10.9 0.1 copy.40
  11.0 0.1 copy.41
  11.1 0.1 copy.42
  11.2 0.1 copy.43
  11.4 0.1 copy.44
  11.5 1.0 concatenate.13.shard_ref
  12.5 60.6 %small_gather.1.wq_ref.wk_ref.wv_ref.wo_ref.small_ref.refs_8_ = bf16[768,3328]{1,0:T(8,128)(2,1)} custom-call(bf16[96,3328]{1,0:T(8,128)(2,1)} %concatenate.13.shard_ref), custom_call_target="tpu_custom_call" | custom-call | tf_op jit(solution)/shard_map/small_gather/pallas_call | solution.py:772
  73.1 0.2 copy.39
  73.4 1.0 copy.46.docs_column_ref
  74.4 0.2 copy.45
  74.6 4.4 routing.1
  78.9 0.8 copy-done.1
  79.7 0.6 copy-done.2
  80.4 0.8 pad_convert_fusion.resid_ref
  81.2 33.4 %attention_forward.1 = (bf16[1024,768]{1,0:T(8,128)(2,1)}, bf16[1024,768]{1,0:T(8,128)(2,1)}, bf16[1024,768]{1,0:T(8,128)(2,1)}, bf16[1024,768]{1,0:T(8,128)(2,1...) custom-call(bf16[1024,768]{1,0:T(8,128)(2,1)} %bitcast.64, ...), custom_call_target="tpu_custom_call" | custom-call | flops 8053063680 | bytes 18874368 | tf_op jit(solution)/shard_map/attention_forward/pallas_call | solution.py:148
  114.6 11.7 %dispatch.1 = (bf16[2048,768]{1,0:T(8,128)(2,1)}, bf16[2048,768]{1,0:T(8,128)(2,1)}) custom-call(s32[8,1024]{1,0:T(8,128)} %copy-done.2, f32[1024,128]{1,0:T(8,128)} %get-tuple-element.56.aux_ref.refs_4_, bf16[1024,768]{1,0:T(8,128)(2,1)} %get-tuple-element.57.normed_ref.refs_5_, bf16[1024,768]{1,0:T(8,128)(2,1)} %bitcast.62), custom_call_target="tpu_custom_call" | custom-call | flops 6442450944 | bytes 9437184 | tf_op jit(solution)/shard_map/dispatch/pallas_call | solution.py:388
  126.3 143.4 %expert_gather.1 = (bf16[2,2048,768]{2,1,0:T(8,128)(2,1)}, bf16[4,512,768]{2,1,0:T(8,128)(2,1)}, bf16[4,512,768]{2,1,0:T(8,128)(2,1)}) custom-call(bf16[2,256,768]{2,1,0:T(8,128)(2,1)} %refs_0_.1, bf16[4,512,768]{2,1,0:T(8,128)(2,1)} %bitcast.39, bf16[4,512,768]{2,1,0:T(8,128)(2,1)} %bitcast.40), custom_call_target="tpu_custom_call" | custom-call | tf_op jit(solution)/shard_map/expert_gather/pallas_call | solution.py:942
  269.7 37.8 %experts.2 = (bf16[2,768,2048]{2,1,0:T(8,128)(2,1)}, bf16[2048,768]{1,0:T(8,128)(2,1)}, bf16[4,2,256,768]{3,2,1,0:T(8,128)(2,1)}) custom-call(bf16[4,2,256,768]{3,2,1,0:T(8,128)(2,1)} %bitcast.58, bf16[4,2,256,768]{3,2,1,0:T(8,128)(2,1)} %bitcast.60, bf16[768,4096]{1,0:T(8,128)(2,1)} %bitcast.56, bf16[768,4096]{1,0:T(8,128)(2,1)} %bitcast.57, ...), custom_call_target="tpu_custom_call" | custom-call | flops 28991029248 | bytes 25165824 | tf_op jit(solution)/shard_map/experts/pallas_call | solution.py:635
  307.5 0.0 reduce-scatter.8.cloned.1.call-start
  307.6 76.0 %experts.3 = (bf16[2,768,2048]{2,1,0:T(8,128)(2,1)}, bf16[2048,768]{1,0:T(8,128)(2,1)}, bf16[4,2,256,768]{3,2,1,0:T(8,128)(2,1)}, bf16[4,2,256,768]{3,2,1,0:T(8,128)(2,1)}) custom-call(bf16[4,2,256,768]{3,2,1,0:T(8,128)(2,1)} %bitcast.59, bf16[4,2,256,768]{3,2,1,0:T(8,128)(2,1)} %bitcast.61, bf16[768,4096]{1,0:T(8,128)(2,1)} %bitcast.54, ...), custom_call_target="tpu_custom_call" | custom-call | flops 28991029248 | bytes 25165824 | tf_op jit(solution)/shard_map/experts/pallas_call | solution.py:635
  383.7 0.0 reduce-scatter.6.cloned.1.call-start
  383.7 0.5 reduce-scatter.6.cloned.1.call-update
  384.3 4.0 dynamic-slice_bitcast_fusion
  388.3 0.0 collective-permute-start
  388.3 21.3 %combine.1 = (bf16[1024,768]{1,0:T(8,128)(2,1)}, bf16[1024,12]{1,0:T(8,128)(2,1)}, f32[1024,768]{1,0:T(8,128)}, f32[768,128]{1,0:T(8,128)}) custom-call(bf16[4,2,256,768]{3,2,1,0:T(8,128)(2,1)} %get-tuple-element.67.refs_0_, bf16[4,2,256,768]{3,2,1,0:T(8,128)(2,1)} %get-tuple-element.68.refs_1_, s32[1024,128]{1,0:T(8,128)} %copy-done.1, s32[1024,2]{1,0:T(8,128)} %bitcast.34, ...), custom_call_target="tpu_custom_call" | custom-call | flops 9663676416 | bytes 17301504 | tf_op jit(solution)/shard_map/combine/pallas_call | solution.py:507
  409.6 56.4 %attention_backward.1 = (bf16[1024,768]{1,0:T(8,128)(2,1)}, bf16[768,768]{1,0:T(8,128)(2,1)}, bf16[768,768]{1,0:T(8,128)(2,1)}, bf16[768,768]{1,0:T(8,128)(2,1)}...) custom-call(f32[1024,768]{1,0:T(8,128)} %get-tuple-element.72.grad_middle_ref, ...), custom_call_target="tpu_custom_call" | custom-call | flops 17716740096 | bytes 25165824 | tf_op jit(solution)/shard_map/attention_backward/pallas_call | solution.py:277
  465.9 13.5 %collective-permute-done = bf16[2,4,96,2048]{3,2,1,0:T(8,128)(2,1)} collective-permute-done((bf16[2,4,96,2048]{3,2,1,0:T(8,128)(2,1)}, bf16[2,4,96,2048]{3,2,1,0:T(8,128)(2,1)}, u32[]{:S(2)}, u32[]{:S(2)}) %collective-permute-start) | collective-permute-done | bytes 3145760 | tf_op jit(solution)/shard_map/ppermute | solution.py:1283
  479.5 5.1 fusion.part_ref
  484.6 183.0 %final_reduce.1 = (f32[96,4096]{1,0:T(8,128)}, f32[96,3328]{1,0:T(8,128)}) custom-call(bf16[2,4,96,2048]{3,2,1,0:T(8,128)(2,1)} %fusion.part_ref, bf16[8,96,768]{2,1,0:T(8,128)(2,1)} %bitcast.42, bf16[8,96,768]{2,1,0:T(8,128)(2,1)} %bitcast.43, bf16[8,96,768]{2,1,0:T(8,128)(2,1)} %bitcast.44, bf16[8,96,768]{2,1,0:T(8,128)(2,1)} %bitcast.45, ...), custom_call_target="tpu_custom_call" | custom-call | tf_op jit(solution)/shard_map/final_reduce/pallas_call | solution.py:1173
  667.6 2.2 slice.41
  669.8 1.7 slice.42
  671.5 0.8 slice.45
  672.3 0.9 slice.46
  673.2 0.9 slice.47
  674.0 0.7 copy.50
  674.7 0.7 copy.51
  675.4 0.6 copy.52
  676.0 0.8 copy.49
  676.8 1.6 slice_reduce_fusion
  678.4 2.4 maximum_convert_fusion.1
  680.7 1.2 fusion.2
  681.9 0.1 maximum_convert_fusion
  682.1 1.9 pad_maximum_fusion
  (44 shorter events, 0.2 us)
Async XLA Ops:
  7.2 3.7 copy-start.11
  7.2 3.8 copy-start.12
  7.2 3.9 copy-start.13
  7.2 4.0 copy-start.14
  7.2 4.1 copy-start.15
  7.2 4.3 copy-start.4
  7.2 4.3 copy-start.7
  7.3 262.4 %all-gather.7.cloned.1.call-start = ((), (), s32[]{:S(2)}) async-start(), calls=%async_computation.7 | async-start | bytes 7077888 | tf_op jit(solution)/shard_map/all_gather | solution.py:1246
  10.0 297.5 %all-gather.5.cloned.1.call-start = ((), (), s32[]{:S(2)}) async-start(), calls=%async_computation.6 | async-start | bytes 7077888 | tf_op jit(solution)/shard_map/all_gather | solution.py:1246
  10.8 377.5 %reduce-scatter.4.cloned.1.call-start = ((), (), s32[]{:S(2)}) async-start(), calls=%async_computation.3 | async-start | bytes 3538944 | tf_op jit(solution)/shard_map/reduce_scatter | solution.py:1279
  12.5 60.6 %copy-start.9 = (s32[1,1024,2]{1,2,0:T(2,128)S(1)}, s32[1,1024,2]{1,2,0:T(2,128)}, u32[]{:S(2)}) copy-start(s32[1,1024,2]{1,2,0:T(2,128)} %param.18) | copy-start | bytes 24580
  12.5 60.8 %copy-start.10 = (s32[1,1024]{1,0:T(1,128)S(1)}, s32[1,1024]{1,0:T(1,128)}, u32[]{:S(2)}) copy-start(s32[1,1024]{1,0:T(1,128)} %docs_row_ref.3) | copy-start | bytes 12292
  12.5 61.9 %copy-start.8 = (bf16[1,1024,12]{1,2,0:T(8,128)(2,1)S(1)}, bf16[1,1024,12]{1,2,0:T(8,128)(2,1)}, u32[]{:S(2)}) copy-start(bf16[1,1024,12]{1,2,0:T(8,128)(2,1)} %param.17) | copy-start | bytes 73732
  73.3 7.8 %copy-start = (s32[1,1024,2]{2,1,0:T(8,128)}, s32[1,1024,2]{2,1,0:T(8,128)S(1)}, u32[]{:S(2)}) copy-start(s32[1,1024,2]{2,1,0:T(8,128)S(1)} %copy.39) | copy-start | bytes 24580
  78.9 0.8 copy-start.1
  79.7 0.6 copy-start.2
  307.5 370.9 %reduce-scatter.8.cloned.1.call-start = ((), (), s32[]{:S(2)}) async-start(), calls=%async_computation.5 | async-start | bytes 3538944 | tf_op jit(solution)/shard_map/reduce_scatter | solution.py:1279
  383.7 297.1 %reduce-scatter.6.cloned.1.call-start = ((), (), s32[]{:S(2)}) async-start(), calls=%async_computation.4 | async-start | bytes 7077888 | tf_op jit(solution)/shard_map/reduce_scatter | solution.py:1289
  388.3 91.2 %collective-permute-start = (bf16[2,4,96,2048]{3,2,1,0:T(8,128)(2,1)}, bf16[2,4,96,2048]{3,2,1,0:T(8,128)(2,1)}, u32[]{:S(2)}, u32[]{:S(2)}) collective-permute-start(bf16[2,4,96,2048]{3,2,1,0:T(8,128)(2,1)} %dynamic-slice_bitcast_fusion), channel_id=1, source_target_pairs={{0,4},{4,0},{8,12},{12,8},{16,20},{20,16},{24,28},{28,24},{1,5},{5... | collective-permute-start | bytes 9437192 | tf_op jit(solution)/shard_map/ppermute | solution.py:1283
  388.3 91.2 %slice-start = ((s8[6291456]{0:T(1024)(128)(4,1)}), s8[4194304]{0:T(1024)(128)(4,1)S(1)}, s32[]{:S(2)}) async-start(s8[6291456]{0:T(1024)(128)(4,1)} %bitcast.36), calls=%async_computation.8 | async-start | bytes 8388608
  409.6 69.9 %slice-start.1 = ((s8[6291456]{0:T(1024)(128)(4,1)}), s8[2097152]{0:T(1024)(128)(4,1)S(1)}, s32[]{:S(2)}) async-start(s8[6291456]{0:T(1024)(128)(4,1)} %bitcast.36), calls=%async_computation.9 | async-start | bytes 4194304
  484.6 191.4 %copy-start.6 = (bf16[1024,12]{1,0:T(8,128)(2,1)S(1)}, bf16[1024,12]{1,0:T(8,128)(2,1)}, u32[]{:S(2)}) copy-start(bf16[1024,12]{1,0:T(8,128)(2,1)} %get-tuple-element.80) | copy-start | bytes 73732
  667.6 10.8 %copy-start.5 = (bf16[256,768]{1,0:T(8,128)(2,1)S(1)}, bf16[256,768]{1,0:T(8,128)(2,1)}, u32[]{:S(2)}) copy-start(bf16[256,768]{1,0:T(8,128)(2,1)} %reduce-scatter.4.cloned.1.call-done) | copy-start | bytes 1179652
  678.4 3.7 copy-start.3
Sparse Core Ops, SparseCore 0:
  10.8 119.0 all-gather.6
  132.7 147.6 all-gather.4
  307.6 75.0 reduce-scatter.3
  386.1 91.9 reduce-scatter.7
  481.5 175.7 reduce-scatter.5

commit v5 on v4

--- a/solution.py
+++ b/solution.py
@@ -60,14 +60,30 @@
     return docs_column[low:high, :] == docs_row[:, i * BLOCK : (i + 1) * BLOCK]
 
 
-def attention_forward_kernel(
-    tokens_ref, wq_ref, wk_ref, wv_ref, wo_ref, small_ref, docs_row_ref, docs_column_ref,
-    cosine_ref, sine_ref, routes_ref, resid_ref,
-    normed_ref, q_ref, k_ref, v_ref, attended_ref, middle_ref, normed_two_ref, aux_ref,
-    branch_ref,
-):
+def attention_forward_kernel(linked, *refs):
+    (
+        tokens_ref, wq_ref, wk_ref, wv_ref, wo_ref, small_ref, docs_row_ref, docs_column_ref,
+        cosine_ref, sine_ref, routes_ref, resid_ref,
+    ) = refs[:12]
+    (
+        normed_ref, q_ref, k_ref, v_ref, attended_ref, middle_ref, normed_two_ref, aux_ref,
+    ) = refs[12 + bool(linked) : 20 + bool(linked)]
     step = pl.program_id(0)
     rows = tokens_ref.shape[0]
+    if linked:
+        branch_ref = refs[22]
+        line = LineGather(refs[12].at[0], refs[21], linked, *refs[23:])
+
+        @pl.when(step == 0)
+        def _():
+            greet(line.peers())
+            line.start()
+
+        @pl.when(step == 2)
+        def _():
+            line.relay(1)
+    else:
+        branch_ref = refs[20]
 
     @pl.when(step == 0)
     def _():
@@ -135,9 +151,16 @@
         for at, column in enumerate(columns):
             aux = jnp.where(lanes == at, column, aux)
         aux_ref[...] = aux
-
-
-def attention_forward(tokens, packed, docs_row, docs_column, cosine, sine, routes, resid):
+        if linked:
+            line.relay(2)
+            line.relay(3)
+            line.finish()
+
+
+def attention_forward(
+    tokens, packed, docs_row, docs_column, cosine, sine, routes, resid, shards=None,
+    dp_count=None, collective=None,
+):
     rows, width = tokens.shape
     groups = width // GROUP
     low = jnp.bfloat16
@@ -145,15 +168,22 @@
     column = lambda at: pl.BlockSpec((width, GROUP), lambda j: (0, at + j))
     out_column = pl.BlockSpec((rows, GROUP), lambda j: (0, j))
     full = jax.ShapeDtypeStruct((rows, width), low)
+    linked = shards is not None
+    anywhere = pl.BlockSpec(memory_space=pl.ANY)
+    links = {"collective_id": collective, "has_side_effects": True} if linked else {}
+    gathered = []
+    if linked:
+        gathered = [jax.ShapeDtypeStruct((dp_count * shards.shape[1], shards.shape[2]), low)]
     return pl.pallas_call(
-        attention_forward_kernel,
+        functools.partial(attention_forward_kernel, dp_count if linked else 0),
         grid=(groups,),
         out_shape=[full] * 5
         + [
             jax.ShapeDtypeStruct((rows, width), jnp.float32),
             full,
             jax.ShapeDtypeStruct((rows, 128), jnp.float32),
-        ],
+        ]
+        + gathered,
         in_specs=[
             whole((rows, width)),
             column(0),
@@ -167,13 +197,16 @@
             whole((rows, 128)),
             whole((rows, 2)),
             whole((rows, 128)),
-        ],
+        ]
+        + [anywhere] * linked,
         out_specs=[whole((rows, width))]
         + [out_column] * 4
-        + [whole((rows, width)), whole((rows, width)), whole((rows, 128))],
-        scratch_shapes=[pltpu.VMEM((rows, width), jnp.float32)],
+        + [whole((rows, width)), whole((rows, width)), whole((rows, 128))]
+        + [anywhere] * linked,
+        scratch_shapes=[pltpu.VMEM((rows, width), jnp.float32)]
+        + (gather_semaphores(dp_count) if linked else []),
         compiler_params=pltpu.CompilerParams(
-            dimension_semantics=("arbitrary",), vmem_limit_bytes=56 * 2**20
+            dimension_semantics=("arbitrary",), vmem_limit_bytes=56 * 2**20, **links
         ),
         cost_estimate=pl.CostEstimate(
             flops=2 * rows * width * 4 * width + 8 * rows * rows * width // 2,
@@ -181,7 +214,10 @@
             transcendentals=rows * rows * HEADS // 2,
         ),
         name="attention_forward",
-    )(tokens, packed, packed, packed, packed, packed, docs_row, docs_column, cosine, sine, routes, resid)
+    )(
+        tokens, packed, packed, packed, packed, packed, docs_row, docs_column, cosine, sine, routes,
+        resid, *([shards] if linked else []),
+    )
 
 
 def attention_backward_kernel(
@@ -537,8 +573,13 @@
     )(*parts, spots, routes, aux, normed, middle, cot, packed)
 
 
-def experts_kernel(linked, *refs):
-    if linked:
+def experts_kernel(linked, dp_count, *refs):
+    if dp_count:
+        (
+            rows_ref, grads_ref, w_gate_ref, w_up_ref, w_down_ref, shards_ref, grad_gu_ref,
+            grad_down_ref, both_ref, full_ref, turned_ref, out_ref, back_ref, *line_sems,
+        ) = refs
+    elif linked:
         (
             rows_ref, grads_ref, w_gate_ref, w_up_ref, w_down_ref, before_ref,
             grad_gu_ref, grad_down_ref, first_in, second_in,
@@ -554,6 +595,18 @@
     rows = rows_ref[...].reshape(-1, width)
     grads = grads_ref[...].reshape(-1, width)
 
+    if dp_count:
+        line = LineGather(shards_ref.at[1], full_ref, dp_count, *line_sems)
+
+        @pl.when(step == 0)
+        def _():
+            greet(line.peers())
+            line.start()
+
+        @pl.when(step == 2)
+        def _():
+            line.relay(1)
+
     if linked:
         me, mine = place()
         owner_count = both_ref.shape[0]
@@ -613,13 +666,17 @@
         shape = (both_ref.shape[0],) + both_ref.shape[2:]
         both_ref[:, 0] = out_ref[...].astype(jnp.bfloat16).reshape(shape)
         both_ref[:, 1] = back_ref[...].astype(jnp.bfloat16).reshape(shape)
+        if dp_count:
+            for hop in range(2, line.outer_count):
+                line.relay(hop)
+            line.finish()
         if linked:
             trade_start(1, both_ref, second_in)
             trade_finish(0, before_ref, first_in)
             trade_finish(1, both_ref, second_in)
 
 
-def experts(arrived, arrived_grad, gate_up, down, at, before=None, collective=None):
+def experts(arrived, arrived_grad, gate_up, down, at, before=None, shards=None, dp_count=0, collective=None):
     owners, _, cap, width = arrived.shape
     hidden = down.shape[1]
     count = owners * cap
@@ -631,15 +688,20 @@
     )
     anywhere = pl.BlockSpec(memory_space=pl.ANY)
     both = jax.ShapeDtypeStruct((owners, 2, cap, width), jnp.bfloat16)
-    links = {"collective_id": collective, "has_side_effects": True} if linked else {}
+    gathers = shards is not None
+    links = {"collective_id": collective, "has_side_effects": True} if linked or gathers else {}
+    full = []
+    if gathers:
+        full = [jax.ShapeDtypeStruct((dp_count * shards.shape[1], shards.shape[2]), jnp.bfloat16)]
     return pl.pallas_call(
-        functools.partial(experts_kernel, linked),
+        functools.partial(experts_kernel, linked, dp_count),
         grid=(steps,),
         out_shape=[
             jax.ShapeDtypeStruct((2, width, hidden), jnp.bfloat16),
             jax.ShapeDtypeStruct((hidden, width), jnp.bfloat16),
         ]
-        + [both] * (2 if linked else 1),
+        + [both] * (2 if linked else 1)
+        + full,
         in_specs=[
             pairs,
             pairs,
@@ -647,12 +709,13 @@
             pl.BlockSpec((width, block), lambda j: (0, steps + j)),
             pl.BlockSpec((1, block, width), lambda j: (at, j, 0)),
         ]
-        + [anywhere] * linked,
+        + [anywhere] * (linked + gathers),
         out_specs=[
             pl.BlockSpec((2, width, block), lambda j: (0, 0, j)),
             pl.BlockSpec((block, width), lambda j: (j, 0)),
         ]
-        + ([anywhere] * 2 if linked else [pl.BlockSpec(both.shape, lambda j: (0, 0, 0, 0))]),
+        + ([anywhere] * 2 if linked else [pl.BlockSpec(both.shape, lambda j: (0, 0, 0, 0))])
+        + [anywhere] * gathers,
         scratch_shapes=[
             pltpu.VMEM((width, count), jnp.bfloat16),
             pltpu.VMEM((count, width), jnp.float32),
@@ -666,7 +729,8 @@
             ]
             if linked
             else []
-        ),
+        )
+        + (gather_semaphores(dp_count) if gathers else []),
         compiler_params=pltpu.CompilerParams(
             dimension_semantics=("arbitrary",), vmem_limit_bytes=58 * 2**20, **links
         ),
@@ -676,7 +740,7 @@
             transcendentals=count * hidden,
         ),
         name="experts",
-    )(arrived, arrived_grad, gate_up, gate_up, down, *([before] if linked else []))
+    )(arrived, arrived_grad, gate_up, gate_up, down, *([before] if linked else []), *([shards] if gathers else []))
 
 
 def dp_grid(dp_count):
@@ -960,6 +1024,106 @@
         compiler_params=pltpu.CompilerParams(collective_id=collective, has_side_effects=True),
         name="expert_gather",
     )(*shards, *trades)
+
+
+class LineGather:
+    def __init__(self, shard, full, dp_count, send_sem, recv_sem, own_sem):
+        self.shard, self.full, self.dp_count = shard, full, dp_count
+        self.send_sem, self.recv_sem, self.own_sem = send_sem, recv_sem, own_sem
+        self.outer_count, self.inner_count = dp_grid(dp_count)
+        self.me, self.mine = place()
+        self.outer, self.inner = self.me // self.inner_count, self.me % self.inner_count
+        self.inner_peers = [
+            lax.rem(self.inner + k, self.inner_count) for k in range(1, self.inner_count)
+        ]
+        self.can_up, self.can_down = self.outer < self.outer_count - 1, self.outer > 0
+
+    def peers(self):
+        below = lax.rem(self.outer + self.outer_count - 1, self.outer_count)
+        above = lax.rem(self.outer + 1, self.outer_count)
+        return [(peer * self.inner_count + self.inner, self.mine) for peer in (below, above)] + [
+            (self.outer * self.inner_count + peer, self.mine) for peer in self.inner_peers
+        ]
+
+    def spot(self, chunk):
+        rows = self.shard.shape[0]
+        return self.full.at[pl.ds(pl.multiple_of(chunk * rows, 8), rows), :]
+
+    def copy(self, source, chunk, device, way, at):
+        return pltpu.make_async_remote_copy(
+            src_ref=source,
+            dst_ref=self.spot(chunk),
+            send_sem=self.send_sem.at[way, at, chunk],
+            recv_sem=self.recv_sem.at[chunk],
+            device_id=(device, self.mine),
+            device_id_type=MESH,
+        )
+
+    def up(self, source, chunk):
+        return self.copy(source, chunk, (self.outer + 1) * self.inner_count + self.inner, 1, 0)
+
+    def down(self, source, chunk):
+        return self.copy(source, chunk, (self.outer - 1) * self.inner_count + self.inner, 2, 0)
+
+    def across(self, source, chunk):
+        return [
+            self.copy(source, chunk, self.outer * self.inner_count + peer, 0, at)
+            for at, peer in enumerate(self.inner_peers)
+        ]
+
+    def keep(self):
+        return pltpu.make_async_copy(self.shard, self.spot(self.me), self.own_sem)
+
+    def arrived(self, chunk):
+        pltpu.make_async_copy(self.spot(chunk), self.spot(chunk), self.recv_sem.at[chunk]).wait()
+
+    def start(self):
+        for copy in self.across(self.shard, self.me):
+            copy.start()
+        pl.when(self.can_up)(lambda: self.up(self.shard, self.me).start())
+        pl.when(self.can_down)(lambda: self.down(self.shard, self.me).start())
+        self.keep().start()
+
+    def relay(self, step):
+        low, high = self.outer - step, self.outer + step
+
+        def pass_on(source, upward):
+            chunk = source * self.inner_count + self.inner
+            self.arrived(chunk)
+            if upward:
+                pl.when(self.can_up)(lambda: self.up(self.spot(chunk), chunk).start())
+            else:
+                pl.when(self.can_down)(lambda: self.down(self.spot(chunk), chunk).start())
+            for copy in self.across(self.spot(chunk), chunk):
+                copy.start()
+
+        pl.when(low >= 0)(lambda: pass_on(low, True))
+        pl.when(high < self.outer_count)(lambda: pass_on(high, False))
+
+    def finish(self):
+        self.keep().wait()
+        for peer in self.inner_peers:
+            for plane in range(self.outer_count):
+                self.arrived(plane * self.inner_count + peer)
+        for plane in range(self.outer_count):
+            chunk = plane * self.inner_count + self.inner
+            for copy in self.across(self.spot(chunk), chunk):
+                copy.wait_send()
+            pl.when(self.can_up & (self.outer >= plane))(
+                lambda chunk=chunk: self.up(self.spot(chunk), chunk).wait_send()
+            )
+            pl.when(self.can_down & (self.outer <= plane))(
+                lambda chunk=chunk: self.down(self.spot(chunk), chunk).wait_send()
+            )
+
+
+def gather_semaphores(dp_count):
+    inner_count = dp_grid(dp_count)[1]
+    return [
+        pltpu.SemaphoreType.DMA((3, max(1, inner_count - 1), dp_count)),
+        pltpu.SemaphoreType.DMA((dp_count,)),
+        pltpu.SemaphoreType.DMA,
+    ]
 
 
 def by_rows(count, body):
@@ -1216,7 +1380,7 @@
     out_grad,
 ):
     dp_count, owner_count = lax.axis_size("dp"), lax.axis_size("expert")
-    own_links = dp_count == 8 and owner_count == 4
+    own_links = dp_count == 8 and owner_count == 4 and w_gate_up.shape[0] == 2
     seq_count, length, width = tokens.shape
     assert seq_count == 1
     rows = seq_count * length
@@ -1242,12 +1406,18 @@
         packed_full = small_gather(packed, dp_count, 1)
     else:
         packed_full = lax.all_gather(packed, "dp", axis=0, tiled=True)
-    gate_up_full = [
-        lax.all_gather(w_gate_up[e], "dp", axis=0, tiled=True) for e in range(local_count)
-    ]
-    normed_one, queries, keys, values, attended, middle, normed_two, aux = attention_forward(
-        inputs, packed_full, docs_row, docs_column, cosine, sine, route_rows, resid
-    )
+    attend = functools.partial(
+        attention_forward, inputs, packed_full, docs_row, docs_column, cosine, sine, route_rows, resid
+    )
+    if own_links:
+        *forward, first_gate_up = attend(w_gate_up, dp_count, 5)
+        gate_up_full = [first_gate_up]
+    else:
+        forward = attend()
+        gate_up_full = [
+            lax.all_gather(w_gate_up[e], "dp", axis=0, tiled=True) for e in range(local_count)
+        ]
+    normed_one, queries, keys, values, attended, middle, normed_two, aux = forward
     send_rows, send_grads = dispatch(spot_rows, aux, normed_two, cot, expert_count * CAP)
     send_rows = send_rows.reshape(owner_count, local_count * CAP, width)
     send_grads = send_grads.reshape(owner_count, local_count * CAP, width)
@@ -1266,16 +1436,17 @@
 
     parts, gu_parts, down_parts = [], [], []
     for e in range(local_count):
-        if own_links and e == local_count - 1:
-            grad_gu, grad_down, *parts = experts(
-                arrived, arrived_grad, gate_up_full[e], down_full, e, both, 4
+        run = functools.partial(experts, arrived, arrived_grad, gate_up_full[e], down_full, e)
+        if own_links and e == 0:
+            grad_gu, grad_down, both, second_gate_up = run(
+                shards=w_gate_up, dp_count=dp_count, collective=6
             )
+            gate_up_full.append(second_gate_up)
+        elif own_links:
+            grad_gu, grad_down, *parts = run(before=both, collective=4)
         else:
-            grad_gu, grad_down, both = experts(
-                arrived, arrived_grad, gate_up_full[e], down_full, e
-            )
-            if not own_links:
-                parts.append(exchange(both))
+            grad_gu, grad_down, both = run()
+            parts.append(exchange(both))
         down_parts.append(lax.psum_scatter(grad_down, "dp", scatter_dimension=0, tiled=True))
         if own_links and e == local_count - 1:
             inner = lax.axis_index("dp") % 2

time: 697 us -> 711 us (1.020)
  Pallas kernels: 628 us -> 644 us
    pallas_call x3, Pallas kernels: 147 us -> 240 us  [the longest x2 155 us: experts(): pl.pallas_call(functools.partial(experts_kernel, linked, dp_count), grid=...]
    pallas_call x1, Pallas kernels: 143 us -> 75.9 us  [expert_gather(): pl.pallas_call(functools.partial(expert_gather_kernel, dp_count, len(shar...]
    pallas_call x1, Pallas kernels: 60.6 us -> 48.3 us  [small_gather(): pl.pallas_call(functools.partial(small_gather_kernel, dp_count), out_shap...]
  transfers between devices with their start and end apart: 6 -> 4, of which waited for: 1 -> 1; matrix products, arithmetic and copies ran while one was open for 4% -> 3% of each run, Pallas kernels for 91% -> 48%
where the time goes in v5:
time: 711 us; the launch traced here: 707 us
  Pallas kernels  644 us (91%)
  local copies, waits for them, and re-layouts  24.7 us (3%)
  between operations  14.4 us (2%)
  waiting for transfers between devices  13 us (2%)
  other arithmetic  10.3 us (1%)
    pallas_call x1, Pallas kernels, final_reduce(): pl.pallas_call(functools.partial(final_reduce_kernel, len(smalls)), out_s...  185 us
    pallas_call x2, Pallas kernels, experts(): pl.pallas_call(functools.partial(experts_kernel, linked, dp_count), grid=...  155 us
    pallas_call x1, Pallas kernels, attention_forward(): pl.pallas_call(functools.partial(attention_forward_kernel, dp_count if li...  85.3 us
    pallas_call x1, Pallas kernels, expert_gather(): pl.pallas_call(functools.partial(expert_gather_kernel, dp_count, len(shar...  75.9 us
    pallas_call x1, Pallas kernels, attention_backward(): pl.pallas_call(attention_backward_kernel, grid=(groups,), out_shape=[jax....  56.3 us
    pallas_call x1, Pallas kernels, small_gather(): pl.pallas_call(functools.partial(small_gather_kernel, dp_count), out_shap...  48.3 us
    pallas_call x1, Pallas kernels, combine(): pl.pallas_call(functools.partial(combine_kernel, expert_count, local_coun...  21.3 us
  transfers between devices with their start and end apart: 4, of which 1 were waited for; matrix products, arithmetic and copies ran while one was open for 3% of the time, Pallas kernels for 48%

profile of v5, /device:TPU:19, one launch (start us, length us, event | category | flops | bytes accessed | tf_op | source)
XLA Modules:
  0.0 706.5 jit_solution(15866613944127497995)
XLA Ops:
  7.2 0.0 reduce-scatter.4.cloned.1.call-start
  7.2 0.8 copy.40
  8.0 0.8 copy.41
  8.8 0.8 copy.42
  9.6 0.8 copy.43
  10.4 0.8 copy.44
  11.2 2.0 concatenate.13.shard_ref
  13.1 48.3 %small_gather.1.refs_1_.refs_2_.refs_3_.refs_4_.refs_5_.refs_8_.wq_ref.wk_ref.wv_ref.wo_ref.small_ref = bf16[768,3328]{1,0:T(8,128)(2,1)} custom-call(bf16[96,3328]{1,0:T(8,128)(2,1)} %concatenate.13.shard_ref), custom_call_target="tpu_custom_call" | custom-call | tf_op jit(solution)/shard_map/small_gather/pallas_call | solution.py:836
  61.4 0.2 copy.39
  61.7 0.0 copy-start
  61.7 1.0 copy.46.refs_7_.docs_column_ref
  62.7 0.2 copy.45
  62.9 0.8 pad_convert_fusion.refs_11_
  63.7 4.3 routing.1
  68.1 0.8 copy-done.1
  68.9 0.6 copy-done.2
  69.5 85.3 %attention_forward.1 = (bf16[1024,768]{1,0:T(8,128)(2,1)}, bf16[1024,768]{1,0:T(8,128)(2,1)}, bf16[1024,768]{1,0:T(8,128)(2,1)}, bf16[1024,768]{1,0:T(8,128)(2,1...) custom-call(bf16[1024,768]{1,0:T(8,128)(2,1)} %bitcast.39, ...), custom_call_target="tpu_custom_call" | custom-call | flops 8053063680 | bytes 18874368 | tf_op jit(solution)/shard_map/attention_forward/pallas_call | solution.py:177
  154.8 12.1 %dispatch.1 = (bf16[2048,768]{1,0:T(8,128)(2,1)}, bf16[2048,768]{1,0:T(8,128)(2,1)}) custom-call(s32[8,1024]{1,0:T(8,128)} %copy-done.2, f32[1024,128]{1,0:T(8,128)} %get-tuple-element.58.aux_ref.refs_4_, bf16[1024,768]{1,0:T(8,128)(2,1)} %get-tuple-element.59.normed_ref.refs_5_, bf16[1024,768]{1,0:T(8,128)(2,1)} %bitcast.58), custom_call_target="tpu_custom_call" | custom-call | flops 6442450944 | bytes 9437184 | tf_op jit(solution)/shard_map/dispatch/pallas_call | solution.py:424
  166.9 75.9 %expert_gather.1 = (bf16[2,2048,768]{2,1,0:T(8,128)(2,1)}, bf16[4,512,768]{2,1,0:T(8,128)(2,1)}, bf16[4,512,768]{2,1,0:T(8,128)(2,1)}) custom-call(bf16[2,256,768]{2,1,0:T(8,128)(2,1)} %refs_0_.1, bf16[4,512,768]{2,1,0:T(8,128)(2,1)} %bitcast.37, bf16[4,512,768]{2,1,0:T(8,128)(2,1)} %bitcast.38), custom_call_target="tpu_custom_call" | custom-call | tf_op jit(solution)/shard_map/expert_gather/pallas_call | solution.py:1006
  242.8 78.4 %experts.2 = (bf16[2,768,2048]{2,1,0:T(8,128)(2,1)}, bf16[2048,768]{1,0:T(8,128)(2,1)}, bf16[4,2,256,768]{3,2,1,0:T(8,128)(2,1)}, bf16[768,4096]{1,0:T(8,128)(2,1)}) custom-call(bf16[4,2,256,768]{3,2,1,0:T(8,128)(2,1)} %bitcast.54, bf16[4,2,256,768]{3,2,1,0:T(8,128)(2,1)} %bitcast.56, bf16[768,4096]{1,0:T(8,128)(2,1)} %get-tuple-element.64.refs_2_.refs_3_, ...), custom_call_target="tpu_custom_call" | custom-call | flops 28991029248 | bytes 25165824 | tf_op jit(solution)/shard_map/experts/pallas_call | solution.py:696
  321.1 0.0 reduce-scatter.4.cloned.1.call-update
  321.2 0.0 reduce-scatter.8.cloned.1.call-start
  321.2 76.5 %experts.3 = (bf16[2,768,2048]{2,1,0:T(8,128)(2,1)}, bf16[2048,768]{1,0:T(8,128)(2,1)}, bf16[4,2,256,768]{3,2,1,0:T(8,128)(2,1)}, bf16[4,2,256,768]{3,2,1,0:T(8,128)(2,1)}) custom-call(bf16[4,2,256,768]{3,2,1,0:T(8,128)(2,1)} %bitcast.55, bf16[4,2,256,768]{3,2,1,0:T(8,128)(2,1)} %bitcast.57, bf16[768,4096]{1,0:T(8,128)(2,1)} %get-tuple-element.66.refs_2_.refs_3_, ...), custom_call_target="tpu_custom_call" | custom-call | flops 28991029248 | bytes 25165824 | tf_op jit(solution)/shard_map/experts/pallas_call | solution.py:696
  397.8 0.0 reduce-scatter.8.cloned.1.call-update
  397.8 0.0 reduce-scatter.6.cloned.1.call-start
  397.8 0.7 reduce-scatter.6.cloned.1.call-update
  398.5 4.0 dynamic-slice_bitcast_fusion
  402.5 0.3 collective-permute-start
  402.8 21.3 %combine.1 = (bf16[1024,768]{1,0:T(8,128)(2,1)}, bf16[1024,12]{1,0:T(8,128)(2,1)}, f32[1024,768]{1,0:T(8,128)}, f32[768,128]{1,0:T(8,128)}) custom-call(bf16[4,2,256,768]{3,2,1,0:T(8,128)(2,1)} %get-tuple-element.71.refs_0_, bf16[4,2,256,768]{3,2,1,0:T(8,128)(2,1)} %get-tuple-element.72.refs_1_, s32[1024,128]{1,0:T(8,128)} %copy-done.1, s32[1024,2]{1,0:T(8,128)} %bitcast.32, ...), custom_call_target="tpu_custom_call" | custom-call | flops 9663676416 | bytes 17301504 | tf_op jit(solution)/shard_map/combine/pallas_call | solution.py:543
  424.1 0.0 slice-start.1
  424.1 56.3 %attention_backward.1 = (bf16[1024,768]{1,0:T(8,128)(2,1)}, bf16[768,768]{1,0:T(8,128)(2,1)}, bf16[768,768]{1,0:T(8,128)(2,1)}, bf16[768,768]{1,0:T(8,128)(2,1)}...) custom-call(f32[1024,768]{1,0:T(8,128)} %get-tuple-element.76.grad_middle_ref, ...), custom_call_target="tpu_custom_call" | custom-call | flops 17716740096 | bytes 25165824 | tf_op jit(solution)/shard_map/attention_backward/pallas_call | solution.py:313
  480.4 12.3 %collective-permute-done = bf16[2,4,96,2048]{3,2,1,0:T(8,128)(2,1)} collective-permute-done((bf16[2,4,96,2048]{3,2,1,0:T(8,128)(2,1)}, bf16[2,4,96,2048]{3,2,1,0:T(8,128)(2,1)}, u32[]{:S(2)}, u32[]{:S(2)}) %collective-permute-start) | collective-permute-done | bytes 3145760 | tf_op jit(solution)/shard_map/ppermute | solution.py:1454
  492.6 5.1 fusion.part_ref
  497.8 185.4 %final_reduce.1 = (f32[96,4096]{1,0:T(8,128)}, f32[96,3328]{1,0:T(8,128)}) custom-call(bf16[2,4,96,2048]{3,2,1,0:T(8,128)(2,1)} %fusion.part_ref, bf16[8,96,768]{2,1,0:T(8,128)(2,1)} %bitcast.42, bf16[8,96,768]{2,1,0:T(8,128)(2,1)} %bitcast.43, bf16[8,96,768]{2,1,0:T(8,128)(2,1)} %bitcast.44, bf16[8,96,768]{2,1,0:T(8,128)(2,1)} %bitcast.45, ...), custom_call_target="tpu_custom_call" | custom-call | tf_op jit(solution)/shard_map/final_reduce/pallas_call | solution.py:1337
  683.2 2.2 slice.33
  685.4 1.7 slice.34
  687.1 0.8 slice.37
  687.9 0.9 slice.38
  688.8 0.9 slice.39
  689.6 0.7 copy.50
  690.3 0.7 copy.51
  691.0 0.6 copy.52
  691.6 0.8 copy.49
  692.4 1.6 slice_reduce_fusion
  694.0 2.4 maximum_convert_fusion.1
  696.3 1.2 fusion.1
  697.5 0.1 maximum_convert_fusion
  697.7 1.9 pad_maximum_fusion
  (23 shorter events, 0.0 us)
Async XLA Ops:
  7.2 395.6 %reduce-scatter.4.cloned.1.call-start = ((), (), s32[]{:S(2)}) async-start(), calls=%async_computation.3 | async-start | bytes 3538944 | tf_op jit(solution)/shard_map/reduce_scatter | solution.py:1450
  13.1 48.3 %copy-start.8 = (s32[1,1024,2]{1,2,0:T(2,128)S(1)}, s32[1,1024,2]{1,2,0:T(2,128)}, u32[]{:S(2)}) copy-start(s32[1,1024,2]{1,2,0:T(2,128)} %param.18) | copy-start | bytes 24580
  13.1 48.5 %copy-start.7 = (s32[1,1024]{1,0:T(1,128)S(1)}, s32[1,1024]{1,0:T(1,128)}, u32[]{:S(2)}) copy-start(s32[1,1024]{1,0:T(1,128)} %docs_row_ref.1) | copy-start | bytes 12292
  13.1 49.6 %copy-start.6 = (bf16[1,1024,12]{1,2,0:T(8,128)(2,1)S(1)}, bf16[1,1024,12]{1,2,0:T(8,128)(2,1)}, u32[]{:S(2)}) copy-start(bf16[1,1024,12]{1,2,0:T(8,128)(2,1)} %param.17) | copy-start | bytes 73732
  61.7 7.8 %copy-start = (s32[1,1024,2]{2,1,0:T(8,128)}, s32[1,1024,2]{2,1,0:T(8,128)S(1)}, u32[]{:S(2)}) copy-start(s32[1,1024,2]{2,1,0:T(8,128)S(1)} %copy.39) | copy-start | bytes 24580
  68.1 0.8 copy-start.1
  68.9 0.6 copy-start.2
  321.2 372.8 %reduce-scatter.8.cloned.1.call-start = ((), (), s32[]{:S(2)}) async-start(), calls=%async_computation.5 | async-start | bytes 3538944 | tf_op jit(solution)/shard_map/reduce_scatter | solution.py:1450
  397.8 298.6 %reduce-scatter.6.cloned.1.call-start = ((), (), s32[]{:S(2)}) async-start(), calls=%async_computation.4 | async-start | bytes 7077888 | tf_op jit(solution)/shard_map/reduce_scatter | solution.py:1460
  402.5 90.1 %collective-permute-start = (bf16[2,4,96,2048]{3,2,1,0:T(8,128)(2,1)}, bf16[2,4,96,2048]{3,2,1,0:T(8,128)(2,1)}, u32[]{:S(2)}, u32[]{:S(2)}) collective-permute-start(bf16[2,4,96,2048]{3,2,1,0:T(8,128)(2,1)} %dynamic-slice_bitcast_fusion), channel_id=1, source_target_pairs={{0,4},{4,0},{8,12},{12,8},{16,20},{20,16},{24,28},{28,24},{1,5},{5... | collective-permute-start | bytes 9437192 | tf_op jit(solution)/shard_map/ppermute | solution.py:1454
  402.8 89.8 %slice-start = ((s8[6291456]{0:T(1024)(128)(4,1)}), s8[4194304]{0:T(1024)(128)(4,1)S(1)}, s32[]{:S(2)}) async-start(s8[6291456]{0:T(1024)(128)(4,1)} %bitcast.34), calls=%async_computation.6 | async-start | bytes 8388608
  424.1 68.6 %slice-start.1 = ((s8[6291456]{0:T(1024)(128)(4,1)}), s8[2097152]{0:T(1024)(128)(4,1)S(1)}, s32[]{:S(2)}) async-start(s8[6291456]{0:T(1024)(128)(4,1)} %bitcast.34), calls=%async_computation.7 | async-start | bytes 4194304
  497.8 193.8 %copy-start.5 = (bf16[1024,12]{1,0:T(8,128)(2,1)S(1)}, bf16[1024,12]{1,0:T(8,128)(2,1)}, u32[]{:S(2)}) copy-start(bf16[1024,12]{1,0:T(8,128)(2,1)} %get-tuple-element.84) | copy-start | bytes 73732
  683.2 10.8 %copy-start.4 = (bf16[256,768]{1,0:T(8,128)(2,1)S(1)}, bf16[256,768]{1,0:T(8,128)(2,1)}, u32[]{:S(2)}) copy-start(bf16[256,768]{1,0:T(8,128)(2,1)} %reduce-scatter.4.cloned.1.call-done) | copy-start | bytes 1179652
  694.0 3.7 copy-start.3
Sparse Core Ops, SparseCore 0:
  321.3 74.9 reduce-scatter.3
  399.8 91.9 reduce-scatter.7
  495.3 175.5 reduce-scatter.5

commit v6 on v5

--- a/solution.py
+++ b/solution.py
@@ -220,15 +220,29 @@
     )
 
 
-def attention_backward_kernel(
-    grad_middle_ref, q_ref, k_ref, v_ref, attended_ref, normed_ref, tokens_ref,
-    wq_ref, wk_ref, wv_ref, wo_ref, small_ref, docs_row_ref, docs_column_ref,
-    cosine_ref, sine_ref, small_grad_ref,
-    token_grad_ref, gq_ref, gk_ref, gv_ref, go_ref, small_out_ref,
-    branch_ref, back_ref, turned_ref, key_acc, value_acc, query_acc,
-):
+def attention_backward_kernel(count, *refs):
+    (
+        grad_middle_ref, q_ref, k_ref, v_ref, attended_ref, normed_ref, tokens_ref,
+        wq_ref, wk_ref, wv_ref, wo_ref, small_ref, docs_row_ref, docs_column_ref,
+        cosine_ref, sine_ref, small_grad_ref,
+    ) = refs[:17]
+    sources, refs = refs[17 : 17 + count], refs[17 + count :]
+    token_grad_ref, gq_ref, gk_ref, gv_ref, go_ref, small_out_ref = refs[:6]
+    totals, refs = refs[6 : 6 + count], refs[6 + count :]
+    branch_ref, back_ref, turned_ref, key_acc, value_acc, query_acc = refs[:6]
     step = pl.program_id(0)
     rows, width = tokens_ref.shape
+    if count:
+        line = line_reduce(sources, totals, refs[6:])
+
+        @pl.when(step == 0)
+        def _():
+            greet(line.peers())
+            line.each_plane(line.start)
+
+        @pl.when(step == 2)
+        def _():
+            line.each_plane(lambda o: line.pass_on(o, 0))
 
     @pl.when(step == 0)
     def _():
@@ -297,11 +311,19 @@
         small_grad = jnp.where(lane_ids(small_grad.shape) == 18, column, small_grad)
         small_out_ref[:, :128] = small_grad.astype(jnp.bfloat16)
         small_out_ref[:, 128:] = jnp.zeros((width, 128), jnp.bfloat16)
+        if count:
+
+            def rest(o):
+                for k in range(1, 4):
+                    line.pass_on(o, k)
+                line.finish(o)
+
+            line.each_plane(rest)
 
 
 def attention_backward(
     grad_middle, queries, keys, values, attended, normed, tokens, packed, docs_row, docs_column,
-    cosine, sine, small_grad,
+    cosine, sine, small_grad, sources=(), collective=None,
 ):
     rows, width = tokens.shape
     groups = width // GROUP
@@ -310,31 +332,42 @@
     column = lambda at: pl.BlockSpec((width, GROUP), lambda j: (0, at + j))
     by_group = pl.BlockSpec((rows, GROUP), lambda j: (0, j))
     weight = jax.ShapeDtypeStruct((width, width), low)
+    linked = len(sources) > 0
+    links = {"collective_id": collective, "has_side_effects": True} if linked else {}
+    sums = []
+    for source in sources:
+        sides = source.shape[0] if len(source.shape) == 3 else 1
+        sums.append((source.shape[-2] // 8, sides * source.shape[-1]))
+    once = lambda shape: pl.BlockSpec(
+        shape, lambda j: (0, 0), pipeline_mode=pl.Buffered(1)
+    )
     return pl.pallas_call(
-        attention_backward_kernel,
+        functools.partial(attention_backward_kernel, len(sources)),
         grid=(groups,),
         out_shape=[jax.ShapeDtypeStruct((rows, width), low)]
         + [weight] * 4
-        + [jax.ShapeDtypeStruct((width, 256), low)],
+        + [jax.ShapeDtypeStruct((width, 256), low)]
+        + [jax.ShapeDtypeStruct(shape, jnp.float32) for shape in sums],
         in_specs=[
-            whole((rows, width)),
+            once((rows, width)),
             by_group,
             by_group,
             by_group,
             by_group,
-            whole((rows, width)),
-            whole((rows, width)),
+            once((rows, width)),
+            once((rows, width)),
             column(0),
             column(groups),
             column(2 * groups),
             pl.BlockSpec((GROUP, width), lambda j: (j, 3)),
             pl.BlockSpec((width, 256), lambda j: (0, 12)),
-            whole((1, rows)),
-            whole((rows, 1)),
-            whole((rows, 128)),
-            whole((rows, 128)),
-            whole((width, 128)),
-        ],
+            once((1, rows)),
+            once((rows, 1)),
+            once((rows, 128)),
+            once((rows, 128)),
+            once((width, 128)),
+        ]
+        + [pl.BlockSpec(memory_space=pl.ANY)] * len(sources),
         out_specs=[
             whole((rows, width)),
             column(0),
@@ -342,7 +375,8 @@
             column(0),
             pl.BlockSpec((GROUP, width), lambda j: (j, 0)),
             whole((width, 256)),
-        ],
+        ]
+        + [whole(shape) for shape in sums],
         scratch_shapes=[
             pltpu.VMEM((rows, width), low),
             pltpu.VMEM((rows, width), jnp.float32),
@@ -350,9 +384,10 @@
             pltpu.VMEM((rows, 128), jnp.float32),
             pltpu.VMEM((rows, 128), jnp.float32),
             pltpu.VMEM((rows, 128), jnp.float32),
-        ],
+        ]
+        + (reduce_scratch(sources) if linked else []),
         compiler_params=pltpu.CompilerParams(
-            dimension_semantics=("arbitrary",), vmem_limit_bytes=56 * 2**20
+            dimension_semantics=("arbitrary",), vmem_limit_bytes=61 * 2**20, **links
         ),
         cost_estimate=pl.CostEstimate(
             flops=4 * rows * width * 4 * width + 20 * rows * rows * width // 2,
@@ -362,7 +397,7 @@
         name="attention_backward",
     )(
         grad_middle, queries, keys, values, attended, normed, tokens, packed, packed, packed,
-        packed, packed, docs_row, docs_column, cosine, sine, small_grad,
+        packed, packed, docs_row, docs_column, cosine, sine, small_grad, *sources,
     )
 
 
@@ -596,7 +631,9 @@
     grads = grads_ref[...].reshape(-1, width)
 
     if dp_count:
-        line = LineGather(shards_ref.at[1], full_ref, dp_count, *line_sems)
+        line = LineGather(
+            shards_ref.at[1, :, 0 : full_ref.shape[1]], full_ref, dp_count, *line_sems
+        )
 
         @pl.when(step == 0)
         def _():
@@ -676,7 +713,7 @@
             trade_finish(1, both_ref, second_in)
 
 
-def experts(arrived, arrived_grad, gate_up, down, at, before=None, shards=None, dp_count=0, collective=None):
+def experts(arrived, arrived_grad, gate, up, down, at, before=None, shards=None, dp_count=0, collective=None):
     owners, _, cap, width = arrived.shape
     hidden = down.shape[1]
     count = owners * cap
@@ -692,7 +729,7 @@
     links = {"collective_id": collective, "has_side_effects": True} if linked or gathers else {}
     full = []
     if gathers:
-        full = [jax.ShapeDtypeStruct((dp_count * shards.shape[1], shards.shape[2]), jnp.bfloat16)]
+        full = [jax.ShapeDtypeStruct((dp_count * shards.shape[1], hidden), jnp.bfloat16)]
     return pl.pallas_call(
         functools.partial(experts_kernel, linked, dp_count),
         grid=(steps,),
@@ -706,7 +743,7 @@
             pairs,
             pairs,
             pl.BlockSpec((width, block), lambda j: (0, j)),
-            pl.BlockSpec((width, block), lambda j: (0, steps + j)),
+            pl.BlockSpec((width, block), lambda j: (0, up.shape[1] // block - steps + j)),
             pl.BlockSpec((1, block, width), lambda j: (at, j, 0)),
         ]
         + [anywhere] * (linked + gathers),
@@ -740,7 +777,10 @@
             transcendentals=count * hidden,
         ),
         name="experts",
-    )(arrived, arrived_grad, gate_up, gate_up, down, *([before] if linked else []), *([shards] if gathers else []))
+    )(
+        arrived, arrived_grad, gate, up, down, *([before] if linked else []),
+        *([shards] if gathers else []),
+    )
 
 
 def dp_grid(dp_count):
@@ -1134,11 +1174,141 @@
     lax.fori_loop(0, count // 16, step, 0)
 
 
-def final_reduce_kernel(small_count, part_ref, *refs):
+class LineReduce:
+    def __init__(self, sources, totals, owns, ins, lows, highs, own_sem, in_send, in_recv, line_send, line_recv):
+        self.sources, self.totals = sources, totals
+        self.owns, self.ins, self.lows, self.highs = owns, ins, lows, highs
+        self.own_sem, self.in_send, self.in_recv = own_sem, in_send, in_recv
+        self.line_send, self.line_recv = line_send, line_recv
+        self.me, self.mine = place()
+        self.outer, self.inner = self.me // 2, self.me % 2
+        self.every = range(len(sources))
+
+    def peers(self):
+        low, high = lax.rem(self.outer + 3, 4), lax.rem(self.outer + 1, 4)
+        return [
+            (self.me + 1 - 2 * self.inner, self.mine),
+            (low * 2 + self.inner, self.mine),
+            (high * 2 + self.inner, self.mine),
+        ]
+
+    def order(self, o):
+        return sorted(range(4), key=lambda plane: (-abs(plane - o), plane))
+
+    def chunk(self, p, at):
+        source = self.sources[p]
+        rows = self.owns[p].shape[-2]
+        here = pl.ds(pl.multiple_of(at * rows, 16), rows)
+        return source.at[:, here, :] if len(source.shape) == 3 else source.at[here, :]
+
+    def own_copy(self, p, plane):
+        return pltpu.make_async_copy(
+            self.chunk(p, plane * 2 + self.inner), self.owns[p].at[plane], self.own_sem.at[p, plane]
+        )
+
+    def in_copy(self, p, plane):
+        return pltpu.make_async_remote_copy(
+            src_ref=self.chunk(p, plane * 2 + 1 - self.inner),
+            dst_ref=self.ins[p].at[plane],
+            send_sem=self.in_send.at[p, plane],
+            recv_sem=self.in_recv.at[p, plane],
+            device_id=(self.me + 1 - 2 * self.inner, self.mine),
+            device_id_type=MESH,
+        )
+
+    def line_copy(self, p, plane, upward, device_plane):
+        target = self.lows[p].at[plane - 1] if upward else self.highs[p].at[plane]
+        return pltpu.make_async_remote_copy(
+            src_ref=self.ins[p].at[plane],
+            dst_ref=target,
+            send_sem=self.line_send.at[p, 0 if upward else 1, plane],
+            recv_sem=self.line_recv.at[p, 0 if upward else 1, plane],
+            device_id=(device_plane * 2 + self.inner, self.mine),
+            device_id_type=MESH,
+        )
+
+    def start(self, o):
+        for plane in self.order(o):
+            for p in self.every:
+                self.in_copy(p, plane).start()
+        for plane in self.order(o):
+            for p in self.every:
+                self.own_copy(p, plane).start()
+
+    def line_start(self, o, p, plane):
+        return self.line_copy(p, plane, plane > o, o + 1 if plane > o else o - 1)
+
+    def pass_on(self, o, k):
+        plane = self.order(o)[k]
+        for p in self.every:
+            self.own_copy(p, plane).wait()
+            self.in_copy(p, plane).wait_recv()
+            terms = [self.owns[p].at[plane]]
+            if o > 0 and plane >= o:
+                self.line_copy(p, plane, True, o).wait_recv()
+                terms.append(self.lows[p].at[plane - 1])
+            if o < 3 and plane <= o:
+                self.line_copy(p, plane, False, o).wait_recv()
+                terms.append(self.highs[p].at[plane])
+            held = self.ins[p].at[plane]
+            last = plane == o
+            sides = held.shape[0] if len(held.shape) == 3 else 0
+
+            def body(at, p=p, terms=terms, held=held, last=last, sides=sides):
+                here = pl.ds(pl.multiple_of(at, 16), 16)
+                for side in range(max(1, sides)):
+                    spot = (side, here) if sides else (here,)
+                    total = held[spot].astype(jnp.float32)
+                    for term in terms:
+                        total = total + term[spot].astype(jnp.float32)
+                    if last:
+                        size = total.shape[-1]
+                        self.totals[p][here, side * size : (side + 1) * size] = total
+                    else:
+                        held[spot] = total.astype(held.dtype)
+
+            by_rows(held.shape[-2], body)
+            if not last:
+                self.line_start(o, p, plane).start()
+
+    def finish(self, o):
+        for plane in range(4):
+            for p in self.every:
+                self.in_copy(p, plane).wait_send()
+                if plane != o:
+                    self.line_start(o, p, plane).wait_send()
+
+    def each_plane(self, body):
+        for o in range(4):
+            pl.when(self.outer == o)(functools.partial(body, o))
+
+
+def reduce_scratch(sources):
+    shapes = []
+    for planes in (4, 4, 3, 3):
+        for source in sources:
+            rows = source.shape[-2] // 8
+            shapes.append(pltpu.VMEM((planes,) + source.shape[:-2] + (rows, source.shape[-1]), jnp.bfloat16))
+    count = len(sources)
+    return shapes + [
+        pltpu.SemaphoreType.DMA((count, 4)),
+        pltpu.SemaphoreType.DMA((count, 4)),
+        pltpu.SemaphoreType.DMA((count, 4)),
+        pltpu.SemaphoreType.DMA((count, 2, 4)),
+        pltpu.SemaphoreType.DMA((count, 2, 4)),
+    ]
+
+
+def line_reduce(sources, totals, scratch):
+    count = len(sources)
+    buffers = [scratch[n * count : (n + 1) * count] for n in range(4)]
+    return LineReduce(sources, totals, *buffers, *scratch[4 * count :])
+
+
+def final_reduce_kernel(small_count, *refs):
     small_refs, refs = refs[:small_count], refs[small_count:]
     (
-        part_out, small_out, swap, part_in, part_low, part_high, small_in, small_low, small_high,
-        final_low, final_in,
+        small_out, swap, small_in, small_low, small_high, final_low, final_in,
         swap_send, swap_recv, in_send, in_recv, line_send, line_recv, last_send, last_recv,
     ) = refs
     outer_count, inner_count = 4, 2
@@ -1148,7 +1318,6 @@
     mate, across = mine + 1 - 2 * side, lax.rem(mine + 2, 4)
     beside = me + 1 - 2 * inner
     half_rows = small_refs[0].shape[1] // 2
-    part_rows = part_ref.shape[2]
     starts = [sum(ref.shape[2] for ref in small_refs[:n]) for n in range(small_count + 1)]
 
     def remote(source, target, device, send_at, recv_at):
@@ -1161,12 +1330,9 @@
             device_id_type=MESH,
         )
 
-    barrier = pltpu.get_barrier_semaphore()
     low_peer = lax.rem(outer + outer_count - 1, outer_count) * inner_count + inner
     high_peer = lax.rem(outer + 1, outer_count) * inner_count + inner
-    for device in ((me, mate), (me, across), (beside, mine), (low_peer, mine), (high_peer, mine)):
-        pl.semaphore_signal(barrier, inc=1, device_id=device, device_id_type=MESH)
-    pl.semaphore_wait(barrier, 5)
+    greet([(me, mate), (me, across), (beside, mine), (low_peer, mine), (high_peer, mine)])
 
     mate_rows = pl.ds(pl.multiple_of((1 - side) * half_rows, 16), half_rows)
     own_rows = pl.ds(pl.multiple_of(side * half_rows, 16), half_rows)
@@ -1189,15 +1355,14 @@
             in_recv.at[plane],
         )
 
-    def line_copy(p, plane, upward, device_plane, source):
-        target = ((part_low, small_low), (part_high, small_high))[0 if upward else 1][p].at[plane]
+    def line_copy(plane, upward, device_plane):
         way = 0 if upward else 1
         return remote(
-            source,
-            target,
+            small_in.at[plane],
+            (small_low if upward else small_high).at[plane],
             (device_plane * inner_count + inner, mine),
-            line_send.at[p, way, plane],
-            line_recv.at[p, way, plane],
+            line_send.at[way, plane],
+            line_recv.at[way, plane],
         )
 
     def wide(values):
@@ -1218,95 +1383,43 @@
     def at_plane(o):
         order = sorted(range(outer_count), key=lambda t: (-abs(t - o), t))
 
-        def arrive(p, plane, upward):
-            line_copy(p, plane, upward, o, part_in.at[0] if p == 0 else small_in.at[0]).wait_recv()
-
-        def held(plane):
-            relayed = (plane > o > 0) or (plane < o < outer_count - 1)
-            return part_in.at[plane] if relayed else part_ref.at[:, plane]
-
-        def line_start(p, plane):
-            source = held(plane) if p == 0 else small_in.at[plane]
-            return line_copy(p, plane, plane > o, o + 1 if plane > o else o - 1, source)
+        def line_start(plane):
+            return line_copy(plane, plane > o, o + 1 if plane > o else o - 1)
 
         for n in range(small_count):
             swap_copy(n).start()
-        for plane in order:
-            if (plane > o and o == 0) or (plane < o and o == outer_count - 1):
-                line_start(0, plane).start()
         for n in range(small_count):
             swap_copy(n).wait_recv()
         for plane in order:
-            for column in range(inner_count):
-                add_own(plane * inner_count + column)
+            add_own(plane * inner_count + 1 - inner)
             inner_copy(plane).start()
         for plane in order:
-            upward = plane > o
-            if plane != o and 0 < o < outer_count - 1:
-                arrive(0, plane, upward)
-                lines = part_low if upward else part_high
-
-                def relay(at, plane=plane, lines=lines):
-                    here = pl.ds(pl.multiple_of(at, 16), 16)
-                    part_in[plane, :, here, :] = (
-                        wide(part_ref[:, plane, here, :]) + wide(lines[plane, :, here, :])
-                    ).astype(part_in.dtype)
-
-                by_rows(part_rows, relay)
-                line_start(0, plane).start()
+            add_own(plane * inner_count + inner)
             inner_copy(plane).wait_recv()
-            relayed = plane != o and 0 < o < outer_count - 1
-            lines = small_low if upward else small_high
-            if relayed:
-                arrive(1, plane, upward)
-
-            def gather(at, plane=plane, lines=lines, relayed=relayed):
+            terms = [swap.at[plane * inner_count + inner]]
+            if o > 0 and plane >= o:
+                line_copy(plane, True, o).wait_recv()
+                terms.append(small_low.at[plane])
+            if o < outer_count - 1 and plane <= o:
+                line_copy(plane, False, o).wait_recv()
+                terms.append(small_high.at[plane])
+            target = final_low if plane == o else small_in.at[plane]
+
+            def gather(at, plane=plane, terms=terms, target=target):
                 here = pl.ds(pl.multiple_of(at, 16), 16)
-                total = wide(small_in[plane, here, :]) + wide(swap[plane * inner_count + inner, here, :])
-                if relayed:
-                    total = total + wide(lines[plane, here, :])
-                small_in[plane, here, :] = total.astype(small_in.dtype)
+                total = wide(small_in[plane, here, :])
+                for term in terms:
+                    total = total + wide(term[here, :])
+                target[here, :] = total.astype(target.dtype)
 
             by_rows(half_rows, gather)
             if plane != o:
-                line_start(1, plane).start()
-        for p in (1, 0):
-            if o > 0:
-                arrive(p, o, True)
-            if o < outer_count - 1:
-                arrive(p, o, False)
-            if p == 1:
-
-                def finish_small(at):
-                    here = pl.ds(pl.multiple_of(at, 16), 16)
-                    total = wide(small_in[o, here, :])
-                    if o > 0:
-                        total = total + wide(small_low[o, here, :])
-                    if o < outer_count - 1:
-                        total = total + wide(small_high[o, here, :])
-                    final_low[here, :] = total.astype(final_low.dtype)
-
-                by_rows(half_rows, finish_small)
-                remote(final_low, final_in, (me, across), last_send.at[0], last_recv.at[0]).start()
-            else:
-
-                def finish_part(at):
-                    here = pl.ds(pl.multiple_of(at, 16), 16)
-                    for side_at in range(2):
-                        total = wide(part_ref[side_at, o, here, :])
-                        if o > 0:
-                            total = total + wide(part_low[o, side_at, here, :])
-                        if o < outer_count - 1:
-                            total = total + wide(part_high[o, side_at, here, :])
-                        size = total.shape[1]
-                        part_out[here, side_at * size : (side_at + 1) * size] = total
-
-                by_rows(part_rows, finish_part)
+                line_start(plane).start()
+        remote(final_low, final_in, (me, across), last_send.at[0], last_recv.at[0]).start()
         for plane in range(outer_count):
             inner_copy(plane).wait_send()
             if plane != o:
-                line_start(0, plane).wait_send()
-                line_start(1, plane).wait_send()
+                line_start(plane).wait_send()
         for n in range(small_count):
             swap_copy(n).wait_send()
 
@@ -1327,23 +1440,19 @@
     mate_copy.wait()
 
 
-def final_reduce(part, smalls, collective):
-    sides, planes, part_rows, part_columns = part.shape
+def final_reduce(smalls, collective):
     chunk_count, small_rows, _ = smalls[0].shape
     small_columns = sum(small.shape[2] for small in smalls)
     low = jnp.bfloat16
+    planes = 4
     in_vmem = pl.BlockSpec(memory_space=pltpu.VMEM)
     half = small_rows // 2
     return pl.pallas_call(
         functools.partial(final_reduce_kernel, len(smalls)),
-        out_shape=[
-            jax.ShapeDtypeStruct((part_rows, sides * part_columns), jnp.float32),
-            jax.ShapeDtypeStruct((small_rows, small_columns), jnp.float32),
-        ],
-        in_specs=[in_vmem] * (1 + len(smalls)),
-        out_specs=[in_vmem] * 2,
+        out_shape=jax.ShapeDtypeStruct((small_rows, small_columns), jnp.float32),
+        in_specs=[in_vmem] * len(smalls),
+        out_specs=in_vmem,
         scratch_shapes=[pltpu.VMEM((chunk_count, half, small_columns), low)]
-        + [pltpu.VMEM((planes, sides, part_rows, part_columns), low)] * 3
         + [pltpu.VMEM((planes, half, small_columns), low)] * 3
         + [pltpu.VMEM((half, small_columns), low)] * 2
         + [
@@ -1351,16 +1460,16 @@
             pltpu.SemaphoreType.DMA((len(smalls),)),
             pltpu.SemaphoreType.DMA((planes,)),
             pltpu.SemaphoreType.DMA((planes,)),
-            pltpu.SemaphoreType.DMA((2, 2, planes)),
-            pltpu.SemaphoreType.DMA((2, 2, planes)),
+            pltpu.SemaphoreType.DMA((2, planes)),
+            pltpu.SemaphoreType.DMA((2, planes)),
             pltpu.SemaphoreType.DMA((2,)),
             pltpu.SemaphoreType.DMA((2,)),
         ],
         compiler_params=pltpu.CompilerParams(
-            collective_id=collective, has_side_effects=True, vmem_limit_bytes=58 * 2**20
+            collective_id=collective, has_side_effects=True, vmem_limit_bytes=40 * 2**20
         ),
         name="final_reduce",
-    )(part, *smalls)
+    )(*smalls)
 
 
 def shards(
@@ -1409,14 +1518,12 @@
     attend = functools.partial(
         attention_forward, inputs, packed_full, docs_row, docs_column, cosine, sine, route_rows, resid
     )
+    gather = functools.partial(lax.all_gather, axis_name="dp", axis=0, tiled=True)
+    gates = [gather(w_gate_up[e]) for e in range(1 if own_links else local_count)]
+    ups = list(gates)
     if own_links:
-        *forward, first_gate_up = attend(w_gate_up, dp_count, 5)
-        gate_up_full = [first_gate_up]
-    else:
-        forward = attend()
-        gate_up_full = [
-            lax.all_gather(w_gate_up[e], "dp", axis=0, tiled=True) for e in range(local_count)
-        ]
+        ups.append(gather(w_gate_up[1, :, hidden_count:]))
+    forward = attend()
     normed_one, queries, keys, values, attended, middle, normed_two, aux = forward
     send_rows, send_grads = dispatch(spot_rows, aux, normed_two, cot, expert_count * CAP)
     send_rows = send_rows.reshape(owner_count, local_count * CAP, width)
@@ -1434,57 +1541,46 @@
     arrived = arrived.reshape(owner_count, local_count, CAP, width)
     arrived_grad = arrived_grad.reshape(owner_count, local_count, CAP, width)
 
-    parts, gu_parts, down_parts = [], [], []
+    parts, gu_parts, down_parts, sources = [], [], [], []
     for e in range(local_count):
-        run = functools.partial(experts, arrived, arrived_grad, gate_up_full[e], down_full, e)
+        run = functools.partial(experts, arrived, arrived_grad, gates[e], ups[e], down_full, e)
         if own_links and e == 0:
-            grad_gu, grad_down, both, second_gate_up = run(
+            grad_gu, grad_down, both, next_gate = run(
                 shards=w_gate_up, dp_count=dp_count, collective=6
             )
-            gate_up_full.append(second_gate_up)
+            gates.append(next_gate)
         elif own_links:
             grad_gu, grad_down, *parts = run(before=both, collective=4)
         else:
             grad_gu, grad_down, both = run()
             parts.append(exchange(both))
-        down_parts.append(lax.psum_scatter(grad_down, "dp", scatter_dimension=0, tiled=True))
         if own_links and e == local_count - 1:
-            inner = lax.axis_index("dp") % 2
-            grad_gu = grad_gu.reshape(2, dp_count // 2, 2, width // dp_count, hidden_count)
-            theirs = lax.ppermute(
-                lax.dynamic_index_in_dim(grad_gu, 1 - inner, 2, False),
-                "dp",
-                [(i, i + 1 - 2 * (i % 2)) for i in range(dp_count)],
+            sources = [grad_gu, grad_down]
+        else:
+            down_parts.append(
+                lax.psum_scatter(grad_down, "dp", scatter_dimension=0, tiled=True)
             )
-        else:
             gu_part = lax.psum_scatter(grad_gu, "dp", scatter_dimension=1, tiled=True)
-            gu_parts.append(
-                jnp.concatenate([gu_part[0], gu_part[1]], -1).astype(jnp.float32)
-            )
-
+            gu_parts.append(jnp.concatenate([gu_part[0], gu_part[1]], -1).astype(jnp.float32))
     if own_links:
         parts, down_parts[0] = lax.optimization_barrier((parts, down_parts[0]))
+    down_parts = [part.astype(jnp.float32) for part in down_parts]
     output, logit_grad, grad_middle, small_grad = combine(
         parts, spots, route_rows, aux, normed_two, middle, cot, packed_full, choice_count, expert_count
     )
-    token_grad, *weight_grads = attention_backward(
-        grad_middle, queries, keys, values, attended, normed_one, inputs, packed_full, docs_row,
-        docs_column, cosine, sine, small_grad,
+    backward = functools.partial(
+        attention_backward, grad_middle, queries, keys, values, attended, normed_one, inputs,
+        packed_full, docs_row, docs_column, cosine, sine, small_grad,
     )
     if own_links:
-        part_width = width // dp_count
-        theirs, weight_grads = lax.optimization_barrier((theirs, weight_grads))
-        linked = (
-            lax.dynamic_index_in_dim(grad_gu, inner, 2, False).astype(jnp.float32)
-            + theirs.astype(jnp.float32)
-        ).astype(jnp.bfloat16)
-        gu_part, packed_part = final_reduce(
-            linked,
-            [grad.reshape(dp_count, part_width, grad.shape[1]) for grad in weight_grads],
-            3,
+        token_grad, *weight_grads, gu_part, down_part = backward(sources, 7)
+        gu_parts.append(gu_part)
+        down_parts.append(down_part)
+        packed_part = final_reduce(
+            [grad.reshape(dp_count, width // dp_count, grad.shape[1]) for grad in weight_grads], 3
         )
-        gu_parts = gu_parts + [gu_part]
     else:
+        token_grad, *weight_grads = backward()
         packed_part = lax.psum_scatter(
             jnp.concatenate(weight_grads, 1), "dp", scatter_dimension=0, tiled=True
         )
@@ -1504,7 +1600,7 @@
         small_part[:, 12:16],
         small_part[:, 16:18],
         jnp.stack(gu_parts),
-        jnp.stack(down_parts).astype(jnp.float32),
+        jnp.stack(down_parts),
     )
 
 

time: 711 us -> 654 us (0.920)
  Pallas kernels: 644 us -> 597 us
    pallas_call x1, Pallas kernels: 185 us -> 50.3 us  [final_reduce(): pl.pallas_call(functools.partial(final_reduce_kernel, len(smalls)), out_s...]
    pallas_call x1, Pallas kernels: 56.3 us -> 158 us  [attention_backward(): pl.pallas_call(functools.partial(attention_backward_kernel, len(sources))...]
    pallas_call x1, Pallas kernels: 85.3 us -> 33.1 us  [attention_forward(): pl.pallas_call(functools.partial(attention_forward_kernel, dp_count if li...]
    pallas_call x1, Pallas kernels: 75.9 us -> 110 us  [expert_gather(): pl.pallas_call(functools.partial(expert_gather_kernel, dp_count, len(shar...]
    pallas_call x1, Pallas kernels: 48.3 us -> 76.9 us  [small_gather(): pl.pallas_call(functools.partial(small_gather_kernel, dp_count), out_shap...]
    pallas_call x2, Pallas kernels: 155 us -> 132 us  [experts(): pl.pallas_call(functools.partial(experts_kernel, linked, dp_count), grid=...]
    ppermute x1 -> x0, waiting for transfers between devices: 12.3 us -> none  [shards(): lax.ppermute(lax.dynamic_index_in_dim(grad_gu, 1 - inner, 2, False), 'dp'...]
    convert_element_type x2 -> x0, other arithmetic: 7.5 us -> none  [the longest x1 5.14 us: shards(): linked = (lax.dynamic_index_in_dim(grad_gu, inner, 2, False).astype(jnp.f...]
  transfers between devices with their start and end apart: 4 -> 4, of which waited for: 1 -> 1; matrix products, arithmetic and copies ran while one was open for 3% -> 2% of each run, Pallas kernels for 48% -> 92%
where the time goes in v6:
time: 654 us; the launch traced here: 648 us
  Pallas kernels  597 us (91%)
  local copies, waits for them, and re-layouts  23.8 us (4%)
  between operations  14.5 us (2%)
  waiting for transfers between devices  7.72 us (1%)
    pallas_call x1, Pallas kernels, attention_backward(): pl.pallas_call(functools.partial(attention_backward_kernel, len(sources))...  158 us
    pallas_call x2, Pallas kernels, experts(): pl.pallas_call(functools.partial(experts_kernel, linked, dp_count), grid=...  132 us
    pallas_call x1, Pallas kernels, expert_gather(): pl.pallas_call(functools.partial(expert_gather_kernel, dp_count, len(shar...  110 us
    pallas_call x1, Pallas kernels, small_gather(): pl.pallas_call(functools.partial(small_gather_kernel, dp_count), out_shap...  76.9 us
    pallas_call x1, Pallas kernels, final_reduce(): pl.pallas_call(functools.partial(final_reduce_kernel, len(smalls)), out_s...  50.3 us
    pallas_call x1, Pallas kernels, attention_forward(): pl.pallas_call(functools.partial(attention_forward_kernel, dp_count if li...  33.1 us
    pallas_call x1, Pallas kernels, combine(): pl.pallas_call(functools.partial(combine_kernel, expert_count, local_coun...  21.1 us
    unnamed x56, local copies, waits for them, and re-layouts  13.6 us
  transfers between devices with their start and end apart: 4, of which 1 were waited for; matrix products, arithmetic and copies ran while one was open for 2% of the time, Pallas kernels for 92%

profile of v6, /device:TPU:19, one launch (start us, length us, event | category | flops | bytes accessed | tf_op | source)
XLA Modules:
  0.0 647.7 jit_solution(3305248511080069871)
XLA Ops:
  7.3 2.1 slice.39
  9.5 1.8 slice.40
  11.4 0.1 copy.43
  11.5 0.1 copy.44
  11.6 0.1 copy.40
  11.8 0.1 copy.41
  11.9 0.1 copy.42
  12.0 0.2 copy.45
  12.2 1.1 copy.46.refs_7_.refs_13_
  13.3 0.2 copy.39
  13.5 4.3 routing.1
  17.9 0.8 copy-done.6
  18.7 0.6 copy-done.7
  19.3 1.2 concatenate.13.shard_ref
  20.5 76.9 %small_gather.1.refs_1_.refs_2_.refs_3_.refs_4_.refs_5_.refs_8_.refs_7_.refs_9_.refs_10_.refs_11_ = bf16[768,3328]{1,0:T(8,128)(2,1)} custom-call(bf16[96,3328]{1,0:T(8,128)(2,1)} %concatenate.13.shard_ref), custom_call_target="tpu_custom_call" | custom-call | tf_op jit(solution)/shard_map/small_gather/pallas_call | solution.py:876
  97.4 0.8 pad_convert_fusion.refs_11_
  98.2 33.1 %attention_forward.1 = (bf16[1024,768]{1,0:T(8,128)(2,1)}, bf16[1024,768]{1,0:T(8,128)(2,1)}, bf16[1024,768]{1,0:T(8,128)(2,1)}, bf16[1024,768]{1,0:T(8,128)(2,1...) custom-call(bf16[1024,768]{1,0:T(8,128)(2,1)} %bitcast.53, ...), custom_call_target="tpu_custom_call" | custom-call | flops 8053063680 | bytes 18874368 | tf_op jit(solution)/shard_map/attention_forward/pallas_call | solution.py:177
  131.4 12.1 %dispatch.1 = (bf16[2048,768]{1,0:T(8,128)(2,1)}, bf16[2048,768]{1,0:T(8,128)(2,1)}) custom-call(s32[8,1024]{1,0:T(8,128)} %copy-done.7, f32[1024,128]{1,0:T(8,128)} %get-tuple-element.51.aux_ref.refs_4_, bf16[1024,768]{1,0:T(8,128)(2,1)} %get-tuple-element.52.normed_ref.refs_5_, bf16[1024,768]{1,0:T(8,128)(2,1)} %bitcast.51), custom_call_target="tpu_custom_call" | custom-call | flops 6442450944 | bytes 9437184 | tf_op jit(solution)/shard_map/dispatch/pallas_call | solution.py:459
  143.4 109.6 %expert_gather.1 = (bf16[2,2048,768]{2,1,0:T(8,128)(2,1)}, bf16[4,512,768]{2,1,0:T(8,128)(2,1)}, bf16[4,512,768]{2,1,0:T(8,128)(2,1)}) custom-call(bf16[2,256,768]{2,1,0:T(8,128)(2,1)} %refs_0_.1, bf16[4,512,768]{2,1,0:T(8,128)(2,1)} %bitcast.34, bf16[4,512,768]{2,1,0:T(8,128)(2,1)} %bitcast.35), custom_call_target="tpu_custom_call" | custom-call | tf_op jit(solution)/shard_map/expert_gather/pallas_call | solution.py:1046
  253.1 55.8 %experts.2 = (bf16[2,768,2048]{2,1,0:T(8,128)(2,1)}, bf16[2048,768]{1,0:T(8,128)(2,1)}, bf16[4,2,256,768]{3,2,1,0:T(8,128)(2,1)}, bf16[768,2048]{1,0:T(8,128)(2,1)}) custom-call(bf16[4,2,256,768]{3,2,1,0:T(8,128)(2,1)} %bitcast.47, bf16[4,2,256,768]{3,2,1,0:T(8,128)(2,1)} %bitcast.49, bf16[768,4096]{1,0:T(8,128)(2,1)} %bitcast.44, ...), custom_call_target="tpu_custom_call" | custom-call | flops 28991029248 | bytes 25165824 | tf_op jit(solution)/shard_map/experts/pallas_call | solution.py:733
  308.9 0.5 reduce-scatter.5.cloned.1.call-update
  309.5 76.3 %experts.3 = (bf16[2,768,2048]{2,1,0:T(8,128)(2,1)}, bf16[2048,768]{1,0:T(8,128)(2,1)}, bf16[4,2,256,768]{3,2,1,0:T(8,128)(2,1)}, bf16[4,2,256,768]{3,2,1,0:T(8,128)(2,1)}) custom-call(bf16[4,2,256,768]{3,2,1,0:T(8,128)(2,1)} %bitcast.48, bf16[4,2,256,768]{3,2,1,0:T(8,128)(2,1)} %bitcast.50, bf16[768,2048]{1,0:T(8,128)(2,1)} %get-tuple-element.58.refs_2_, ...), custom_call_target="tpu_custom_call" | custom-call | flops 28991029248 | bytes 25165824 | tf_op jit(solution)/shard_map/experts/pallas_call | solution.py:733
  385.8 7.1 %reduce-scatter.3.cloned.1.call-done = bf16[256,768]{1,0:T(8,128)(2,1)} async-done(((bf16[2048,768]{1,0:T(8,128)(2,1)}), bf16[256,768]{1,0:T(8,128)(2,1)}) %reduce-scatter.3.cloned.1.call-update) | async-done | bytes 393232 | tf_op jit(solution)/shard_map/reduce_scatter | solution.py:1561
  392.9 21.1 %combine.1 = (bf16[1024,768]{1,0:T(8,128)(2,1)}, bf16[1024,12]{1,0:T(8,128)(2,1)}, f32[1024,768]{1,0:T(8,128)}, f32[768,128]{1,0:T(8,128)}) custom-call(bf16[4,2,256,768]{3,2,1,0:T(8,128)(2,1)} %get-tuple-element.63.refs_0_, bf16[4,2,256,768]{3,2,1,0:T(8,128)(2,1)} %get-tuple-element.64.refs_1_, s32[1024,128]{1,0:T(8,128)} %copy-done.6, s32[1024,2]{1,0:T(8,128)} %bitcast.28, ...), custom_call_target="tpu_custom_call" | custom-call | flops 9663676416 | bytes 17301504 | tf_op jit(solution)/shard_map/combine/pallas_call | solution.py:578
  414.0 158.0 %attention_backward.1 = (bf16[1024,768]{1,0:T(8,128)(2,1)}, bf16[768,768]{1,0:T(8,128)(2,1)}, bf16[768,768]{1,0:T(8,128)(2,1)}, bf16[768,768]{1,0:T(8,128)(2,1)}...) custom-call(f32[1024,768]{1,0:T(8,128)} %get-tuple-element.68.refs_0_, ...), custom_call_target="tpu_custom_call" | custom-call | flops 17716740096 | bytes 25165824 | tf_op jit(solution)/shard_map/attention_backward/pallas_call | solution.py:344
  572.0 1.3 copy-done.1
  573.2 1.3 copy-done.2
  574.5 1.3 copy-done.3
  575.8 1.3 copy-done.4
  577.1 1.0 copy-done.5
  578.1 50.3 %final_reduce.1 = f32[96,3328]{1,0:T(8,128)S(1)} custom-call(bf16[8,96,768]{2,1,0:T(8,128)(2,1)S(1)} %bitcast.29, bf16[8,96,768]{2,1,0:T(8,128)(2,1)S(1)} %bitcast.30, bf16[8,96,768]{2,1,0:T(8,128)(2,1)S(1)} %bitcast.31, bf16[8,96,768]{2,1,0:T(8,128)(2,1)S(1)} %bitcast.32, bf16[8,96,256]{2,1,0:T(8,128)(2,1)S(1)} %bitcast.33), custom_call_target="tpu_custom_call" | custom-call | tf_op jit(solution)/shard_map/final_reduce/pallas_call | solution.py:1450
  628.3 0.1 slice.46
  628.4 0.1 slice.47
  628.5 0.7 slice.42
  629.2 1.0 slice.41
  630.2 0.8 copy.48
  631.0 0.7 copy.50
  631.6 0.7 copy.49
  632.3 0.6 copy.51
  632.9 0.7 slice_reduce_fusion
  633.6 0.1 bitcast_convert_fusion
  633.7 1.2 pad_maximum_fusion.1
  634.9 1.2 fusion
  636.1 0.1 maximum_convert_fusion
  636.3 1.3 copy-done.9
  637.5 1.9 pad_maximum_fusion
  639.4 0.1 copy-done.8
  639.6 1.1 copy.53
  (49 shorter events, 0.3 us)
Async XLA Ops:
  7.2 4.2 copy-start.20
  7.2 4.3 copy-start.21
  7.2 4.4 copy-start.18
  7.2 4.5 copy-start.19
  7.2 4.7 copy-start.22
  7.2 4.8 copy-start.15
  7.2 245.9 %all-gather.5.cloned.1.call-start = ((), (), s32[]{:S(2)}) async-start(), calls=%async_computation.4 | async-start | bytes 7077888 | tf_op jit(solution)/shard_map/all_gather | solution.py:1522
  9.4 2.9 copy-start.17
  9.4 3.9 copy-start.16
  9.4 9.9 %copy-start.11 = (bf16[96,2304]{1,0:T(8,128)(2,1)S(1)}, bf16[96,2304]{1,0:T(8,128)(2,1)}, u32[]{:S(2)}) copy-start(bf16[96,2304]{1,0:T(8,128)(2,1)} %param.20) | copy-start | bytes 1327108
  9.4 9.9 %copy-start.14 = (bf16[96,768]{1,0:T(8,128)(2,1)S(1)}, bf16[96,768]{1,0:T(8,128)(2,1)}, u32[]{:S(2)}) copy-start(bf16[96,768]{1,0:T(8,128)(2,1)} %param.21) | copy-start | bytes 442372
  9.4 300.1 %all-gather.7.cloned.1.call-start = ((), (), s32[]{:S(2)}) async-start(), calls=%async_computation.5 | async-start | bytes 3538944 | tf_op jit(solution)/shard_map/all_gather | solution.py:1525
  11.3 381.6 %reduce-scatter.3.cloned.1.call-start = ((), (), s32[]{:S(2)}) async-start(), calls=%async_computation.2 | async-start | bytes 3538944 | tf_op jit(solution)/shard_map/reduce_scatter | solution.py:1561
  13.5 83.9 %copy-start = (s32[1,1024,2]{2,1,0:T(8,128)}, s32[1,1024,2]{2,1,0:T(8,128)S(1)}, u32[]{:S(2)}) copy-start(s32[1,1024,2]{2,1,0:T(8,128)S(1)} %copy.39) | copy-start | bytes 24580
  17.9 0.8 copy-start.6
  18.7 0.6 copy-start.7
  308.9 326.1 %reduce-scatter.5.cloned.1.call-start = ((), (), s32[]{:S(2)}) async-start(), calls=%async_computation.3 | async-start | bytes 7077888 | tf_op jit(solution)/shard_map/reduce_scatter | solution.py:1563
  572.0 1.3 copy-start.1
  573.2 1.3 copy-start.2
  574.5 1.3 copy-start.3
  575.8 1.3 copy-start.4
  577.1 1.0 copy-start.5
  628.3 1.9 copy-start.13
  628.4 5.2 copy-start.12
  629.2 4.5 copy-start.10
  636.1 1.4 copy-start.9
  637.5 2.0 copy-start.8
Sparse Core Ops, SparseCore 0:
  10.8 133.0 all-gather.4
  146.1 90.7 all-gather.6
  309.0 83.8 reduce-scatter.2
  396.3 160.8 reduce-scatter.4

commit v7 on v6

--- a/solution.py
+++ b/solution.py
@@ -452,14 +452,17 @@
     grads_ref[...] = (nn(chosen, cot_ref[...]) * gates).astype(jnp.bfloat16)
 
 
-def dispatch(spots, aux, normed, cot, slot_count):
+def dispatch(spots, aux, normed, cot, owner_count, local_count):
     rows, width = normed.shape
+    slot_count = owner_count * local_count * CAP
     whole = lambda shape: pl.BlockSpec(shape, lambda j: (0, 0))
-    block = pl.BlockSpec((CAP, width), lambda j: (j, 0))
+    block = pl.BlockSpec(
+        (None, None, CAP, width), lambda j: (j % local_count, j // local_count, 0, 0)
+    )
     return pl.pallas_call(
         dispatch_kernel,
         grid=(slot_count // CAP,),
-        out_shape=[jax.ShapeDtypeStruct((slot_count, width), jnp.bfloat16)] * 2,
+        out_shape=[jax.ShapeDtypeStruct((local_count, owner_count, CAP, width), jnp.bfloat16)] * 2,
         in_specs=[whole((8, rows)), whole((rows, 128)), whole((rows, width)), whole((rows, width))],
         out_specs=[block, block],
         scratch_shapes=[pltpu.VMEM((8, rows), jnp.float32)],
@@ -608,75 +611,53 @@
     )(*parts, spots, routes, aux, normed, middle, cot, packed)
 
 
-def experts_kernel(linked, dp_count, *refs):
-    if dp_count:
-        (
-            rows_ref, grads_ref, w_gate_ref, w_up_ref, w_down_ref, shards_ref, grad_gu_ref,
-            grad_down_ref, both_ref, full_ref, turned_ref, out_ref, back_ref, *line_sems,
-        ) = refs
-    elif linked:
-        (
-            rows_ref, grads_ref, w_gate_ref, w_up_ref, w_down_ref, before_ref,
-            grad_gu_ref, grad_down_ref, first_in, second_in,
-            turned_ref, out_ref, back_ref, both_ref, send_sem, recv_sem,
-        ) = refs
-    else:
-        (
-            rows_ref, grads_ref, w_gate_ref, w_up_ref, w_down_ref, grad_gu_ref, grad_down_ref,
-            both_ref, turned_ref, out_ref, back_ref,
-        ) = refs
+def experts_kernel(mode, dp_count, *refs):
+    rows_ref, grads_ref, w_gate_ref, w_up_ref, w_down_ref = refs[:5]
+    if mode == 0:
+        grad_gu_ref, grad_down_ref, both_ref, turned_ref, out_ref, back_ref = refs[5:]
+    if mode == 1:
+        next_rows, next_grads, shards_ref, grad_gu_ref, grad_down_ref, both_ref = refs[5:11]
+        rows_out, grads_out, full_ref, turned_ref, out_ref, back_ref = refs[11:17]
+        sems = refs[17:]
+    if mode == 2:
+        before_ref, source_ref, grad_gu_ref, grad_down_ref, first_in, second_in, total_ref = refs[5:12]
+        turned_ref, out_ref, back_ref, both_ref = refs[12:16]
+        sems = refs[16:]
     step = pl.program_id(0)
     width = rows_ref.shape[-1]
     rows = rows_ref[...].reshape(-1, width)
     grads = grads_ref[...].reshape(-1, width)
-
-    if dp_count:
-        line = LineGather(
-            shards_ref.at[1, :, 0 : full_ref.shape[1]], full_ref, dp_count, *line_sems
-        )
+    if mode == 1:
+        line = LineGather(shards_ref.at[1], full_ref, dp_count, *sems[:3])
+        trades = [
+            Trade(next_rows.at[1], rows_out, *sems[3:5]),
+            Trade(next_grads.at[1], grads_out, *sems[5:7]),
+        ]
 
         @pl.when(step == 0)
         def _():
-            greet(line.peers())
+            greet(line.peers() + trades[0].peers())
             line.start()
-
-        @pl.when(step == 2)
-        def _():
-            line.relay(1)
-
-    if linked:
-        me, mine = place()
-        owner_count = both_ref.shape[0]
-        peers = [lax.rem(mine + k, owner_count) for k in range(1, owner_count)]
-
-        def trade(n, source, target, k, peer):
-            return pltpu.make_async_remote_copy(
-                src_ref=source.at[peer],
-                dst_ref=target.at[mine],
-                send_sem=send_sem.at[n, k],
-                recv_sem=recv_sem.at[n, mine],
-                device_id=(me, peer),
-                device_id_type=MESH,
-            )
-
-        def keep(n, source, target):
-            return pltpu.make_async_copy(source.at[mine], target.at[mine], send_sem.at[n, 0])
-
-        def trade_start(n, source, target):
-            for k, peer in enumerate(peers):
-                trade(n, source, target, k + 1, peer).start()
-            keep(n, source, target).start()
-
-        def trade_finish(n, source, target):
-            keep(n, source, target).wait()
-            for k, peer in enumerate(peers):
-                pltpu.make_async_copy(target.at[peer], target.at[peer], recv_sem.at[n, peer]).wait()
-                trade(n, source, target, k + 1, peer).wait_send()
+            for trade in trades:
+                trade.start()
+
+        for hop in range(1, line.outer_count):
+            pl.when(step == hop)(functools.partial(line.relay, hop))
+
+    if mode == 2:
+        trades = [Trade(before_ref, first_in, *sems[:2]), Trade(both_ref, second_in, *sems[2:4])]
+        line = line_reduce([source_ref], [total_ref], sems[4:])
 
         @pl.when(step == 0)
         def _():
-            greet([(me, peer) for peer in peers])
-            trade_start(0, before_ref, first_in)
+            greet(line.peers() + trades[0].peers())
+            line.each_plane(line.start)
+            trades[0].start()
+
+        for hop in range(3):
+            pl.when(step == hop + 1)(
+                functools.partial(line.each_plane, functools.partial(line.pass_on, k=hop))
+            )
 
     @pl.when(step == 0)
     def _():
@@ -684,7 +665,7 @@
         out_ref[...] = jnp.zeros_like(out_ref)
         back_ref[...] = jnp.zeros_like(back_ref)
 
-    w_gate, w_up, w_down = w_gate_ref[...], w_up_ref[...], w_down_ref[0]
+    w_gate, w_up, w_down = w_gate_ref[...], w_up_ref[...], w_down_ref[...]
     gate, up = nn(rows, w_gate), nn(rows, w_up)
     squashed = 1.0 / (1.0 + jnp.exp(-gate))
     silu = gate * squashed
@@ -703,73 +684,77 @@
         shape = (both_ref.shape[0],) + both_ref.shape[2:]
         both_ref[:, 0] = out_ref[...].astype(jnp.bfloat16).reshape(shape)
         both_ref[:, 1] = back_ref[...].astype(jnp.bfloat16).reshape(shape)
-        if dp_count:
-            for hop in range(2, line.outer_count):
-                line.relay(hop)
+        if mode == 1:
             line.finish()
-        if linked:
-            trade_start(1, both_ref, second_in)
-            trade_finish(0, before_ref, first_in)
-            trade_finish(1, both_ref, second_in)
-
-
-def experts(arrived, arrived_grad, gate, up, down, at, before=None, shards=None, dp_count=0, collective=None):
-    owners, _, cap, width = arrived.shape
-    hidden = down.shape[1]
+            for trade in trades:
+                trade.finish()
+        if mode == 2:
+            trades[1].start()
+
+            def rest(o):
+                line.pass_on(o, 3)
+                line.finish(o)
+
+            line.each_plane(rest)
+            for trade in trades:
+                trade.finish()
+
+
+def experts(rows, grads, gate, up, down, mode=0, dp_count=0, extras=(), collective=None):
+    owners, cap, width = rows.shape
+    hidden = down.shape[0]
     count = owners * cap
     block = FF_BLOCK if count <= 1024 else FF_BLOCK // 4
     steps = hidden // block
-    linked = before is not None
-    pairs = pl.BlockSpec(
-        (owners, 1, cap, width), lambda j: (0, at, 0, 0), pipeline_mode=pl.Buffered(1)
-    )
+    low = jnp.bfloat16
+    pairs = pl.BlockSpec((owners, cap, width), lambda j: (0, 0, 0), pipeline_mode=pl.Buffered(1))
     anywhere = pl.BlockSpec(memory_space=pl.ANY)
-    both = jax.ShapeDtypeStruct((owners, 2, cap, width), jnp.bfloat16)
-    gathers = shards is not None
-    links = {"collective_id": collective, "has_side_effects": True} if linked or gathers else {}
-    full = []
-    if gathers:
-        full = [jax.ShapeDtypeStruct((dp_count * shards.shape[1], hidden), jnp.bfloat16)]
+    both = jax.ShapeDtypeStruct((owners, 2, cap, width), low)
+    links = {"collective_id": collective, "has_side_effects": True} if mode else {}
+    out_shape = [
+        jax.ShapeDtypeStruct((2, width, hidden), low),
+        jax.ShapeDtypeStruct((hidden, width), low),
+    ]
+    out_specs = [
+        pl.BlockSpec((2, width, block), lambda j: (0, 0, j)),
+        pl.BlockSpec((block, width), lambda j: (j, 0)),
+    ]
+    scratch = [
+        pltpu.VMEM((width, count), low),
+        pltpu.VMEM((count, width), jnp.float32),
+        pltpu.VMEM((count, width), jnp.float32),
+    ]
+    if mode < 2:
+        out_shape.append(both)
+        out_specs.append(pl.BlockSpec(both.shape, lambda j: (0, 0, 0, 0)))
+    if mode == 1:
+        shards = extras[2]
+        out_shape += [jax.ShapeDtypeStruct(rows.shape, low)] * 2
+        out_shape.append(jax.ShapeDtypeStruct((dp_count * shards.shape[1], shards.shape[2]), low))
+        out_specs += [anywhere] * 3
+        scratch += gather_semaphores(dp_count) + trade_semaphores(owners) + trade_semaphores(owners)
+    if mode == 2:
+        total = (hidden // 8, width)
+        out_shape += [both, both, jax.ShapeDtypeStruct(total, jnp.float32)]
+        out_specs += [anywhere] * 2 + [pl.BlockSpec(total, lambda j: (0, 0))]
+        scratch.append(pltpu.VMEM(both.shape, low))
+        scratch += trade_semaphores(owners) + trade_semaphores(owners) + reduce_scratch([extras[1]])
     return pl.pallas_call(
-        functools.partial(experts_kernel, linked, dp_count),
+        functools.partial(experts_kernel, mode, dp_count),
         grid=(steps,),
-        out_shape=[
-            jax.ShapeDtypeStruct((2, width, hidden), jnp.bfloat16),
-            jax.ShapeDtypeStruct((hidden, width), jnp.bfloat16),
-        ]
-        + [both] * (2 if linked else 1)
-        + full,
+        out_shape=out_shape,
         in_specs=[
             pairs,
             pairs,
             pl.BlockSpec((width, block), lambda j: (0, j)),
             pl.BlockSpec((width, block), lambda j: (0, up.shape[1] // block - steps + j)),
-            pl.BlockSpec((1, block, width), lambda j: (at, j, 0)),
-        ]
-        + [anywhere] * (linked + gathers),
-        out_specs=[
-            pl.BlockSpec((2, width, block), lambda j: (0, 0, j)),
             pl.BlockSpec((block, width), lambda j: (j, 0)),
         ]
-        + ([anywhere] * 2 if linked else [pl.BlockSpec(both.shape, lambda j: (0, 0, 0, 0))])
-        + [anywhere] * gathers,
-        scratch_shapes=[
-            pltpu.VMEM((width, count), jnp.bfloat16),
-            pltpu.VMEM((count, width), jnp.float32),
-            pltpu.VMEM((count, width), jnp.float32),
-        ]
-        + (
-            [
-                pltpu.VMEM(both.shape, jnp.bfloat16),
-                pltpu.SemaphoreType.DMA((2, owners)),
-                pltpu.SemaphoreType.DMA((2, owners)),
-            ]
-            if linked
-            else []
-        )
-        + (gather_semaphores(dp_count) if gathers else []),
+        + [anywhere] * len(extras),
+        out_specs=out_specs,
+        scratch_shapes=scratch,
         compiler_params=pltpu.CompilerParams(
-            dimension_semantics=("arbitrary",), vmem_limit_bytes=58 * 2**20, **links
+            dimension_semantics=("arbitrary",), vmem_limit_bytes=60 * 2**20, **links
         ),
         cost_estimate=pl.CostEstimate(
             flops=18 * count * width * hidden,
@@ -777,10 +762,7 @@
             transcendentals=count * hidden,
         ),
         name="experts",
-    )(
-        arrived, arrived_grad, gate, up, down, *([before] if linked else []),
-        *([shards] if gathers else []),
-    )
+    )(rows, grads, gate, up, down, *extras)
 
 
 def dp_grid(dp_count):
@@ -890,182 +872,6 @@
     )(shard)
 
 
-def expert_gather_kernel(dp_count, tensor_count, cuts, crossed, owner_count, trade_count, *refs):
-    given = tensor_count + trade_count
-    shards, outgoing = refs[:tensor_count], refs[tensor_count:given]
-    fulls, incoming = refs[given : given + tensor_count], refs[given + tensor_count : 2 * given]
-    send_sem, recv_sem, own_sem, trade_send, trade_recv = refs[2 * given :]
-    outer_count, inner_count = dp_grid(dp_count)
-    me, mine = place()
-    outer, inner = me // inner_count, me % inner_count
-    below, above = lax.rem(outer + outer_count - 1, outer_count), lax.rem(outer + 1, outer_count)
-    inner_peers = [lax.rem(inner + k, inner_count) for k in range(1, inner_count)]
-    greet(
-        [(peer * inner_count + inner, mine) for peer in (below, above)]
-        + [(outer * inner_count + peer, mine) for peer in inner_peers]
-        + [(me, lax.rem(mine + k, owner_count)) for k in range(1, owner_count) if trade_count]
-    )
-    trades = []
-    for t in range(trade_count):
-        for k in range(1, owner_count):
-            peer = lax.rem(mine + k, owner_count)
-            trade = pltpu.make_async_remote_copy(
-                src_ref=outgoing[t].at[peer],
-                dst_ref=incoming[t].at[mine],
-                send_sem=trade_send.at[t, k],
-                recv_sem=trade_recv.at[t, mine],
-                device_id=(me, peer),
-                device_id_type=MESH,
-            )
-            trade.start()
-            trades.append(trade)
-        keep = pltpu.make_async_copy(
-            outgoing[t].at[mine], incoming[t].at[mine], trade_send.at[t, 0]
-        )
-        keep.start()
-    pieces = [
-        (t, e, c) for t in range(tensor_count) for e in range(shards[t].shape[0]) for c in range(cuts[t])
-    ]
-
-    def spot(p, chunk):
-        t, e, c = pieces[p]
-        rows = shards[t].shape[1]
-        part = rows // cuts[t]
-        return fulls[t].at[e, pl.ds(pl.multiple_of(chunk * rows + c * part, 8), part), :]
-
-    def copy_of(p, source, chunk, device, send_at):
-        return pltpu.make_async_remote_copy(
-            src_ref=source,
-            dst_ref=spot(p, chunk),
-            send_sem=send_at,
-            recv_sem=recv_sem.at[p, chunk],
-            device_id=device,
-            device_id_type=MESH,
-        )
-
-    def source_of(p):
-        t, e, c = pieces[p]
-        part = shards[t].shape[1] // cuts[t]
-        return shards[t].at[e, pl.ds(c * part, part), :]
-
-    def inner_sends(p, source, chunk):
-        return [
-            copy_of(p, source, chunk, (outer * inner_count + peer, mine), send_sem.at[p, 0, j, chunk])
-            for j, peer in enumerate(inner_peers)
-        ]
-
-    def up(p, source, chunk):
-        return copy_of(p, source, chunk, (above * inner_count + inner, mine), send_sem.at[p, 1, 0, chunk])
-
-    def down(p, source, chunk):
-        return copy_of(p, source, chunk, (below * inner_count + inner, mine), send_sem.at[p, 2, 0, chunk])
-
-    def arrived(p, chunk):
-        pltpu.make_async_copy(spot(p, chunk), spot(p, chunk), recv_sem.at[p, chunk]).wait()
-
-    can_up, can_down = outer < outer_count - 1, outer > 0
-    every = range(len(pieces))
-    own = []
-    for p in every:
-        for copy in inner_sends(p, source_of(p), me):
-            copy.start()
-        pl.when(can_up)(lambda p=p: up(p, source_of(p), me).start())
-        pl.when(can_down)(lambda p=p: down(p, source_of(p), me).start())
-        copy = pltpu.make_async_copy(source_of(p), spot(p, me), own_sem.at[p])
-        copy.start()
-        own.append(copy)
-
-    def passing(p, chunk, upward):
-        arrived(p, chunk)
-        if upward:
-            pl.when(can_up)(lambda: up(p, spot(p, chunk), chunk).start())
-        else:
-            pl.when(can_down)(lambda: down(p, spot(p, chunk), chunk).start())
-
-    for p in every:
-        if p in crossed:
-            for peer in inner_peers:
-                chunk = outer * inner_count + peer
-                arrived(p, chunk)
-                pl.when(can_up)(lambda p=p, chunk=chunk: up(p, spot(p, chunk), chunk).start())
-                pl.when(can_down)(lambda p=p, chunk=chunk: down(p, spot(p, chunk), chunk).start())
-    for step in range(1, outer_count):
-        low, high = outer - step, outer + step
-        for p in every:
-            for upward, there, source in ((True, low >= 0, low), (False, high < outer_count, high)):
-
-                def relay(p=p, upward=upward, source=source):
-                    chunk = source * inner_count + inner
-                    passing(p, chunk, upward)
-                    if p in crossed:
-                        for peer in inner_peers:
-                            passing(p, source * inner_count + peer, upward)
-                    else:
-                        for copy in inner_sends(p, spot(p, chunk), chunk):
-                            copy.start()
-
-                pl.when(there)(relay)
-    for t in range(trade_count):
-        pltpu.make_async_copy(
-            outgoing[t].at[mine], incoming[t].at[mine], trade_send.at[t, 0]
-        ).wait()
-        for k in range(1, owner_count):
-            there = incoming[t].at[lax.rem(mine + k, owner_count)]
-            pltpu.make_async_copy(
-                there, there, trade_recv.at[t, lax.rem(mine + k, owner_count)]
-            ).wait()
-    for trade in trades:
-        trade.wait_send()
-    for p in every:
-        own[p].wait()
-        if p not in crossed:
-            for peer in inner_peers:
-                for plane in range(outer_count):
-                    arrived(p, plane * inner_count + peer)
-        for copy in inner_sends(p, source_of(p), me):
-            copy.wait_send()
-        if p not in crossed:
-            for k in range(1, outer_count):
-                chunk = lax.rem(outer + k, outer_count) * inner_count + inner
-                for copy in inner_sends(p, spot(p, chunk), chunk):
-                    copy.wait_send()
-        columns = range(inner_count) if p in crossed else [inner]
-        for plane in range(outer_count):
-            for column in columns:
-                chunk = plane * inner_count + column
-                pl.when(can_up & (outer >= plane))(lambda p=p, chunk=chunk: up(p, spot(p, chunk), chunk).wait_send())
-                pl.when(can_down & (outer <= plane))(lambda p=p, chunk=chunk: down(p, spot(p, chunk), chunk).wait_send())
-
-
-def expert_gather(shards, dp_count, collective, cuts=None, crossed=(), owner_count=1, trades=()):
-    outer_count, inner_count = dp_grid(dp_count)
-    cuts = cuts or [1] * len(shards)
-    piece_count = sum(shard.shape[0] * cut for shard, cut in zip(shards, cuts))
-    anywhere = pl.BlockSpec(memory_space=pl.ANY)
-    given = len(shards) + len(trades)
-    return pl.pallas_call(
-        functools.partial(
-            expert_gather_kernel, dp_count, len(shards), cuts, crossed, owner_count, len(trades)
-        ),
-        out_shape=[
-            jax.ShapeDtypeStruct((s.shape[0], dp_count * s.shape[1], s.shape[2]), s.dtype)
-            for s in shards
-        ]
-        + [jax.ShapeDtypeStruct(t.shape, t.dtype) for t in trades],
-        in_specs=[anywhere] * given,
-        out_specs=[anywhere] * given,
-        scratch_shapes=[
-            pltpu.SemaphoreType.DMA((piece_count, 3, max(1, inner_count - 1), dp_count)),
-            pltpu.SemaphoreType.DMA((piece_count, dp_count)),
-            pltpu.SemaphoreType.DMA((piece_count,)),
-            pltpu.SemaphoreType.DMA((max(1, len(trades)), owner_count)),
-            pltpu.SemaphoreType.DMA((max(1, len(trades)), owner_count)),
-        ],
-        compiler_params=pltpu.CompilerParams(collective_id=collective, has_side_effects=True),
-        name="expert_gather",
-    )(*shards, *trades)
-
-
 class LineGather:
     def __init__(self, shard, full, dp_count, send_sem, recv_sem, own_sem):
         self.shard, self.full, self.dp_count = shard, full, dp_count
@@ -1172,6 +978,82 @@
         return carry
 
     lax.fori_loop(0, count // 16, step, 0)
+
+
+class Trade:
+    def __init__(self, source, target, send_sem, recv_sem):
+        self.source, self.target, self.send_sem, self.recv_sem = source, target, send_sem, recv_sem
+        self.me, self.mine = place()
+        count = target.shape[0]
+        self.partners = [lax.rem(self.mine + k, count) for k in range(1, count)]
+
+    def peers(self):
+        return [(self.me, peer) for peer in self.partners]
+
+    def copy(self, k):
+        peer = self.partners[k]
+        return pltpu.make_async_remote_copy(
+            src_ref=self.source.at[peer],
+            dst_ref=self.target.at[self.mine],
+            send_sem=self.send_sem.at[k + 1],
+            recv_sem=self.recv_sem.at[self.mine],
+            device_id=(self.me, peer),
+            device_id_type=MESH,
+        )
+
+    def keep(self):
+        return pltpu.make_async_copy(
+            self.source.at[self.mine], self.target.at[self.mine], self.send_sem.at[0]
+        )
+
+    def start(self):
+        for k in range(len(self.partners)):
+            self.copy(k).start()
+        self.keep().start()
+
+    def finish(self):
+        self.keep().wait()
+        for k, peer in enumerate(self.partners):
+            there = self.target.at[peer]
+            pltpu.make_async_copy(there, there, self.recv_sem.at[peer]).wait()
+            self.copy(k).wait_send()
+
+
+def trade_semaphores(owner_count):
+    return [pltpu.SemaphoreType.DMA((owner_count,)), pltpu.SemaphoreType.DMA((owner_count,))]
+
+
+def expert_gather_kernel(dp_count, rows_ref, grads_ref, shards_ref, rows_out, grads_out, full_ref, *sems):
+    line = LineGather(shards_ref.at[0], full_ref, dp_count, *sems[:3])
+    trades = [Trade(rows_ref.at[0], rows_out, *sems[3:5]), Trade(grads_ref.at[0], grads_out, *sems[5:7])]
+    greet(line.peers() + trades[0].peers())
+    line.start()
+    for trade in trades:
+        trade.start()
+    for hop in range(1, line.outer_count):
+        line.relay(hop)
+    line.finish()
+    for trade in trades:
+        trade.finish()
+
+
+def expert_gather(rows, grads, shards, dp_count, collective):
+    anywhere = pl.BlockSpec(memory_space=pl.ANY)
+    return pl.pallas_call(
+        functools.partial(expert_gather_kernel, dp_count),
+        out_shape=[
+            jax.ShapeDtypeStruct(rows.shape[1:], rows.dtype),
+            jax.ShapeDtypeStruct(grads.shape[1:], grads.dtype),
+            jax.ShapeDtypeStruct((dp_count * shards.shape[1], shards.shape[2]), shards.dtype),
+        ],
+        in_specs=[anywhere] * 3,
+        out_specs=[anywhere] * 3,
+        scratch_shapes=gather_semaphores(dp_count)
+        + trade_semaphores(rows.shape[1])
+        + trade_semaphores(rows.shape[1]),
+        compiler_params=pltpu.CompilerParams(collective_id=collective, has_side_effects=True),
+        name="expert_gather",
+    )(rows, grads, shards)
 
 
 class LineReduce:
@@ -1515,55 +1397,40 @@
         packed_full = small_gather(packed, dp_count, 1)
     else:
         packed_full = lax.all_gather(packed, "dp", axis=0, tiled=True)
-    attend = functools.partial(
-        attention_forward, inputs, packed_full, docs_row, docs_column, cosine, sine, route_rows, resid
-    )
     gather = functools.partial(lax.all_gather, axis_name="dp", axis=0, tiled=True)
-    gates = [gather(w_gate_up[e]) for e in range(1 if own_links else local_count)]
-    ups = list(gates)
+    first_gate_up = gather(w_gate_up[0])
     if own_links:
-        ups.append(gather(w_gate_up[1, :, hidden_count:]))
-    forward = attend()
-    normed_one, queries, keys, values, attended, middle, normed_two, aux = forward
-    send_rows, send_grads = dispatch(spot_rows, aux, normed_two, cot, expert_count * CAP)
-    send_rows = send_rows.reshape(owner_count, local_count * CAP, width)
-    send_grads = send_grads.reshape(owner_count, local_count * CAP, width)
-    exchange = functools.partial(
-        lax.all_to_all, axis_name="expert", split_axis=0, concat_axis=0, tiled=True
-    )
+        second_down = gather(w_down[1])
+    normed_one, queries, keys, values, attended, middle, normed_two, aux = attention_forward(
+        inputs, packed_full, docs_row, docs_column, cosine, sine, route_rows, resid
+    )
+    send_rows, send_grads = dispatch(spot_rows, aux, normed_two, cot, owner_count, local_count)
     if own_links:
-        down_full, arrived, arrived_grad = expert_gather(
-            [w_down], dp_count, 2, owner_count=owner_count, trades=[send_rows, send_grads]
+        rows_in, grads_in, first_down = expert_gather(send_rows, send_grads, w_down, dp_count, 2)
+        grad_gu, grad_down, both, next_rows, next_grads, second_gate_up = experts(
+            rows_in, grads_in, first_gate_up, first_gate_up, first_down, 1, dp_count,
+            [send_rows, send_grads, w_gate_up], 6,
         )
+        gu_parts = [lax.psum_scatter(grad_gu, "dp", scatter_dimension=1, tiled=True)]
+        second_gu, second_grad_down, *parts, down_part = experts(
+            next_rows, next_grads, second_gate_up, second_gate_up, second_down, 2, dp_count,
+            [both, grad_down], 4,
+        )
+        down_parts = [down_part]
     else:
-        down_full = lax.all_gather(w_down, "dp", axis=1, tiled=True)
-        arrived, arrived_grad = exchange(send_rows), exchange(send_grads)
-    arrived = arrived.reshape(owner_count, local_count, CAP, width)
-    arrived_grad = arrived_grad.reshape(owner_count, local_count, CAP, width)
-
-    parts, gu_parts, down_parts, sources = [], [], [], []
-    for e in range(local_count):
-        run = functools.partial(experts, arrived, arrived_grad, gates[e], ups[e], down_full, e)
-        if own_links and e == 0:
-            grad_gu, grad_down, both, next_gate = run(
-                shards=w_gate_up, dp_count=dp_count, collective=6
+        exchange = functools.partial(
+            lax.all_to_all, axis_name="expert", split_axis=0, concat_axis=0, tiled=True
+        )
+        parts, gu_parts, down_parts = [], [], []
+        for e in range(local_count):
+            gate_up = first_gate_up if e == 0 else gather(w_gate_up[e])
+            grad_gu, grad_down, both = experts(
+                exchange(send_rows[e]), exchange(send_grads[e]), gate_up, gate_up, gather(w_down[e])
             )
-            gates.append(next_gate)
-        elif own_links:
-            grad_gu, grad_down, *parts = run(before=both, collective=4)
-        else:
-            grad_gu, grad_down, both = run()
             parts.append(exchange(both))
-        if own_links and e == local_count - 1:
-            sources = [grad_gu, grad_down]
-        else:
-            down_parts.append(
-                lax.psum_scatter(grad_down, "dp", scatter_dimension=0, tiled=True)
-            )
-            gu_part = lax.psum_scatter(grad_gu, "dp", scatter_dimension=1, tiled=True)
-            gu_parts.append(jnp.concatenate([gu_part[0], gu_part[1]], -1).astype(jnp.float32))
-    if own_links:
-        parts, down_parts[0] = lax.optimization_barrier((parts, down_parts[0]))
+            gu_parts.append(lax.psum_scatter(grad_gu, "dp", scatter_dimension=1, tiled=True))
+            down_parts.append(lax.psum_scatter(grad_down, "dp", scatter_dimension=0, tiled=True))
+    gu_parts = [jnp.concatenate([part[0], part[1]], -1).astype(jnp.float32) for part in gu_parts]
     down_parts = [part.astype(jnp.float32) for part in down_parts]
     output, logit_grad, grad_middle, small_grad = combine(
         parts, spots, route_rows, aux, normed_two, middle, cot, packed_full, choice_count, expert_count
@@ -1573,7 +1440,7 @@
         packed_full, docs_row, docs_column, cosine, sine, small_grad,
     )
     if own_links:
-        token_grad, *weight_grads, gu_part, down_part = backward(sources, 7)
+        token_grad, *weight_grads, gu_part, down_part = backward([second_gu, second_grad_down], 7)
         gu_parts.append(gu_part)
         down_parts.append(down_part)
         packed_part = final_reduce(

time: 654 us -> 633 us (0.968)
  Pallas kernels: 597 us -> 588 us
  waiting for transfers between devices: 7.72 us -> 0.09 us
    pallas_call x3, Pallas kernels: 242 us -> 285 us  [the longest x2 198 us: experts(): pl.pallas_call(functools.partial(experts_kernel, mode, dp_count), grid=(s...]
    pallas_call x1, Pallas kernels: 158 us -> 120 us  [attention_backward(): pl.pallas_call(functools.partial(attention_backward_kernel, len(sources))...]
    pallas_call x1, Pallas kernels: 76.9 us -> 60.1 us  [small_gather(): pl.pallas_call(functools.partial(small_gather_kernel, dp_count), out_shap...]
    reduce_scatter x2 -> x1, waiting for transfers between devices: 7.11 us -> 0.01 us  [shards(): lax.psum_scatter(grad_gu, 'dp', scatter_dimension=1, tiled=True)]
    unnamed x56 -> x58, local copies, waits for them, and re-layouts: 13.6 us -> 13.6 us
  transfers between devices with their start and end apart: 4 -> 3, of which waited for: 1 -> 0; matrix products, arithmetic and copies ran while one was open for 2% -> 2% of each run, Pallas kernels for 92% -> 93%
where the time goes in v7:
time: 633 us; the launch traced here: 629 us
  Pallas kernels  588 us (93%)
  local copies, waits for them, and re-layouts  22.5 us (4%)
  between operations  14.5 us (2%)
    pallas_call x2, Pallas kernels, experts(): pl.pallas_call(functools.partial(experts_kernel, mode, dp_count), grid=(s...  198 us
    pallas_call x1, Pallas kernels, attention_backward(): pl.pallas_call(functools.partial(attention_backward_kernel, len(sources))...  120 us
    pallas_call x1, Pallas kernels, expert_gather(): pl.pallas_call(functools.partial(expert_gather_kernel, dp_count), out_sha...  87.2 us
    pallas_call x1, Pallas kernels, small_gather(): pl.pallas_call(functools.partial(small_gather_kernel, dp_count), out_shap...  60.1 us
    pallas_call x1, Pallas kernels, final_reduce(): pl.pallas_call(functools.partial(final_reduce_kernel, len(smalls)), out_s...  51.9 us
    pallas_call x1, Pallas kernels, attention_forward(): pl.pallas_call(functools.partial(attention_forward_kernel, dp_count if li...  33.4 us
    pallas_call x1, Pallas kernels, combine(): pl.pallas_call(functools.partial(combine_kernel, expert_count, local_coun...  21.2 us
    unnamed x58, local copies, waits for them, and re-layouts  13.6 us
  transfers between devices with their start and end apart: 3, of which 0 were waited for; matrix products, arithmetic and copies ran while one was open for 2% of the time, Pallas kernels for 93%

profile of v7, /device:TPU:19, one launch (start us, length us, event | category | flops | bytes accessed | tf_op | source)
XLA Modules:
  0.0 629.0 jit_solution(18383091237576614067)
XLA Ops:
  7.3 0.0 all-gather.5.cloned.1.call-start
  7.3 2.1 slice.39
  9.5 0.0 all-gather.7.cloned.1.call-start
  9.5 0.8 slice.40
  10.4 0.0 reduce-scatter.2.cloned.1.call-start
  10.4 0.1 copy.40
  10.5 0.1 copy.41
  10.7 0.1 copy.42
  10.8 0.1 copy.43
  10.9 0.1 copy.44
  11.1 1.0 concatenate.13.shard_ref
  12.1 60.1 %small_gather.1.refs_1_.refs_2_.refs_3_.refs_4_.refs_5_.refs_8_.refs_7_.refs_9_.refs_10_.refs_11_ = bf16[768,3328]{1,0:T(8,128)(2,1)} custom-call(bf16[96,3328]{1,0:T(8,128)(2,1)} %concatenate.13.shard_ref), custom_call_target="tpu_custom_call" | custom-call | tf_op jit(solution)/shard_map/small_gather/pallas_call | solution.py:858
  72.2 0.2 copy.39
  72.5 1.0 copy.46.refs_7_.refs_13_
  73.5 0.2 copy.45
  73.7 4.4 routing.1
  78.0 0.8 copy-done.6
  78.8 0.6 copy-done.7
  79.5 0.8 pad_convert_fusion.refs_11_
  80.3 33.4 %attention_forward.1 = (bf16[1024,768]{1,0:T(8,128)(2,1)}, bf16[1024,768]{1,0:T(8,128)(2,1)}, bf16[1024,768]{1,0:T(8,128)(2,1)}, bf16[1024,768]{1,0:T(8,128)(2,1...) custom-call(bf16[1024,768]{1,0:T(8,128)(2,1)} %bitcast.42, ...), custom_call_target="tpu_custom_call" | custom-call | flops 8053063680 | bytes 18874368 | tf_op jit(solution)/shard_map/attention_forward/pallas_call | solution.py:177
  113.7 11.8 %dispatch.1 = (bf16[2,4,256,768]{3,2,1,0:T(8,128)(2,1)}, bf16[2,4,256,768]{3,2,1,0:T(8,128)(2,1)}) custom-call(s32[8,1024]{1,0:T(8,128)} %copy-done.7, f32[1024,128]{1,0:T(8,128)} %get-tuple-element.51.aux_ref.refs_4_, bf16[1024,768]{1,0:T(8,128)(2,1)} %get-tuple-element.52.normed_ref.refs_5_, bf16[1024,768]{1,0:T(8,128)(2,1)} %bitcast.40), custom_call_target="tpu_custom_call" | custom-call | flops 6442450944 | bytes 9437184 | tf_op jit(solution)/shard_map/dispatch/pallas_call | solution.py:462
  125.4 87.2 %expert_gather.1 = (bf16[4,256,768]{2,1,0:T(8,128)(2,1)}, bf16[4,256,768]{2,1,0:T(8,128)(2,1)}, bf16[2048,768]{1,0:T(8,128)(2,1)}) custom-call(bf16[2,4,256,768]{3,2,1,0:T(8,128)(2,1)} %get-tuple-element.53.rows_ref.refs_5_, bf16[2,4,256,768]{3,2,1,0:T(8,128)(2,1)} %get-tuple-element.54.grads_ref.refs_6_, bf16[2,256,768]{2,1,0:T(8,128)(2,1)} %shards_ref.1), custom_call_target="tpu_custom_call" | custom-call | tf_op jit(solution)/shard_map/expert_gather/pallas_call | solution.py:1042
  212.6 85.3 %experts.2 = (bf16[2,768,2048]{2,1,0:T(8,128)(2,1)}, bf16[2048,768]{1,0:T(8,128)(2,1)}, bf16[4,2,256,768]{3,2,1,0:T(8,128)(2,1)}, bf16[4,256,768]{2,1,0:T(8,128)...) custom-call(bf16[4,256,768]{2,1,0:T(8,128)(2,1)} %get-tuple-element.55.refs_0_, ...), custom_call_target="tpu_custom_call" | custom-call | flops 28991029248 | bytes 25165824 | tf_op jit(solution)/shard_map/experts/pallas_call | solution.py:742
  298.0 113.0 %experts.3 = (bf16[2,768,2048]{2,1,0:T(8,128)(2,1)}, bf16[2048,768]{1,0:T(8,128)(2,1)}, bf16[4,2,256,768]{3,2,1,0:T(8,128)(2,1)}, bf16[4,2,256,768]{3,2,1,0:T(8,128)(2,1)}, f32[256,768]{1,0:T(8,128)}) custom-call(bf16[4,256,768]{2,1,0:T(8,128)(2,1)} %get-tuple-element.58.refs_0_, bf16[4,256,768]{2,1,0:T(8,128)(2,1)} %get-tuple-element.59.refs_1_, ...), custom_call_target="tpu_custom_call" | custom-call | flops 28991029248 | bytes 25165824 | tf_op jit(solution)/shard_map/experts/pallas_call | solution.py:742
  411.0 21.2 %combine.1 = (bf16[1024,768]{1,0:T(8,128)(2,1)}, bf16[1024,12]{1,0:T(8,128)(2,1)}, f32[1024,768]{1,0:T(8,128)}, f32[768,128]{1,0:T(8,128)}) custom-call(bf16[4,2,256,768]{3,2,1,0:T(8,128)(2,1)} %get-tuple-element.63.refs_0_, bf16[4,2,256,768]{3,2,1,0:T(8,128)(2,1)} %get-tuple-element.64.refs_1_, s32[1024,128]{1,0:T(8,128)} %copy-done.6, s32[1024,2]{1,0:T(8,128)} %bitcast.22, ...), custom_call_target="tpu_custom_call" | custom-call | flops 9663676416 | bytes 17301504 | tf_op jit(solution)/shard_map/combine/pallas_call | solution.py:581
  432.2 119.5 %attention_backward.1 = (bf16[1024,768]{1,0:T(8,128)(2,1)}, bf16[768,768]{1,0:T(8,128)(2,1)}, bf16[768,768]{1,0:T(8,128)(2,1)}, bf16[768,768]{1,0:T(8,128)(2,1)}...) custom-call(f32[1024,768]{1,0:T(8,128)} %get-tuple-element.68.refs_0_, ...), custom_call_target="tpu_custom_call" | custom-call | flops 17716740096 | bytes 25165824 | tf_op jit(solution)/shard_map/attention_backward/pallas_call | solution.py:344
  551.7 1.3 copy-done.1
  553.0 1.3 copy-done.2
  554.3 1.3 copy-done.3
  555.5 1.3 copy-done.4
  556.8 1.0 copy-done.5
  557.8 51.9 %final_reduce.1 = f32[96,3328]{1,0:T(8,128)S(1)} custom-call(bf16[8,96,768]{2,1,0:T(8,128)(2,1)S(1)} %bitcast.23, bf16[8,96,768]{2,1,0:T(8,128)(2,1)S(1)} %bitcast.24, bf16[8,96,768]{2,1,0:T(8,128)(2,1)S(1)} %bitcast.25, bf16[8,96,768]{2,1,0:T(8,128)(2,1)S(1)} %bitcast.26, bf16[8,96,256]{2,1,0:T(8,128)(2,1)S(1)} %bitcast.27), custom_call_target="tpu_custom_call" | custom-call | tf_op jit(solution)/shard_map/final_reduce/pallas_call | solution.py:1332
  609.7 1.0 slice.41
  610.7 0.7 slice.42
  611.4 0.1 slice.46
  611.5 0.1 slice.47
  611.6 0.7 copy.49
  612.3 0.7 copy.50
  612.9 0.6 copy.51
  613.5 0.8 copy.48
  614.3 0.7 slice_reduce_fusion
  615.0 1.2 pad_maximum_fusion.1
  616.3 1.2 fusion
  617.4 0.1 maximum_convert_fusion
  617.6 1.3 copy-done.10
  618.8 1.9 pad_maximum_fusion
  620.7 0.1 copy-done.9
  620.9 1.1 copy.53
  (47 shorter events, 0.2 us)
Async XLA Ops:
  7.2 2.4 copy-start.8
  7.2 3.2 copy-start.19
  7.2 3.3 copy-start.20
  7.2 3.5 copy-start.21
  7.2 3.6 copy-start.22
  7.2 3.7 copy-start.23
  7.2 3.8 copy-start.13
  7.3 3.8 copy-start.15
  7.3 205.4 %all-gather.5.cloned.1.call-start = ((), (), s32[]{:S(2)}) async-start(), calls=%async_computation.2 | async-start | bytes 7077888 | tf_op jit(solution)/shard_map/all_gather | solution.py:1401
  9.5 288.5 %all-gather.7.cloned.1.call-start = ((), (), s32[]{:S(2)}) async-start(), calls=%async_computation.3 | async-start | bytes 3538944 | tf_op jit(solution)/shard_map/all_gather | solution.py:1403
  10.4 605.9 %reduce-scatter.2.cloned.1.call-start = ((), (), s32[]{:S(2)}) async-start(), calls=%async_computation.1 | async-start | bytes 7077888 | tf_op jit(solution)/shard_map/reduce_scatter | solution.py:1414
  12.1 60.1 %copy-start.17 = (s32[1,1024,2]{1,2,0:T(2,128)S(1)}, s32[1,1024,2]{1,2,0:T(2,128)}, u32[]{:S(2)}) copy-start(s32[1,1024,2]{1,2,0:T(2,128)} %param.18) | copy-start | bytes 24580
  12.1 60.4 %copy-start.18 = (s32[1,1024]{1,0:T(1,128)S(1)}, s32[1,1024]{1,0:T(1,128)}, u32[]{:S(2)}) copy-start(s32[1,1024]{1,0:T(1,128)} %refs_12_.1) | copy-start | bytes 12292
  12.1 61.4 %copy-start.16 = (bf16[1,1024,12]{1,2,0:T(8,128)(2,1)S(1)}, bf16[1,1024,12]{1,2,0:T(8,128)(2,1)}, u32[]{:S(2)}) copy-start(bf16[1,1024,12]{1,2,0:T(8,128)(2,1)} %param.17) | copy-start | bytes 73732
  72.4 7.8 %copy-start = (s32[1,1024,2]{2,1,0:T(8,128)}, s32[1,1024,2]{2,1,0:T(8,128)S(1)}, u32[]{:S(2)}) copy-start(s32[1,1024,2]{2,1,0:T(8,128)S(1)} %copy.39) | copy-start | bytes 24580
  78.0 0.8 copy-start.6
  78.8 0.6 copy-start.7
  551.7 1.3 copy-start.1
  553.0 1.3 copy-start.2
  554.3 1.3 copy-start.3
  555.5 1.3 copy-start.4
  556.8 1.0 copy-start.5
  609.7 3.9 copy-start.14
  609.7 5.3 copy-start.11
  609.7 5.3 copy-start.12
  617.4 1.4 copy-start.10
  618.8 2.0 copy-start.9
Sparse Core Ops, SparseCore 0:
  10.9 118.6 all-gather.4
  131.7 80.2 all-gather.6
  298.1 150.3 reduce-scatter.1

commit v8 on v7

--- a/solution.py
+++ b/solution.py
@@ -782,98 +782,10 @@
     pl.semaphore_wait(barrier, len(peers))
 
 
-def small_gather_kernel(dp_count, shard_ref, full_ref, send_sem, pass_sem, recv_sem, mate_sem, own_sem):
-    outer_count, inner_count = dp_grid(dp_count)
-    me, mine = place()
-    outer, inner = me // inner_count, me % inner_count
-    rows, columns = shard_ref.shape
-    half = columns // 2
-    side = pl.multiple_of((mine % 2) * half, 128)
-    mate = mine + 1 - 2 * (mine % 2)
-    outer_peers = [lax.rem(outer + k, outer_count) for k in range(1, outer_count)]
-    inner_peers = [lax.rem(inner + k, inner_count) for k in range(1, inner_count)]
-    greet(
-        [(peer * inner_count + inner, mine) for peer in outer_peers]
-        + [(outer * inner_count + peer, mine) for peer in inner_peers]
-        + [(me, mate)]
-    )
-
-    def spot(chunk):
-        return full_ref.at[pl.ds(pl.multiple_of(chunk * rows, 8), rows), pl.ds(side, half)]
-
-    sent = []
-
-    def send(source, chunk, device, send_at, recv_at):
-        copy = pltpu.make_async_remote_copy(
-            src_ref=source,
-            dst_ref=spot(chunk),
-            send_sem=send_at,
-            recv_sem=recv_at,
-            device_id=device,
-            device_id_type=MESH,
-        )
-        copy.start()
-        sent.append(copy)
-
-    def arrived(chunk):
-        pltpu.make_async_copy(spot(chunk), spot(chunk), recv_sem.at[chunk]).wait()
-
-    own_half = shard_ref.at[:, pl.ds(side, half)]
-    for k, peer in enumerate(outer_peers):
-        send(own_half, me, (peer * inner_count + inner, mine), send_sem.at[0, k], recv_sem.at[me])
-    for k, peer in enumerate(inner_peers):
-        send(own_half, me, (outer * inner_count + peer, mine), send_sem.at[1, k], recv_sem.at[me])
-    own = pltpu.make_async_copy(
-        shard_ref, full_ref.at[pl.ds(pl.multiple_of(me * rows, 8), rows), :], own_sem
-    )
-    own.start()
-    chunks = []
-    for k, peer in enumerate(outer_peers):
-        chunk = peer * inner_count + inner
-        arrived(chunk)
-        for j, other in enumerate(inner_peers):
-            send(spot(chunk), chunk, (outer * inner_count + other, mine), send_sem.at[2 + k, j], recv_sem.at[chunk])
-        send(spot(chunk), chunk, (me, mate), pass_sem.at[len(chunks)], mate_sem.at[chunk])
-        chunks.append(chunk)
-    for other in inner_peers:
-        for peer in [outer] + outer_peers:
-            chunk = peer * inner_count + other
-            arrived(chunk)
-            send(spot(chunk), chunk, (me, mate), pass_sem.at[len(chunks)], mate_sem.at[chunk])
-            chunks.append(chunk)
-    own.wait()
-    for chunk in chunks:
-        there = full_ref.at[
-            pl.ds(pl.multiple_of(chunk * rows, 8), rows), pl.ds(pl.multiple_of(half - side, 128), half)
-        ]
-        pltpu.make_async_copy(there, there, mate_sem.at[chunk]).wait()
-    for copy in sent:
-        copy.wait_send()
-
-
-def small_gather(shard, dp_count, collective):
-    outer_count, inner_count = dp_grid(dp_count)
-    rows, columns = shard.shape
-    lanes = max(outer_count, inner_count)
-    return pl.pallas_call(
-        functools.partial(small_gather_kernel, dp_count),
-        out_shape=jax.ShapeDtypeStruct((dp_count * rows, columns), shard.dtype),
-        in_specs=[pl.BlockSpec(memory_space=pl.ANY)],
-        out_specs=pl.BlockSpec(memory_space=pl.ANY),
-        scratch_shapes=[
-            pltpu.SemaphoreType.DMA((outer_count + 1, lanes)),
-            pltpu.SemaphoreType.DMA((dp_count,)),
-            pltpu.SemaphoreType.DMA((dp_count,)),
-            pltpu.SemaphoreType.DMA((dp_count,)),
-            pltpu.SemaphoreType.DMA,
-        ],
-        compiler_params=pltpu.CompilerParams(collective_id=collective, has_side_effects=True),
-        name="small_gather",
-    )(shard)
-
-
 class LineGather:
-    def __init__(self, shard, full, dp_count, send_sem, recv_sem, own_sem):
+    def __init__(self, shard, full, dp_count, send_sem, recv_sem, own_sem, columns=None, also=None):
+        self.columns = slice(None) if columns is None else columns
+        self.also = also or (lambda chunk: None)
         self.shard, self.full, self.dp_count = shard, full, dp_count
         self.send_sem, self.recv_sem, self.own_sem = send_sem, recv_sem, own_sem
         self.outer_count, self.inner_count = dp_grid(dp_count)
@@ -893,7 +805,7 @@
 
     def spot(self, chunk):
         rows = self.shard.shape[0]
-        return self.full.at[pl.ds(pl.multiple_of(chunk * rows, 8), rows), :]
+        return self.full.at[pl.ds(pl.multiple_of(chunk * rows, 8), rows), self.columns]
 
     def copy(self, source, chunk, device, way, at):
         return pltpu.make_async_remote_copy(
@@ -942,6 +854,7 @@
                 pl.when(self.can_down)(lambda: self.down(self.spot(chunk), chunk).start())
             for copy in self.across(self.spot(chunk), chunk):
                 copy.start()
+            self.also(chunk)
 
         pl.when(low >= 0)(lambda: pass_on(low, True))
         pl.when(high < self.outer_count)(lambda: pass_on(high, False))
@@ -949,8 +862,10 @@
     def finish(self):
         self.keep().wait()
         for peer in self.inner_peers:
-            for plane in range(self.outer_count):
-                self.arrived(plane * self.inner_count + peer)
+            for k in range(self.outer_count):
+                chunk = lax.rem(self.outer + k, self.outer_count) * self.inner_count + peer
+                self.arrived(chunk)
+                self.also(chunk)
         for plane in range(self.outer_count):
             chunk = plane * self.inner_count + self.inner
             for copy in self.across(self.spot(chunk), chunk):
@@ -1054,6 +969,77 @@
         compiler_params=pltpu.CompilerParams(collective_id=collective, has_side_effects=True),
         name="expert_gather",
     )(rows, grads, shards)
+
+
+def small_gather_kernel(
+    dp_count, expert_count, shard_ref, routes_ref, full_ref, columns_ref, rows_ref,
+    send_sem, recv_sem, own_sem, pass_sem, mate_sem, all_sem,
+):
+    me, mine = place()
+    rows, columns = shard_ref.shape
+    half = columns // 2
+    side = mine % 2
+    mate = mine + 1 - 2 * side
+    own_columns = pl.ds(pl.multiple_of(side * half, 128), half)
+    mate_columns = pl.ds(pl.multiple_of((1 - side) * half, 128), half)
+
+    def there(chunk, lanes):
+        return full_ref.at[pl.ds(pl.multiple_of(chunk * rows, 8), rows), lanes]
+
+    def pass_copy(chunk):
+        return pltpu.make_async_remote_copy(
+            src_ref=there(chunk, own_columns),
+            dst_ref=there(chunk, own_columns),
+            send_sem=pass_sem.at[chunk],
+            recv_sem=mate_sem.at[chunk],
+            device_id=(me, mate),
+            device_id_type=MESH,
+        )
+
+    line = LineGather(
+        shard_ref.at[:, own_columns], full_ref, dp_count, send_sem, recv_sem, own_sem,
+        own_columns, lambda chunk: pass_copy(chunk).start(),
+    )
+    greet(line.peers() + [(me, mate)])
+    line.start()
+    other = pltpu.make_async_copy(shard_ref.at[:, mate_columns], there(me, mate_columns), all_sem)
+    other.start()
+    routing_kernel(expert_count, routes_ref, columns_ref, rows_ref)
+    for hop in range(1, line.outer_count):
+        line.relay(hop)
+    line.finish()
+    other.wait()
+    for k in range(1, dp_count):
+        chunk = lax.rem(me + k, dp_count)
+        target = there(chunk, mate_columns)
+        pltpu.make_async_copy(target, target, mate_sem.at[chunk]).wait()
+        pass_copy(chunk).wait_send()
+
+
+def small_gather(shard, routes, expert_count, dp_count, collective):
+    rows, columns = shard.shape
+    tokens = routes.shape[0]
+    anywhere, in_vmem = pl.BlockSpec(memory_space=pl.ANY), pl.BlockSpec(memory_space=pltpu.VMEM)
+    return pl.pallas_call(
+        functools.partial(small_gather_kernel, dp_count, expert_count),
+        out_shape=[
+            jax.ShapeDtypeStruct((dp_count * rows, columns), shard.dtype),
+            jax.ShapeDtypeStruct((tokens, 128), jnp.int32),
+            jax.ShapeDtypeStruct((8, tokens), jnp.int32),
+        ],
+        in_specs=[anywhere, in_vmem],
+        out_specs=[anywhere, in_vmem, in_vmem],
+        scratch_shapes=gather_semaphores(dp_count)
+        + [
+            pltpu.SemaphoreType.DMA((dp_count,)),
+            pltpu.SemaphoreType.DMA((dp_count,)),
+            pltpu.SemaphoreType.DMA,
+        ],
+        compiler_params=pltpu.CompilerParams(
+            collective_id=collective, has_side_effects=True, vmem_limit_bytes=60 * 2**20
+        ),
+        name="small_gather",
+    )(shard, routes)
 
 
 class LineReduce:
@@ -1387,20 +1373,24 @@
     inputs = tokens.reshape(rows, width)
     cot = out_grad.reshape(rows, width)
     route_rows = routes.reshape(rows, 2)
-    spots, spot_rows = routing(route_rows, expert_count)
     cosine, sine = rotary_lanes(length, width // HEADS)
     docs_row, docs_column = doc_ids.reshape(1, rows), doc_ids.reshape(rows, 1)
     resid = jnp.pad(
         resid_logits.reshape(rows, choice_count).astype(jnp.float32), ((0, 0), (0, 128 - choice_count))
     )
     if own_links:
-        packed_full = small_gather(packed, dp_count, 1)
+        packed_full, spots, spot_rows = small_gather(packed, route_rows, expert_count, dp_count, 1)
     else:
+        spots, spot_rows = routing(route_rows, expert_count)
         packed_full = lax.all_gather(packed, "dp", axis=0, tiled=True)
     gather = functools.partial(lax.all_gather, axis_name="dp", axis=0, tiled=True)
-    first_gate_up = gather(w_gate_up[0])
     if own_links:
-        second_down = gather(w_down[1])
+        first_gate_up, second_down, packed_full = lax.optimization_barrier(
+            (w_gate_up[0], w_down[1], packed_full)
+        )
+        first_gate_up, second_down = gather(first_gate_up), gather(second_down)
+    else:
+        first_gate_up = gather(w_gate_up[0])
     normed_one, queries, keys, values, attended, middle, normed_two, aux = attention_forward(
         inputs, packed_full, docs_row, docs_column, cosine, sine, route_rows, resid
     )

time: 633 us -> 626 us (0.989)
  Pallas kernels: 588 us -> 576 us
    pallas_call x2, Pallas kernels: 198 us -> 232 us  [experts(): pl.pallas_call(functools.partial(experts_kernel, mode, dp_count), grid=(s...]
    pallas_call x2 -> x1, Pallas kernels: 64.5 us -> 35.8 us  [small_gather(): pl.pallas_call(functools.partial(small_gather_kernel, dp_count, expert_co...]
    pallas_call x1, Pallas kernels: 87.2 us -> 73.4 us  [expert_gather(): pl.pallas_call(functools.partial(expert_gather_kernel, dp_count), out_sha...]
    unnamed x58 -> x40, local copies, waits for them, and re-layouts: 13.6 us -> 15.8 us
  transfers between devices with their start and end apart: 3 -> 3, of which waited for: 0 -> 0; matrix products, arithmetic and copies ran while one was open for 2% -> 1% of each run, Pallas kernels for 93% -> 87%
where the time goes in v8:
time: 626 us; the launch traced here: 621 us
  Pallas kernels  576 us (92%)
  local copies, waits for them, and re-layouts  25.9 us (4%)
  between operations  14.4 us (2%)
    pallas_call x2, Pallas kernels, experts(): pl.pallas_call(functools.partial(experts_kernel, mode, dp_count), grid=(s...  232 us
    pallas_call x1, Pallas kernels, attention_backward(): pl.pallas_call(functools.partial(attention_backward_kernel, len(sources))...  116 us
    pallas_call x1, Pallas kernels, expert_gather(): pl.pallas_call(functools.partial(expert_gather_kernel, dp_count), out_sha...  73.4 us
    pallas_call x1, Pallas kernels, final_reduce(): pl.pallas_call(functools.partial(final_reduce_kernel, len(smalls)), out_s...  51.8 us
    pallas_call x1, Pallas kernels, small_gather(): pl.pallas_call(functools.partial(small_gather_kernel, dp_count, expert_co...  35.8 us
    pallas_call x1, Pallas kernels, attention_forward(): pl.pallas_call(functools.partial(attention_forward_kernel, dp_count if li...  33.1 us
    pallas_call x1, Pallas kernels, combine(): pl.pallas_call(functools.partial(combine_kernel, expert_count, local_coun...  21.3 us
    unnamed x40, local copies, waits for them, and re-layouts  15.8 us
  transfers between devices with their start and end apart: 3, of which 0 were waited for; matrix products, arithmetic and copies ran while one was open for 1% of the time, Pallas kernels for 87%

profile of v8, /device:TPU:19, one launch (start us, length us, event | category | flops | bytes accessed | tf_op | source)
XLA Modules:
  0.0 621.4 jit_solution(12738611278139077746)
XLA Ops:
  7.2 0.0 all-gather.3.cloned.1.call-start
  7.3 1.8 copy.44
  9.1 0.8 copy.39
  9.9 0.8 copy.40
  10.7 0.8 copy.41
  11.4 0.8 copy.42
  12.2 0.8 copy.43
  13.0 2.1 slice_bitcast_fusion
  15.1 0.8 slice_bitcast_fusion.1
  15.9 1.0 concatenate.13.shard_ref
  16.9 35.8 %small_gather.1 = (bf16[768,3328]{1,0:T(8,128)(2,1)}, s32[1024,128]{1,0:T(8,128)}, s32[8,1024]{1,0:T(8,128)}) custom-call(bf16[96,3328]{1,0:T(8,128)(2,1)} %concatenate.13.shard_ref, s32[1024,2]{1,0:T(8,128)} %bitcast.27), custom_call_target="tpu_custom_call" | custom-call | tf_op jit(solution)/shard_map/small_gather/pallas_call | solution.py:1023
  52.7 0.0 all-gather.5.cloned.1.call-start
  52.8 0.7 all-gather.5.cloned.1.call-update
  53.5 0.3 reduce-scatter.2.cloned.1.call-start
  53.7 1.0 copy.46.refs_7_.refs_13_
  54.8 0.2 copy.45
  55.0 0.8 pad_convert_fusion.refs_11_
  55.8 33.1 %attention_forward.1 = (bf16[1024,768]{1,0:T(8,128)(2,1)}, bf16[1024,768]{1,0:T(8,128)(2,1)}, bf16[1024,768]{1,0:T(8,128)(2,1)}, bf16[1024,768]{1,0:T(8,128)(2,1...) custom-call(bf16[1024,768]{1,0:T(8,128)(2,1)} %bitcast.41, ...), custom_call_target="tpu_custom_call" | custom-call | flops 8053063680 | bytes 18874368 | tf_op jit(solution)/shard_map/attention_forward/pallas_call | solution.py:177
  88.9 11.8 %dispatch.1 = (bf16[2,4,256,768]{3,2,1,0:T(8,128)(2,1)}, bf16[2,4,256,768]{3,2,1,0:T(8,128)(2,1)}) custom-call(s32[8,1024]{1,0:T(8,128)} %get-tuple-element.54.spots_ref, f32[1024,128]{1,0:T(8,128)} %get-tuple-element.57.aux_ref.refs_4_, bf16[1024,768]{1,0:T(8,128)(2,1)} %get-tuple-element.58.normed_ref.refs_5_, bf16[1024,768]{1,0:T(8,128)(2,1)} %bitcast.39), custom_call_target="tpu_custom_call" | custom-call | flops 6442450944 | bytes 9437184 | tf_op jit(solution)/shard_map/dispatch/pallas_call | solution.py:462
  100.7 73.4 %expert_gather.1 = (bf16[4,256,768]{2,1,0:T(8,128)(2,1)}, bf16[4,256,768]{2,1,0:T(8,128)(2,1)}, bf16[2048,768]{1,0:T(8,128)(2,1)}) custom-call(bf16[2,4,256,768]{3,2,1,0:T(8,128)(2,1)} %get-tuple-element.59.rows_ref.refs_5_, bf16[2,4,256,768]{3,2,1,0:T(8,128)(2,1)} %get-tuple-element.60.grads_ref.refs_6_, bf16[2,256,768]{2,1,0:T(8,128)(2,1)} %shards_ref.1), custom_call_target="tpu_custom_call" | custom-call | tf_op jit(solution)/shard_map/expert_gather/pallas_call | solution.py:957
  174.1 0.0 all-gather.3.cloned.1.call-done.refs_2_.refs_3_
  174.1 114.4 %experts.2 = (bf16[2,768,2048]{2,1,0:T(8,128)(2,1)}, bf16[2048,768]{1,0:T(8,128)(2,1)}, bf16[4,2,256,768]{3,2,1,0:T(8,128)(2,1)}, bf16[4,256,768]{2,1,0:T(8,128)...) custom-call(bf16[4,256,768]{2,1,0:T(8,128)(2,1)} %get-tuple-element.61.refs_0_, ...), custom_call_target="tpu_custom_call" | custom-call | flops 28991029248 | bytes 25165824 | tf_op jit(solution)/shard_map/experts/pallas_call | solution.py:742
  288.6 0.0 all-gather.5.cloned.1.call-done.refs_4_
  288.6 117.9 %experts.3 = (bf16[2,768,2048]{2,1,0:T(8,128)(2,1)}, bf16[2048,768]{1,0:T(8,128)(2,1)}, bf16[4,2,256,768]{3,2,1,0:T(8,128)(2,1)}, bf16[4,2,256,768]{3,2,1,0:T(8,128)(2,1)}, f32[256,768]{1,0:T(8,128)}) custom-call(bf16[4,256,768]{2,1,0:T(8,128)(2,1)} %get-tuple-element.65.refs_0_, bf16[4,256,768]{2,1,0:T(8,128)(2,1)} %get-tuple-element.66.refs_1_, ...), custom_call_target="tpu_custom_call" | custom-call | flops 28991029248 | bytes 25165824 | tf_op jit(solution)/shard_map/experts/pallas_call | solution.py:742
  406.6 21.3 %combine.1 = (bf16[1024,768]{1,0:T(8,128)(2,1)}, bf16[1024,12]{1,0:T(8,128)(2,1)}, f32[1024,768]{1,0:T(8,128)}, f32[768,128]{1,0:T(8,128)}) custom-call(bf16[4,2,256,768]{3,2,1,0:T(8,128)(2,1)} %get-tuple-element.71.refs_0_, bf16[4,2,256,768]{3,2,1,0:T(8,128)(2,1)} %get-tuple-element.72.refs_1_, s32[1024,128]{1,0:T(8,128)} %get-tuple-element.73.refs_2_, ...), custom_call_target="tpu_custom_call" | custom-call | flops 9663676416 | bytes 17301504 | tf_op jit(solution)/shard_map/combine/pallas_call | solution.py:581
  427.9 116.4 %attention_backward.1 = (bf16[1024,768]{1,0:T(8,128)(2,1)}, bf16[768,768]{1,0:T(8,128)(2,1)}, bf16[768,768]{1,0:T(8,128)(2,1)}, bf16[768,768]{1,0:T(8,128)(2,1)}...) custom-call(f32[1024,768]{1,0:T(8,128)} %get-tuple-element.76.refs_0_, ...), custom_call_target="tpu_custom_call" | custom-call | flops 17716740096 | bytes 25165824 | tf_op jit(solution)/shard_map/attention_backward/pallas_call | solution.py:344
  544.3 1.3 copy-done
  545.6 1.3 copy-done.1
  546.8 1.3 copy-done.2
  548.1 1.3 copy-done.3
  549.4 1.0 copy-done.4
  550.4 51.8 %final_reduce.1 = f32[96,3328]{1,0:T(8,128)S(1)} custom-call(bf16[8,96,768]{2,1,0:T(8,128)(2,1)S(1)} %bitcast.22, bf16[8,96,768]{2,1,0:T(8,128)(2,1)S(1)} %bitcast.23, bf16[8,96,768]{2,1,0:T(8,128)(2,1)S(1)} %bitcast.24, bf16[8,96,768]{2,1,0:T(8,128)(2,1)S(1)} %bitcast.25, bf16[8,96,256]{2,1,0:T(8,128)(2,1)S(1)} %bitcast.26), custom_call_target="tpu_custom_call" | custom-call | tf_op jit(solution)/shard_map/final_reduce/pallas_call | solution.py:1318
  602.2 1.0 slice.41
  603.1 0.7 slice.42
  603.9 0.1 slice.46
  603.9 0.1 slice.47
  604.0 0.7 copy.49
  604.7 0.7 copy.50
  605.4 0.6 copy.51
  606.0 0.8 copy.48
  606.8 0.7 slice_reduce_fusion
  607.5 1.2 pad_maximum_fusion.1
  608.7 1.2 fusion
  609.9 0.1 maximum_convert_fusion
  610.0 1.3 copy-done.7
  611.3 1.9 pad_maximum_fusion
  613.2 0.1 copy-done.6
  613.3 1.1 copy.53
  (28 shorter events, 0.1 us)
Async XLA Ops:
  7.2 7.9 %copy-start.5 = (bf16[2,256,768]{2,1,0:T(8,128)(2,1)S(1)}, bf16[2,256,768]{2,1,0:T(8,128)(2,1)}, u32[]{:S(2)}) copy-start(bf16[2,256,768]{2,1,0:T(8,128)(2,1)} %shards_ref.1) | copy-start | bytes 2359300
  7.2 8.7 %copy-start.10 = (bf16[96,2304]{1,0:T(8,128)(2,1)S(1)}, bf16[96,2304]{1,0:T(8,128)(2,1)}, u32[]{:S(2)}) copy-start(bf16[96,2304]{1,0:T(8,128)(2,1)} %param.20) | copy-start | bytes 1327108
  7.2 8.6 %copy-start.12 = (bf16[96,768]{1,0:T(8,128)(2,1)S(1)}, bf16[96,768]{1,0:T(8,128)(2,1)}, u32[]{:S(2)}) copy-start(bf16[96,768]{1,0:T(8,128)(2,1)} %param.21) | copy-start | bytes 442372
  7.2 166.9 %all-gather.3.cloned.1.call-start = ((), (), s32[]{:S(2)}) async-start(), calls=%async_computation.1 | async-start | bytes 7077888 | tf_op jit(solution)/shard_map/all_gather | solution.py:1391
  15.9 37.9 %copy-start.14 = (s32[1,1024]{1,0:T(1,128)S(1)}, s32[1,1024]{1,0:T(1,128)}, u32[]{:S(2)}) copy-start(s32[1,1024]{1,0:T(1,128)} %refs_12_.1) | copy-start | bytes 12292
  16.9 37.9 %copy-start.13 = (bf16[1,1024,12]{1,2,0:T(8,128)(2,1)S(1)}, bf16[1,1024,12]{1,2,0:T(8,128)(2,1)}, u32[]{:S(2)}) copy-start(bf16[1,1024,12]{1,2,0:T(8,128)(2,1)} %param.17) | copy-start | bytes 73732
  52.7 235.9 %all-gather.5.cloned.1.call-start = ((), (), s32[]{:S(2)}) async-start(), calls=%async_computation.2 | async-start | bytes 3538944 | tf_op jit(solution)/shard_map/all_gather | solution.py:1391
  53.5 555.3 %reduce-scatter.2.cloned.1.call-start = ((), (), s32[]{:S(2)}) async-start(), calls=%async_computation.3 | async-start | bytes 7077888 | tf_op jit(solution)/shard_map/reduce_scatter | solution.py:1404
  544.3 1.3 copy-start
  545.6 1.3 copy-start.1
  546.8 1.3 copy-start.2
  548.1 1.3 copy-start.3
  549.4 1.0 copy-start.4
  602.1 3.9 copy-start.11
  602.1 5.3 copy-start.8
  602.2 5.3 copy-start.9
  609.9 1.4 copy-start.7
  611.3 2.0 copy-start.6
Sparse Core Ops, SparseCore 0:
  52.8 113.7 all-gather.2
  168.8 97.4 all-gather.4
  288.7 156.1 reduce-scatter.1

commit v9 on v8

--- a/solution.py
+++ b/solution.py
@@ -72,16 +72,15 @@
     rows = tokens_ref.shape[0]
     if linked:
         branch_ref = refs[22]
-        line = LineGather(refs[12].at[0], refs[21], linked, *refs[23:])
+        line = LineGather(refs[12].at[1], refs[21], linked, *refs[23:])
 
         @pl.when(step == 0)
         def _():
             greet(line.peers())
             line.start()
 
-        @pl.when(step == 2)
-        def _():
-            line.relay(1)
+        for hop in range(1, 3):
+            pl.when(step == hop)(functools.partial(line.relay, hop))
     else:
         branch_ref = refs[20]
 
@@ -152,7 +151,6 @@
             aux = jnp.where(lanes == at, column, aux)
         aux_ref[...] = aux
         if linked:
-            line.relay(2)
             line.relay(3)
             line.finish()
 
@@ -734,7 +732,7 @@
         out_specs += [anywhere] * 3
         scratch += gather_semaphores(dp_count) + trade_semaphores(owners) + trade_semaphores(owners)
     if mode == 2:
-        total = (hidden // 8, width)
+        total = (width // 8, 2 * hidden)
         out_shape += [both, both, jax.ShapeDtypeStruct(total, jnp.float32)]
         out_specs += [anywhere] * 2 + [pl.BlockSpec(total, lambda j: (0, 0))]
         scratch.append(pltpu.VMEM(both.shape, low))
@@ -1385,15 +1383,18 @@
         packed_full = lax.all_gather(packed, "dp", axis=0, tiled=True)
     gather = functools.partial(lax.all_gather, axis_name="dp", axis=0, tiled=True)
     if own_links:
-        first_gate_up, second_down, packed_full = lax.optimization_barrier(
-            (w_gate_up[0], w_down[1], packed_full)
-        )
-        first_gate_up, second_down = gather(first_gate_up), gather(second_down)
+        first_gate_up, packed_full = lax.optimization_barrier((w_gate_up[0], packed_full))
+        first_gate_up = gather(first_gate_up)
     else:
         first_gate_up = gather(w_gate_up[0])
-    normed_one, queries, keys, values, attended, middle, normed_two, aux = attention_forward(
-        inputs, packed_full, docs_row, docs_column, cosine, sine, route_rows, resid
+    attend = functools.partial(
+        attention_forward, inputs, packed_full, docs_row, docs_column, cosine, sine, route_rows, resid
     )
+    if own_links:
+        *forward, second_down = attend(w_down, dp_count, 5)
+    else:
+        forward = attend()
+    normed_one, queries, keys, values, attended, middle, normed_two, aux = forward
     send_rows, send_grads = dispatch(spot_rows, aux, normed_two, cot, owner_count, local_count)
     if own_links:
         rows_in, grads_in, first_down = expert_gather(send_rows, send_grads, w_down, dp_count, 2)
@@ -1401,12 +1402,14 @@
             rows_in, grads_in, first_gate_up, first_gate_up, first_down, 1, dp_count,
             [send_rows, send_grads, w_gate_up], 6,
         )
-        gu_parts = [lax.psum_scatter(grad_gu, "dp", scatter_dimension=1, tiled=True)]
-        second_gu, second_grad_down, *parts, down_part = experts(
+        down_parts = [lax.psum_scatter(grad_down, "dp", scatter_dimension=0, tiled=True)]
+        second_gu, grad_down, *parts, gu_part = experts(
             next_rows, next_grads, second_gate_up, second_gate_up, second_down, 2, dp_count,
-            [both, grad_down], 4,
+            [both, grad_gu], 4,
         )
-        down_parts = [down_part]
+        parts, down_parts[0] = lax.optimization_barrier((parts, down_parts[0]))
+        down_parts.append(lax.psum_scatter(grad_down, "dp", scatter_dimension=0, tiled=True))
+        gu_parts = [gu_part]
     else:
         exchange = functools.partial(
             lax.all_to_all, axis_name="expert", split_axis=0, concat_axis=0, tiled=True
@@ -1418,9 +1421,9 @@
                 exchange(send_rows[e]), exchange(send_grads[e]), gate_up, gate_up, gather(w_down[e])
             )
             parts.append(exchange(both))
-            gu_parts.append(lax.psum_scatter(grad_gu, "dp", scatter_dimension=1, tiled=True))
+            gu_part = lax.psum_scatter(grad_gu, "dp", scatter_dimension=1, tiled=True)
+            gu_parts.append(jnp.concatenate([gu_part[0], gu_part[1]], -1).astype(jnp.float32))
             down_parts.append(lax.psum_scatter(grad_down, "dp", scatter_dimension=0, tiled=True))
-    gu_parts = [jnp.concatenate([part[0], part[1]], -1).astype(jnp.float32) for part in gu_parts]
     down_parts = [part.astype(jnp.float32) for part in down_parts]
     output, logit_grad, grad_middle, small_grad = combine(
         parts, spots, route_rows, aux, normed_two, middle, cot, packed_full, choice_count, expert_count
@@ -1430,9 +1433,8 @@
         packed_full, docs_row, docs_column, cosine, sine, small_grad,
     )
     if own_links:
-        token_grad, *weight_grads, gu_part, down_part = backward([second_gu, second_grad_down], 7)
+        token_grad, *weight_grads, gu_part = backward([second_gu], 7)
         gu_parts.append(gu_part)
-        down_parts.append(down_part)
         packed_part = final_reduce(
             [grad.reshape(dp_count, width // dp_count, grad.shape[1]) for grad in weight_grads], 3
         )

time: 626 us -> 632 us (level)
    pallas_call x1, Pallas kernels: 33.1 us -> 68.2 us  [attention_forward(): pl.pallas_call(functools.partial(attention_forward_kernel, dp_count if li...]
    pallas_call x2, Pallas kernels: 232 us -> 214 us  [experts(): pl.pallas_call(functools.partial(experts_kernel, mode, dp_count), grid=(s...]
    pallas_call x1, Pallas kernels: 116 us -> 109 us  [attention_backward(): pl.pallas_call(functools.partial(attention_backward_kernel, len(sources))...]
    unnamed x40 -> x36, local copies, waits for them, and re-layouts: 15.8 us -> 15.8 us
  transfers between devices with their start and end apart: 3 -> 3, of which waited for: 0 -> 0; matrix products, arithmetic and copies ran while one was open for 1% -> 2% of each run, Pallas kernels for 87% -> 73%
where the time goes in v9:
time: 632 us; the launch traced here: 625 us
  Pallas kernels  578 us (91%)
  local copies, waits for them, and re-layouts  25.4 us (4%)
  between operations  14.4 us (2%)
  other arithmetic  6.51 us (1%)
    pallas_call x2, Pallas kernels, experts(): pl.pallas_call(functools.partial(experts_kernel, mode, dp_count), grid=(s...  214 us
    pallas_call x1, Pallas kernels, attention_backward(): pl.pallas_call(functools.partial(attention_backward_kernel, len(sources))...  109 us
    pallas_call x1, Pallas kernels, expert_gather(): pl.pallas_call(functools.partial(expert_gather_kernel, dp_count), out_sha...  68.6 us
    pallas_call x1, Pallas kernels, attention_forward(): pl.pallas_call(functools.partial(attention_forward_kernel, dp_count if li...  68.2 us
    pallas_call x1, Pallas kernels, final_reduce(): pl.pallas_call(functools.partial(final_reduce_kernel, len(smalls)), out_s...  49.9 us
    pallas_call x1, Pallas kernels, small_gather(): pl.pallas_call(functools.partial(small_gather_kernel, dp_count, expert_co...  35.8 us
    pallas_call x1, Pallas kernels, combine(): pl.pallas_call(functools.partial(combine_kernel, expert_count, local_coun...  21.2 us
    unnamed x36, local copies, waits for them, and re-layouts  15.8 us
  transfers between devices with their start and end apart: 3, of which 0 were waited for; matrix products, arithmetic and copies ran while one was open for 2% of the time, Pallas kernels for 73%

profile of v9, /device:TPU:19, one launch (start us, length us, event | category | flops | bytes accessed | tf_op | source)
XLA Modules:
  0.0 624.7 jit_solution(17922019294292332107)
XLA Ops:
  7.2 0.0 all-gather.2.cloned.1.call-start
  7.2 0.8 copy.42
  8.1 0.8 copy.43
  8.9 0.8 copy.39
  9.7 0.8 copy.40
  10.5 0.8 copy.41
  11.2 1.7 copy.44
  12.9 2.1 slice_bitcast_fusion
  15.0 0.0 copy-start.11
  15.0 0.0 copy-start.12
  15.1 1.0 concatenate.3.shard_ref
  16.1 35.8 %small_gather.1 = (bf16[768,3328]{1,0:T(8,128)(2,1)}, s32[1024,128]{1,0:T(8,128)}, s32[8,1024]{1,0:T(8,128)}) custom-call(bf16[96,3328]{1,0:T(8,128)(2,1)} %concatenate.3.shard_ref, s32[1024,2]{1,0:T(8,128)} %bitcast.26), custom_call_target="tpu_custom_call" | custom-call | tf_op jit(solution)/shard_map/small_gather/pallas_call | solution.py:1021
  51.8 0.0 all-gather.2.cloned.1.call-update
  51.9 0.0 reduce-scatter.3.cloned.1.call-start
  51.9 0.2 copy.45
  52.1 1.0 copy.46.refs_7_.refs_13_
  53.2 0.8 pad_convert_fusion.refs_11_
  54.0 68.2 %attention_forward.1 = (bf16[1024,768]{1,0:T(8,128)(2,1)}, bf16[1024,768]{1,0:T(8,128)(2,1)}, bf16[1024,768]{1,0:T(8,128)(2,1)}, bf16[1024,768]{1,0:T(8,128)(2,1...) custom-call(bf16[1024,768]{1,0:T(8,128)(2,1)} %bitcast.29, ...), custom_call_target="tpu_custom_call" | custom-call | flops 8053063680 | bytes 18874368 | tf_op jit(solution)/shard_map/attention_forward/pallas_call | solution.py:175
  122.2 11.8 %dispatch.1 = (bf16[2,4,256,768]{3,2,1,0:T(8,128)(2,1)}, bf16[2,4,256,768]{3,2,1,0:T(8,128)(2,1)}) custom-call(s32[8,1024]{1,0:T(8,128)} %get-tuple-element.56.spots_ref, f32[1024,128]{1,0:T(8,128)} %get-tuple-element.59.aux_ref.refs_4_, bf16[1024,768]{1,0:T(8,128)(2,1)} %get-tuple-element.60.normed_ref.refs_5_, bf16[1024,768]{1,0:T(8,128)(2,1)} %bitcast.41), custom_call_target="tpu_custom_call" | custom-call | flops 6442450944 | bytes 9437184 | tf_op jit(solution)/shard_map/dispatch/pallas_call | solution.py:460
  134.0 68.6 %expert_gather.1 = (bf16[4,256,768]{2,1,0:T(8,128)(2,1)}, bf16[4,256,768]{2,1,0:T(8,128)(2,1)}, bf16[2048,768]{1,0:T(8,128)(2,1)}) custom-call(bf16[2,4,256,768]{3,2,1,0:T(8,128)(2,1)} %get-tuple-element.61.rows_ref.refs_5_, bf16[2,4,256,768]{3,2,1,0:T(8,128)(2,1)} %get-tuple-element.62.grads_ref.refs_6_, bf16[2,256,768]{2,1,0:T(8,128)(2,1)} %shards_ref.1), custom_call_target="tpu_custom_call" | custom-call | tf_op jit(solution)/shard_map/expert_gather/pallas_call | solution.py:955
  202.7 0.0 all-gather.2.cloned.1.call-done.refs_2_.refs_3_
  202.7 84.6 %experts.2 = (bf16[2,768,2048]{2,1,0:T(8,128)(2,1)}, bf16[2048,768]{1,0:T(8,128)(2,1)}, bf16[4,2,256,768]{3,2,1,0:T(8,128)(2,1)}, bf16[4,256,768]{2,1,0:T(8,128)...) custom-call(bf16[4,256,768]{2,1,0:T(8,128)(2,1)} %get-tuple-element.63.refs_0_, ...), custom_call_target="tpu_custom_call" | custom-call | flops 28991029248 | bytes 25165824 | tf_op jit(solution)/shard_map/experts/pallas_call | solution.py:740
  287.3 0.0 reduce-scatter.3.cloned.1.call-update
  287.3 0.0 reduce-scatter.5.cloned.1.call-start
  287.4 129.5 %experts.3 = (bf16[2,768,2048]{2,1,0:T(8,128)(2,1)}, bf16[2048,768]{1,0:T(8,128)(2,1)}, bf16[4,2,256,768]{3,2,1,0:T(8,128)(2,1)}, bf16[4,2,256,768]{3,2,1,0:T(8,128)(2,1)}, f32[96,4096]{1,0:T(8,128)}) custom-call(bf16[4,256,768]{2,1,0:T(8,128)(2,1)} %get-tuple-element.67.refs_0_, bf16[4,256,768]{2,1,0:T(8,128)(2,1)} %get-tuple-element.68.refs_1_, ...), custom_call_target="tpu_custom_call" | custom-call | flops 28991029248 | bytes 25165824 | tf_op jit(solution)/shard_map/experts/pallas_call | solution.py:740
  416.8 0.0 reduce-scatter.5.cloned.1.call-update
  416.9 0.0 reduce-scatter.3.cloned.1.call-done
  416.9 21.2 %combine.1 = (bf16[1024,768]{1,0:T(8,128)(2,1)}, bf16[1024,12]{1,0:T(8,128)(2,1)}, f32[1024,768]{1,0:T(8,128)}, f32[768,128]{1,0:T(8,128)}) custom-call(bf16[4,2,256,768]{3,2,1,0:T(8,128)(2,1)} %get-tuple-element.76.refs_0_, bf16[4,2,256,768]{3,2,1,0:T(8,128)(2,1)} %get-tuple-element.77.refs_1_, s32[1024,128]{1,0:T(8,128)} %get-tuple-element.78.refs_2_, ...), custom_call_target="tpu_custom_call" | custom-call | flops 9663676416 | bytes 17301504 | tf_op jit(solution)/shard_map/combine/pallas_call | solution.py:579
  438.1 108.7 %attention_backward.1 = (bf16[1024,768]{1,0:T(8,128)(2,1)}, bf16[768,768]{1,0:T(8,128)(2,1)}, bf16[768,768]{1,0:T(8,128)(2,1)}, bf16[768,768]{1,0:T(8,128)(2,1)}...) custom-call(f32[1024,768]{1,0:T(8,128)} %get-tuple-element.81.refs_0_, ...), custom_call_target="tpu_custom_call" | custom-call | flops 17716740096 | bytes 25165824 | tf_op jit(solution)/shard_map/attention_backward/pallas_call | solution.py:342
  546.8 1.3 copy-done
  548.0 1.3 copy-done.1
  549.3 1.3 copy-done.2
  550.6 1.3 copy-done.3
  551.8 1.0 copy-done.4
  552.8 49.9 %final_reduce.1 = f32[96,3328]{1,0:T(8,128)S(1)} custom-call(bf16[8,96,768]{2,1,0:T(8,128)(2,1)S(1)} %bitcast.21, bf16[8,96,768]{2,1,0:T(8,128)(2,1)S(1)} %bitcast.22, bf16[8,96,768]{2,1,0:T(8,128)(2,1)S(1)} %bitcast.23, bf16[8,96,768]{2,1,0:T(8,128)(2,1)S(1)} %bitcast.24, bf16[8,96,256]{2,1,0:T(8,128)(2,1)S(1)} %bitcast.25), custom_call_target="tpu_custom_call" | custom-call | tf_op jit(solution)/shard_map/final_reduce/pallas_call | solution.py:1316
  602.7 0.7 slice.36
  603.4 0.6 slice.35
  604.0 0.1 slice.37
  604.1 0.7 slice.32
  604.9 1.0 slice.31
  605.8 0.8 copy.48
  606.6 1.4 copy.50
  608.0 1.5 copy.49
  609.5 0.6 copy.51
  610.2 0.7 slice_reduce_fusion
  610.9 2.2 maximum_convert_fusion
  613.1 3.4 pad_maximum_fusion
  616.5 1.1 copy.53
  (21 shorter events, 0.0 us)
Async XLA Ops:
  7.2 7.8 %copy-start.10 = (bf16[96,768]{1,0:T(8,128)(2,1)S(1)}, bf16[96,768]{1,0:T(8,128)(2,1)}, u32[]{:S(2)}) copy-start(bf16[96,768]{1,0:T(8,128)(2,1)} %param.21) | copy-start | bytes 442372
  7.2 7.8 %copy-start.7 = (bf16[96,2304]{1,0:T(8,128)(2,1)S(1)}, bf16[96,2304]{1,0:T(8,128)(2,1)}, u32[]{:S(2)}) copy-start(bf16[96,2304]{1,0:T(8,128)(2,1)} %param.20) | copy-start | bytes 1327108
  7.2 195.5 %all-gather.2.cloned.1.call-start = ((), (), s32[]{:S(2)}) async-start(), calls=%async_computation.2 | async-start | bytes 7077888 | tf_op jit(solution)/shard_map/all_gather | solution.py:1387
  15.0 36.9 %copy-start.11 = (bf16[1,1024,12]{1,2,0:T(8,128)(2,1)S(1)}, bf16[1,1024,12]{1,2,0:T(8,128)(2,1)}, u32[]{:S(2)}) copy-start(bf16[1,1024,12]{1,2,0:T(8,128)(2,1)} %param.17) | copy-start | bytes 73732
  15.0 37.1 %copy-start.12 = (s32[1,1024]{1,0:T(1,128)S(1)}, s32[1,1024]{1,0:T(1,128)}, u32[]{:S(2)}) copy-start(s32[1,1024]{1,0:T(1,128)} %refs_12_.3) | copy-start | bytes 12292
  51.9 365.0 %reduce-scatter.3.cloned.1.call-start = ((), (), s32[]{:S(2)}) async-start(), calls=%async_computation.3 | async-start | bytes 3538944 | tf_op jit(solution)/shard_map/reduce_scatter | solution.py:1405
  287.3 323.5 %reduce-scatter.5.cloned.1.call-start = ((), (), s32[]{:S(2)}) async-start(), calls=%async_computation.4 | async-start | bytes 3538944 | tf_op jit(solution)/shard_map/reduce_scatter | solution.py:1411
  546.8 1.3 copy-start
  548.0 1.3 copy-start.1
  549.3 1.3 copy-start.2
  550.6 1.3 copy-start.3
  551.8 1.0 copy-start.4
  602.7 3.1 copy-start.9
  603.4 7.4 %copy-start.8 = (bf16[256,768]{1,0:T(8,128)(2,1)S(1)}, bf16[256,768]{1,0:T(8,128)(2,1)}, u32[]{:S(2)}) copy-start(bf16[256,768]{1,0:T(8,128)(2,1)} %reduce-scatter.3.cloned.1.call-done) | copy-start | bytes 1179652
  605.8 7.3 %copy-start.6 = (f32[96,4096]{1,0:T(8,128)S(1)}, f32[96,4096]{1,0:T(8,128)}, u32[]{:S(2)}) copy-start(f32[96,4096]{1,0:T(8,128)} %get-tuple-element.96) | copy-start | bytes 4718596
  613.1 3.4 copy-start.5
Sparse Core Ops, SparseCore 0:
  52.0 132.7 all-gather.1
  287.4 110.5 reduce-scatter.2
  417.0 94.5 reduce-scatter.4

commit v10 on v9

--- a/solution.py
+++ b/solution.py
@@ -12,7 +12,7 @@
 BLOCK = 256
 CAP = 256
 GROUP = 256
-FF_BLOCK = 512
+FF_BLOCK = 256
 MESH = pl.DeviceIdType.MESH
 epsilon = 1e-06
 
@@ -72,7 +72,7 @@
     rows = tokens_ref.shape[0]
     if linked:
         branch_ref = refs[22]
-        line = LineGather(refs[12].at[1], refs[21], linked, *refs[23:])
+        line = PairGather(refs[12].at[0], refs[21], linked, refs[23:])
 
         @pl.when(step == 0)
         def _():
@@ -202,7 +202,7 @@
         + [whole((rows, width)), whole((rows, width)), whole((rows, 128))]
         + [anywhere] * linked,
         scratch_shapes=[pltpu.VMEM((rows, width), jnp.float32)]
-        + (gather_semaphores(dp_count) if linked else []),
+        + (pair_semaphores(dp_count) if linked else []),
         compiler_params=pltpu.CompilerParams(
             dimension_semantics=("arbitrary",), vmem_limit_bytes=56 * 2**20, **links
         ),
@@ -231,16 +231,14 @@
     step = pl.program_id(0)
     rows, width = tokens_ref.shape
     if count:
-        line = line_reduce(sources, totals, refs[6:])
+        line = GroupReduce(sources, totals, refs[6:])
 
         @pl.when(step == 0)
         def _():
             greet(line.peers())
-            line.each_plane(line.start)
-
-        @pl.when(step == 2)
-        def _():
-            line.each_plane(lambda o: line.pass_on(o, 0))
+            line.start()
+
+        pl.when(step == 2)(lambda: line.pass_on(0))
 
     @pl.when(step == 0)
     def _():
@@ -310,13 +308,9 @@
         small_out_ref[:, :128] = small_grad.astype(jnp.bfloat16)
         small_out_ref[:, 128:] = jnp.zeros((width, 128), jnp.bfloat16)
         if count:
-
-            def rest(o):
-                for k in range(1, 4):
-                    line.pass_on(o, k)
-                line.finish(o)
-
-            line.each_plane(rest)
+            for k in range(1, 4):
+                line.pass_on(k)
+            line.finish()
 
 
 def attention_backward(
@@ -383,7 +377,7 @@
             pltpu.VMEM((rows, 128), jnp.float32),
             pltpu.VMEM((rows, 128), jnp.float32),
         ]
-        + (reduce_scratch(sources) if linked else []),
+        + [shape for source in sources for shape in reduce_scratch(source)],
         compiler_params=pltpu.CompilerParams(
             dimension_semantics=("arbitrary",), vmem_limit_bytes=61 * 2**20, **links
         ),
@@ -614,48 +608,53 @@
     if mode == 0:
         grad_gu_ref, grad_down_ref, both_ref, turned_ref, out_ref, back_ref = refs[5:]
     if mode == 1:
-        next_rows, next_grads, shards_ref, grad_gu_ref, grad_down_ref, both_ref = refs[5:11]
-        rows_out, grads_out, full_ref, turned_ref, out_ref, back_ref = refs[11:17]
-        sems = refs[17:]
+        next_rows, next_grads, *shard_refs = refs[5:9]
+        grad_gu_ref, grad_down_ref, both_ref, rows_out, grads_out, *full_refs = refs[9:16]
+        turned_ref, out_ref, back_ref = refs[16:19]
+        sems = refs[19:]
     if mode == 2:
-        before_ref, source_ref, grad_gu_ref, grad_down_ref, first_in, second_in, total_ref = refs[5:12]
-        turned_ref, out_ref, back_ref, both_ref = refs[12:16]
-        sems = refs[16:]
+        before_ref, *sources = refs[5:8]
+        grad_gu_ref, grad_down_ref, first_in, second_in, *totals = refs[8:14]
+        turned_ref, out_ref, back_ref, both_ref = refs[14:18]
+        sems = refs[18:]
     step = pl.program_id(0)
     width = rows_ref.shape[-1]
     rows = rows_ref[...].reshape(-1, width)
     grads = grads_ref[...].reshape(-1, width)
     if mode == 1:
-        line = LineGather(shards_ref.at[1], full_ref, dp_count, *sems[:3])
+        lines = [
+            PairGather(shard.at[1], full, dp_count, sems[6 * n : 6 * n + 6])
+            for n, (shard, full) in enumerate(zip(shard_refs, full_refs))
+        ]
         trades = [
-            Trade(next_rows.at[1], rows_out, *sems[3:5]),
-            Trade(next_grads.at[1], grads_out, *sems[5:7]),
+            Trade(next_rows.at[1], rows_out, *sems[12:14]),
+            Trade(next_grads.at[1], grads_out, *sems[14:16]),
         ]
+
+        @pl.when(step == 0)
+        def _():
+            greet(lines[0].peers() + trades[0].peers())
+            for line in lines + trades:
+                line.start()
+
+        for hop in range(1, 4):
+
+            @pl.when(step == 2 * hop)
+            def _(hop=hop):
+                for line in lines:
+                    line.relay(hop)
+
+    if mode == 2:
+        trades = [Trade(before_ref, first_in, *sems[:2]), Trade(both_ref, second_in, *sems[2:4])]
+        line = GroupReduce(sources, totals, sems[4:])
 
         @pl.when(step == 0)
         def _():
             greet(line.peers() + trades[0].peers())
             line.start()
-            for trade in trades:
-                trade.start()
-
-        for hop in range(1, line.outer_count):
-            pl.when(step == hop)(functools.partial(line.relay, hop))
-
-    if mode == 2:
-        trades = [Trade(before_ref, first_in, *sems[:2]), Trade(both_ref, second_in, *sems[2:4])]
-        line = line_reduce([source_ref], [total_ref], sems[4:])
-
-        @pl.when(step == 0)
-        def _():
-            greet(line.peers() + trades[0].peers())
-            line.each_plane(line.start)
             trades[0].start()
 
-        for hop in range(3):
-            pl.when(step == hop + 1)(
-                functools.partial(line.each_plane, functools.partial(line.pass_on, k=hop))
-            )
+        pl.when(step == 4)(lambda: line.pass_on(0))
 
     @pl.when(step == 0)
     def _():
@@ -683,17 +682,13 @@
         both_ref[:, 0] = out_ref[...].astype(jnp.bfloat16).reshape(shape)
         both_ref[:, 1] = back_ref[...].astype(jnp.bfloat16).reshape(shape)
         if mode == 1:
-            line.finish()
-            for trade in trades:
-                trade.finish()
+            for part in lines + trades:
+                part.finish()
         if mode == 2:
             trades[1].start()
-
-            def rest(o):
-                line.pass_on(o, 3)
-                line.finish(o)
-
-            line.each_plane(rest)
+            for k in range(1, 4):
+                line.pass_on(k)
+            line.finish()
             for trade in trades:
                 trade.finish()
 
@@ -702,7 +697,7 @@
     owners, cap, width = rows.shape
     hidden = down.shape[0]
     count = owners * cap
-    block = FF_BLOCK if count <= 1024 else FF_BLOCK // 4
+    block = FF_BLOCK if count <= 1024 else FF_BLOCK // 2
     steps = hidden // block
     low = jnp.bfloat16
     pairs = pl.BlockSpec((owners, cap, width), lambda j: (0, 0, 0), pipeline_mode=pl.Buffered(1))
@@ -726,17 +721,21 @@
         out_shape.append(both)
         out_specs.append(pl.BlockSpec(both.shape, lambda j: (0, 0, 0, 0)))
     if mode == 1:
-        shards = extras[2]
         out_shape += [jax.ShapeDtypeStruct(rows.shape, low)] * 2
-        out_shape.append(jax.ShapeDtypeStruct((dp_count * shards.shape[1], shards.shape[2]), low))
-        out_specs += [anywhere] * 3
-        scratch += gather_semaphores(dp_count) + trade_semaphores(owners) + trade_semaphores(owners)
+        for shards in extras[2:]:
+            out_shape.append(jax.ShapeDtypeStruct((dp_count * shards.shape[1], shards.shape[2]), low))
+        out_specs += [anywhere] * 4
+        scratch += pair_semaphores(dp_count) * 2 + trade_semaphores(owners) * 2
     if mode == 2:
-        total = (width // 8, 2 * hidden)
-        out_shape += [both, both, jax.ShapeDtypeStruct(total, jnp.float32)]
-        out_specs += [anywhere] * 2 + [pl.BlockSpec(total, lambda j: (0, 0))]
+        out_shape += [both, both]
+        out_specs += [anywhere] * 2
+        for shape in ((width // 8, 2 * hidden), (hidden // 8, width)):
+            out_shape.append(jax.ShapeDtypeStruct(shape, jnp.float32))
+            out_specs.append(pl.BlockSpec(shape, lambda j: (0, 0)))
         scratch.append(pltpu.VMEM(both.shape, low))
-        scratch += trade_semaphores(owners) + trade_semaphores(owners) + reduce_scratch([extras[1]])
+        scratch += trade_semaphores(owners) * 2
+        for source in extras[1:]:
+            scratch += reduce_scratch(source)
     return pl.pallas_call(
         functools.partial(experts_kernel, mode, dp_count),
         grid=(steps,),
@@ -781,10 +780,16 @@
 
 
 class LineGather:
-    def __init__(self, shard, full, dp_count, send_sem, recv_sem, own_sem, columns=None, also=None):
+    def __init__(
+        self, shard, full, dp_count, send_sem, recv_sem, own_sem, columns=None, also=None, span=None, crossed=False
+    ):
         self.columns = slice(None) if columns is None else columns
         self.also = also or (lambda chunk: None)
-        self.shard, self.full, self.dp_count = shard, full, dp_count
+        self.stride = shard.shape[0]
+        self.first, self.count = span or (0, self.stride)
+        self.crossed = crossed
+        self.shard = shard.at[self.first : self.first + self.count, :] if span else shard
+        self.full, self.dp_count = full, dp_count
         self.send_sem, self.recv_sem, self.own_sem = send_sem, recv_sem, own_sem
         self.outer_count, self.inner_count = dp_grid(dp_count)
         self.me, self.mine = place()
@@ -792,6 +797,7 @@
         self.inner_peers = [
             lax.rem(self.inner + k, self.inner_count) for k in range(1, self.inner_count)
         ]
+        self.lanes = [self.inner] + (self.inner_peers if crossed else [])
         self.can_up, self.can_down = self.outer < self.outer_count - 1, self.outer > 0
 
     def peers(self):
@@ -802,8 +808,8 @@
         ]
 
     def spot(self, chunk):
-        rows = self.shard.shape[0]
-        return self.full.at[pl.ds(pl.multiple_of(chunk * rows, 8), rows), self.columns]
+        start = pl.multiple_of(chunk * self.stride + self.first, 8)
+        return self.full.at[pl.ds(start, self.count), self.columns]
 
     def copy(self, source, chunk, device, way, at):
         return pltpu.make_async_remote_copy(
@@ -840,40 +846,89 @@
         pl.when(self.can_down)(lambda: self.down(self.shard, self.me).start())
         self.keep().start()
 
+    def turn_in(self):
+        if self.crossed:
+            for peer in self.inner_peers:
+                chunk = self.outer * self.inner_count + peer
+                self.arrived(chunk)
+                pl.when(self.can_up)(lambda: self.up(self.spot(chunk), chunk).start())
+                pl.when(self.can_down)(lambda: self.down(self.spot(chunk), chunk).start())
+
     def relay(self, step):
         low, high = self.outer - step, self.outer + step
 
         def pass_on(source, upward):
-            chunk = source * self.inner_count + self.inner
-            self.arrived(chunk)
-            if upward:
-                pl.when(self.can_up)(lambda: self.up(self.spot(chunk), chunk).start())
-            else:
-                pl.when(self.can_down)(lambda: self.down(self.spot(chunk), chunk).start())
-            for copy in self.across(self.spot(chunk), chunk):
-                copy.start()
-            self.also(chunk)
+            for lane in self.lanes:
+                chunk = source * self.inner_count + lane
+                self.arrived(chunk)
+                if upward:
+                    pl.when(self.can_up)(lambda: self.up(self.spot(chunk), chunk).start())
+                else:
+                    pl.when(self.can_down)(lambda: self.down(self.spot(chunk), chunk).start())
+                if not self.crossed:
+                    for copy in self.across(self.spot(chunk), chunk):
+                        copy.start()
+                    self.also(chunk)
 
         pl.when(low >= 0)(lambda: pass_on(low, True))
         pl.when(high < self.outer_count)(lambda: pass_on(high, False))
 
     def finish(self):
         self.keep().wait()
-        for peer in self.inner_peers:
-            for k in range(self.outer_count):
-                chunk = lax.rem(self.outer + k, self.outer_count) * self.inner_count + peer
-                self.arrived(chunk)
-                self.also(chunk)
+        if self.crossed:
+            for copy in self.across(self.shard, self.me):
+                copy.wait_send()
+        else:
+            for peer in self.inner_peers:
+                for k in range(self.outer_count):
+                    chunk = lax.rem(self.outer + k, self.outer_count) * self.inner_count + peer
+                    self.arrived(chunk)
+                    self.also(chunk)
         for plane in range(self.outer_count):
-            chunk = plane * self.inner_count + self.inner
-            for copy in self.across(self.spot(chunk), chunk):
-                copy.wait_send()
-            pl.when(self.can_up & (self.outer >= plane))(
-                lambda chunk=chunk: self.up(self.spot(chunk), chunk).wait_send()
-            )
-            pl.when(self.can_down & (self.outer <= plane))(
-                lambda chunk=chunk: self.down(self.spot(chunk), chunk).wait_send()
-            )
+            for lane in self.lanes:
+                chunk = plane * self.inner_count + lane
+                if not self.crossed:
+                    for copy in self.across(self.spot(chunk), chunk):
+                        copy.wait_send()
+                pl.when(self.can_up & (self.outer >= plane))(
+                    lambda chunk=chunk: self.up(self.spot(chunk), chunk).wait_send()
+                )
+                pl.when(self.can_down & (self.outer <= plane))(
+                    lambda chunk=chunk: self.down(self.spot(chunk), chunk).wait_send()
+                )
+
+
+def crossed_rows(rows):
+    return max(1, (rows + 48) // 96) * 16
+
+
+class PairGather:
+    def __init__(self, shard, full, dp_count, sems):
+        rows = shard.shape[0]
+        rest = crossed_rows(rows)
+        self.parts = [
+            LineGather(shard, full, dp_count, *sems[:3], span=(rows - rest, rest), crossed=True),
+            LineGather(shard, full, dp_count, *sems[3:6], span=(0, rows - rest)),
+        ]
+        self.peers = self.parts[0].peers
+
+    def start(self):
+        for part in self.parts:
+            part.start()
+
+    def relay(self, step):
+        if step == 1:
+            self.parts[0].turn_in()
+        for part in self.parts:
+            part.relay(step)
+
+    def finish(self):
+        for part in self.parts:
+            part.finish()
+
+
+def pair_semaphores(dp_count):
+    return gather_semaphores(dp_count) + gather_semaphores(dp_count)
 
 
 def gather_semaphores(dp_count):
@@ -937,13 +992,13 @@
 
 
 def expert_gather_kernel(dp_count, rows_ref, grads_ref, shards_ref, rows_out, grads_out, full_ref, *sems):
-    line = LineGather(shards_ref.at[0], full_ref, dp_count, *sems[:3])
-    trades = [Trade(rows_ref.at[0], rows_out, *sems[3:5]), Trade(grads_ref.at[0], grads_out, *sems[5:7])]
+    line = PairGather(shards_ref.at[0], full_ref, dp_count, sems[:6])
+    trades = [Trade(rows_ref.at[0], rows_out, *sems[6:8]), Trade(grads_ref.at[0], grads_out, *sems[8:10])]
     greet(line.peers() + trades[0].peers())
     line.start()
     for trade in trades:
         trade.start()
-    for hop in range(1, line.outer_count):
+    for hop in range(1, 4):
         line.relay(hop)
     line.finish()
     for trade in trades:
@@ -961,7 +1016,7 @@
         ],
         in_specs=[anywhere] * 3,
         out_specs=[anywhere] * 3,
-        scratch_shapes=gather_semaphores(dp_count)
+        scratch_shapes=pair_semaphores(dp_count)
         + trade_semaphores(rows.shape[1])
         + trade_semaphores(rows.shape[1]),
         compiler_params=pltpu.CompilerParams(collective_id=collective, has_side_effects=True),
@@ -1041,14 +1096,15 @@
 
 
 class LineReduce:
-    def __init__(self, sources, totals, owns, ins, lows, highs, own_sem, in_send, in_recv, line_send, line_recv):
-        self.sources, self.totals = sources, totals
-        self.owns, self.ins, self.lows, self.highs = owns, ins, lows, highs
-        self.own_sem, self.in_send, self.in_recv = own_sem, in_send, in_recv
-        self.line_send, self.line_recv = line_send, line_recv
+    def __init__(self, source, total, scratch):
+        self.source, self.total = source, total
+        self.owns, self.ins, self.lows, self.highs = scratch[:4]
+        self.held, self.cross_lows, self.cross_highs, self.cross_in = scratch[4:8]
+        self.own_sem, self.in_send, self.in_recv, self.line_send, self.line_recv = scratch[8:13]
+        self.held_sem, self.cross_send, self.cross_recv, self.turn_sem = scratch[13:17]
         self.me, self.mine = place()
         self.outer, self.inner = self.me // 2, self.me % 2
-        self.every = range(len(sources))
+        self.main, self.rest = self.owns.shape[-2], self.held.shape[-2]
 
     def peers(self):
         low, high = lax.rem(self.outer + 3, 4), lax.rem(self.outer + 1, 4)
@@ -1061,114 +1117,206 @@
     def order(self, o):
         return sorted(range(4), key=lambda plane: (-abs(plane - o), plane))
 
-    def chunk(self, p, at):
-        source = self.sources[p]
-        rows = self.owns[p].shape[-2]
-        here = pl.ds(pl.multiple_of(at * rows, 16), rows)
-        return source.at[:, here, :] if len(source.shape) == 3 else source.at[here, :]
-
-    def own_copy(self, p, plane):
+    def chunk(self, at, rest):
+        start = at * (self.main + self.rest) + (self.main if rest else 0)
+        here = pl.ds(pl.multiple_of(start, 16), self.rest if rest else self.main)
+        return self.source.at[:, here, :] if len(self.source.shape) == 3 else self.source.at[here, :]
+
+    def lane(self, j):
+        return self.inner if j == 0 else 1 - self.inner
+
+    def own_copy(self, plane):
         return pltpu.make_async_copy(
-            self.chunk(p, plane * 2 + self.inner), self.owns[p].at[plane], self.own_sem.at[p, plane]
-        )
-
-    def in_copy(self, p, plane):
+            self.chunk(plane * 2 + self.inner, False), self.owns.at[plane], self.own_sem.at[plane]
+        )
+
+    def held_copy(self, j, plane):
+        return pltpu.make_async_copy(
+            self.chunk(plane * 2 + self.lane(j), True), self.held.at[j, plane], self.held_sem.at[j, plane]
+        )
+
+    def remote(self, source, target, device, send_sem, recv_sem):
         return pltpu.make_async_remote_copy(
-            src_ref=self.chunk(p, plane * 2 + 1 - self.inner),
-            dst_ref=self.ins[p].at[plane],
-            send_sem=self.in_send.at[p, plane],
-            recv_sem=self.in_recv.at[p, plane],
-            device_id=(self.me + 1 - 2 * self.inner, self.mine),
+            src_ref=source,
+            dst_ref=target,
+            send_sem=send_sem,
+            recv_sem=recv_sem,
+            device_id=(device, self.mine),
             device_id_type=MESH,
         )
 
-    def line_copy(self, p, plane, upward, device_plane):
-        target = self.lows[p].at[plane - 1] if upward else self.highs[p].at[plane]
-        return pltpu.make_async_remote_copy(
-            src_ref=self.ins[p].at[plane],
-            dst_ref=target,
-            send_sem=self.line_send.at[p, 0 if upward else 1, plane],
-            recv_sem=self.line_recv.at[p, 0 if upward else 1, plane],
-            device_id=(device_plane * 2 + self.inner, self.mine),
-            device_id_type=MESH,
+    def in_copy(self, plane):
+        return self.remote(
+            self.chunk(plane * 2 + 1 - self.inner, False),
+            self.ins.at[plane],
+            self.me + 1 - 2 * self.inner,
+            self.in_send.at[plane],
+            self.in_recv.at[plane],
+        )
+
+    def line_copy(self, plane, upward, device_plane):
+        way = 0 if upward else 1
+        return self.remote(
+            self.ins.at[plane],
+            self.lows.at[plane - 1] if upward else self.highs.at[plane],
+            device_plane * 2 + self.inner,
+            self.line_send.at[way, plane],
+            self.line_recv.at[way, plane],
+        )
+
+    def cross_copy(self, j, plane, upward, device_plane):
+        way = 0 if upward else 1
+        return self.remote(
+            self.held.at[j, plane],
+            self.cross_lows.at[j, plane - 1] if upward else self.cross_highs.at[j, plane],
+            device_plane * 2 + self.inner,
+            self.cross_send.at[j, way, plane],
+            self.cross_recv.at[j, way, plane],
+        )
+
+    def turn_copy(self, o):
+        return self.remote(
+            self.held.at[1, o],
+            self.cross_in,
+            self.me + 1 - 2 * self.inner,
+            self.turn_sem.at[0],
+            self.turn_sem.at[1],
         )
 
     def start(self, o):
         for plane in self.order(o):
-            for p in self.every:
-                self.in_copy(p, plane).start()
+            for j in range(2):
+                self.held_copy(j, plane).start()
         for plane in self.order(o):
-            for p in self.every:
-                self.own_copy(p, plane).start()
-
-    def line_start(self, o, p, plane):
-        return self.line_copy(p, plane, plane > o, o + 1 if plane > o else o - 1)
+            self.in_copy(plane).start()
+        for plane in self.order(o):
+            self.own_copy(plane).start()
+
+    def next_plane(self, o, plane):
+        return (plane > o, o + 1 if plane > o else o - 1)
+
+    def incoming(self, o, plane):
+        ways = []
+        if o > 0 and plane >= o:
+            ways.append(True)
+        if o < 3 and plane <= o:
+            ways.append(False)
+        return ways
+
+    def add(self, target, terms, total_row=None):
+        sides = target.shape[0] if len(target.shape) == 3 else 0
+
+        def body(at):
+            here = pl.ds(pl.multiple_of(at, 16), 16)
+            for side in range(max(1, sides)):
+                spot = (side, here) if sides else (here,)
+                total = target[spot].astype(jnp.float32)
+                for term in terms:
+                    total = total + term[spot].astype(jnp.float32)
+                if total_row is None:
+                    target[spot] = total.astype(target.dtype)
+                else:
+                    there = pl.ds(pl.multiple_of(total_row + at, 16), 16)
+                    size = total.shape[-1]
+                    self.total[there, side * size : (side + 1) * size] = total
+
+        by_rows(target.shape[-2], body)
 
     def pass_on(self, o, k):
         plane = self.order(o)[k]
-        for p in self.every:
-            self.own_copy(p, plane).wait()
-            self.in_copy(p, plane).wait_recv()
-            terms = [self.owns[p].at[plane]]
-            if o > 0 and plane >= o:
-                self.line_copy(p, plane, True, o).wait_recv()
-                terms.append(self.lows[p].at[plane - 1])
-            if o < 3 and plane <= o:
-                self.line_copy(p, plane, False, o).wait_recv()
-                terms.append(self.highs[p].at[plane])
-            held = self.ins[p].at[plane]
-            last = plane == o
-            sides = held.shape[0] if len(held.shape) == 3 else 0
-
-            def body(at, p=p, terms=terms, held=held, last=last, sides=sides):
-                here = pl.ds(pl.multiple_of(at, 16), 16)
-                for side in range(max(1, sides)):
-                    spot = (side, here) if sides else (here,)
-                    total = held[spot].astype(jnp.float32)
-                    for term in terms:
-                        total = total + term[spot].astype(jnp.float32)
-                    if last:
-                        size = total.shape[-1]
-                        self.totals[p][here, side * size : (side + 1) * size] = total
-                    else:
-                        held[spot] = total.astype(held.dtype)
-
-            by_rows(held.shape[-2], body)
-            if not last:
-                self.line_start(o, p, plane).start()
+        ways = self.incoming(o, plane)
+        for j in (1, 0):
+            self.held_copy(j, plane).wait()
+            terms = []
+            for upward in ways:
+                self.cross_copy(j, plane, upward, o).wait_recv()
+                terms.append(
+                    self.cross_lows.at[j, plane - 1] if upward else self.cross_highs.at[j, plane]
+                )
+            if plane != o:
+                if terms:
+                    self.add(self.held.at[j, plane], terms)
+                self.cross_copy(j, plane, *self.next_plane(o, plane)).start()
+            elif j == 1:
+                self.add(self.held.at[1, o], terms)
+                self.turn_copy(o).start()
+            else:
+                last_terms = terms + [self.cross_in]
+        self.own_copy(plane).wait()
+        self.in_copy(plane).wait_recv()
+        terms = [self.owns.at[plane]]
+        for upward in ways:
+            self.line_copy(plane, upward, o).wait_recv()
+            terms.append(self.lows.at[plane - 1] if upward else self.highs.at[plane])
+        if plane != o:
+            self.add(self.ins.at[plane], terms)
+            self.line_copy(plane, *self.next_plane(o, plane)).start()
+        else:
+            self.add(self.ins.at[plane], terms, 0)
+            self.turn_copy(o).wait_recv()
+            self.add(self.held.at[0, o], last_terms, self.main)
 
     def finish(self, o):
+        self.turn_copy(o).wait_send()
         for plane in range(4):
-            for p in self.every:
-                self.in_copy(p, plane).wait_send()
-                if plane != o:
-                    self.line_start(o, p, plane).wait_send()
+            self.in_copy(plane).wait_send()
+            if plane != o:
+                self.line_copy(plane, *self.next_plane(o, plane)).wait_send()
+                for j in range(2):
+                    self.cross_copy(j, plane, *self.next_plane(o, plane)).wait_send()
+
+
+def reduce_scratch(source):
+    rows = source.shape[-2] // 8
+    rest = crossed_rows(rows)
+    lead, columns = source.shape[:-2], source.shape[-1]
+    low = jnp.bfloat16
+
+    def buffer(front, count):
+        return pltpu.VMEM(front + lead + (count, columns), low)
+
+    return [
+        buffer((4,), rows - rest),
+        buffer((4,), rows - rest),
+        buffer((3,), rows - rest),
+        buffer((3,), rows - rest),
+        buffer((2, 4), rest),
+        buffer((2, 3), rest),
+        buffer((2, 3), rest),
+        buffer((), rest),
+        pltpu.SemaphoreType.DMA((4,)),
+        pltpu.SemaphoreType.DMA((4,)),
+        pltpu.SemaphoreType.DMA((4,)),
+        pltpu.SemaphoreType.DMA((2, 4)),
+        pltpu.SemaphoreType.DMA((2, 4)),
+        pltpu.SemaphoreType.DMA((2, 4)),
+        pltpu.SemaphoreType.DMA((2, 2, 4)),
+        pltpu.SemaphoreType.DMA((2, 2, 4)),
+        pltpu.SemaphoreType.DMA((2,)),
+    ]
+
+
+class GroupReduce:
+    def __init__(self, sources, totals, scratch):
+        self.lines = [
+            LineReduce(source, total, scratch[17 * n : 17 * n + 17])
+            for n, (source, total) in enumerate(zip(sources, totals))
+        ]
+        self.outer = self.lines[0].outer
+        self.peers = self.lines[0].peers
 
     def each_plane(self, body):
         for o in range(4):
             pl.when(self.outer == o)(functools.partial(body, o))
 
-
-def reduce_scratch(sources):
-    shapes = []
-    for planes in (4, 4, 3, 3):
-        for source in sources:
-            rows = source.shape[-2] // 8
-            shapes.append(pltpu.VMEM((planes,) + source.shape[:-2] + (rows, source.shape[-1]), jnp.bfloat16))
-    count = len(sources)
-    return shapes + [
-        pltpu.SemaphoreType.DMA((count, 4)),
-        pltpu.SemaphoreType.DMA((count, 4)),
-        pltpu.SemaphoreType.DMA((count, 4)),
-        pltpu.SemaphoreType.DMA((count, 2, 4)),
-        pltpu.SemaphoreType.DMA((count, 2, 4)),
-    ]
-
-
-def line_reduce(sources, totals, scratch):
-    count = len(sources)
-    buffers = [scratch[n * count : (n + 1) * count] for n in range(4)]
-    return LineReduce(sources, totals, *buffers, *scratch[4 * count :])
+    def start(self):
+        self.each_plane(lambda o: [line.start(o) and None for line in self.lines] and None)
+
+    def pass_on(self, k):
+        self.each_plane(lambda o: [line.pass_on(o, k) for line in self.lines] and None)
+
+    def finish(self):
+        self.each_plane(lambda o: [line.finish(o) for line in self.lines] and None)
 
 
 def final_reduce_kernel(small_count, *refs):
@@ -1382,41 +1530,33 @@
         spots, spot_rows = routing(route_rows, expert_count)
         packed_full = lax.all_gather(packed, "dp", axis=0, tiled=True)
     gather = functools.partial(lax.all_gather, axis_name="dp", axis=0, tiled=True)
-    if own_links:
-        first_gate_up, packed_full = lax.optimization_barrier((w_gate_up[0], packed_full))
-        first_gate_up = gather(first_gate_up)
-    else:
-        first_gate_up = gather(w_gate_up[0])
     attend = functools.partial(
         attention_forward, inputs, packed_full, docs_row, docs_column, cosine, sine, route_rows, resid
     )
     if own_links:
-        *forward, second_down = attend(w_down, dp_count, 5)
+        *forward, first_gate_up = attend(w_gate_up, dp_count, 5)
     else:
         forward = attend()
     normed_one, queries, keys, values, attended, middle, normed_two, aux = forward
     send_rows, send_grads = dispatch(spot_rows, aux, normed_two, cot, owner_count, local_count)
     if own_links:
         rows_in, grads_in, first_down = expert_gather(send_rows, send_grads, w_down, dp_count, 2)
-        grad_gu, grad_down, both, next_rows, next_grads, second_gate_up = experts(
+        grad_gu, grad_down, both, next_rows, next_grads, second_gate_up, second_down = experts(
             rows_in, grads_in, first_gate_up, first_gate_up, first_down, 1, dp_count,
-            [send_rows, send_grads, w_gate_up], 6,
-        )
-        down_parts = [lax.psum_scatter(grad_down, "dp", scatter_dimension=0, tiled=True)]
-        second_gu, grad_down, *parts, gu_part = experts(
+            [send_rows, send_grads, w_gate_up, w_down], 6,
+        )
+        second_gu, second_grad_down, *parts, gu_part, down_part = experts(
             next_rows, next_grads, second_gate_up, second_gate_up, second_down, 2, dp_count,
-            [both, grad_gu], 4,
-        )
-        parts, down_parts[0] = lax.optimization_barrier((parts, down_parts[0]))
-        down_parts.append(lax.psum_scatter(grad_down, "dp", scatter_dimension=0, tiled=True))
-        gu_parts = [gu_part]
+            [both, grad_gu, grad_down], 4,
+        )
+        gu_parts, down_parts = [gu_part], [down_part]
     else:
         exchange = functools.partial(
             lax.all_to_all, axis_name="expert", split_axis=0, concat_axis=0, tiled=True
         )
         parts, gu_parts, down_parts = [], [], []
         for e in range(local_count):
-            gate_up = first_gate_up if e == 0 else gather(w_gate_up[e])
+            gate_up = gather(w_gate_up[e])
             grad_gu, grad_down, both = experts(
                 exchange(send_rows[e]), exchange(send_grads[e]), gate_up, gate_up, gather(w_down[e])
             )
@@ -1433,8 +1573,9 @@
         packed_full, docs_row, docs_column, cosine, sine, small_grad,
     )
     if own_links:
-        token_grad, *weight_grads, gu_part = backward([second_gu], 7)
+        token_grad, *weight_grads, gu_part, down_part = backward([second_gu, second_grad_down], 7)
         gu_parts.append(gu_part)
+        down_parts.append(down_part)
         packed_part = final_reduce(
             [grad.reshape(dp_count, width // dp_count, grad.shape[1]) for grad in weight_grads], 3
         )

time: 632 us -> 696 us (1.10)
  Pallas kernels: 578 us -> 663 us
  between operations: 14.4 us -> 1 us
    pallas_call x1, Pallas kernels: 109 us -> 160 us  [attention_backward(): pl.pallas_call(functools.partial(attention_backward_kernel, len(sources))...]
    pallas_call x2, Pallas kernels: 214 us -> 257 us  [experts(): pl.pallas_call(functools.partial(experts_kernel, mode, dp_count), grid=(s...]
    pallas_call x1, Pallas kernels: 68.6 us -> 49 us  [expert_gather(): pl.pallas_call(functools.partial(expert_gather_kernel, dp_count), out_sha...]
    pallas_call x1, Pallas kernels: 68.2 us -> 75.8 us  [attention_forward(): pl.pallas_call(functools.partial(attention_forward_kernel, dp_count if li...]
    unnamed x36 -> x38, local copies, waits for them, and re-layouts: 15.8 us -> 15.7 us
  transfers between devices with their start and end apart: 3 -> 0, of which waited for: 0 -> 0; matrix products, arithmetic and copies ran while one was open for 2% -> 0% of each run, Pallas kernels for 73% -> 0%
where the time goes in v10:
time: 696 us; the launch traced here: 691 us
  Pallas kernels  663 us (95%)
  local copies, waits for them, and re-layouts  22.7 us (3%)
    pallas_call x2, Pallas kernels, experts(): pl.pallas_call(functools.partial(experts_kernel, mode, dp_count), grid=(s...  257 us
    pallas_call x1, Pallas kernels, attention_backward(): pl.pallas_call(functools.partial(attention_backward_kernel, len(sources))...  160 us
    pallas_call x1, Pallas kernels, attention_forward(): pl.pallas_call(functools.partial(attention_forward_kernel, dp_count if li...  75.8 us
    pallas_call x1, Pallas kernels, final_reduce(): pl.pallas_call(functools.partial(final_reduce_kernel, len(smalls)), out_s...  52.1 us
    pallas_call x1, Pallas kernels, expert_gather(): pl.pallas_call(functools.partial(expert_gather_kernel, dp_count), out_sha...  49 us
    pallas_call x1, Pallas kernels, small_gather(): pl.pallas_call(functools.partial(small_gather_kernel, dp_count, expert_co...  35.7 us
    pallas_call x1, Pallas kernels, combine(): pl.pallas_call(functools.partial(combine_kernel, expert_count, local_coun...  21.2 us
    unnamed x38, local copies, waits for them, and re-layouts  15.7 us

profile of v10, /device:TPU:19, one launch (start us, length us, event | category | flops | bytes accessed | tf_op | source)
XLA Modules:
  0.0 690.7 jit_solution(17925951994517527196)
XLA Ops:
  0.6 0.0 copy-start.12
  0.7 0.0 copy-start.10
  0.7 0.8 copy.42
  1.5 0.8 copy.43
  2.3 0.8 copy.39
  3.1 0.8 copy.40
  3.9 0.8 copy.41
  4.7 0.9 copy.45
  5.6 0.8 pad_convert_fusion.refs_11_
  6.5 0.0 copy-done.10
  6.5 1.8 concatenate.3.shard_ref
  8.3 0.0 copy-done.12
  8.3 1.0 copy.46.refs_7_.refs_13_
  9.3 0.0 copy-done.13
  9.3 1.0 copy.44
  10.4 35.7 %small_gather.1 = (bf16[768,3328]{1,0:T(8,128)(2,1)}, s32[1024,128]{1,0:T(8,128)}, s32[8,1024]{1,0:T(8,128)}) custom-call(bf16[96,3328]{1,0:T(8,128)(2,1)} %concatenate.3.shard_ref, s32[1024,2]{1,0:T(8,128)} %bitcast.24), custom_call_target="tpu_custom_call" | custom-call | tf_op jit(solution)/shard_map/small_gather/pallas_call | solution.py:1076
  46.1 75.8 %attention_forward.1 = (bf16[1024,768]{1,0:T(8,128)(2,1)}, bf16[1024,768]{1,0:T(8,128)(2,1)}, bf16[1024,768]{1,0:T(8,128)(2,1)}, bf16[1024,768]{1,0:T(8,128)(2,1...) custom-call(bf16[1024,768]{1,0:T(8,128)(2,1)} %bitcast.27, ...), custom_call_target="tpu_custom_call" | custom-call | flops 8053063680 | bytes 18874368 | tf_op jit(solution)/shard_map/attention_forward/pallas_call | solution.py:175
  121.9 12.0 %dispatch.1 = (bf16[2,4,256,768]{3,2,1,0:T(8,128)(2,1)}, bf16[2,4,256,768]{3,2,1,0:T(8,128)(2,1)}) custom-call(s32[8,1024]{1,0:T(8,128)} %get-tuple-element.54.spots_ref, f32[1024,128]{1,0:T(8,128)} %get-tuple-element.56.aux_ref.refs_4_, bf16[1024,768]{1,0:T(8,128)(2,1)} %get-tuple-element.57.normed_ref.refs_5_, bf16[1024,768]{1,0:T(8,128)(2,1)} %bitcast.39), custom_call_target="tpu_custom_call" | custom-call | flops 6442450944 | bytes 9437184 | tf_op jit(solution)/shard_map/dispatch/pallas_call | solution.py:454
  133.9 49.0 %expert_gather.1 = (bf16[4,256,768]{2,1,0:T(8,128)(2,1)}, bf16[4,256,768]{2,1,0:T(8,128)(2,1)}, bf16[2048,768]{1,0:T(8,128)(2,1)}) custom-call(bf16[2,4,256,768]{3,2,1,0:T(8,128)(2,1)} %get-tuple-element.58.rows_ref.refs_5_, bf16[2,4,256,768]{3,2,1,0:T(8,128)(2,1)} %get-tuple-element.59.grads_ref.refs_6_, bf16[2,256,768]{2,1,0:T(8,128)(2,1)} %refs_8_.2), custom_call_target="tpu_custom_call" | custom-call | tf_op jit(solution)/shard_map/expert_gather/pallas_call | solution.py:1010
  182.9 104.2 %experts.2 = (bf16[2,768,2048]{2,1,0:T(8,128)(2,1)}, bf16[2048,768]{1,0:T(8,128)(2,1)}, bf16[4,2,256,768]{3,2,1,0:T(8,128)(2,1)}, bf16[4,256,768]{2,1,0:T(8,128)...) custom-call(bf16[4,256,768]{2,1,0:T(8,128)(2,1)} %get-tuple-element.60.refs_0_, ...), custom_call_target="tpu_custom_call" | custom-call | flops 28991029248 | bytes 25165824 | tf_op jit(solution)/shard_map/experts/pallas_call | solution.py:739
  287.1 153.1 %experts.3 = (bf16[2,768,2048]{2,1,0:T(8,128)(2,1)}, bf16[2048,768]{1,0:T(8,128)(2,1)}, bf16[4,2,256,768]{3,2,1,0:T(8,128)(2,1)}, bf16[4,2,256,768]{3,2,1,0:T(8,...) custom-call(bf16[4,256,768]{2,1,0:T(8,128)(2,1)} %get-tuple-element.64.refs_0_, ...), custom_call_target="tpu_custom_call" | custom-call | flops 28991029248 | bytes 25165824 | tf_op jit(solution)/shard_map/experts/pallas_call | solution.py:739
  440.2 21.2 %combine.1 = (bf16[1024,768]{1,0:T(8,128)(2,1)}, bf16[1024,12]{1,0:T(8,128)(2,1)}, f32[1024,768]{1,0:T(8,128)}, f32[768,128]{1,0:T(8,128)}) custom-call(bf16[4,2,256,768]{3,2,1,0:T(8,128)(2,1)} %get-tuple-element.71.refs_0_, bf16[4,2,256,768]{3,2,1,0:T(8,128)(2,1)} %get-tuple-element.72.refs_1_, s32[1024,128]{1,0:T(8,128)} %get-tuple-element.73.refs_2_, ...), custom_call_target="tpu_custom_call" | custom-call | flops 9663676416 | bytes 17301504 | tf_op jit(solution)/shard_map/combine/pallas_call | solution.py:573
  461.4 159.9 %attention_backward.1 = (bf16[1024,768]{1,0:T(8,128)(2,1)}, bf16[768,768]{1,0:T(8,128)(2,1)}, bf16[768,768]{1,0:T(8,128)(2,1)}, bf16[768,768]{1,0:T(8,128)(2,1)}...) custom-call(f32[1024,768]{1,0:T(8,128)} %get-tuple-element.76.refs_0_, ...), custom_call_target="tpu_custom_call" | custom-call | flops 17716740096 | bytes 25165824 | tf_op jit(solution)/shard_map/attention_backward/pallas_call | solution.py:336
  621.3 0.0 copy-start
  621.3 1.3 copy-done
  622.6 1.3 copy-done.1
  623.9 1.3 copy-done.2
  625.1 1.3 copy-done.3
  626.4 1.0 copy-done.4
  627.4 52.1 %final_reduce.1 = f32[96,3328]{1,0:T(8,128)S(1)} custom-call(bf16[8,96,768]{2,1,0:T(8,128)(2,1)S(1)} %bitcast.19, bf16[8,96,768]{2,1,0:T(8,128)(2,1)S(1)} %bitcast.20, bf16[8,96,768]{2,1,0:T(8,128)(2,1)S(1)} %bitcast.21, bf16[8,96,768]{2,1,0:T(8,128)(2,1)S(1)} %bitcast.22, bf16[8,96,256]{2,1,0:T(8,128)(2,1)S(1)} %bitcast.23), custom_call_target="tpu_custom_call" | custom-call | tf_op jit(solution)/shard_map/final_reduce/pallas_call | solution.py:1464
  679.6 0.7 slice_reduce_fusion
  680.3 0.0 copy-done.11
  680.3 0.8 copy.48
  681.0 0.1 slice.32
  681.1 0.7 copy.50
  681.8 0.7 copy.49
  682.4 0.1 slice.33
  682.5 0.6 copy.51
  683.2 0.7 slice.28
  683.9 1.0 slice.27
  684.9 0.0 copy-done.8
  684.9 0.0 copy-done.9
  684.9 1.2 pad_maximum_fusion.1
  686.1 0.7 copy-done.6
  686.8 0.5 copy-done.7
  687.3 1.9 pad_maximum_fusion
  689.2 0.1 copy-done.5
  689.3 1.1 copy.53
  (13 shorter events, 0.0 us)
Async XLA Ops:
  0.6 7.7 %copy-start.12 = (s32[1,1024]{1,0:T(1,128)S(1)}, s32[1,1024]{1,0:T(1,128)}, u32[]{:S(2)}) copy-start(s32[1,1024]{1,0:T(1,128)} %refs_12_.3) | copy-start | bytes 12292
  0.7 5.8 copy-start.10
  2.3 7.1 %copy-start.13 = (s32[1,1024,2]{1,2,0:T(2,128)S(1)}, s32[1,1024,2]{1,2,0:T(2,128)}, u32[]{:S(2)}) copy-start(s32[1,1024,2]{1,2,0:T(2,128)} %param.18) | copy-start | bytes 24580
  621.3 1.3 copy-start
  622.6 1.3 copy-start.1
  623.9 1.3 copy-start.2
  625.1 1.3 copy-start.3
  626.4 1.0 copy-start.4
  627.4 52.8 %copy-start.11 = (bf16[1024,12]{1,0:T(8,128)(2,1)S(1)}, bf16[1024,12]{1,0:T(8,128)(2,1)}, u32[]{:S(2)}) copy-start(bf16[1024,12]{1,0:T(8,128)(2,1)} %get-tuple-element.86) | copy-start | bytes 73732
  680.3 4.6 copy-start.8
  680.3 4.6 copy-start.9
  684.9 2.0 copy-start.6
  684.9 2.4 copy-start.7
  687.3 2.0 copy-start.5

commit v11 on v8

--- a/solution.py
+++ b/solution.py
@@ -233,16 +233,15 @@
     step = pl.program_id(0)
     rows, width = tokens_ref.shape
     if count:
-        line = line_reduce(sources, totals, refs[6:])
+        line = line_reduce(sources[0], totals[0], refs[6:], 2)
 
         @pl.when(step == 0)
         def _():
             greet(line.peers())
             line.each_plane(line.start)
 
-        @pl.when(step == 2)
-        def _():
-            line.each_plane(lambda o: line.pass_on(o, 0))
+        pl.when(step == 1)(lambda: line.turns([0], []))
+        pl.when(step == 2)(lambda: line.turns([1], [0]))
 
     @pl.when(step == 0)
     def _():
@@ -312,13 +311,8 @@
         small_out_ref[:, :128] = small_grad.astype(jnp.bfloat16)
         small_out_ref[:, 128:] = jnp.zeros((width, 128), jnp.bfloat16)
         if count:
-
-            def rest(o):
-                for k in range(1, 4):
-                    line.pass_on(o, k)
-                line.finish(o)
-
-            line.each_plane(rest)
+            line.turns([2, 3], [1, 2, 3])
+            line.each_plane(line.finish)
 
 
 def attention_backward(
@@ -385,7 +379,7 @@
             pltpu.VMEM((rows, 128), jnp.float32),
             pltpu.VMEM((rows, 128), jnp.float32),
         ]
-        + (reduce_scratch(sources) if linked else []),
+        + (reduce_scratch(sources[0], 2) if linked else []),
         compiler_params=pltpu.CompilerParams(
             dimension_semantics=("arbitrary",), vmem_limit_bytes=61 * 2**20, **links
         ),
@@ -628,25 +622,36 @@
     rows = rows_ref[...].reshape(-1, width)
     grads = grads_ref[...].reshape(-1, width)
     if mode == 1:
-        line = LineGather(shards_ref.at[1], full_ref, dp_count, *sems[:3])
+        half = full_ref.shape[1] // 2
+        lines = []
+        for n in range(2):
+            columns = slice(n * half, n * half + half)
+            lines.append(
+                LineGather(
+                    shards_ref.at[1, :, columns], full_ref, dp_count, *sems[3 * n : 3 * n + 3], columns
+                )
+            )
         trades = [
-            Trade(next_rows.at[1], rows_out, *sems[3:5]),
-            Trade(next_grads.at[1], grads_out, *sems[5:7]),
+            Trade(next_rows.at[1], rows_out, *sems[6:8]),
+            Trade(next_grads.at[1], grads_out, *sems[8:10]),
         ]
 
         @pl.when(step == 0)
         def _():
-            greet(line.peers() + trades[0].peers())
-            line.start()
-            for trade in trades:
-                trade.start()
-
-        for hop in range(1, line.outer_count):
-            pl.when(step == hop)(functools.partial(line.relay, hop))
+            greet(lines[0].peers() + trades[0].peers())
+            for part in lines + trades:
+                part.start()
+
+        for hop in range(1, 4):
+
+            @pl.when(step == hop)
+            def _(hop=hop):
+                for part in lines:
+                    part.relay(hop)
 
     if mode == 2:
         trades = [Trade(before_ref, first_in, *sems[:2]), Trade(both_ref, second_in, *sems[2:4])]
-        line = line_reduce([source_ref], [total_ref], sems[4:])
+        line = line_reduce(source_ref, total_ref, sems[4:], 2)
 
         @pl.when(step == 0)
         def _():
@@ -654,10 +659,7 @@
             line.each_plane(line.start)
             trades[0].start()
 
-        for hop in range(3):
-            pl.when(step == hop + 1)(
-                functools.partial(line.each_plane, functools.partial(line.pass_on, k=hop))
-            )
+        pl.when(step == 2)(lambda: line.turns([0], []))
 
     @pl.when(step == 0)
     def _():
@@ -685,17 +687,12 @@
         both_ref[:, 0] = out_ref[...].astype(jnp.bfloat16).reshape(shape)
         both_ref[:, 1] = back_ref[...].astype(jnp.bfloat16).reshape(shape)
         if mode == 1:
-            line.finish()
-            for trade in trades:
-                trade.finish()
+            for part in lines + trades:
+                part.finish()
         if mode == 2:
             trades[1].start()
-
-            def rest(o):
-                line.pass_on(o, 3)
-                line.finish(o)
-
-            line.each_plane(rest)
+            line.turns([1, 2, 3], [0, 1, 2, 3])
+            line.each_plane(line.finish)
             for trade in trades:
                 trade.finish()
 
@@ -732,13 +729,13 @@
         out_shape += [jax.ShapeDtypeStruct(rows.shape, low)] * 2
         out_shape.append(jax.ShapeDtypeStruct((dp_count * shards.shape[1], shards.shape[2]), low))
         out_specs += [anywhere] * 3
-        scratch += gather_semaphores(dp_count) + trade_semaphores(owners) + trade_semaphores(owners)
+        scratch += gather_semaphores(dp_count) * 2 + trade_semaphores(owners) + trade_semaphores(owners)
     if mode == 2:
-        total = (hidden // 8, width)
+        total = (width // 8, 2 * hidden)
         out_shape += [both, both, jax.ShapeDtypeStruct(total, jnp.float32)]
         out_specs += [anywhere] * 2 + [pl.BlockSpec(total, lambda j: (0, 0))]
         scratch.append(pltpu.VMEM(both.shape, low))
-        scratch += trade_semaphores(owners) + trade_semaphores(owners) + reduce_scratch([extras[1]])
+        scratch += trade_semaphores(owners) + trade_semaphores(owners) + reduce_scratch(extras[1], 2)
     return pl.pallas_call(
         functools.partial(experts_kernel, mode, dp_count),
         grid=(steps,),
@@ -1150,14 +1147,32 @@
         for o in range(4):
             pl.when(self.outer == o)(functools.partial(body, o))
 
-
-def reduce_scratch(sources):
+    def turns(self, ends, middles):
+        def body(o):
+            for k in ends if o in (0, 3) else middles:
+                self.pass_on(o, k)
+
+        self.each_plane(body)
+
+
+def pieces_of(source, cut):
+    columns = source.shape[-1]
+    size = columns // cut
+    fronts = [(side,) for side in range(source.shape[0])] if len(source.shape) == 3 else [()]
+    return [
+        (front, slice(c * size, c * size + size), slice(n * columns + c * size, n * columns + c * size + size))
+        for n, front in enumerate(fronts)
+        for c in range(cut)
+    ]
+
+
+def reduce_scratch(source, cut):
+    rows = source.shape[-2] // 8
+    size = source.shape[-1] // cut
+    count = len(pieces_of(source, cut))
     shapes = []
     for planes in (4, 4, 3, 3):
-        for source in sources:
-            rows = source.shape[-2] // 8
-            shapes.append(pltpu.VMEM((planes,) + source.shape[:-2] + (rows, source.shape[-1]), jnp.bfloat16))
-    count = len(sources)
+        shapes += [pltpu.VMEM((planes, rows, size), jnp.bfloat16)] * count
     return shapes + [
         pltpu.SemaphoreType.DMA((count, 4)),
         pltpu.SemaphoreType.DMA((count, 4)),
@@ -1167,16 +1182,19 @@
     ]
 
 
-def line_reduce(sources, totals, scratch):
-    count = len(sources)
+def line_reduce(source, total, scratch, cut):
+    pieces = pieces_of(source, cut)
+    count = len(pieces)
     buffers = [scratch[n * count : (n + 1) * count] for n in range(4)]
+    sources = [source.at[front + (slice(None), columns)] for front, columns, _ in pieces]
+    totals = [total.at[:, columns] for _, _, columns in pieces]
     return LineReduce(sources, totals, *buffers, *scratch[4 * count :])
 
 
 def final_reduce_kernel(small_count, *refs):
     small_refs, refs = refs[:small_count], refs[small_count:]
     (
-        small_out, swap, small_in, small_low, small_high, final_low, final_in,
+        small_out, swap, small_own, small_in, small_low, small_high, final_low, final_in, own_sem,
         swap_send, swap_recv, in_send, in_recv, line_send, line_recv, last_send, last_recv,
     ) = refs
     outer_count, inner_count = 4, 2
@@ -1214,6 +1232,11 @@
             swap_recv.at[n],
         )
 
+    def own_copy(n):
+        return pltpu.make_async_copy(
+            small_refs[n].at[:, own_rows, :], small_own.at[:, :, starts[n] : starts[n + 1]], own_sem.at[n]
+        )
+
     def inner_copy(plane):
         return remote(
             swap.at[plane * inner_count + 1 - inner],
@@ -1239,12 +1262,9 @@
     def add_own(chunk):
         def body(at):
             here = pl.ds(pl.multiple_of(at, 16), 16)
-            there = pl.ds(pl.multiple_of(side * half_rows + at, 16), 16)
-            for n in range(small_count):
-                columns = slice(starts[n], starts[n + 1])
-                swap[chunk, here, columns] = (
-                    wide(swap[chunk, here, columns]) + wide(small_refs[n][chunk, there, :])
-                ).astype(swap.dtype)
+            swap[chunk, here, :] = (
+                wide(swap[chunk, here, :]) + wide(small_own[chunk, here, :])
+            ).astype(swap.dtype)
 
         by_rows(half_rows, body)
 
@@ -1256,8 +1276,10 @@
 
         for n in range(small_count):
             swap_copy(n).start()
+            own_copy(n).start()
         for n in range(small_count):
             swap_copy(n).wait_recv()
+            own_copy(n).wait()
         for plane in order:
             add_own(plane * inner_count + 1 - inner)
             inner_copy(plane).start()
@@ -1318,12 +1340,13 @@
     return pl.pallas_call(
         functools.partial(final_reduce_kernel, len(smalls)),
         out_shape=jax.ShapeDtypeStruct((small_rows, small_columns), jnp.float32),
-        in_specs=[in_vmem] * len(smalls),
+        in_specs=[pl.BlockSpec(memory_space=pl.ANY)] * len(smalls),
         out_specs=in_vmem,
-        scratch_shapes=[pltpu.VMEM((chunk_count, half, small_columns), low)]
+        scratch_shapes=[pltpu.VMEM((chunk_count, half, small_columns), low)] * 2
         + [pltpu.VMEM((planes, half, small_columns), low)] * 3
         + [pltpu.VMEM((half, small_columns), low)] * 2
         + [
+            pltpu.SemaphoreType.DMA((len(smalls),)),
             pltpu.SemaphoreType.DMA((len(smalls),)),
             pltpu.SemaphoreType.DMA((len(smalls),)),
             pltpu.SemaphoreType.DMA((planes,)),
@@ -1334,7 +1357,7 @@
             pltpu.SemaphoreType.DMA((2,)),
         ],
         compiler_params=pltpu.CompilerParams(
-            collective_id=collective, has_side_effects=True, vmem_limit_bytes=40 * 2**20
+            collective_id=collective, has_side_effects=True, vmem_limit_bytes=60 * 2**20
         ),
         name="final_reduce",
     )(*smalls)
@@ -1401,12 +1424,14 @@
             rows_in, grads_in, first_gate_up, first_gate_up, first_down, 1, dp_count,
             [send_rows, send_grads, w_gate_up], 6,
         )
-        gu_parts = [lax.psum_scatter(grad_gu, "dp", scatter_dimension=1, tiled=True)]
-        second_gu, second_grad_down, *parts, down_part = experts(
+        down_parts = [lax.psum_scatter(grad_down, "dp", scatter_dimension=0, tiled=True)]
+        second_gu, grad_down, *parts, gu_part = experts(
             next_rows, next_grads, second_gate_up, second_gate_up, second_down, 2, dp_count,
-            [both, grad_down], 4,
-        )
-        down_parts = [down_part]
+            [both, grad_gu], 4,
+        )
+        parts, down_parts[0] = lax.optimization_barrier((parts, down_parts[0]))
+        down_parts.append(lax.psum_scatter(grad_down, "dp", scatter_dimension=0, tiled=True))
+        gu_parts = [gu_part]
     else:
         exchange = functools.partial(
             lax.all_to_all, axis_name="expert", split_axis=0, concat_axis=0, tiled=True
@@ -1418,9 +1443,9 @@
                 exchange(send_rows[e]), exchange(send_grads[e]), gate_up, gate_up, gather(w_down[e])
             )
             parts.append(exchange(both))
-            gu_parts.append(lax.psum_scatter(grad_gu, "dp", scatter_dimension=1, tiled=True))
+            gu_part = lax.psum_scatter(grad_gu, "dp", scatter_dimension=1, tiled=True)
+            gu_parts.append(jnp.concatenate([gu_part[0], gu_part[1]], -1).astype(jnp.float32))
             down_parts.append(lax.psum_scatter(grad_down, "dp", scatter_dimension=0, tiled=True))
-    gu_parts = [jnp.concatenate([part[0], part[1]], -1).astype(jnp.float32) for part in gu_parts]
     down_parts = [part.astype(jnp.float32) for part in down_parts]
     output, logit_grad, grad_middle, small_grad = combine(
         parts, spots, route_rows, aux, normed_two, middle, cot, packed_full, choice_count, expert_count
@@ -1430,9 +1455,8 @@
         packed_full, docs_row, docs_column, cosine, sine, small_grad,
     )
     if own_links:
-        token_grad, *weight_grads, gu_part, down_part = backward([second_gu, second_grad_down], 7)
+        token_grad, *weight_grads, gu_part = backward([second_gu], 7)
         gu_parts.append(gu_part)
-        down_parts.append(down_part)
         packed_part = final_reduce(
             [grad.reshape(dp_count, width // dp_count, grad.shape[1]) for grad in weight_grads], 3
         )

time: 626 us -> 593 us (0.947)
  Pallas kernels: 576 us -> 545 us
    pallas_call x1, Pallas kernels: 116 us -> 93.3 us  [attention_backward(): pl.pallas_call(functools.partial(attention_backward_kernel, len(sources))...]
    pallas_call x2, Pallas kernels: 232 us -> 220 us  [experts(): pl.pallas_call(functools.partial(experts_kernel, mode, dp_count), grid=(s...]
    unnamed x40 -> x30, local copies, waits for them, and re-layouts: 15.8 us -> 9.86 us
  transfers between devices with their start and end apart: 3 -> 4, of which waited for: 0 -> 0; matrix products, arithmetic and copies ran while one was open for 1% -> 2% of each run, Pallas kernels for 87% -> 87%
where the time goes in v11:
time: 593 us; the launch traced here: 588 us
  Pallas kernels  545 us (92%)
  local copies, waits for them, and re-layouts  21.4 us (4%)
  between operations  14.1 us (2%)
  other arithmetic  6.57 us (1%)
    pallas_call x2, Pallas kernels, experts(): pl.pallas_call(functools.partial(experts_kernel, mode, dp_count), grid=(s...  220 us
    pallas_call x1, Pallas kernels, attention_backward(): pl.pallas_call(functools.partial(attention_backward_kernel, len(sources))...  93.3 us
    pallas_call x1, Pallas kernels, expert_gather(): pl.pallas_call(functools.partial(expert_gather_kernel, dp_count), out_sha...  73.3 us
    pallas_call x1, Pallas kernels, final_reduce(): pl.pallas_call(functools.partial(final_reduce_kernel, len(smalls)), out_s...  55.8 us
    pallas_call x1, Pallas kernels, small_gather(): pl.pallas_call(functools.partial(small_gather_kernel, dp_count, expert_co...  35.8 us
    pallas_call x1, Pallas kernels, attention_forward(): pl.pallas_call(functools.partial(attention_forward_kernel, dp_count if li...  33.1 us
    pallas_call x1, Pallas kernels, combine(): pl.pallas_call(functools.partial(combine_kernel, expert_count, local_coun...  21.2 us
  transfers between devices with their start and end apart: 4, of which 0 were waited for; matrix products, arithmetic and copies ran while one was open for 2% of the time, Pallas kernels for 87%

profile of v11, /device:TPU:19, one launch (start us, length us, event | category | flops | bytes accessed | tf_op | source)
XLA Modules:
  0.0 587.9 jit_solution(10199655432728816738)
XLA Ops:
  7.2 0.0 copy-start.1
  7.2 0.0 all-gather.3.cloned.1.call-start
  7.3 1.8 copy.44
  9.1 0.8 copy.39
  9.9 0.8 copy.40
  10.6 0.8 copy.41
  11.4 0.8 copy.42
  12.2 0.8 copy.43
  13.0 2.1 slice_bitcast_fusion
  15.0 0.8 slice_bitcast_fusion.1
  15.8 0.0 copy-done.7
  15.8 0.0 copy-start.9
  15.9 1.0 concatenate.3.shard_ref
  16.9 35.8 %small_gather.1 = (bf16[768,3328]{1,0:T(8,128)(2,1)}, s32[1024,128]{1,0:T(8,128)}, s32[8,1024]{1,0:T(8,128)}) custom-call(bf16[96,3328]{1,0:T(8,128)(2,1)} %concatenate.3.shard_ref, s32[1024,2]{1,0:T(8,128)} %bitcast.23), custom_call_target="tpu_custom_call" | custom-call | tf_op jit(solution)/shard_map/small_gather/pallas_call | solution.py:1020
  52.7 0.0 all-gather.3.cloned.1.call-update
  52.7 0.0 all-gather.5.cloned.1.call-start
  52.8 0.7 all-gather.5.cloned.1.call-update
  53.5 0.3 reduce-scatter.3.cloned.1.call-start
  53.8 1.0 copy.46.refs_7_.refs_13_
  54.8 0.2 copy.45
  55.0 0.8 pad_convert_fusion.refs_11_
  55.9 33.1 %attention_forward.1 = (bf16[1024,768]{1,0:T(8,128)(2,1)}, bf16[1024,768]{1,0:T(8,128)(2,1)}, bf16[1024,768]{1,0:T(8,128)(2,1)}, bf16[1024,768]{1,0:T(8,128)(2,1...) custom-call(bf16[1024,768]{1,0:T(8,128)(2,1)} %bitcast.43, ...), custom_call_target="tpu_custom_call" | custom-call | flops 8053063680 | bytes 18874368 | tf_op jit(solution)/shard_map/attention_forward/pallas_call | solution.py:177
  89.0 11.8 %dispatch.1 = (bf16[2,4,256,768]{3,2,1,0:T(8,128)(2,1)}, bf16[2,4,256,768]{3,2,1,0:T(8,128)(2,1)}) custom-call(s32[8,1024]{1,0:T(8,128)} %get-tuple-element.56.spots_ref, f32[1024,128]{1,0:T(8,128)} %get-tuple-element.59.aux_ref.refs_4_, bf16[1024,768]{1,0:T(8,128)(2,1)} %get-tuple-element.60.normed_ref.refs_5_, bf16[1024,768]{1,0:T(8,128)(2,1)} %bitcast.41), custom_call_target="tpu_custom_call" | custom-call | flops 6442450944 | bytes 9437184 | tf_op jit(solution)/shard_map/dispatch/pallas_call | solution.py:456
  100.8 73.3 %expert_gather.1 = (bf16[4,256,768]{2,1,0:T(8,128)(2,1)}, bf16[4,256,768]{2,1,0:T(8,128)(2,1)}, bf16[2048,768]{1,0:T(8,128)(2,1)}) custom-call(bf16[2,4,256,768]{3,2,1,0:T(8,128)(2,1)} %get-tuple-element.61.rows_ref.refs_5_, bf16[2,4,256,768]{3,2,1,0:T(8,128)(2,1)} %get-tuple-element.62.grads_ref.refs_6_, bf16[2,256,768]{2,1,0:T(8,128)(2,1)} %shards_ref.1), custom_call_target="tpu_custom_call" | custom-call | tf_op jit(solution)/shard_map/expert_gather/pallas_call | solution.py:954
  174.1 0.0 all-gather.3.cloned.1.call-done.refs_2_.refs_3_
  174.1 106.8 %experts.2 = (bf16[2,768,2048]{2,1,0:T(8,128)(2,1)}, bf16[2048,768]{1,0:T(8,128)(2,1)}, bf16[4,2,256,768]{3,2,1,0:T(8,128)(2,1)}, bf16[4,256,768]{2,1,0:T(8,128)...) custom-call(bf16[4,256,768]{2,1,0:T(8,128)(2,1)} %get-tuple-element.63.refs_0_, ...), custom_call_target="tpu_custom_call" | custom-call | flops 28991029248 | bytes 25165824 | tf_op jit(solution)/shard_map/experts/pallas_call | solution.py:739
  280.9 0.0 reduce-scatter.3.cloned.1.call-update
  280.9 0.0 reduce-scatter.5.cloned.1.call-start
  281.0 0.0 all-gather.5.cloned.1.call-done.refs_4_
  281.0 113.5 %experts.3 = (bf16[2,768,2048]{2,1,0:T(8,128)(2,1)}, bf16[2048,768]{1,0:T(8,128)(2,1)}, bf16[4,2,256,768]{3,2,1,0:T(8,128)(2,1)}, bf16[4,2,256,768]{3,2,1,0:T(8,128)(2,1)}, f32[96,4096]{1,0:T(8,128)}) custom-call(bf16[4,256,768]{2,1,0:T(8,128)(2,1)} %get-tuple-element.67.refs_0_, bf16[4,256,768]{2,1,0:T(8,128)(2,1)} %get-tuple-element.68.refs_1_, ...), custom_call_target="tpu_custom_call" | custom-call | flops 28991029248 | bytes 25165824 | tf_op jit(solution)/shard_map/experts/pallas_call | solution.py:739
  394.6 0.0 reduce-scatter.5.cloned.1.call-update
  394.6 0.0 reduce-scatter.3.cloned.1.call-done
  394.6 21.2 %combine.1 = (bf16[1024,768]{1,0:T(8,128)(2,1)}, bf16[1024,12]{1,0:T(8,128)(2,1)}, f32[1024,768]{1,0:T(8,128)}, f32[768,128]{1,0:T(8,128)}) custom-call(bf16[4,2,256,768]{3,2,1,0:T(8,128)(2,1)} %get-tuple-element.76.refs_0_, bf16[4,2,256,768]{3,2,1,0:T(8,128)(2,1)} %get-tuple-element.77.refs_1_, s32[1024,128]{1,0:T(8,128)} %get-tuple-element.78.refs_2_, ...), custom_call_target="tpu_custom_call" | custom-call | flops 9663676416 | bytes 17301504 | tf_op jit(solution)/shard_map/combine/pallas_call | solution.py:575
  415.8 93.3 %attention_backward.1 = (bf16[1024,768]{1,0:T(8,128)(2,1)}, bf16[768,768]{1,0:T(8,128)(2,1)}, bf16[768,768]{1,0:T(8,128)(2,1)}, bf16[768,768]{1,0:T(8,128)(2,1)}...) custom-call(f32[1024,768]{1,0:T(8,128)} %get-tuple-element.81.refs_0_, ...), custom_call_target="tpu_custom_call" | custom-call | flops 17716740096 | bytes 25165824 | tf_op jit(solution)/shard_map/attention_backward/pallas_call | solution.py:338
  509.0 55.8 %final_reduce.1 = f32[96,3328]{1,0:T(8,128)} custom-call(bf16[8,96,768]{2,1,0:T(8,128)(2,1)} %bitcast.29, bf16[8,96,768]{2,1,0:T(8,128)(2,1)} %bitcast.30, bf16[8,96,768]{2,1,0:T(8,128)(2,1)} %bitcast.31, bf16[8,96,768]{2,1,0:T(8,128)(2,1)} %bitcast.32, bf16[8,96,256]{2,1,0:T(8,128)(2,1)} %bitcast.36), custom_call_target="tpu_custom_call" | custom-call | tf_op jit(solution)/shard_map/final_reduce/pallas_call | solution.py:1340
  564.8 0.0 slice-start
  564.8 2.3 slice.35
  567.1 0.7 slice.36
  567.9 0.7 slice.40
  568.6 0.7 slice.41
  569.3 0.7 copy.49
  569.9 1.4 copy.50
  571.4 1.4 copy.51
  572.8 0.8 copy.48
  573.6 0.7 slice_reduce_fusion
  574.3 2.2 maximum_convert_fusion
  576.5 3.5 pad_maximum_fusion
  580.0 1.1 copy.53
  (20 shorter events, 0.0 us)
Async XLA Ops:
  7.2 7.9 %copy-start.1 = (bf16[2,256,768]{2,1,0:T(8,128)(2,1)S(1)}, bf16[2,256,768]{2,1,0:T(8,128)(2,1)}, u32[]{:S(2)}) copy-start(bf16[2,256,768]{2,1,0:T(8,128)(2,1)} %shards_ref.1) | copy-start | bytes 2359300
  7.2 8.6 %copy-start.4 = (bf16[96,2304]{1,0:T(8,128)(2,1)S(1)}, bf16[96,2304]{1,0:T(8,128)(2,1)}, u32[]{:S(2)}) copy-start(bf16[96,2304]{1,0:T(8,128)(2,1)} %param.20) | copy-start | bytes 1327108
  7.2 8.6 %copy-start.7 = (bf16[96,768]{1,0:T(8,128)(2,1)S(1)}, bf16[96,768]{1,0:T(8,128)(2,1)}, u32[]{:S(2)}) copy-start(bf16[96,768]{1,0:T(8,128)(2,1)} %param.21) | copy-start | bytes 442372
  7.2 166.9 %all-gather.3.cloned.1.call-start = ((), (), s32[]{:S(2)}) async-start(), calls=%async_computation.2 | async-start | bytes 7077888 | tf_op jit(solution)/shard_map/all_gather | solution.py:1414
  15.8 38.0 %copy-start.9 = (s32[1,1024]{1,0:T(1,128)S(1)}, s32[1,1024]{1,0:T(1,128)}, u32[]{:S(2)}) copy-start(s32[1,1024]{1,0:T(1,128)} %refs_12_.1) | copy-start | bytes 12292
  16.9 38.0 %copy-start.8 = (bf16[1,1024,12]{1,2,0:T(8,128)(2,1)S(1)}, bf16[1,1024,12]{1,2,0:T(8,128)(2,1)}, u32[]{:S(2)}) copy-start(bf16[1,1024,12]{1,2,0:T(8,128)(2,1)} %param.17) | copy-start | bytes 73732
  52.7 228.3 %all-gather.5.cloned.1.call-start = ((), (), s32[]{:S(2)}) async-start(), calls=%async_computation.3 | async-start | bytes 3538944 | tf_op jit(solution)/shard_map/all_gather | solution.py:1414
  53.5 341.1 %reduce-scatter.3.cloned.1.call-start = ((), (), s32[]{:S(2)}) async-start(), calls=%async_computation.4 | async-start | bytes 3538944 | tf_op jit(solution)/shard_map/reduce_scatter | solution.py:1427
  280.9 293.3 %reduce-scatter.5.cloned.1.call-start = ((), (), s32[]{:S(2)}) async-start(), calls=%async_computation.5 | async-start | bytes 3538944 | tf_op jit(solution)/shard_map/reduce_scatter | solution.py:1433
  564.8 2.3 copy-start
  564.8 4.4 slice-start
  564.8 8.0 %copy-start.6 = (bf16[1024,12]{1,0:T(8,128)(2,1)S(1)}, bf16[1024,12]{1,0:T(8,128)(2,1)}, u32[]{:S(2)}) copy-start(bf16[1024,12]{1,0:T(8,128)(2,1)} %get-tuple-element.90) | copy-start | bytes 73732
  564.8 9.4 %copy-start.5 = (bf16[256,768]{1,0:T(8,128)(2,1)S(1)}, bf16[256,768]{1,0:T(8,128)(2,1)}, u32[]{:S(2)}) copy-start(bf16[256,768]{1,0:T(8,128)(2,1)} %reduce-scatter.3.cloned.1.call-done) | copy-start | bytes 1179652
  567.9 8.7 %copy-start.3 = (f32[96,4096]{1,0:T(8,128)S(1)}, f32[96,4096]{1,0:T(8,128)}, u32[]{:S(2)}) copy-start(f32[96,4096]{1,0:T(8,128)} %get-tuple-element.96) | copy-start | bytes 4718596
  576.5 3.5 copy-start.2
Sparse Core Ops, SparseCore 0:
  52.8 114.3 all-gather.2
  169.4 97.4 all-gather.4
  281.1 112.3 reduce-scatter.2
  396.9 94.9 reduce-scatter.4

commit v12 on v11

--- a/solution.py
+++ b/solution.py
@@ -62,17 +62,17 @@
 
 def attention_forward_kernel(linked, *refs):
     (
-        tokens_ref, wq_ref, wk_ref, wv_ref, wo_ref, small_ref, docs_row_ref, docs_column_ref,
-        cosine_ref, sine_ref, routes_ref, resid_ref,
-    ) = refs[:12]
+        tokens_ref, wq_ref, wk_ref, wv_ref, wo_ref, small_ref, docs_row_ref,
+        cosine_ref, sine_ref, table_ref,
+    ) = refs[:10]
     (
         normed_ref, q_ref, k_ref, v_ref, attended_ref, middle_ref, normed_two_ref, aux_ref,
-    ) = refs[12 + bool(linked) : 20 + bool(linked)]
+    ) = refs[10 + bool(linked) : 18 + bool(linked)]
     step = pl.program_id(0)
     rows = tokens_ref.shape[0]
     if linked:
-        branch_ref = refs[22]
-        line = LineGather(refs[12].at[0], refs[21], linked, *refs[23:])
+        branch_ref = refs[20]
+        line = LineGather(refs[10].at[0], refs[19], linked, *refs[21:])
 
         @pl.when(step == 0)
         def _():
@@ -83,7 +83,7 @@
         def _():
             line.relay(1)
     else:
-        branch_ref = refs[20]
+        branch_ref = refs[18]
 
     @pl.when(step == 0)
     def _():
@@ -103,7 +103,7 @@
                 part = turn(part, cosine, sine)
             out_ref[:, half * 128 : half * 128 + 128] = part.astype(jnp.bfloat16)
 
-    docs_row, docs_column = docs_row_ref[...], docs_column_ref[...]
+    docs_row, docs_column = docs_row_ref[...], table_ref[:, 18:19].astype(jnp.int32)
     for i in range(rows // BLOCK):
         low, high = key_span(i)
         here = slice(i * BLOCK, (i + 1) * BLOCK)
@@ -133,7 +133,7 @@
         scale = lax.rsqrt(jnp.mean(middle * middle, -1, keepdims=True) + epsilon)
         normed_two = (middle * scale * gains).astype(jnp.bfloat16)
         normed_two_ref[...] = normed_two
-        logits = nn(normed_two, small) + resid_ref[...].astype(jnp.float32)
+        logits = nn(normed_two, small) + table_ref[...]
         lanes = lane_ids(logits.shape)
 
         def lane(at):
@@ -144,7 +144,7 @@
             first, second = jnp.exp(first - peak), jnp.exp(second - peak)
             return first / (first + second), second / (first + second)
 
-        columns = list(two(lane(routes_ref[:, 0:1]), lane(routes_ref[:, 1:2])))
+        columns = list(two(*[lane(table_ref[:, 16 + s : 17 + s].astype(jnp.int32)) for s in range(2)]))
         columns += list(two(lane(12), lane(13))) + list(two(lane(14), lane(15)))
         columns.append(scale)
         aux = jnp.zeros_like(logits)
@@ -158,7 +158,7 @@
 
 
 def attention_forward(
-    tokens, packed, docs_row, docs_column, cosine, sine, routes, resid, shards=None,
+    tokens, packed, docs_row, cosine, sine, table, shards=None,
     dp_count=None, collective=None,
 ):
     rows, width = tokens.shape
@@ -192,10 +192,8 @@
             pl.BlockSpec((GROUP, width), lambda j: (j, 3)),
             pl.BlockSpec((width, 256), lambda j: (0, 12)),
             whole((1, rows)),
-            whole((rows, 1)),
             whole((rows, 128)),
             whole((rows, 128)),
-            whole((rows, 2)),
             whole((rows, 128)),
         ]
         + [anywhere] * linked,
@@ -215,15 +213,15 @@
         ),
         name="attention_forward",
     )(
-        tokens, packed, packed, packed, packed, packed, docs_row, docs_column, cosine, sine, routes,
-        resid, *([shards] if linked else []),
+        tokens, packed, packed, packed, packed, packed, docs_row, cosine, sine, table,
+        *([shards] if linked else []),
     )
 
 
 def attention_backward_kernel(count, *refs):
     (
         grad_middle_ref, q_ref, k_ref, v_ref, attended_ref, normed_ref, tokens_ref,
-        wq_ref, wk_ref, wv_ref, wo_ref, small_ref, docs_row_ref, docs_column_ref,
+        wq_ref, wk_ref, wv_ref, wo_ref, small_ref, docs_row_ref, table_ref,
         cosine_ref, sine_ref, small_grad_ref,
     ) = refs[:17]
     sources, refs = refs[17 : 17 + count], refs[17 + count :]
@@ -233,7 +231,7 @@
     step = pl.program_id(0)
     rows, width = tokens_ref.shape
     if count:
-        line = line_reduce(sources[0], totals[0], refs[6:], 2)
+        line = line_reduce(sources[0], totals[0], refs[6:], 2, (1,))
 
         @pl.when(step == 0)
         def _():
@@ -252,7 +250,7 @@
     grad_attended = nt(grad_branch, wo_ref[...]).astype(jnp.bfloat16)
     go_ref[...] = tn(attended_ref[...], grad_branch).astype(jnp.bfloat16)
     cosine, sine = cosine_ref[...], sine_ref[...]
-    docs_row, docs_column = docs_row_ref[...], docs_column_ref[...]
+    docs_row, docs_column = docs_row_ref[...], table_ref[:, 18:19].astype(jnp.int32)
     for pair in range(2):
         lanes = slice(pair * 128, pair * 128 + 128)
         key_acc[...] = jnp.zeros_like(key_acc)
@@ -316,7 +314,7 @@
 
 
 def attention_backward(
-    grad_middle, queries, keys, values, attended, normed, tokens, packed, docs_row, docs_column,
+    grad_middle, queries, keys, values, attended, normed, tokens, packed, docs_row, table,
     cosine, sine, small_grad, sources=(), collective=None,
 ):
     rows, width = tokens.shape
@@ -330,8 +328,7 @@
     links = {"collective_id": collective, "has_side_effects": True} if linked else {}
     sums = []
     for source in sources:
-        sides = source.shape[0] if len(source.shape) == 3 else 1
-        sums.append((source.shape[-2] // 8, sides * source.shape[-1]))
+        sums.append((source.shape[-2] // 8, source.shape[-1]))
     once = lambda shape: pl.BlockSpec(
         shape, lambda j: (0, 0), pipeline_mode=pl.Buffered(1)
     )
@@ -356,7 +353,7 @@
             pl.BlockSpec((GROUP, width), lambda j: (j, 3)),
             pl.BlockSpec((width, 256), lambda j: (0, 12)),
             once((1, rows)),
-            once((rows, 1)),
+            once((rows, 128)),
             once((rows, 128)),
             once((rows, 128)),
             once((width, 128)),
@@ -379,7 +376,7 @@
             pltpu.VMEM((rows, 128), jnp.float32),
             pltpu.VMEM((rows, 128), jnp.float32),
         ]
-        + (reduce_scratch(sources[0], 2) if linked else []),
+        + (reduce_scratch(sources[0], 2, (1,)) if linked else []),
         compiler_params=pltpu.CompilerParams(
             dimension_semantics=("arbitrary",), vmem_limit_bytes=61 * 2**20, **links
         ),
@@ -391,15 +388,16 @@
         name="attention_backward",
     )(
         grad_middle, queries, keys, values, attended, normed, tokens, packed, packed, packed,
-        packed, packed, docs_row, docs_column, cosine, sine, small_grad, *sources,
-    )
-
-
-def routing_kernel(expert_count, routes_ref, columns_ref, rows_ref):
-    rows = routes_ref.shape[0]
+        packed, packed, docs_row, table, cosine, sine, small_grad, *sources,
+    )
+
+
+def routing_kernel(expert_count, table_ref, columns_ref, rows_ref):
+    rows = table_ref.shape[0]
     lanes = lane_ids((rows, 128))
-    first = (lanes == routes_ref[:, 0:1]).astype(jnp.float32)
-    second = (lanes == routes_ref[:, 1:2]).astype(jnp.float32)
+    routes = [table_ref[:, 16 + s : 17 + s].astype(jnp.int32) for s in range(2)]
+    first = (lanes == routes[0]).astype(jnp.float32)
+    second = (lanes == routes[1]).astype(jnp.float32)
     down = lax.broadcasted_iota(jnp.int32, (rows, rows), 0)
     lower = (down > lane_ids((rows, rows))).astype(jnp.bfloat16)
     before_first = nn(lower, first.astype(jnp.bfloat16))
@@ -407,7 +405,7 @@
     spots = []
     for picked, before, at in ((first, before_first, 0), (second, before_second, 1)):
         rank = jnp.sum(picked * before, -1, keepdims=True)
-        route = routes_ref[:, at : at + 1]
+        route = routes[at]
         spot = route.astype(jnp.float32) * CAP + rank
         spots.append(jnp.where(route < expert_count, spot, jnp.full_like(spot, 2.0 * expert_count * CAP)))
     both = jnp.where(lanes == 0, spots[0], jnp.where(lanes == 1, spots[1], 0.0))
@@ -415,8 +413,8 @@
     rows_ref[...] = jnp.transpose(both)[0:8, :].astype(jnp.int32)
 
 
-def routing(routes, expert_count):
-    rows = routes.shape[0]
+def routing(table, expert_count):
+    rows = table.shape[0]
     return pl.pallas_call(
         functools.partial(routing_kernel, expert_count),
         out_shape=[
@@ -425,25 +423,31 @@
         ],
         compiler_params=pltpu.CompilerParams(vmem_limit_bytes=40 * 2**20),
         name="routing",
-    )(routes)
-
-
-def dispatch_kernel(spots_ref, aux_ref, normed_ref, cot_ref, rows_ref, grads_ref, gates_ref):
+    )(table)
+
+
+def dispatch_kernel(local_count, spots_ref, aux_ref, normed_ref, cot_ref, rows_ref, grads_ref, gates_ref):
     step = pl.program_id(0)
 
     @pl.when(step == 0)
     def _():
         gates_ref[...] = jnp.transpose(aux_ref[...])[0:8, :]
 
-    shape = (rows_ref.shape[0], normed_ref.shape[0])
-    slots = step * rows_ref.shape[0] + lax.broadcasted_iota(jnp.int32, shape, 0)
+    owners, width = rows_ref.shape[0], rows_ref.shape[2]
+    shape = (owners * CAP, normed_ref.shape[0])
+    place_in = lax.broadcasted_iota(jnp.int32, shape, 0)
+    first_owner = step // local_count * owners
+    slots = (first_owner + place_in // CAP) * (local_count * CAP)
+    slots = slots + step % local_count * CAP + place_in % CAP
     first, second = slots == spots_ref[0:1, :], slots == spots_ref[1:2, :]
     gates = jnp.sum(
         jnp.where(first, gates_ref[0:1, :], jnp.where(second, gates_ref[1:2, :], 0.0)), -1, keepdims=True
     )
     chosen = jnp.where(first | second, 1.0, 0.0).astype(jnp.bfloat16)
-    rows_ref[...] = nn(chosen, normed_ref[...]).astype(jnp.bfloat16)
-    grads_ref[...] = (nn(chosen, cot_ref[...]) * gates).astype(jnp.bfloat16)
+    rows_ref[...] = nn(chosen, normed_ref[...]).astype(jnp.bfloat16).reshape(owners, CAP, width)
+    grads_ref[...] = (
+        (nn(chosen, cot_ref[...]) * gates).astype(jnp.bfloat16).reshape(owners, CAP, width)
+    )
 
 
 def dispatch(spots, aux, normed, cot, owner_count, local_count):
@@ -451,11 +455,11 @@
     slot_count = owner_count * local_count * CAP
     whole = lambda shape: pl.BlockSpec(shape, lambda j: (0, 0))
     block = pl.BlockSpec(
-        (None, None, CAP, width), lambda j: (j % local_count, j // local_count, 0, 0)
+        (None, 2, CAP, width), lambda j: (j % local_count, j // local_count, 0, 0)
     )
     return pl.pallas_call(
-        dispatch_kernel,
-        grid=(slot_count // CAP,),
+        functools.partial(dispatch_kernel, local_count),
+        grid=(slot_count // CAP // 2,),
         out_shape=[jax.ShapeDtypeStruct((local_count, owner_count, CAP, width), jnp.bfloat16)] * 2,
         in_specs=[whole((8, rows)), whole((rows, 128)), whole((rows, width)), whole((rows, width))],
         out_specs=[block, block],
@@ -478,14 +482,28 @@
 
 
 def combine_kernel(
-    expert_count, local_count, *refs
+    expert_count, local_count, linked, *refs
 ):
     parts, refs = refs[:local_count], refs[local_count:]
-    (
-        spots_ref, routes_ref, aux_ref, normed_ref, middle_ref, cot_ref, small_ref,
-        output_ref, logit_ref, grad_middle_ref, small_out_ref, vectors_ref, small_grad_ref,
-    ) = refs
+    spots_ref, table_ref, aux_ref, normed_ref, middle_ref, cot_ref, small_ref = refs[:7]
+    refs = refs[7:]
+    if linked:
+        source_ref, refs = refs[0], refs[1:]
+    output_ref, logit_ref, grad_middle_ref, small_out_ref = refs[:4]
+    refs = refs[4:]
+    if linked:
+        total_ref, refs = refs[0], refs[1:]
+    vectors_ref, small_grad_ref = refs[:2]
     step = pl.program_id(0)
+    if linked:
+        line = line_reduce(source_ref, total_ref, refs[2:], 2, (0,))
+
+        @pl.when(step == 0)
+        def _():
+            greet(line.peers())
+            line.each_plane(line.start)
+
+        pl.when(step == 1)(lambda: line.turns([0], []))
 
     @pl.when(step == 0)
     def _():
@@ -505,12 +523,13 @@
         hits = [slots == spots_ref[:, s : s + 1] for s in range(2)]
         chosen = [jnp.where(hit, 1.0, 0.0).astype(jnp.bfloat16) for hit in hits]
         returned = parts[e][:, 0].reshape(count, width)
+        both = nn(jnp.concatenate(chosen, 0), returned)
         for s in range(2):
-            picks[s] = picks[s] + nn(chosen[s], returned)
+            picks[s] = picks[s] + both[s * rows : (s + 1) * rows, :]
         back = back + nn(chosen[0] + chosen[1], parts[e][:, 1].reshape(count, width))
     inner = [total(pick * cot) for pick in picks]
     gates = [aux_ref[:, s : s + 1] for s in range(2)]
-    routes = [routes_ref[:, s : s + 1] for s in range(2)]
+    routes = [table_ref[:, 16 + s : 17 + s].astype(jnp.int32) for s in range(2)]
     dot_copy = total(cot * normed)
 
     def weight_of(route):
@@ -563,38 +582,53 @@
         column = jnp.transpose(jnp.broadcast_to(vectors_ref[8:9, :], (128, width)))
         small_grad = small_grad_ref[...]
         small_out_ref[...] = jnp.where(lane_ids(small_grad.shape) == 19, column, small_grad)
-
-
-def combine(parts, spots, routes, aux, normed, middle, cot, packed, choice_count, expert_count):
+        if linked:
+            line.turns([1, 2, 3], [0, 1, 2, 3])
+            line.each_plane(line.finish)
+
+
+def combine(
+    parts, spots, table, aux, normed, middle, cot, packed, choice_count, expert_count, source=None,
+    collective=None,
+):
     rows, width = normed.shape
     local_count = len(parts)
     slot_count = expert_count * CAP
-    size = 256
+    size = 512
+    linked = source is not None
+    links = {"collective_id": collective, "has_side_effects": True} if linked else {}
     block = lambda columns: pl.BlockSpec((size, columns), lambda j: (j, 0))
     whole = lambda shape: pl.BlockSpec(shape, lambda j: (0,) * len(shape))
+    once = lambda shape: pl.BlockSpec(
+        shape, lambda j: (0,) * len(shape), pipeline_mode=pl.Buffered(1)
+    )
     return pl.pallas_call(
-        functools.partial(combine_kernel, expert_count, local_count),
+        functools.partial(combine_kernel, expert_count, local_count, linked),
         grid=(rows // size,),
         out_shape=[
             jax.ShapeDtypeStruct((rows, width), jnp.bfloat16),
             jax.ShapeDtypeStruct((rows, choice_count), jnp.bfloat16),
             jax.ShapeDtypeStruct((rows, width), jnp.float32),
             jax.ShapeDtypeStruct((width, 128), jnp.float32),
-        ],
-        in_specs=[whole(part.shape) for part in parts]
+        ]
+        + ([jax.ShapeDtypeStruct((width // 8, source.shape[2]), jnp.float32)] if linked else []),
+        in_specs=[once(part.shape) for part in parts]
         + [
             block(128),
-            block(2),
+            block(128),
             block(128),
             block(width),
             block(width),
             block(width),
             pl.BlockSpec((width, 256), lambda j: (0, 12)),
-        ],
-        out_specs=[block(width), block(choice_count), block(width), whole((width, 128))],
-        scratch_shapes=[pltpu.VMEM((16, width), jnp.float32), pltpu.VMEM((width, 128), jnp.float32)],
+        ]
+        + [pl.BlockSpec(memory_space=pl.ANY)] * linked,
+        out_specs=[block(width), block(choice_count), block(width), whole((width, 128))]
+        + ([whole((width // 8, source.shape[2]))] if linked else []),
+        scratch_shapes=[pltpu.VMEM((16, width), jnp.float32), pltpu.VMEM((width, 128), jnp.float32)]
+        + (reduce_scratch(source, 2, (0,)) if linked else []),
         compiler_params=pltpu.CompilerParams(
-            dimension_semantics=("arbitrary",), vmem_limit_bytes=56 * 2**20
+            dimension_semantics=("arbitrary",), vmem_limit_bytes=58 * 2**20, **links
         ),
         cost_estimate=pl.CostEstimate(
             flops=6 * slot_count * rows * width,
@@ -602,7 +636,7 @@
             transcendentals=0,
         ),
         name="combine",
-    )(*parts, spots, routes, aux, normed, middle, cot, packed)
+    )(*parts, spots, table, aux, normed, middle, cot, packed, *([source] if linked else []))
 
 
 def experts_kernel(mode, dp_count, *refs):
@@ -969,8 +1003,9 @@
 
 
 def small_gather_kernel(
-    dp_count, expert_count, shard_ref, routes_ref, full_ref, columns_ref, rows_ref,
-    send_sem, recv_sem, own_sem, pass_sem, mate_sem, all_sem,
+    dp_count, expert_count, shard_ref, routes_ref, docs_ref, resid_ref, gate_up_ref, down_ref,
+    full_ref, columns_ref, rows_ref, table_ref, gate_up_out, down_out,
+    send_sem, recv_sem, own_sem, pass_sem, mate_sem, all_sem, slice_sem, stack_ref,
 ):
     me, mine = place()
     rows, columns = shard_ref.shape
@@ -1001,11 +1036,24 @@
     line.start()
     other = pltpu.make_async_copy(shard_ref.at[:, mate_columns], there(me, mate_columns), all_sem)
     other.start()
-    routing_kernel(expert_count, routes_ref, columns_ref, rows_ref)
+    slices = [
+        pltpu.make_async_copy(gate_up_ref.at[0], gate_up_out, slice_sem.at[0]),
+        pltpu.make_async_copy(down_ref.at[1], down_out, slice_sem.at[1]),
+    ]
+    for part in slices:
+        part.start()
+    stack_ref[...] = jnp.zeros_like(stack_ref)
+    stack_ref[0 : resid_ref.shape[0], :] = resid_ref[...].astype(jnp.float32)
+    stack_ref[16:18, :] = routes_ref[...].astype(jnp.float32)
+    stack_ref[18:19, :] = docs_ref[...].astype(jnp.float32)
+    table_ref[...] = jnp.transpose(stack_ref[...])
+    routing_kernel(expert_count, table_ref, columns_ref, rows_ref)
     for hop in range(1, line.outer_count):
         line.relay(hop)
     line.finish()
     other.wait()
+    for part in slices:
+        part.wait()
     for k in range(1, dp_count):
         chunk = lax.rem(me + k, dp_count)
         target = there(chunk, mate_columns)
@@ -1013,9 +1061,9 @@
         pass_copy(chunk).wait_send()
 
 
-def small_gather(shard, routes, expert_count, dp_count, collective):
+def small_gather(shard, routes, docs, resid, gate_up, down, expert_count, dp_count, collective):
     rows, columns = shard.shape
-    tokens = routes.shape[0]
+    tokens = routes.shape[1]
     anywhere, in_vmem = pl.BlockSpec(memory_space=pl.ANY), pl.BlockSpec(memory_space=pltpu.VMEM)
     return pl.pallas_call(
         functools.partial(small_gather_kernel, dp_count, expert_count),
@@ -1023,20 +1071,25 @@
             jax.ShapeDtypeStruct((dp_count * rows, columns), shard.dtype),
             jax.ShapeDtypeStruct((tokens, 128), jnp.int32),
             jax.ShapeDtypeStruct((8, tokens), jnp.int32),
+            jax.ShapeDtypeStruct((tokens, 128), jnp.float32),
+            jax.ShapeDtypeStruct(gate_up.shape[1:], gate_up.dtype),
+            jax.ShapeDtypeStruct(down.shape[1:], down.dtype),
         ],
-        in_specs=[anywhere, in_vmem],
-        out_specs=[anywhere, in_vmem, in_vmem],
+        in_specs=[anywhere] + [in_vmem] * 3 + [anywhere] * 2,
+        out_specs=[anywhere] + [in_vmem] * 3 + [anywhere] * 2,
         scratch_shapes=gather_semaphores(dp_count)
         + [
             pltpu.SemaphoreType.DMA((dp_count,)),
             pltpu.SemaphoreType.DMA((dp_count,)),
             pltpu.SemaphoreType.DMA,
+            pltpu.SemaphoreType.DMA((2,)),
+            pltpu.VMEM((128, tokens), jnp.float32),
         ],
         compiler_params=pltpu.CompilerParams(
             collective_id=collective, has_side_effects=True, vmem_limit_bytes=60 * 2**20
         ),
         name="small_gather",
-    )(shard, routes)
+    )(shard, routes, docs, resid, gate_up, down)
 
 
 class LineReduce:
@@ -1155,10 +1208,12 @@
         self.each_plane(body)
 
 
-def pieces_of(source, cut):
+def pieces_of(source, cut, sides=None):
     columns = source.shape[-1]
     size = columns // cut
-    fronts = [(side,) for side in range(source.shape[0])] if len(source.shape) == 3 else [()]
+    fronts = [()]
+    if len(source.shape) == 3:
+        fronts = [(side,) for side in (range(source.shape[0]) if sides is None else sides)]
     return [
         (front, slice(c * size, c * size + size), slice(n * columns + c * size, n * columns + c * size + size))
         for n, front in enumerate(fronts)
@@ -1166,10 +1221,10 @@
     ]
 
 
-def reduce_scratch(source, cut):
+def reduce_scratch(source, cut, sides=None):
     rows = source.shape[-2] // 8
     size = source.shape[-1] // cut
-    count = len(pieces_of(source, cut))
+    count = len(pieces_of(source, cut, sides))
     shapes = []
     for planes in (4, 4, 3, 3):
         shapes += [pltpu.VMEM((planes, rows, size), jnp.bfloat16)] * count
@@ -1182,8 +1237,8 @@
     ]
 
 
-def line_reduce(source, total, scratch, cut):
-    pieces = pieces_of(source, cut)
+def line_reduce(source, total, scratch, cut, sides=None):
+    pieces = pieces_of(source, cut, sides)
     count = len(pieces)
     buffers = [scratch[n * count : (n + 1) * count] for n in range(4)]
     sources = [source.at[front + (slice(None), columns)] for front, columns, _ in pieces]
@@ -1397,25 +1452,26 @@
     cot = out_grad.reshape(rows, width)
     route_rows = routes.reshape(rows, 2)
     cosine, sine = rotary_lanes(length, width // HEADS)
-    docs_row, docs_column = doc_ids.reshape(1, rows), doc_ids.reshape(rows, 1)
-    resid = jnp.pad(
-        resid_logits.reshape(rows, choice_count).astype(jnp.float32), ((0, 0), (0, 128 - choice_count))
-    )
+    docs_row = doc_ids.reshape(1, rows)
+    resid_rows = resid_logits.reshape(rows, choice_count)
     if own_links:
-        packed_full, spots, spot_rows = small_gather(packed, route_rows, expert_count, dp_count, 1)
+        packed_full, spots, spot_rows, table, gate_up_shard, down_shard = small_gather(
+            packed, route_rows.T, docs_row, resid_rows.T, w_gate_up, w_down, expert_count, dp_count, 1
+        )
     else:
-        spots, spot_rows = routing(route_rows, expert_count)
+        columns = [
+            resid_rows, jnp.zeros((rows, 16 - choice_count)), route_rows, docs_row.T, jnp.zeros((rows, 109))
+        ]
+        table = jnp.concatenate([column.astype(jnp.float32) for column in columns], 1)
+        spots, spot_rows = routing(table, expert_count)
         packed_full = lax.all_gather(packed, "dp", axis=0, tiled=True)
     gather = functools.partial(lax.all_gather, axis_name="dp", axis=0, tiled=True)
     if own_links:
-        first_gate_up, second_down, packed_full = lax.optimization_barrier(
-            (w_gate_up[0], w_down[1], packed_full)
-        )
-        first_gate_up, second_down = gather(first_gate_up), gather(second_down)
+        first_gate_up, second_down = gather(gate_up_shard), gather(down_shard)
     else:
         first_gate_up = gather(w_gate_up[0])
     normed_one, queries, keys, values, attended, middle, normed_two, aux = attention_forward(
-        inputs, packed_full, docs_row, docs_column, cosine, sine, route_rows, resid
+        inputs, packed_full, docs_row, cosine, sine, table
     )
     send_rows, send_grads = dispatch(spot_rows, aux, normed_two, cot, owner_count, local_count)
     if own_links:
@@ -1447,16 +1503,20 @@
             gu_parts.append(jnp.concatenate([gu_part[0], gu_part[1]], -1).astype(jnp.float32))
             down_parts.append(lax.psum_scatter(grad_down, "dp", scatter_dimension=0, tiled=True))
     down_parts = [part.astype(jnp.float32) for part in down_parts]
-    output, logit_grad, grad_middle, small_grad = combine(
-        parts, spots, route_rows, aux, normed_two, middle, cot, packed_full, choice_count, expert_count
-    )
+    mix = functools.partial(
+        combine, parts, spots, table, aux, normed_two, middle, cot, packed_full, choice_count, expert_count
+    )
+    if own_links:
+        output, logit_grad, grad_middle, small_grad, gate_part = mix(second_gu, 5)
+    else:
+        output, logit_grad, grad_middle, small_grad = mix()
     backward = functools.partial(
         attention_backward, grad_middle, queries, keys, values, attended, normed_one, inputs,
-        packed_full, docs_row, docs_column, cosine, sine, small_grad,
+        packed_full, docs_row, table, cosine, sine, small_grad,
     )
     if own_links:
-        token_grad, *weight_grads, gu_part = backward([second_gu], 7)
-        gu_parts.append(gu_part)
+        token_grad, *weight_grads, up_part = backward([second_gu], 7)
+        gu_parts.append(jnp.concatenate([gate_part, up_part], 1))
         packed_part = final_reduce(
             [grad.reshape(dp_count, width // dp_count, grad.shape[1]) for grad in weight_grads], 3
         )

time: 593 us -> 631 us (1.064)
  Pallas kernels: 545 us -> 578 us
    pallas_call x1, Pallas kernels: 21.2 us -> 66.1 us  [combine(): pl.pallas_call(functools.partial(combine_kernel, expert_count, local_coun...]
    pallas_call x1, Pallas kernels: 93.3 us -> 66.3 us  [attention_backward(): pl.pallas_call(functools.partial(attention_backward_kernel, len(sources))...]
    pallas_call x1, Pallas kernels: 35.8 us -> 59.7 us  [small_gather(): pl.pallas_call(functools.partial(small_gather_kernel, dp_count, expert_co...]
  transfers between devices with their start and end apart: 4 -> 4, of which waited for: 0 -> 2; matrix products, arithmetic and copies ran while one was open for 2% -> 2% of each run, Pallas kernels for 87% -> 83%
where the time goes in v12:
time: 631 us; the launch traced here: 622 us
  Pallas kernels  578 us (92%)
  local copies, waits for them, and re-layouts  19.9 us (3%)
  between operations  14.2 us (2%)
    pallas_call x2, Pallas kernels, experts(): pl.pallas_call(functools.partial(experts_kernel, mode, dp_count), grid=(s...  216 us
    pallas_call x1, Pallas kernels, expert_gather(): pl.pallas_call(functools.partial(expert_gather_kernel, dp_count), out_sha...  72.9 us
    pallas_call x1, Pallas kernels, attention_backward(): pl.pallas_call(functools.partial(attention_backward_kernel, len(sources))...  66.3 us
    pallas_call x1, Pallas kernels, combine(): pl.pallas_call(functools.partial(combine_kernel, expert_count, local_coun...  66.1 us
    pallas_call x1, Pallas kernels, small_gather(): pl.pallas_call(functools.partial(small_gather_kernel, dp_count, expert_co...  59.7 us
    pallas_call x1, Pallas kernels, final_reduce(): pl.pallas_call(functools.partial(final_reduce_kernel, len(smalls)), out_s...  53.6 us
    pallas_call x1, Pallas kernels, attention_forward(): pl.pallas_call(functools.partial(attention_forward_kernel, dp_count if li...  32.9 us
  transfers between devices with their start and end apart: 4, of which 2 were waited for; matrix products, arithmetic and copies ran while one was open for 2% of the time, Pallas kernels for 83%

profile of v12, /device:TPU:19, one launch (start us, length us, event | category | flops | bytes accessed | tf_op | source)
XLA Modules:
  0.0 622.1 jit_solution(9168697044370633341)
XLA Ops:
  7.2 0.0 all-gather.3.cloned.1.call-start
  7.2 0.8 copy.37
  8.0 0.8 copy.38
  8.8 0.8 copy.39
  9.6 0.8 copy.40
  10.4 0.8 copy.41
  11.2 2.0 concatenate.6.shard_ref
  13.1 59.7 %small_gather.1 = (bf16[768,3328]{1,0:T(8,128)(2,1)}, s32[1024,128]{1,0:T(8,128)}, s32[8,1024]{1,0:T(8,128)}, f32[1024,128]{1,0:T(8,128)}, bf16[96,4096]{1,0:T(8,128)(2,1)}, /*index=5*/bf16[256,768]{1,0:T(8,128)(2,1)}) custom-call(bf16[96,3328]{1,0:T(8,128)(2,1)} %concatenate.6.shard_ref, s32[2,1024]{1,0:T(2,128)} %bitcast.35, s32[1,1024]{1,0:T(1,128)} %refs_12_.1, ...), custom_call_target="tpu_custom_call" | custom-call | tf_op jit(solution)/shard_map/small_gather/pallas_call | solution.py:1068
  72.9 0.0 all-gather.3.cloned.1.call-update
  72.9 0.0 all-gather.5.cloned.1.call-start
  72.9 0.7 all-gather.5.cloned.1.call-update
  73.7 0.2 reduce-scatter.3.cloned.1.call-start
  73.9 32.9 %attention_forward.1 = (bf16[1024,768]{1,0:T(8,128)(2,1)}, bf16[1024,768]{1,0:T(8,128)(2,1)}, bf16[1024,768]{1,0:T(8,128)(2,1)}, bf16[1024,768]{1,0:T(8,128)(2,1...) custom-call(bf16[1024,768]{1,0:T(8,128)(2,1)} %bitcast.40, ...), custom_call_target="tpu_custom_call" | custom-call | flops 8053063680 | bytes 18874368 | tf_op jit(solution)/shard_map/attention_forward/pallas_call | solution.py:177
  106.8 11.2 %dispatch.1 = (bf16[2,4,256,768]{3,2,1,0:T(8,128)(2,1)}, bf16[2,4,256,768]{3,2,1,0:T(8,128)(2,1)}) custom-call(s32[8,1024]{1,0:T(8,128)} %get-tuple-element.57.spots_ref, f32[1024,128]{1,0:T(8,128)} %get-tuple-element.60.aux_ref.refs_4_, bf16[1024,768]{1,0:T(8,128)(2,1)} %get-tuple-element.61.normed_ref.refs_5_, bf16[1024,768]{1,0:T(8,128)(2,1)} %bitcast.38), custom_call_target="tpu_custom_call" | custom-call | flops 6442450944 | bytes 9437184 | tf_op jit(solution)/shard_map/dispatch/pallas_call | solution.py:460
  118.1 72.9 %expert_gather.1 = (bf16[4,256,768]{2,1,0:T(8,128)(2,1)}, bf16[4,256,768]{2,1,0:T(8,128)(2,1)}, bf16[2048,768]{1,0:T(8,128)(2,1)}) custom-call(bf16[2,4,256,768]{3,2,1,0:T(8,128)(2,1)} %get-tuple-element.62.rows_ref.refs_5_, bf16[2,4,256,768]{3,2,1,0:T(8,128)(2,1)} %get-tuple-element.63.grads_ref.refs_6_, bf16[2,256,768]{2,1,0:T(8,128)(2,1)} %shards_ref.1), custom_call_target="tpu_custom_call" | custom-call | tf_op jit(solution)/shard_map/expert_gather/pallas_call | solution.py:988
  191.0 2.6 all-gather.3.cloned.1.call-done.refs_2_.refs_3_
  193.6 102.0 %experts.2 = (bf16[2,768,2048]{2,1,0:T(8,128)(2,1)}, bf16[2048,768]{1,0:T(8,128)(2,1)}, bf16[4,2,256,768]{3,2,1,0:T(8,128)(2,1)}, bf16[4,256,768]{2,1,0:T(8,128)...) custom-call(bf16[4,256,768]{2,1,0:T(8,128)(2,1)} %get-tuple-element.64.refs_0_, ...), custom_call_target="tpu_custom_call" | custom-call | flops 28991029248 | bytes 25165824 | tf_op jit(solution)/shard_map/experts/pallas_call | solution.py:773
  295.6 0.0 reduce-scatter.3.cloned.1.call-update
  295.6 0.0 reduce-scatter.5.cloned.1.call-start
  295.7 0.0 all-gather.5.cloned.1.call-done.refs_4_
  295.7 113.6 %experts.3 = (bf16[2,768,2048]{2,1,0:T(8,128)(2,1)}, bf16[2048,768]{1,0:T(8,128)(2,1)}, bf16[4,2,256,768]{3,2,1,0:T(8,128)(2,1)}, bf16[4,2,256,768]{3,2,1,0:T(8,128)(2,1)}, f32[96,4096]{1,0:T(8,128)}) custom-call(bf16[4,256,768]{2,1,0:T(8,128)(2,1)} %get-tuple-element.68.refs_0_, bf16[4,256,768]{2,1,0:T(8,128)(2,1)} %get-tuple-element.69.refs_1_, ...), custom_call_target="tpu_custom_call" | custom-call | flops 28991029248 | bytes 25165824 | tf_op jit(solution)/shard_map/experts/pallas_call | solution.py:773
  409.3 0.0 reduce-scatter.5.cloned.1.call-update
  409.4 1.6 reduce-scatter.3.cloned.1.call-done
  410.9 66.1 %combine.1 = (bf16[1024,768]{1,0:T(8,128)(2,1)}, bf16[1024,12]{1,0:T(8,128)(2,1)}, f32[1024,768]{1,0:T(8,128)}, f32[768,128]{1,0:T(8,128)}, f32[96,2048]{1,0:T(8,128)}) custom-call(bf16[4,2,256,768]{3,2,1,0:T(8,128)(2,1)} %get-tuple-element.77.refs_0_, bf16[4,2,256,768]{3,2,1,0:T(8,128)(2,1)} %get-tuple-element.78.refs_1_, ...), custom_call_target="tpu_custom_call" | custom-call | flops 9663676416 | bytes 17301504 | tf_op jit(solution)/shard_map/combine/pallas_call | solution.py:605
  477.0 66.3 %attention_backward.1 = (bf16[1024,768]{1,0:T(8,128)(2,1)}, bf16[768,768]{1,0:T(8,128)(2,1)}, bf16[768,768]{1,0:T(8,128)(2,1)}, bf16[768,768]{1,0:T(8,128)(2,1)}...) custom-call(f32[1024,768]{1,0:T(8,128)} %get-tuple-element.83.refs_0_, ...), custom_call_target="tpu_custom_call" | custom-call | flops 17716740096 | bytes 25165824 | tf_op jit(solution)/shard_map/attention_backward/pallas_call | solution.py:335
  543.4 53.6 %final_reduce.1 = f32[96,3328]{1,0:T(8,128)} custom-call(bf16[8,96,768]{2,1,0:T(8,128)(2,1)} %bitcast.26, bf16[8,96,768]{2,1,0:T(8,128)(2,1)} %bitcast.27, bf16[8,96,768]{2,1,0:T(8,128)(2,1)} %bitcast.28, bf16[8,96,768]{2,1,0:T(8,128)(2,1)} %bitcast.29, bf16[8,96,256]{2,1,0:T(8,128)(2,1)} %bitcast.32), custom_call_target="tpu_custom_call" | custom-call | tf_op jit(solution)/shard_map/final_reduce/pallas_call | solution.py:1395
  597.0 0.0 copy-start
  597.0 0.0 slice-start
  597.1 0.0 copy-start.7
  597.1 2.3 slice.27
  599.3 0.7 slice.28
  600.1 0.7 slice.32
  600.8 0.7 slice.33
  601.5 0.0 slice-done
  601.5 0.7 copy.43
  602.2 1.4 copy.44
  603.6 1.4 copy.45
  605.0 0.8 copy.42
  605.8 0.7 slice_reduce_fusion
  606.5 0.0 copy-done.6
  606.5 2.2 maximum_convert_fusion
  608.8 0.1 maximum_bitcast_fusion
  608.9 1.3 copy-done.3
  610.2 1.9 pad_maximum_fusion
  612.0 0.1 copy-done.1
  612.2 1.1 copy.48
  613.3 0.8 copy-done.2
  614.2 1.1 copy.49
  (12 shorter events, 0.0 us)
Async XLA Ops:
  7.2 186.4 %all-gather.3.cloned.1.call-start = ((), (), s32[]{:S(2)}) async-start(), calls=%async_computation.2 | async-start | bytes 7077888 | tf_op jit(solution)/shard_map/all_gather | solution.py:1470
  72.9 222.8 %all-gather.5.cloned.1.call-start = ((), (), s32[]{:S(2)}) async-start(), calls=%async_computation.3 | async-start | bytes 3538944 | tf_op jit(solution)/shard_map/all_gather | solution.py:1470
  73.7 337.3 %reduce-scatter.3.cloned.1.call-start = ((), (), s32[]{:S(2)}) async-start(), calls=%async_computation.4 | async-start | bytes 3538944 | tf_op jit(solution)/shard_map/reduce_scatter | solution.py:1483
  295.6 310.9 %reduce-scatter.5.cloned.1.call-start = ((), (), s32[]{:S(2)}) async-start(), calls=%async_computation.5 | async-start | bytes 3538944 | tf_op jit(solution)/shard_map/reduce_scatter | solution.py:1489
  597.0 2.3 copy-start
  597.0 4.4 slice-start
  597.1 8.0 %copy-start.7 = (bf16[1024,12]{1,0:T(8,128)(2,1)S(1)}, bf16[1024,12]{1,0:T(8,128)(2,1)}, u32[]{:S(2)}) copy-start(bf16[1024,12]{1,0:T(8,128)(2,1)} %get-tuple-element.91) | copy-start | bytes 73732
  597.1 9.4 %copy-start.6 = (bf16[256,768]{1,0:T(8,128)(2,1)S(1)}, bf16[256,768]{1,0:T(8,128)(2,1)}, u32[]{:S(2)}) copy-start(bf16[256,768]{1,0:T(8,128)(2,1)} %reduce-scatter.3.cloned.1.call-done) | copy-start | bytes 1179652
  600.1 8.7 %copy-start.4 = (f32[96,2048]{1,0:T(8,128)S(1)}, f32[96,2048]{1,0:T(8,128)}, u32[]{:S(2)}) copy-start(f32[96,2048]{1,0:T(8,128)} %get-tuple-element.98) | copy-start | bytes 2359300
  600.1 8.7 %copy-start.5 = (f32[96,2048]{1,0:T(8,128)S(1)}, f32[96,2048]{1,0:T(8,128)}, u32[]{:S(2)}) copy-start(f32[96,2048]{1,0:T(8,128)} %get-tuple-element.99) | copy-start | bytes 2359300
  608.8 1.4 copy-start.3
  610.2 2.0 copy-start.1
  612.2 2.0 copy-start.2
Sparse Core Ops, SparseCore 0:
  73.0 120.5 all-gather.2
  195.8 93.0 all-gather.4
  295.7 115.1 reduce-scatter.2
  414.4 103.7 reduce-scatter.4

commit v13 on v12

--- a/solution.py
+++ b/solution.py
@@ -231,7 +231,7 @@
     step = pl.program_id(0)
     rows, width = tokens_ref.shape
     if count:
-        line = line_reduce(sources[0], totals[0], refs[6:], 2, (1,))
+        line = line_reduce(sources[0], totals[0], refs[6:], 2)
 
         @pl.when(step == 0)
         def _():
@@ -306,8 +306,7 @@
         column = jnp.transpose(jnp.broadcast_to(gain_grad, (128, width)))
         small_grad = small_grad_ref[...]
         small_grad = jnp.where(lane_ids(small_grad.shape) == 18, column, small_grad)
-        small_out_ref[:, :128] = small_grad.astype(jnp.bfloat16)
-        small_out_ref[:, 128:] = jnp.zeros((width, 128), jnp.bfloat16)
+        small_out_ref[...] = small_grad.astype(jnp.bfloat16)
         if count:
             line.turns([2, 3], [1, 2, 3])
             line.each_plane(line.finish)
@@ -328,7 +327,7 @@
     links = {"collective_id": collective, "has_side_effects": True} if linked else {}
     sums = []
     for source in sources:
-        sums.append((source.shape[-2] // 8, source.shape[-1]))
+        sums.append((source.shape[-2] // 8, source.shape[0] * source.shape[-1]))
     once = lambda shape: pl.BlockSpec(
         shape, lambda j: (0, 0), pipeline_mode=pl.Buffered(1)
     )
@@ -337,7 +336,7 @@
         grid=(groups,),
         out_shape=[jax.ShapeDtypeStruct((rows, width), low)]
         + [weight] * 4
-        + [jax.ShapeDtypeStruct((width, 256), low)]
+        + [jax.ShapeDtypeStruct((width, 128), low)]
         + [jax.ShapeDtypeStruct(shape, jnp.float32) for shape in sums],
         in_specs=[
             once((rows, width)),
@@ -365,7 +364,7 @@
             column(0),
             column(0),
             pl.BlockSpec((GROUP, width), lambda j: (j, 0)),
-            whole((width, 256)),
+            whole((width, 128)),
         ]
         + [whole(shape) for shape in sums],
         scratch_shapes=[
@@ -376,7 +375,7 @@
             pltpu.VMEM((rows, 128), jnp.float32),
             pltpu.VMEM((rows, 128), jnp.float32),
         ]
-        + (reduce_scratch(sources[0], 2, (1,)) if linked else []),
+        + (reduce_scratch(sources[0], 2) if linked else []),
         compiler_params=pltpu.CompilerParams(
             dimension_semantics=("arbitrary",), vmem_limit_bytes=61 * 2**20, **links
         ),
@@ -1003,65 +1002,70 @@
 
 
 def small_gather_kernel(
-    dp_count, expert_count, shard_ref, routes_ref, docs_ref, resid_ref, gate_up_ref, down_ref,
-    full_ref, columns_ref, rows_ref, table_ref, gate_up_out, down_out,
-    send_sem, recv_sem, own_sem, pass_sem, mate_sem, all_sem, slice_sem, stack_ref,
+    dp_count, expert_count, shard_ref, routes_ref, docs_ref, resid_ref,
+    full_ref, columns_ref, rows_ref, table_ref, pass_sem, mate_sem, all_sem, stack_ref, *sems,
 ):
     me, mine = place()
     rows, columns = shard_ref.shape
     half = columns // 2
     side = mine % 2
     mate = mine + 1 - 2 * side
-    own_columns = pl.ds(pl.multiple_of(side * half, 128), half)
     mate_columns = pl.ds(pl.multiple_of((1 - side) * half, 128), half)
+    first = half // 256 * 128
+    spans = [(0, first), (first, half - first)]
 
     def there(chunk, lanes):
         return full_ref.at[pl.ds(pl.multiple_of(chunk * rows, 8), rows), lanes]
 
-    def pass_copy(chunk):
+    def columns_at(n, of):
+        start, size = spans[n]
+        return pl.ds(pl.multiple_of(of * half + start, 128), size)
+
+    def pass_copy(n, chunk):
+        here = there(chunk, columns_at(n, side))
         return pltpu.make_async_remote_copy(
-            src_ref=there(chunk, own_columns),
-            dst_ref=there(chunk, own_columns),
-            send_sem=pass_sem.at[chunk],
-            recv_sem=mate_sem.at[chunk],
+            src_ref=here,
+            dst_ref=here,
+            send_sem=pass_sem.at[n, chunk],
+            recv_sem=mate_sem.at[n, chunk],
             device_id=(me, mate),
             device_id_type=MESH,
         )
 
-    line = LineGather(
-        shard_ref.at[:, own_columns], full_ref, dp_count, send_sem, recv_sem, own_sem,
-        own_columns, lambda chunk: pass_copy(chunk).start(),
-    )
-    greet(line.peers() + [(me, mate)])
-    line.start()
+    lines = []
+    for n in range(2):
+        lines.append(
+            LineGather(
+                shard_ref.at[:, columns_at(n, side)], full_ref, dp_count, *sems[3 * n : 3 * n + 3],
+                columns_at(n, side), lambda chunk, n=n: pass_copy(n, chunk).start(),
+            )
+        )
+    greet(lines[0].peers() + [(me, mate)])
+    for line in lines:
+        line.start()
     other = pltpu.make_async_copy(shard_ref.at[:, mate_columns], there(me, mate_columns), all_sem)
     other.start()
-    slices = [
-        pltpu.make_async_copy(gate_up_ref.at[0], gate_up_out, slice_sem.at[0]),
-        pltpu.make_async_copy(down_ref.at[1], down_out, slice_sem.at[1]),
-    ]
-    for part in slices:
-        part.start()
     stack_ref[...] = jnp.zeros_like(stack_ref)
     stack_ref[0 : resid_ref.shape[0], :] = resid_ref[...].astype(jnp.float32)
     stack_ref[16:18, :] = routes_ref[...].astype(jnp.float32)
     stack_ref[18:19, :] = docs_ref[...].astype(jnp.float32)
     table_ref[...] = jnp.transpose(stack_ref[...])
     routing_kernel(expert_count, table_ref, columns_ref, rows_ref)
-    for hop in range(1, line.outer_count):
-        line.relay(hop)
-    line.finish()
+    for hop in range(1, lines[0].outer_count):
+        for line in lines:
+            line.relay(hop)
+    for line in lines:
+        line.finish()
     other.wait()
-    for part in slices:
-        part.wait()
     for k in range(1, dp_count):
         chunk = lax.rem(me + k, dp_count)
-        target = there(chunk, mate_columns)
-        pltpu.make_async_copy(target, target, mate_sem.at[chunk]).wait()
-        pass_copy(chunk).wait_send()
-
-
-def small_gather(shard, routes, docs, resid, gate_up, down, expert_count, dp_count, collective):
+        for n in range(2):
+            target = there(chunk, columns_at(n, 1 - side))
+            pltpu.make_async_copy(target, target, mate_sem.at[n, chunk]).wait()
+            pass_copy(n, chunk).wait_send()
+
+
+def small_gather(shard, routes, docs, resid, expert_count, dp_count, collective):
     rows, columns = shard.shape
     tokens = routes.shape[1]
     anywhere, in_vmem = pl.BlockSpec(memory_space=pl.ANY), pl.BlockSpec(memory_space=pltpu.VMEM)
@@ -1072,24 +1076,21 @@
             jax.ShapeDtypeStruct((tokens, 128), jnp.int32),
             jax.ShapeDtypeStruct((8, tokens), jnp.int32),
             jax.ShapeDtypeStruct((tokens, 128), jnp.float32),
-            jax.ShapeDtypeStruct(gate_up.shape[1:], gate_up.dtype),
-            jax.ShapeDtypeStruct(down.shape[1:], down.dtype),
         ],
-        in_specs=[anywhere] + [in_vmem] * 3 + [anywhere] * 2,
-        out_specs=[anywhere] + [in_vmem] * 3 + [anywhere] * 2,
-        scratch_shapes=gather_semaphores(dp_count)
-        + [
-            pltpu.SemaphoreType.DMA((dp_count,)),
-            pltpu.SemaphoreType.DMA((dp_count,)),
+        in_specs=[anywhere] + [in_vmem] * 3,
+        out_specs=[anywhere] + [in_vmem] * 3,
+        scratch_shapes=[
+            pltpu.SemaphoreType.DMA((2, dp_count)),
+            pltpu.SemaphoreType.DMA((2, dp_count)),
             pltpu.SemaphoreType.DMA,
-            pltpu.SemaphoreType.DMA((2,)),
             pltpu.VMEM((128, tokens), jnp.float32),
-        ],
+        ]
+        + gather_semaphores(dp_count) * 2,
         compiler_params=pltpu.CompilerParams(
             collective_id=collective, has_side_effects=True, vmem_limit_bytes=60 * 2**20
         ),
         name="small_gather",
-    )(shard, routes, docs, resid, gate_up, down)
+    )(shard, routes, docs, resid)
 
 
 class LineReduce:
@@ -1278,6 +1279,9 @@
     mate_rows = pl.ds(pl.multiple_of((1 - side) * half_rows, 16), half_rows)
     own_rows = pl.ds(pl.multiple_of(side * half_rows, 16), half_rows)
 
+    middle = starts[-1] // 256 * 128
+    spans = [slice(0, middle), slice(middle, starts[-1])]
+
     def swap_copy(n):
         return remote(
             small_refs[n].at[:, mate_rows, :],
@@ -1292,33 +1296,38 @@
             small_refs[n].at[:, own_rows, :], small_own.at[:, :, starts[n] : starts[n + 1]], own_sem.at[n]
         )
 
-    def inner_copy(plane):
+    def inner_copy(p, plane):
         return remote(
-            swap.at[plane * inner_count + 1 - inner],
-            small_in.at[plane],
+            swap.at[plane * inner_count + 1 - inner, :, spans[p]],
+            small_in.at[plane, :, spans[p]],
             (beside, mine),
-            in_send.at[plane],
-            in_recv.at[plane],
-        )
-
-    def line_copy(plane, upward, device_plane):
+            in_send.at[p, plane],
+            in_recv.at[p, plane],
+        )
+
+    def line_copy(p, plane, upward, device_plane):
         way = 0 if upward else 1
         return remote(
-            small_in.at[plane],
-            (small_low if upward else small_high).at[plane],
+            small_in.at[plane, :, spans[p]],
+            (small_low if upward else small_high).at[plane, :, spans[p]],
             (device_plane * inner_count + inner, mine),
-            line_send.at[way, plane],
-            line_recv.at[way, plane],
+            line_send.at[p, way, plane],
+            line_recv.at[p, way, plane],
+        )
+
+    def last_copy(p):
+        return remote(
+            final_low.at[:, spans[p]], final_in.at[:, spans[p]], (me, across), last_send.at[p], last_recv.at[p]
         )
 
     def wide(values):
         return values.astype(jnp.float32)
 
-    def add_own(chunk):
+    def add_own(chunk, lanes):
         def body(at):
             here = pl.ds(pl.multiple_of(at, 16), 16)
-            swap[chunk, here, :] = (
-                wide(swap[chunk, here, :]) + wide(small_own[chunk, here, :])
+            swap[chunk, here, lanes] = (
+                wide(swap[chunk, here, lanes]) + wide(small_own[chunk, here, lanes])
             ).astype(swap.dtype)
 
         by_rows(half_rows, body)
@@ -1326,8 +1335,8 @@
     def at_plane(o):
         order = sorted(range(outer_count), key=lambda t: (-abs(t - o), t))
 
-        def line_start(plane):
-            return line_copy(plane, plane > o, o + 1 if plane > o else o - 1)
+        def line_start(p, plane):
+            return line_copy(p, plane, plane > o, o + 1 if plane > o else o - 1)
 
         for n in range(small_count):
             swap_copy(n).start()
@@ -1336,41 +1345,46 @@
             swap_copy(n).wait_recv()
             own_copy(n).wait()
         for plane in order:
-            add_own(plane * inner_count + 1 - inner)
-            inner_copy(plane).start()
+            for p in range(2):
+                add_own(plane * inner_count + 1 - inner, spans[p])
+                inner_copy(p, plane).start()
         for plane in order:
-            add_own(plane * inner_count + inner)
-            inner_copy(plane).wait_recv()
-            terms = [swap.at[plane * inner_count + inner]]
-            if o > 0 and plane >= o:
-                line_copy(plane, True, o).wait_recv()
-                terms.append(small_low.at[plane])
-            if o < outer_count - 1 and plane <= o:
-                line_copy(plane, False, o).wait_recv()
-                terms.append(small_high.at[plane])
-            target = final_low if plane == o else small_in.at[plane]
-
-            def gather(at, plane=plane, terms=terms, target=target):
-                here = pl.ds(pl.multiple_of(at, 16), 16)
-                total = wide(small_in[plane, here, :])
-                for term in terms:
-                    total = total + wide(term[here, :])
-                target[here, :] = total.astype(target.dtype)
-
-            by_rows(half_rows, gather)
-            if plane != o:
-                line_start(plane).start()
-        remote(final_low, final_in, (me, across), last_send.at[0], last_recv.at[0]).start()
+            for p in range(2):
+                add_own(plane * inner_count + inner, spans[p])
+                inner_copy(p, plane).wait_recv()
+                terms = [swap.at[plane * inner_count + inner]]
+                if o > 0 and plane >= o:
+                    line_copy(p, plane, True, o).wait_recv()
+                    terms.append(small_low.at[plane])
+                if o < outer_count - 1 and plane <= o:
+                    line_copy(p, plane, False, o).wait_recv()
+                    terms.append(small_high.at[plane])
+                target = final_low if plane == o else small_in.at[plane]
+
+                def gather(at, plane=plane, terms=terms, target=target, lanes=spans[p]):
+                    here = pl.ds(pl.multiple_of(at, 16), 16)
+                    total = wide(small_in[plane, here, lanes])
+                    for term in terms:
+                        total = total + wide(term[here, lanes])
+                    target[here, lanes] = total.astype(target.dtype)
+
+                by_rows(half_rows, gather)
+                if plane != o:
+                    line_start(p, plane).start()
+                else:
+                    last_copy(p).start()
         for plane in range(outer_count):
-            inner_copy(plane).wait_send()
-            if plane != o:
-                line_start(plane).wait_send()
+            for p in range(2):
+                inner_copy(p, plane).wait_send()
+                if plane != o:
+                    line_start(p, plane).wait_send()
         for n in range(small_count):
             swap_copy(n).wait_send()
 
     for o in range(outer_count):
         pl.when(outer == o)(functools.partial(at_plane, o))
-    remote(final_low, final_in, (me, across), last_send.at[0], last_recv.at[0]).wait()
+    for p in range(2):
+        last_copy(p).wait()
 
     def total_body(at):
         here = pl.ds(pl.multiple_of(at, 16), 16)
@@ -1379,7 +1393,7 @@
 
     by_rows(half_rows, total_body)
     mate_copy = remote(
-        small_out.at[own_rows, :], small_out.at[own_rows, :], (me, mate), last_send.at[1], last_recv.at[1]
+        small_out.at[own_rows, :], small_out.at[own_rows, :], (me, mate), last_send.at[2], last_recv.at[2]
     )
     mate_copy.start()
     mate_copy.wait()
@@ -1404,12 +1418,12 @@
             pltpu.SemaphoreType.DMA((len(smalls),)),
             pltpu.SemaphoreType.DMA((len(smalls),)),
             pltpu.SemaphoreType.DMA((len(smalls),)),
-            pltpu.SemaphoreType.DMA((planes,)),
-            pltpu.SemaphoreType.DMA((planes,)),
             pltpu.SemaphoreType.DMA((2, planes)),
             pltpu.SemaphoreType.DMA((2, planes)),
-            pltpu.SemaphoreType.DMA((2,)),
-            pltpu.SemaphoreType.DMA((2,)),
+            pltpu.SemaphoreType.DMA((2, 2, planes)),
+            pltpu.SemaphoreType.DMA((2, 2, planes)),
+            pltpu.SemaphoreType.DMA((3,)),
+            pltpu.SemaphoreType.DMA((3,)),
         ],
         compiler_params=pltpu.CompilerParams(
             collective_id=collective, has_side_effects=True, vmem_limit_bytes=60 * 2**20
@@ -1455,8 +1469,8 @@
     docs_row = doc_ids.reshape(1, rows)
     resid_rows = resid_logits.reshape(rows, choice_count)
     if own_links:
-        packed_full, spots, spot_rows, table, gate_up_shard, down_shard = small_gather(
-            packed, route_rows.T, docs_row, resid_rows.T, w_gate_up, w_down, expert_count, dp_count, 1
+        packed_full, spots, spot_rows, table = small_gather(
+            packed, route_rows.T, docs_row, resid_rows.T, expert_count, dp_count, 1
         )
     else:
         columns = [
@@ -1467,7 +1481,10 @@
         packed_full = lax.all_gather(packed, "dp", axis=0, tiled=True)
     gather = functools.partial(lax.all_gather, axis_name="dp", axis=0, tiled=True)
     if own_links:
-        first_gate_up, second_down = gather(gate_up_shard), gather(down_shard)
+        first_gate_up, second_down, packed_full = lax.optimization_barrier(
+            (w_gate_up[0], w_down[1], packed_full)
+        )
+        first_gate_up, second_down = gather(first_gate_up), gather(second_down)
     else:
         first_gate_up = gather(w_gate_up[0])
     normed_one, queries, keys, values, attended, middle, normed_two, aux = attention_forward(
@@ -1503,20 +1520,16 @@
             gu_parts.append(jnp.concatenate([gu_part[0], gu_part[1]], -1).astype(jnp.float32))
             down_parts.append(lax.psum_scatter(grad_down, "dp", scatter_dimension=0, tiled=True))
     down_parts = [part.astype(jnp.float32) for part in down_parts]
-    mix = functools.partial(
-        combine, parts, spots, table, aux, normed_two, middle, cot, packed_full, choice_count, expert_count
+    output, logit_grad, grad_middle, small_grad = combine(
+        parts, spots, table, aux, normed_two, middle, cot, packed_full, choice_count, expert_count
     )
-    if own_links:
-        output, logit_grad, grad_middle, small_grad, gate_part = mix(second_gu, 5)
-    else:
-        output, logit_grad, grad_middle, small_grad = mix()
     backward = functools.partial(
         attention_backward, grad_middle, queries, keys, values, attended, normed_one, inputs,
         packed_full, docs_row, table, cosine, sine, small_grad,
     )
     if own_links:
-        token_grad, *weight_grads, up_part = backward([second_gu], 7)
-        gu_parts.append(jnp.concatenate([gate_part, up_part], 1))
+        token_grad, *weight_grads, gu_part = backward([second_gu], 7)
+        gu_parts.append(gu_part)
         packed_part = final_reduce(
             [grad.reshape(dp_count, width // dp_count, grad.shape[1]) for grad in weight_grads], 3
         )

time: 631 us -> 583 us (0.924)
  Pallas kernels: 578 us -> 536 us
    pallas_call x1, Pallas kernels: 66.1 us -> 25.8 us  [combine(): pl.pallas_call(functools.partial(combine_kernel, expert_count, local_coun...]
    pallas_call x1, Pallas kernels: 66.3 us -> 97 us  [attention_backward(): pl.pallas_call(functools.partial(attention_backward_kernel, len(sources))...]
    pallas_call x1, Pallas kernels: 59.7 us -> 35 us  [small_gather(): pl.pallas_call(functools.partial(small_gather_kernel, dp_count, expert_co...]
    pallas_call x1, Pallas kernels: 53.6 us -> 44.2 us  [final_reduce(): pl.pallas_call(functools.partial(final_reduce_kernel, len(smalls)), out_s...]
  transfers between devices with their start and end apart: 4 -> 4, of which waited for: 2 -> 2; matrix products, arithmetic and copies ran while one was open for 2% -> 1% of each run, Pallas kernels for 83% -> 87%
where the time goes in v13:
time: 583 us; the launch traced here: 578 us
  Pallas kernels  536 us (92%)
  local copies, waits for them, and re-layouts  17 us (3%)
  between operations  14.4 us (2%)
    pallas_call x2, Pallas kernels, experts(): pl.pallas_call(functools.partial(experts_kernel, mode, dp_count), grid=(s...  216 us
    pallas_call x1, Pallas kernels, attention_backward(): pl.pallas_call(functools.partial(attention_backward_kernel, len(sources))...  97 us
    pallas_call x1, Pallas kernels, expert_gather(): pl.pallas_call(functools.partial(expert_gather_kernel, dp_count), out_sha...  73 us
    pallas_call x1, Pallas kernels, final_reduce(): pl.pallas_call(functools.partial(final_reduce_kernel, len(smalls)), out_s...  44.2 us
    pallas_call x1, Pallas kernels, small_gather(): pl.pallas_call(functools.partial(small_gather_kernel, dp_count, expert_co...  35 us
    pallas_call x1, Pallas kernels, attention_forward(): pl.pallas_call(functools.partial(attention_forward_kernel, dp_count if li...  33 us
    pallas_call x1, Pallas kernels, combine(): pl.pallas_call(functools.partial(combine_kernel, expert_count, local_coun...  25.8 us
  transfers between devices with their start and end apart: 4, of which 2 were waited for; matrix products, arithmetic and copies ran while one was open for 1% of the time, Pallas kernels for 87%

profile of v13, /device:TPU:19, one launch (start us, length us, event | category | flops | bytes accessed | tf_op | source)
XLA Modules:
  0.0 577.5 jit_solution(14615752547505446998)
XLA Ops:
  7.2 0.0 copy-start.1
  7.2 0.0 copy-start.4
  7.2 0.0 copy-start.7
  7.2 0.0 all-gather.3.cloned.1.call-start
  7.3 0.9 copy.37
  8.2 0.8 copy.38
  9.0 0.8 copy.39
  9.7 0.8 copy.40
  10.5 0.8 copy.41
  11.3 2.1 slice_bitcast_fusion
  13.3 0.0 copy-done.1
  13.3 0.8 slice_bitcast_fusion.1
  14.1 0.0 copy-done.7
  14.1 1.0 concatenate.3.shard_ref
  15.1 35.0 %small_gather.1 = (bf16[768,3328]{1,0:T(8,128)(2,1)}, s32[1024,128]{1,0:T(8,128)}, s32[8,1024]{1,0:T(8,128)}, f32[1024,128]{1,0:T(8,128)}) custom-call(bf16[96,3328]{1,0:T(8,128)(2,1)} %concatenate.3.shard_ref, s32[2,1024]{1,0:T(2,128)} %bitcast.38, s32[1,1024]{1,0:T(1,128)} %refs_12_.1, bf16[12,1024]{1,0:T(8,128)(2,1)} %bitcast.37), custom_call_target="tpu_custom_call" | custom-call | tf_op jit(solution)/shard_map/small_gather/pallas_call | solution.py:1072
  50.2 0.0 all-gather.3.cloned.1.call-update
  50.2 0.0 all-gather.5.cloned.1.call-start
  50.3 0.7 all-gather.5.cloned.1.call-update
  51.0 0.3 reduce-scatter.3.cloned.1.call-start
  51.2 33.0 %attention_forward.1 = (bf16[1024,768]{1,0:T(8,128)(2,1)}, bf16[1024,768]{1,0:T(8,128)(2,1)}, bf16[1024,768]{1,0:T(8,128)(2,1)}, bf16[1024,768]{1,0:T(8,128)(2,1...) custom-call(bf16[1024,768]{1,0:T(8,128)(2,1)} %bitcast.43, ...), custom_call_target="tpu_custom_call" | custom-call | flops 8053063680 | bytes 18874368 | tf_op jit(solution)/shard_map/attention_forward/pallas_call | solution.py:177
  84.2 11.3 %dispatch.1 = (bf16[2,4,256,768]{3,2,1,0:T(8,128)(2,1)}, bf16[2,4,256,768]{3,2,1,0:T(8,128)(2,1)}) custom-call(s32[8,1024]{1,0:T(8,128)} %get-tuple-element.57.spots_ref, f32[1024,128]{1,0:T(8,128)} %get-tuple-element.61.aux_ref.refs_4_, bf16[1024,768]{1,0:T(8,128)(2,1)} %get-tuple-element.62.normed_ref.refs_5_, bf16[1024,768]{1,0:T(8,128)(2,1)} %bitcast.41), custom_call_target="tpu_custom_call" | custom-call | flops 6442450944 | bytes 9437184 | tf_op jit(solution)/shard_map/dispatch/pallas_call | solution.py:459
  95.5 73.0 %expert_gather.1 = (bf16[4,256,768]{2,1,0:T(8,128)(2,1)}, bf16[4,256,768]{2,1,0:T(8,128)(2,1)}, bf16[2048,768]{1,0:T(8,128)(2,1)}) custom-call(bf16[2,4,256,768]{3,2,1,0:T(8,128)(2,1)} %get-tuple-element.63.rows_ref.refs_5_, bf16[2,4,256,768]{3,2,1,0:T(8,128)(2,1)} %get-tuple-element.64.grads_ref.refs_6_, bf16[2,256,768]{2,1,0:T(8,128)(2,1)} %shards_ref.1), custom_call_target="tpu_custom_call" | custom-call | tf_op jit(solution)/shard_map/expert_gather/pallas_call | solution.py:987
  168.5 2.8 all-gather.3.cloned.1.call-done.refs_2_.refs_3_
  171.3 101.8 %experts.2 = (bf16[2,768,2048]{2,1,0:T(8,128)(2,1)}, bf16[2048,768]{1,0:T(8,128)(2,1)}, bf16[4,2,256,768]{3,2,1,0:T(8,128)(2,1)}, bf16[4,256,768]{2,1,0:T(8,128)...) custom-call(bf16[4,256,768]{2,1,0:T(8,128)(2,1)} %get-tuple-element.65.refs_0_, ...), custom_call_target="tpu_custom_call" | custom-call | flops 28991029248 | bytes 25165824 | tf_op jit(solution)/shard_map/experts/pallas_call | solution.py:772
  273.1 0.0 reduce-scatter.3.cloned.1.call-update
  273.1 0.0 reduce-scatter.5.cloned.1.call-start
  273.2 0.0 all-gather.5.cloned.1.call-done.refs_4_
  273.2 114.4 %experts.3 = (bf16[2,768,2048]{2,1,0:T(8,128)(2,1)}, bf16[2048,768]{1,0:T(8,128)(2,1)}, bf16[4,2,256,768]{3,2,1,0:T(8,128)(2,1)}, bf16[4,2,256,768]{3,2,1,0:T(8,128)(2,1)}, f32[96,4096]{1,0:T(8,128)}) custom-call(bf16[4,256,768]{2,1,0:T(8,128)(2,1)} %get-tuple-element.69.refs_0_, bf16[4,256,768]{2,1,0:T(8,128)(2,1)} %get-tuple-element.70.refs_1_, ...), custom_call_target="tpu_custom_call" | custom-call | flops 28991029248 | bytes 25165824 | tf_op jit(solution)/shard_map/experts/pallas_call | solution.py:772
  387.6 0.0 reduce-scatter.5.cloned.1.call-update
  387.6 0.9 reduce-scatter.3.cloned.1.call-done
  388.6 25.8 %combine.1 = (bf16[1024,768]{1,0:T(8,128)(2,1)}, bf16[1024,12]{1,0:T(8,128)(2,1)}, f32[1024,768]{1,0:T(8,128)}, f32[768,128]{1,0:T(8,128)}) custom-call(bf16[4,2,256,768]{3,2,1,0:T(8,128)(2,1)} %get-tuple-element.78.refs_0_, bf16[4,2,256,768]{3,2,1,0:T(8,128)(2,1)} %get-tuple-element.79.refs_1_, s32[1024,128]{1,0:T(8,128)} %get-tuple-element.80.refs_2_, ...), custom_call_target="tpu_custom_call" | custom-call | flops 9663676416 | bytes 17301504 | tf_op jit(solution)/shard_map/combine/pallas_call | solution.py:604
  414.4 97.0 %attention_backward.1 = (bf16[1024,768]{1,0:T(8,128)(2,1)}, bf16[768,768]{1,0:T(8,128)(2,1)}, bf16[768,768]{1,0:T(8,128)(2,1)}, bf16[768,768]{1,0:T(8,128)(2,1)}...) custom-call(f32[1024,768]{1,0:T(8,128)} %get-tuple-element.83.refs_0_, ...), custom_call_target="tpu_custom_call" | custom-call | flops 17716740096 | bytes 25165824 | tf_op jit(solution)/shard_map/attention_backward/pallas_call | solution.py:334
  511.4 44.2 %final_reduce.1 = f32[96,3200]{1,0:T(8,128)} custom-call(bf16[8,96,768]{2,1,0:T(8,128)(2,1)} %bitcast.29, bf16[8,96,768]{2,1,0:T(8,128)(2,1)} %bitcast.30, bf16[8,96,768]{2,1,0:T(8,128)(2,1)} %bitcast.31, bf16[8,96,768]{2,1,0:T(8,128)(2,1)} %bitcast.32, bf16[8,96,128]{2,1,0:T(8,128)(2,1)} %bitcast.36), custom_call_target="tpu_custom_call" | custom-call | tf_op jit(solution)/shard_map/final_reduce/pallas_call | solution.py:1409
  555.7 0.0 slice-start
  555.7 2.3 slice.35
  558.0 0.7 slice.36
  558.7 0.7 slice.40
  559.4 0.1 slice.41
  559.5 0.0 slice-done
  559.5 0.7 copy.43
  560.1 1.4 copy.44
  561.6 0.6 copy.45
  562.2 0.0 copy-done.6
  562.2 0.8 copy.42
  563.0 0.7 slice_reduce_fusion
  563.7 2.2 maximum_convert_fusion
  565.9 3.4 pad_maximum_fusion
  569.4 1.1 copy.47
  (12 shorter events, 0.0 us)
Async XLA Ops:
  7.2 6.2 %copy-start.1 = (bf16[2,256,768]{2,1,0:T(8,128)(2,1)S(1)}, bf16[2,256,768]{2,1,0:T(8,128)(2,1)}, u32[]{:S(2)}) copy-start(bf16[2,256,768]{2,1,0:T(8,128)(2,1)} %shards_ref.1) | copy-start | bytes 2359300
  7.2 6.9 %copy-start.4 = (bf16[96,2304]{1,0:T(8,128)(2,1)S(1)}, bf16[96,2304]{1,0:T(8,128)(2,1)}, u32[]{:S(2)}) copy-start(bf16[96,2304]{1,0:T(8,128)(2,1)} %param.20) | copy-start | bytes 1327108
  7.2 6.9 %copy-start.7 = (bf16[96,768]{1,0:T(8,128)(2,1)S(1)}, bf16[96,768]{1,0:T(8,128)(2,1)}, u32[]{:S(2)}) copy-start(bf16[96,768]{1,0:T(8,128)(2,1)} %param.21) | copy-start | bytes 442372
  7.2 164.1 %all-gather.3.cloned.1.call-start = ((), (), s32[]{:S(2)}) async-start(), calls=%async_computation.2 | async-start | bytes 7077888 | tf_op jit(solution)/shard_map/all_gather | solution.py:1487
  50.2 223.0 %all-gather.5.cloned.1.call-start = ((), (), s32[]{:S(2)}) async-start(), calls=%async_computation.3 | async-start | bytes 3538944 | tf_op jit(solution)/shard_map/all_gather | solution.py:1487
  51.0 337.6 %reduce-scatter.3.cloned.1.call-start = ((), (), s32[]{:S(2)}) async-start(), calls=%async_computation.4 | async-start | bytes 3538944 | tf_op jit(solution)/shard_map/reduce_scatter | solution.py:1500
  273.1 290.6 %reduce-scatter.5.cloned.1.call-start = ((), (), s32[]{:S(2)}) async-start(), calls=%async_computation.5 | async-start | bytes 3538944 | tf_op jit(solution)/shard_map/reduce_scatter | solution.py:1506
  555.6 2.3 copy-start
  555.7 3.8 slice-start
  555.7 6.6 %copy-start.6 = (bf16[1024,12]{1,0:T(8,128)(2,1)S(1)}, bf16[1024,12]{1,0:T(8,128)(2,1)}, u32[]{:S(2)}) copy-start(bf16[1024,12]{1,0:T(8,128)(2,1)} %get-tuple-element.92) | copy-start | bytes 73732
  555.7 8.0 %copy-start.5 = (bf16[256,768]{1,0:T(8,128)(2,1)S(1)}, bf16[256,768]{1,0:T(8,128)(2,1)}, u32[]{:S(2)}) copy-start(bf16[256,768]{1,0:T(8,128)(2,1)} %reduce-scatter.3.cloned.1.call-done) | copy-start | bytes 1179652
  558.7 7.3 %copy-start.3 = (f32[96,4096]{1,0:T(8,128)S(1)}, f32[96,4096]{1,0:T(8,128)}, u32[]{:S(2)}) copy-start(f32[96,4096]{1,0:T(8,128)} %get-tuple-element.98) | copy-start | bytes 4718596
  565.9 3.4 copy-start.2
Sparse Core Ops, SparseCore 0:
  50.3 120.9 all-gather.2
  174.0 93.0 all-gather.4
  273.2 115.2 reduce-scatter.2
  392.0 92.8 reduce-scatter.4

commit v14 on v13

--- a/solution.py
+++ b/solution.py
@@ -593,14 +593,11 @@
     rows, width = normed.shape
     local_count = len(parts)
     slot_count = expert_count * CAP
-    size = 512
+    size = 256
     linked = source is not None
     links = {"collective_id": collective, "has_side_effects": True} if linked else {}
     block = lambda columns: pl.BlockSpec((size, columns), lambda j: (j, 0))
     whole = lambda shape: pl.BlockSpec(shape, lambda j: (0,) * len(shape))
-    once = lambda shape: pl.BlockSpec(
-        shape, lambda j: (0,) * len(shape), pipeline_mode=pl.Buffered(1)
-    )
     return pl.pallas_call(
         functools.partial(combine_kernel, expert_count, local_count, linked),
         grid=(rows // size,),
@@ -611,7 +608,7 @@
             jax.ShapeDtypeStruct((width, 128), jnp.float32),
         ]
         + ([jax.ShapeDtypeStruct((width // 8, source.shape[2]), jnp.float32)] if linked else []),
-        in_specs=[once(part.shape) for part in parts]
+        in_specs=[whole(part.shape) for part in parts]
         + [
             block(128),
             block(128),
@@ -968,37 +965,42 @@
     return [pltpu.SemaphoreType.DMA((owner_count,)), pltpu.SemaphoreType.DMA((owner_count,))]
 
 
-def expert_gather_kernel(dp_count, rows_ref, grads_ref, shards_ref, rows_out, grads_out, full_ref, *sems):
-    line = LineGather(shards_ref.at[0], full_ref, dp_count, *sems[:3])
-    trades = [Trade(rows_ref.at[0], rows_out, *sems[3:5]), Trade(grads_ref.at[0], grads_out, *sems[5:7])]
-    greet(line.peers() + trades[0].peers())
-    line.start()
-    for trade in trades:
-        trade.start()
-    for hop in range(1, line.outer_count):
-        line.relay(hop)
-    line.finish()
-    for trade in trades:
-        trade.finish()
-
-
-def expert_gather(rows, grads, shards, dp_count, collective):
+def expert_gather_kernel(
+    dp_count, rows_ref, grads_ref, down_ref, gate_up_ref, rows_out, grads_out, full_ref, up_ref, *sems
+):
+    half = up_ref.shape[1] // 2
+    lines = [LineGather(down_ref.at[0], full_ref, dp_count, *sems[:3])]
+    for n in range(2):
+        columns = slice(n * half, n * half + half)
+        shard = gate_up_ref.at[0, :, (2 + n) * half : (3 + n) * half]
+        lines.append(LineGather(shard, up_ref, dp_count, *sems[3 * n + 3 : 3 * n + 6], columns))
+    trades = [Trade(rows_ref.at[0], rows_out, *sems[9:11]), Trade(grads_ref.at[0], grads_out, *sems[11:13])]
+    greet(lines[0].peers() + trades[0].peers())
+    for part in lines + trades:
+        part.start()
+    for hop in range(1, lines[0].outer_count):
+        for line in lines:
+            line.relay(hop)
+    for part in lines + trades:
+        part.finish()
+
+
+def expert_gather(rows, grads, down, gate_up, dp_count, collective):
     anywhere = pl.BlockSpec(memory_space=pl.ANY)
     return pl.pallas_call(
         functools.partial(expert_gather_kernel, dp_count),
         out_shape=[
             jax.ShapeDtypeStruct(rows.shape[1:], rows.dtype),
             jax.ShapeDtypeStruct(grads.shape[1:], grads.dtype),
-            jax.ShapeDtypeStruct((dp_count * shards.shape[1], shards.shape[2]), shards.dtype),
+            jax.ShapeDtypeStruct((dp_count * down.shape[1], down.shape[2]), down.dtype),
+            jax.ShapeDtypeStruct((dp_count * gate_up.shape[1], gate_up.shape[2] // 2), gate_up.dtype),
         ],
-        in_specs=[anywhere] * 3,
-        out_specs=[anywhere] * 3,
-        scratch_shapes=gather_semaphores(dp_count)
-        + trade_semaphores(rows.shape[1])
-        + trade_semaphores(rows.shape[1]),
+        in_specs=[anywhere] * 4,
+        out_specs=[anywhere] * 4,
+        scratch_shapes=gather_semaphores(dp_count) * 3 + trade_semaphores(rows.shape[1]) * 2,
         compiler_params=pltpu.CompilerParams(collective_id=collective, has_side_effects=True),
         name="expert_gather",
-    )(rows, grads, shards)
+    )(rows, grads, down, gate_up)
 
 
 def small_gather_kernel(
@@ -1481,10 +1483,10 @@
         packed_full = lax.all_gather(packed, "dp", axis=0, tiled=True)
     gather = functools.partial(lax.all_gather, axis_name="dp", axis=0, tiled=True)
     if own_links:
-        first_gate_up, second_down, packed_full = lax.optimization_barrier(
-            (w_gate_up[0], w_down[1], packed_full)
-        )
-        first_gate_up, second_down = gather(first_gate_up), gather(second_down)
+        first_gate, second_down, packed_full = lax.optimization_barrier(
+            (w_gate_up[0, :, :hidden_count], w_down[1], packed_full)
+        )
+        first_gate, second_down = gather(first_gate), gather(second_down)
     else:
         first_gate_up = gather(w_gate_up[0])
     normed_one, queries, keys, values, attended, middle, normed_two, aux = attention_forward(
@@ -1492,9 +1494,11 @@
     )
     send_rows, send_grads = dispatch(spot_rows, aux, normed_two, cot, owner_count, local_count)
     if own_links:
-        rows_in, grads_in, first_down = expert_gather(send_rows, send_grads, w_down, dp_count, 2)
+        rows_in, grads_in, first_down, first_up = expert_gather(
+            send_rows, send_grads, w_down, w_gate_up, dp_count, 2
+        )
         grad_gu, grad_down, both, next_rows, next_grads, second_gate_up = experts(
-            rows_in, grads_in, first_gate_up, first_gate_up, first_down, 1, dp_count,
+            rows_in, grads_in, first_gate, first_up, first_down, 1, dp_count,
             [send_rows, send_grads, w_gate_up], 6,
         )
         down_parts = [lax.psum_scatter(grad_down, "dp", scatter_dimension=0, tiled=True)]
@@ -1502,7 +1506,6 @@
             next_rows, next_grads, second_gate_up, second_gate_up, second_down, 2, dp_count,
             [both, grad_gu], 4,
         )
-        parts, down_parts[0] = lax.optimization_barrier((parts, down_parts[0]))
         down_parts.append(lax.psum_scatter(grad_down, "dp", scatter_dimension=0, tiled=True))
         gu_parts = [gu_part]
     else:
@@ -1523,6 +1526,8 @@
     output, logit_grad, grad_middle, small_grad = combine(
         parts, spots, table, aux, normed_two, middle, cot, packed_full, choice_count, expert_count
     )
+    if own_links:
+        grad_middle, down_parts[0] = lax.optimization_barrier((grad_middle, down_parts[0]))
     backward = functools.partial(
         attention_backward, grad_middle, queries, keys, values, attended, normed_one, inputs,
         packed_full, docs_row, table, cosine, sine, small_grad,

time: 583 us -> 567 us (0.973)
  Pallas kernels: 536 us -> 523 us
    pallas_call x2, Pallas kernels: 216 us -> 184 us  [experts(): pl.pallas_call(functools.partial(experts_kernel, mode, dp_count), grid=(s...]
    pallas_call x1, Pallas kernels: 73 us -> 90.3 us  [expert_gather(): pl.pallas_call(functools.partial(expert_gather_kernel, dp_count), out_sha...]
  transfers between devices with their start and end apart: 4 -> 4, of which waited for: 2 -> 0; matrix products, arithmetic and copies ran while one was open for 1% -> 2% of each run, Pallas kernels for 87% -> 87%
where the time goes in v14:
time: 567 us; the launch traced here: 562 us
  Pallas kernels  523 us (92%)
  local copies, waits for them, and re-layouts  18.6 us (3%)
  between operations  14.1 us (2%)
    pallas_call x2, Pallas kernels, experts(): pl.pallas_call(functools.partial(experts_kernel, mode, dp_count), grid=(s...  184 us
    pallas_call x1, Pallas kernels, attention_backward(): pl.pallas_call(functools.partial(attention_backward_kernel, len(sources))...  96.3 us
    pallas_call x1, Pallas kernels, expert_gather(): pl.pallas_call(functools.partial(expert_gather_kernel, dp_count), out_sha...  90.3 us
    pallas_call x1, Pallas kernels, final_reduce(): pl.pallas_call(functools.partial(final_reduce_kernel, len(smalls)), out_s...  48 us
    pallas_call x1, Pallas kernels, small_gather(): pl.pallas_call(functools.partial(small_gather_kernel, dp_count, expert_co...  35 us
    pallas_call x1, Pallas kernels, attention_forward(): pl.pallas_call(functools.partial(attention_forward_kernel, dp_count if li...  33 us
    pallas_call x1, Pallas kernels, combine(): pl.pallas_call(functools.partial(combine_kernel, expert_count, local_coun...  24.1 us
    pallas_call x1, Pallas kernels, dispatch(): pl.pallas_call(functools.partial(dispatch_kernel, local_count), grid=(slo...  11.7 us
  transfers between devices with their start and end apart: 4, of which 0 were waited for; matrix products, arithmetic and copies ran while one was open for 2% of the time, Pallas kernels for 87%

profile of v14, /device:TPU:19, one launch (start us, length us, event | category | flops | bytes accessed | tf_op | source)
XLA Modules:
  0.0 561.9 jit_solution(11982000200140535574)
XLA Ops:
  7.2 0.0 all-gather.3.cloned.1.call-start
  7.2 0.9 copy.37
  8.1 0.8 copy.38
  8.9 0.8 copy.39
  9.7 0.8 copy.40
  10.4 0.8 copy.41
  11.2 1.8 slice_bitcast_fusion
  13.0 1.8 slice_bitcast_fusion.1
  14.8 0.0 copy-done.5
  14.8 1.0 concatenate.3.shard_ref
  15.8 35.0 %small_gather.1 = (bf16[768,3328]{1,0:T(8,128)(2,1)}, s32[1024,128]{1,0:T(8,128)}, s32[8,1024]{1,0:T(8,128)}, f32[1024,128]{1,0:T(8,128)}) custom-call(bf16[96,3328]{1,0:T(8,128)(2,1)} %concatenate.3.shard_ref, s32[2,1024]{1,0:T(2,128)} %bitcast.39, s32[1,1024]{1,0:T(1,128)} %refs_12_.1, bf16[12,1024]{1,0:T(8,128)(2,1)} %bitcast.38), custom_call_target="tpu_custom_call" | custom-call | tf_op jit(solution)/shard_map/small_gather/pallas_call | solution.py:1074
  50.9 0.0 all-gather.3.cloned.1.call-update
  50.9 0.0 all-gather.5.cloned.1.call-start
  50.9 0.7 all-gather.5.cloned.1.call-update
  51.6 0.3 reduce-scatter.3.cloned.1.call-start
  52.0 33.0 %attention_forward.1 = (bf16[1024,768]{1,0:T(8,128)(2,1)}, bf16[1024,768]{1,0:T(8,128)(2,1)}, bf16[1024,768]{1,0:T(8,128)(2,1)}, bf16[1024,768]{1,0:T(8,128)(2,1...) custom-call(bf16[1024,768]{1,0:T(8,128)(2,1)} %bitcast.44, ...), custom_call_target="tpu_custom_call" | custom-call | flops 8053063680 | bytes 18874368 | tf_op jit(solution)/shard_map/attention_forward/pallas_call | solution.py:177
  84.9 11.7 %dispatch.1 = (bf16[2,4,256,768]{3,2,1,0:T(8,128)(2,1)}, bf16[2,4,256,768]{3,2,1,0:T(8,128)(2,1)}) custom-call(s32[8,1024]{1,0:T(8,128)} %get-tuple-element.57.spots_ref, f32[1024,128]{1,0:T(8,128)} %get-tuple-element.61.aux_ref.refs_4_, bf16[1024,768]{1,0:T(8,128)(2,1)} %get-tuple-element.62.normed_ref.refs_5_, bf16[1024,768]{1,0:T(8,128)(2,1)} %bitcast.42), custom_call_target="tpu_custom_call" | custom-call | flops 6442450944 | bytes 9437184 | tf_op jit(solution)/shard_map/dispatch/pallas_call | solution.py:459
  96.6 90.3 %expert_gather.1 = (bf16[4,256,768]{2,1,0:T(8,128)(2,1)}, bf16[4,256,768]{2,1,0:T(8,128)(2,1)}, bf16[2048,768]{1,0:T(8,128)(2,1)}, bf16[768,2048]{1,0:T(8,128)(2,1)}) custom-call(bf16[2,4,256,768]{3,2,1,0:T(8,128)(2,1)} %get-tuple-element.63.rows_ref.refs_5_, bf16[2,4,256,768]{3,2,1,0:T(8,128)(2,1)} %get-tuple-element.64.grads_ref.refs_6_, ...), custom_call_target="tpu_custom_call" | custom-call | tf_op jit(solution)/shard_map/expert_gather/pallas_call | solution.py:990
  186.9 0.0 all-gather.3.cloned.1.call-done.refs_2_
  187.0 82.9 %experts.2 = (bf16[2,768,2048]{2,1,0:T(8,128)(2,1)}, bf16[2048,768]{1,0:T(8,128)(2,1)}, bf16[4,2,256,768]{3,2,1,0:T(8,128)(2,1)}, bf16[4,256,768]{2,1,0:T(8,128)...) custom-call(bf16[4,256,768]{2,1,0:T(8,128)(2,1)} %get-tuple-element.65.refs_0_, ...), custom_call_target="tpu_custom_call" | custom-call | flops 28991029248 | bytes 25165824 | tf_op jit(solution)/shard_map/experts/pallas_call | solution.py:769
  269.9 0.0 reduce-scatter.3.cloned.1.call-update
  269.9 0.0 reduce-scatter.5.cloned.1.call-start
  269.9 0.0 all-gather.5.cloned.1.call-done.refs_4_
  270.0 101.5 %experts.3 = (bf16[2,768,2048]{2,1,0:T(8,128)(2,1)}, bf16[2048,768]{1,0:T(8,128)(2,1)}, bf16[4,2,256,768]{3,2,1,0:T(8,128)(2,1)}, bf16[4,2,256,768]{3,2,1,0:T(8,128)(2,1)}, f32[96,4096]{1,0:T(8,128)}) custom-call(bf16[4,256,768]{2,1,0:T(8,128)(2,1)} %get-tuple-element.70.refs_0_, bf16[4,256,768]{2,1,0:T(8,128)(2,1)} %get-tuple-element.71.refs_1_, ...), custom_call_target="tpu_custom_call" | custom-call | flops 28991029248 | bytes 25165824 | tf_op jit(solution)/shard_map/experts/pallas_call | solution.py:769
  371.5 0.0 reduce-scatter.5.cloned.1.call-update
  371.5 24.1 %combine.1 = (bf16[1024,768]{1,0:T(8,128)(2,1)}, bf16[1024,12]{1,0:T(8,128)(2,1)}, f32[1024,768]{1,0:T(8,128)}, f32[768,128]{1,0:T(8,128)}) custom-call(bf16[4,2,256,768]{3,2,1,0:T(8,128)(2,1)} %get-tuple-element.76.refs_0_, bf16[4,2,256,768]{3,2,1,0:T(8,128)(2,1)} %get-tuple-element.77.refs_1_, s32[1024,128]{1,0:T(8,128)} %get-tuple-element.78.refs_2_, ...), custom_call_target="tpu_custom_call" | custom-call | flops 9663676416 | bytes 17301504 | tf_op jit(solution)/shard_map/combine/pallas_call | solution.py:601
  395.6 1.7 copy.42
  397.3 1.1 convert_element_type.4
  398.3 96.3 %attention_backward.1 = (bf16[1024,768]{1,0:T(8,128)(2,1)}, bf16[768,768]{1,0:T(8,128)(2,1)}, bf16[768,768]{1,0:T(8,128)(2,1)}, bf16[768,768]{1,0:T(8,128)(2,1)}...) custom-call(f32[1024,768]{1,0:T(8,128)} %get-tuple-element.83.refs_0_, ...), custom_call_target="tpu_custom_call" | custom-call | flops 17716740096 | bytes 25165824 | tf_op jit(solution)/shard_map/attention_backward/pallas_call | solution.py:334
  494.7 48.0 %final_reduce.1 = f32[96,3200]{1,0:T(8,128)} custom-call(bf16[8,96,768]{2,1,0:T(8,128)(2,1)} %bitcast.32, bf16[8,96,768]{2,1,0:T(8,128)(2,1)} %bitcast.33, bf16[8,96,768]{2,1,0:T(8,128)(2,1)} %bitcast.34, bf16[8,96,768]{2,1,0:T(8,128)(2,1)} %bitcast.35, bf16[8,96,128]{2,1,0:T(8,128)(2,1)} %bitcast.37), custom_call_target="tpu_custom_call" | custom-call | tf_op jit(solution)/shard_map/final_reduce/pallas_call | solution.py:1411
  542.7 0.0 slice-start
  542.7 2.2 slice.35
  544.9 0.0 copy-done
  544.9 0.7 slice.36
  545.6 0.1 slice.40
  545.7 0.1 slice.41
  545.8 0.0 slice-done
  545.8 0.7 copy.43
  546.5 0.7 copy.44
  547.1 0.6 copy.45
  547.8 0.7 slice_reduce_fusion
  548.5 1.0 bitcast_convert_fusion
  549.5 1.2 pad_maximum_fusion.1
  550.8 0.7 copy-done.2
  551.5 0.5 copy-done.3
  552.0 1.9 pad_maximum_fusion
  553.8 0.1 copy-done.1
  554.0 1.1 copy.47
  (10 shorter events, 0.0 us)
Async XLA Ops:
  7.2 7.6 %copy-start.4 = (bf16[96,2304]{1,0:T(8,128)(2,1)S(1)}, bf16[96,2304]{1,0:T(8,128)(2,1)}, u32[]{:S(2)}) copy-start(bf16[96,2304]{1,0:T(8,128)(2,1)} %param.20) | copy-start | bytes 1327108
  7.2 7.6 %copy-start.5 = (bf16[96,768]{1,0:T(8,128)(2,1)S(1)}, bf16[96,768]{1,0:T(8,128)(2,1)}, u32[]{:S(2)}) copy-start(bf16[96,768]{1,0:T(8,128)(2,1)} %param.21) | copy-start | bytes 442372
  7.2 179.8 %all-gather.3.cloned.1.call-start = ((), (), s32[]{:S(2)}) async-start(), calls=%async_computation.2 | async-start | bytes 3538944 | tf_op jit(solution)/shard_map/all_gather | solution.py:1489
  50.9 219.1 %all-gather.5.cloned.1.call-start = ((), (), s32[]{:S(2)}) async-start(), calls=%async_computation.3 | async-start | bytes 3538944 | tf_op jit(solution)/shard_map/all_gather | solution.py:1489
  51.6 345.6 %reduce-scatter.3.cloned.1.call-start = ((), (), s32[]{:S(2)}) async-start(), calls=%async_computation.4 | async-start | bytes 3538944 | tf_op jit(solution)/shard_map/reduce_scatter | solution.py:1504
  269.9 278.6 %reduce-scatter.5.cloned.1.call-start = ((), (), s32[]{:S(2)}) async-start(), calls=%async_computation.5 | async-start | bytes 3538944 | tf_op jit(solution)/shard_map/reduce_scatter | solution.py:1509
  542.6 2.3 copy-start
  542.7 3.1 slice-start
  549.5 2.0 copy-start.2
  549.5 2.4 copy-start.3
  552.0 2.0 copy-start.1
Sparse Core Ops, SparseCore 0:
  51.0 68.2 all-gather.2
  121.5 78.5 all-gather.4
  270.0 104.9 reduce-scatter.2
  378.5 91.9 reduce-scatter.4

commit v15 on v14

--- a/solution.py
+++ b/solution.py
@@ -522,9 +522,8 @@
         hits = [slots == spots_ref[:, s : s + 1] for s in range(2)]
         chosen = [jnp.where(hit, 1.0, 0.0).astype(jnp.bfloat16) for hit in hits]
         returned = parts[e][:, 0].reshape(count, width)
-        both = nn(jnp.concatenate(chosen, 0), returned)
         for s in range(2):
-            picks[s] = picks[s] + both[s * rows : (s + 1) * rows, :]
+            picks[s] = picks[s] + nn(chosen[s], returned)
         back = back + nn(chosen[0] + chosen[1], parts[e][:, 1].reshape(count, width))
     inner = [total(pick * cot) for pick in picks]
     gates = [aux_ref[:, s : s + 1] for s in range(2)]
@@ -690,6 +689,7 @@
             trades[0].start()
 
         pl.when(step == 2)(lambda: line.turns([0], []))
+        pl.when(step == 3)(lambda: line.turns([], [0]))
 
     @pl.when(step == 0)
     def _():
@@ -721,7 +721,7 @@
                 part.finish()
         if mode == 2:
             trades[1].start()
-            line.turns([1, 2, 3], [0, 1, 2, 3])
+            line.turns([1, 2, 3], [1, 2, 3])
             line.each_plane(line.finish)
             for trade in trades:
                 trade.finish()

time: 567 us -> 566 us (level)
  no operation moved by 1% of the time
where the time goes in v15:
time: 566 us; the launch traced here: 561 us
  Pallas kernels  522 us (92%)
  local copies, waits for them, and re-layouts  18.6 us (3%)
  between operations  14.1 us (2%)
    pallas_call x2, Pallas kernels, experts(): pl.pallas_call(functools.partial(experts_kernel, mode, dp_count), grid=(s...  188 us
    pallas_call x1, Pallas kernels, attention_backward(): pl.pallas_call(functools.partial(attention_backward_kernel, len(sources))...  92.8 us
    pallas_call x1, Pallas kernels, expert_gather(): pl.pallas_call(functools.partial(expert_gather_kernel, dp_count), out_sha...  90.3 us
    pallas_call x1, Pallas kernels, final_reduce(): pl.pallas_call(functools.partial(final_reduce_kernel, len(smalls)), out_s...  49.8 us
    pallas_call x1, Pallas kernels, small_gather(): pl.pallas_call(functools.partial(small_gather_kernel, dp_count, expert_co...  35 us
    pallas_call x1, Pallas kernels, attention_forward(): pl.pallas_call(functools.partial(attention_forward_kernel, dp_count if li...  33 us
    pallas_call x1, Pallas kernels, combine(): pl.pallas_call(functools.partial(combine_kernel, expert_count, local_coun...  21.6 us
    pallas_call x1, Pallas kernels, dispatch(): pl.pallas_call(functools.partial(dispatch_kernel, local_count), grid=(slo...  11.7 us
  transfers between devices with their start and end apart: 4, of which 0 were waited for; matrix products, arithmetic and copies ran while one was open for 2% of the time, Pallas kernels for 87%

profile of v15, /device:TPU:19, one launch (start us, length us, event | category | flops | bytes accessed | tf_op | source)
XLA Modules:
  0.0 560.8 jit_solution(10477463870143758405)
XLA Ops:
  7.2 0.0 copy-start.4
  7.2 0.0 copy-start.5
  7.2 0.0 all-gather.3.cloned.1.call-start
  7.2 0.9 copy.37
  8.1 0.8 copy.38
  8.9 0.8 copy.39
  9.7 0.8 copy.40
  10.4 0.8 copy.41
  11.2 1.8 slice_bitcast_fusion
  13.0 1.8 slice_bitcast_fusion.1
  14.8 0.0 copy-done.5
  14.8 1.0 concatenate.3.shard_ref
  15.8 35.0 %small_gather.1 = (bf16[768,3328]{1,0:T(8,128)(2,1)}, s32[1024,128]{1,0:T(8,128)}, s32[8,1024]{1,0:T(8,128)}, f32[1024,128]{1,0:T(8,128)}) custom-call(bf16[96,3328]{1,0:T(8,128)(2,1)} %concatenate.3.shard_ref, s32[2,1024]{1,0:T(2,128)} %bitcast.39, s32[1,1024]{1,0:T(1,128)} %refs_12_.1, bf16[12,1024]{1,0:T(8,128)(2,1)} %bitcast.38), custom_call_target="tpu_custom_call" | custom-call | tf_op jit(solution)/shard_map/small_gather/pallas_call | solution.py:1074
  50.9 0.0 all-gather.3.cloned.1.call-update
  50.9 0.0 all-gather.5.cloned.1.call-start
  50.9 0.7 all-gather.5.cloned.1.call-update
  51.6 0.3 reduce-scatter.3.cloned.1.call-start
  52.0 33.0 %attention_forward.1 = (bf16[1024,768]{1,0:T(8,128)(2,1)}, bf16[1024,768]{1,0:T(8,128)(2,1)}, bf16[1024,768]{1,0:T(8,128)(2,1)}, bf16[1024,768]{1,0:T(8,128)(2,1...) custom-call(bf16[1024,768]{1,0:T(8,128)(2,1)} %bitcast.44, ...), custom_call_target="tpu_custom_call" | custom-call | flops 8053063680 | bytes 18874368 | tf_op jit(solution)/shard_map/attention_forward/pallas_call | solution.py:177
  84.9 11.7 %dispatch.1 = (bf16[2,4,256,768]{3,2,1,0:T(8,128)(2,1)}, bf16[2,4,256,768]{3,2,1,0:T(8,128)(2,1)}) custom-call(s32[8,1024]{1,0:T(8,128)} %get-tuple-element.57.spots_ref, f32[1024,128]{1,0:T(8,128)} %get-tuple-element.61.aux_ref.refs_4_, bf16[1024,768]{1,0:T(8,128)(2,1)} %get-tuple-element.62.normed_ref.refs_5_, bf16[1024,768]{1,0:T(8,128)(2,1)} %bitcast.42), custom_call_target="tpu_custom_call" | custom-call | flops 6442450944 | bytes 9437184 | tf_op jit(solution)/shard_map/dispatch/pallas_call | solution.py:459
  96.6 90.3 %expert_gather.1 = (bf16[4,256,768]{2,1,0:T(8,128)(2,1)}, bf16[4,256,768]{2,1,0:T(8,128)(2,1)}, bf16[2048,768]{1,0:T(8,128)(2,1)}, bf16[768,2048]{1,0:T(8,128)(2,1)}) custom-call(bf16[2,4,256,768]{3,2,1,0:T(8,128)(2,1)} %get-tuple-element.63.rows_ref.refs_5_, bf16[2,4,256,768]{3,2,1,0:T(8,128)(2,1)} %get-tuple-element.64.grads_ref.refs_6_, ...), custom_call_target="tpu_custom_call" | custom-call | tf_op jit(solution)/shard_map/expert_gather/pallas_call | solution.py:990
  186.9 0.0 all-gather.3.cloned.1.call-done.refs_2_
  187.0 82.9 %experts.2 = (bf16[2,768,2048]{2,1,0:T(8,128)(2,1)}, bf16[2048,768]{1,0:T(8,128)(2,1)}, bf16[4,2,256,768]{3,2,1,0:T(8,128)(2,1)}, bf16[4,256,768]{2,1,0:T(8,128)...) custom-call(bf16[4,256,768]{2,1,0:T(8,128)(2,1)} %get-tuple-element.65.refs_0_, ...), custom_call_target="tpu_custom_call" | custom-call | flops 28991029248 | bytes 25165824 | tf_op jit(solution)/shard_map/experts/pallas_call | solution.py:769
  269.9 0.0 reduce-scatter.3.cloned.1.call-update
  269.9 0.0 reduce-scatter.5.cloned.1.call-start
  269.9 0.0 all-gather.5.cloned.1.call-done.refs_4_
  270.0 104.7 %experts.3 = (bf16[2,768,2048]{2,1,0:T(8,128)(2,1)}, bf16[2048,768]{1,0:T(8,128)(2,1)}, bf16[4,2,256,768]{3,2,1,0:T(8,128)(2,1)}, bf16[4,2,256,768]{3,2,1,0:T(8,128)(2,1)}, f32[96,4096]{1,0:T(8,128)}) custom-call(bf16[4,256,768]{2,1,0:T(8,128)(2,1)} %get-tuple-element.70.refs_0_, bf16[4,256,768]{2,1,0:T(8,128)(2,1)} %get-tuple-element.71.refs_1_, ...), custom_call_target="tpu_custom_call" | custom-call | flops 28991029248 | bytes 25165824 | tf_op jit(solution)/shard_map/experts/pallas_call | solution.py:769
  374.6 0.0 reduce-scatter.5.cloned.1.call-update
  374.7 21.6 %combine.1 = (bf16[1024,768]{1,0:T(8,128)(2,1)}, bf16[1024,12]{1,0:T(8,128)(2,1)}, f32[1024,768]{1,0:T(8,128)}, f32[768,128]{1,0:T(8,128)}) custom-call(bf16[4,2,256,768]{3,2,1,0:T(8,128)(2,1)} %get-tuple-element.76.refs_0_, bf16[4,2,256,768]{3,2,1,0:T(8,128)(2,1)} %get-tuple-element.77.refs_1_, s32[1024,128]{1,0:T(8,128)} %get-tuple-element.78.refs_2_, ...), custom_call_target="tpu_custom_call" | custom-call | flops 9663676416 | bytes 17301504 | tf_op jit(solution)/shard_map/combine/pallas_call | solution.py:600
  396.3 1.7 copy.42
  398.0 1.1 convert_element_type.4
  399.1 92.8 %attention_backward.1 = (bf16[1024,768]{1,0:T(8,128)(2,1)}, bf16[768,768]{1,0:T(8,128)(2,1)}, bf16[768,768]{1,0:T(8,128)(2,1)}, bf16[768,768]{1,0:T(8,128)(2,1)}...) custom-call(f32[1024,768]{1,0:T(8,128)} %get-tuple-element.83.refs_0_, ...), custom_call_target="tpu_custom_call" | custom-call | flops 17716740096 | bytes 25165824 | tf_op jit(solution)/shard_map/attention_backward/pallas_call | solution.py:334
  491.8 49.8 %final_reduce.1 = f32[96,3200]{1,0:T(8,128)} custom-call(bf16[8,96,768]{2,1,0:T(8,128)(2,1)} %bitcast.32, bf16[8,96,768]{2,1,0:T(8,128)(2,1)} %bitcast.33, bf16[8,96,768]{2,1,0:T(8,128)(2,1)} %bitcast.34, bf16[8,96,768]{2,1,0:T(8,128)(2,1)} %bitcast.35, bf16[8,96,128]{2,1,0:T(8,128)(2,1)} %bitcast.37), custom_call_target="tpu_custom_call" | custom-call | tf_op jit(solution)/shard_map/final_reduce/pallas_call | solution.py:1411
  541.6 0.0 slice-start
  541.6 2.2 slice.35
  543.9 0.7 slice.36
  544.6 0.1 slice.40
  544.7 0.1 slice.41
  544.8 0.7 copy.43
  545.4 0.7 copy.44
  546.1 0.6 copy.45
  546.7 0.7 slice_reduce_fusion
  547.4 1.0 bitcast_convert_fusion
  548.5 1.2 pad_maximum_fusion.1
  549.7 0.7 copy-done.2
  550.5 0.5 copy-done.3
  550.9 1.9 pad_maximum_fusion
  552.8 0.1 copy-done.1
  553.0 1.1 copy.47
  (10 shorter events, 0.0 us)
Async XLA Ops:
  7.2 7.6 %copy-start.4 = (bf16[96,2304]{1,0:T(8,128)(2,1)S(1)}, bf16[96,2304]{1,0:T(8,128)(2,1)}, u32[]{:S(2)}) copy-start(bf16[96,2304]{1,0:T(8,128)(2,1)} %param.20) | copy-start | bytes 1327108
  7.2 7.6 %copy-start.5 = (bf16[96,768]{1,0:T(8,128)(2,1)S(1)}, bf16[96,768]{1,0:T(8,128)(2,1)}, u32[]{:S(2)}) copy-start(bf16[96,768]{1,0:T(8,128)(2,1)} %param.21) | copy-start | bytes 442372
  7.2 179.8 %all-gather.3.cloned.1.call-start = ((), (), s32[]{:S(2)}) async-start(), calls=%async_computation.2 | async-start | bytes 3538944 | tf_op jit(solution)/shard_map/all_gather | solution.py:1489
  50.9 219.1 %all-gather.5.cloned.1.call-start = ((), (), s32[]{:S(2)}) async-start(), calls=%async_computation.3 | async-start | bytes 3538944 | tf_op jit(solution)/shard_map/all_gather | solution.py:1489
  51.6 346.4 %reduce-scatter.3.cloned.1.call-start = ((), (), s32[]{:S(2)}) async-start(), calls=%async_computation.4 | async-start | bytes 3538944 | tf_op jit(solution)/shard_map/reduce_scatter | solution.py:1504
  269.9 277.5 %reduce-scatter.5.cloned.1.call-start = ((), (), s32[]{:S(2)}) async-start(), calls=%async_computation.5 | async-start | bytes 3538944 | tf_op jit(solution)/shard_map/reduce_scatter | solution.py:1509
  541.6 2.3 copy-start
  541.6 3.1 slice-start
  548.5 2.0 copy-start.2
  548.5 2.4 copy-start.3
  550.9 2.0 copy-start.1
Sparse Core Ops, SparseCore 0:
  51.0 68.2 all-gather.2
  121.5 78.5 all-gather.4
  270.0 104.9 reduce-scatter.2
  378.5 94.2 reduce-scatter.4

commit v16 on v15

--- a/solution.py
+++ b/solution.py
@@ -966,7 +966,8 @@
 
 
 def expert_gather_kernel(
-    dp_count, rows_ref, grads_ref, down_ref, gate_up_ref, rows_out, grads_out, full_ref, up_ref, *sems
+    dp_count, spots_ref, aux_ref, normed_ref, cot_ref, down_ref, gate_up_ref,
+    rows_ref, grads_ref, rows_out, grads_out, full_ref, up_ref, *sems
 ):
     half = up_ref.shape[1] // 2
     lines = [LineGather(down_ref.at[0], full_ref, dp_count, *sems[:3])]
@@ -976,8 +977,25 @@
         lines.append(LineGather(shard, up_ref, dp_count, *sems[3 * n + 3 : 3 * n + 6], columns))
     trades = [Trade(rows_ref.at[0], rows_out, *sems[9:11]), Trade(grads_ref.at[0], grads_out, *sems[11:13])]
     greet(lines[0].peers() + trades[0].peers())
-    for part in lines + trades:
+    for part in lines:
         part.start()
+    local_count, owner_count, _, width = rows_ref.shape
+    gates = jnp.transpose(aux_ref[...])[0:8, :]
+    for e in range(local_count):
+        for owner in range(0, owner_count, 2):
+            shape = (2 * CAP, normed_ref.shape[0])
+            within = lax.broadcasted_iota(jnp.int32, shape, 0)
+            slots = (owner + within // CAP) * (local_count * CAP) + e * CAP + within % CAP
+            first, second = slots == spots_ref[0:1, :], slots == spots_ref[1:2, :]
+            weights = jnp.where(first, gates[0:1, :], jnp.where(second, gates[1:2, :], 0.0))
+            chosen = jnp.where(first | second, 1.0, 0.0).astype(jnp.bfloat16)
+            picked = nn(chosen, normed_ref[...]).astype(jnp.bfloat16)
+            scaled = (nn(chosen, cot_ref[...]) * jnp.sum(weights, -1, keepdims=True)).astype(jnp.bfloat16)
+            rows_ref[e, owner : owner + 2] = picked.reshape(2, CAP, width)
+            grads_ref[e, owner : owner + 2] = scaled.reshape(2, CAP, width)
+        if e == 0:
+            for part in trades:
+                part.start()
     for hop in range(1, lines[0].outer_count):
         for line in lines:
             line.relay(hop)
@@ -985,22 +1003,29 @@
         part.finish()
 
 
-def expert_gather(rows, grads, down, gate_up, dp_count, collective):
-    anywhere = pl.BlockSpec(memory_space=pl.ANY)
+def expert_gather(spots, aux, normed, cot, down, gate_up, owner_count, dp_count, collective):
+    anywhere, in_vmem = pl.BlockSpec(memory_space=pl.ANY), pl.BlockSpec(memory_space=pltpu.VMEM)
+    local_count, width = down.shape[0], down.shape[2]
+    send = jax.ShapeDtypeStruct((local_count, owner_count, CAP, width), jnp.bfloat16)
+    arrive = jax.ShapeDtypeStruct((owner_count, CAP, width), jnp.bfloat16)
     return pl.pallas_call(
         functools.partial(expert_gather_kernel, dp_count),
         out_shape=[
-            jax.ShapeDtypeStruct(rows.shape[1:], rows.dtype),
-            jax.ShapeDtypeStruct(grads.shape[1:], grads.dtype),
-            jax.ShapeDtypeStruct((dp_count * down.shape[1], down.shape[2]), down.dtype),
+            send,
+            send,
+            arrive,
+            arrive,
+            jax.ShapeDtypeStruct((dp_count * down.shape[1], width), down.dtype),
             jax.ShapeDtypeStruct((dp_count * gate_up.shape[1], gate_up.shape[2] // 2), gate_up.dtype),
         ],
-        in_specs=[anywhere] * 4,
-        out_specs=[anywhere] * 4,
-        scratch_shapes=gather_semaphores(dp_count) * 3 + trade_semaphores(rows.shape[1]) * 2,
-        compiler_params=pltpu.CompilerParams(collective_id=collective, has_side_effects=True),
+        in_specs=[in_vmem] * 4 + [anywhere] * 2,
+        out_specs=[in_vmem] * 2 + [anywhere] * 4,
+        scratch_shapes=gather_semaphores(dp_count) * 3 + trade_semaphores(owner_count) * 2,
+        compiler_params=pltpu.CompilerParams(
+            collective_id=collective, has_side_effects=True, vmem_limit_bytes=60 * 2**20
+        ),
         name="expert_gather",
-    )(rows, grads, down, gate_up)
+    )(spots, aux, normed, cot, down, gate_up)
 
 
 def small_gather_kernel(
@@ -1492,10 +1517,9 @@
     normed_one, queries, keys, values, attended, middle, normed_two, aux = attention_forward(
         inputs, packed_full, docs_row, cosine, sine, table
     )
-    send_rows, send_grads = dispatch(spot_rows, aux, normed_two, cot, owner_count, local_count)
     if own_links:
-        rows_in, grads_in, first_down, first_up = expert_gather(
-            send_rows, send_grads, w_down, w_gate_up, dp_count, 2
+        send_rows, send_grads, rows_in, grads_in, first_down, first_up = expert_gather(
+            spot_rows, aux, normed_two, cot, w_down, w_gate_up, owner_count, dp_count, 2
         )
         grad_gu, grad_down, both, next_rows, next_grads, second_gate_up = experts(
             rows_in, grads_in, first_gate, first_up, first_down, 1, dp_count,
@@ -1509,6 +1533,7 @@
         down_parts.append(lax.psum_scatter(grad_down, "dp", scatter_dimension=0, tiled=True))
         gu_parts = [gu_part]
     else:
+        send_rows, send_grads = dispatch(spot_rows, aux, normed_two, cot, owner_count, local_count)
         exchange = functools.partial(
             lax.all_to_all, axis_name="expert", split_axis=0, concat_axis=0, tiled=True
         )

time: 566 us -> 575 us (1.016)
  Pallas kernels: 522 us -> 531 us
    pallas_call x1 -> x0, Pallas kernels: 11.7 us -> none  [dispatch(): pl.pallas_call(functools.partial(dispatch_kernel, local_count), grid=(slo...]
    pallas_call x1, Pallas kernels: 90.3 us -> 102 us  [expert_gather(): pl.pallas_call(functools.partial(expert_gather_kernel, dp_count), out_sha...]
    pallas_call x2, Pallas kernels: 188 us -> 196 us  [experts(): pl.pallas_call(functools.partial(experts_kernel, mode, dp_count), grid=(s...]
where the time goes in v16:
time: 575 us; the launch traced here: 570 us
  Pallas kernels  531 us (92%)
  local copies, waits for them, and re-layouts  18.6 us (3%)
  between operations  14.1 us (2%)
    pallas_call x2, Pallas kernels, experts(): pl.pallas_call(functools.partial(experts_kernel, mode, dp_count), grid=(s...  196 us
    pallas_call x1, Pallas kernels, expert_gather(): pl.pallas_call(functools.partial(expert_gather_kernel, dp_count), out_sha...  102 us
    pallas_call x1, Pallas kernels, attention_backward(): pl.pallas_call(functools.partial(attention_backward_kernel, len(sources))...  96.4 us
    pallas_call x1, Pallas kernels, final_reduce(): pl.pallas_call(functools.partial(final_reduce_kernel, len(smalls)), out_s...  46.9 us
    pallas_call x1, Pallas kernels, small_gather(): pl.pallas_call(functools.partial(small_gather_kernel, dp_count, expert_co...  35 us
    pallas_call x1, Pallas kernels, attention_forward(): pl.pallas_call(functools.partial(attention_forward_kernel, dp_count if li...  33.3 us
    pallas_call x1, Pallas kernels, combine(): pl.pallas_call(functools.partial(combine_kernel, expert_count, local_coun...  21.6 us
  transfers between devices with their start and end apart: 4, of which 0 were waited for; matrix products, arithmetic and copies ran while one was open for 2% of the time, Pallas kernels for 87%

profile of v16, /device:TPU:19, one launch (start us, length us, event | category | flops | bytes accessed | tf_op | source)
XLA Modules:
  0.0 569.7 jit_solution(7301851398361458606)
XLA Ops:
  7.2 0.0 copy-start.4
  7.2 0.0 copy-start.5
  7.2 0.0 all-gather.3.cloned.1.call-start
  7.2 0.9 copy.37
  8.1 0.8 copy.38
  8.9 0.8 copy.39
  9.7 0.8 copy.40
  10.4 0.8 copy.41
  11.2 1.8 slice_bitcast_fusion
  13.0 1.8 slice_bitcast_fusion.1
  14.8 1.0 concatenate.3.shard_ref
  15.8 35.0 %small_gather.1 = (bf16[768,3328]{1,0:T(8,128)(2,1)}, s32[1024,128]{1,0:T(8,128)}, s32[8,1024]{1,0:T(8,128)}, f32[1024,128]{1,0:T(8,128)}) custom-call(bf16[96,3328]{1,0:T(8,128)(2,1)} %concatenate.3.shard_ref, s32[2,1024]{1,0:T(2,128)} %bitcast.41, s32[1,1024]{1,0:T(1,128)} %refs_12_.1, bf16[12,1024]{1,0:T(8,128)(2,1)} %bitcast.40), custom_call_target="tpu_custom_call" | custom-call | tf_op jit(solution)/shard_map/small_gather/pallas_call | solution.py:1099
  50.9 0.0 all-gather.3.cloned.1.call-update
  50.9 0.0 all-gather.5.cloned.1.call-start
  50.9 0.7 all-gather.5.cloned.1.call-update
  51.7 0.3 reduce-scatter.3.cloned.1.call-start
  52.0 33.3 %attention_forward.1 = (bf16[1024,768]{1,0:T(8,128)(2,1)}, bf16[1024,768]{1,0:T(8,128)(2,1)}, bf16[1024,768]{1,0:T(8,128)(2,1)}, bf16[1024,768]{1,0:T(8,128)(2,1...) custom-call(bf16[1024,768]{1,0:T(8,128)(2,1)} %bitcast.44, ...), custom_call_target="tpu_custom_call" | custom-call | flops 8053063680 | bytes 18874368 | tf_op jit(solution)/shard_map/attention_forward/pallas_call | solution.py:177
  85.3 101.8 %expert_gather.1 = (bf16[2,4,256,768]{3,2,1,0:T(8,128)(2,1)}, bf16[2,4,256,768]{3,2,1,0:T(8,128)(2,1)}, bf16[4,256,768]{2,1,0:T(8,128)(2,1)}, bf16[4,256,768]{2,...) custom-call(s32[8,1024]{1,0:T(8,128)} %get-tuple-element.57.spots_ref, ...), custom_call_target="tpu_custom_call" | custom-call | tf_op jit(solution)/shard_map/expert_gather/pallas_call | solution.py:1011
  187.0 0.0 all-gather.3.cloned.1.call-done.refs_2_
  187.1 88.5 %experts.2 = (bf16[2,768,2048]{2,1,0:T(8,128)(2,1)}, bf16[2048,768]{1,0:T(8,128)(2,1)}, bf16[4,2,256,768]{3,2,1,0:T(8,128)(2,1)}, bf16[4,256,768]{2,1,0:T(8,128)...) custom-call(bf16[4,256,768]{2,1,0:T(8,128)(2,1)} %get-tuple-element.63.refs_0_, ...), custom_call_target="tpu_custom_call" | custom-call | flops 28991029248 | bytes 25165824 | tf_op jit(solution)/shard_map/experts/pallas_call | solution.py:769
  275.6 0.0 reduce-scatter.3.cloned.1.call-update
  275.6 0.0 reduce-scatter.5.cloned.1.call-start
  275.7 0.0 all-gather.5.cloned.1.call-done.refs_4_
  275.7 107.0 %experts.3 = (bf16[2,768,2048]{2,1,0:T(8,128)(2,1)}, bf16[2048,768]{1,0:T(8,128)(2,1)}, bf16[4,2,256,768]{3,2,1,0:T(8,128)(2,1)}, bf16[4,2,256,768]{3,2,1,0:T(8,128)(2,1)}, f32[96,4096]{1,0:T(8,128)}) custom-call(bf16[4,256,768]{2,1,0:T(8,128)(2,1)} %get-tuple-element.70.refs_0_, bf16[4,256,768]{2,1,0:T(8,128)(2,1)} %get-tuple-element.71.refs_1_, ...), custom_call_target="tpu_custom_call" | custom-call | flops 28991029248 | bytes 25165824 | tf_op jit(solution)/shard_map/experts/pallas_call | solution.py:769
  382.7 0.0 reduce-scatter.5.cloned.1.call-update
  382.7 21.6 %combine.1 = (bf16[1024,768]{1,0:T(8,128)(2,1)}, bf16[1024,12]{1,0:T(8,128)(2,1)}, f32[1024,768]{1,0:T(8,128)}, f32[768,128]{1,0:T(8,128)}) custom-call(bf16[4,2,256,768]{3,2,1,0:T(8,128)(2,1)} %get-tuple-element.76.refs_0_, bf16[4,2,256,768]{3,2,1,0:T(8,128)(2,1)} %get-tuple-element.77.refs_1_, s32[1024,128]{1,0:T(8,128)} %get-tuple-element.78.refs_2_, ...), custom_call_target="tpu_custom_call" | custom-call | flops 9663676416 | bytes 17301504 | tf_op jit(solution)/shard_map/combine/pallas_call | solution.py:600
  404.4 1.7 copy.42
  406.1 1.1 convert_element_type.4
  407.2 96.4 %attention_backward.1 = (bf16[1024,768]{1,0:T(8,128)(2,1)}, bf16[768,768]{1,0:T(8,128)(2,1)}, bf16[768,768]{1,0:T(8,128)(2,1)}, bf16[768,768]{1,0:T(8,128)(2,1)}...) custom-call(f32[1024,768]{1,0:T(8,128)} %get-tuple-element.83.refs_0_, ...), custom_call_target="tpu_custom_call" | custom-call | flops 17716740096 | bytes 25165824 | tf_op jit(solution)/shard_map/attention_backward/pallas_call | solution.py:334
  503.6 46.9 %final_reduce.1 = f32[96,3200]{1,0:T(8,128)} custom-call(bf16[8,96,768]{2,1,0:T(8,128)(2,1)} %bitcast.34, bf16[8,96,768]{2,1,0:T(8,128)(2,1)} %bitcast.35, bf16[8,96,768]{2,1,0:T(8,128)(2,1)} %bitcast.36, bf16[8,96,768]{2,1,0:T(8,128)(2,1)} %bitcast.37, bf16[8,96,128]{2,1,0:T(8,128)(2,1)} %bitcast.39), custom_call_target="tpu_custom_call" | custom-call | tf_op jit(solution)/shard_map/final_reduce/pallas_call | solution.py:1436
  550.5 0.0 slice-start
  550.5 2.2 slice.35
  552.8 0.7 slice.36
  553.5 0.1 slice.40
  553.6 0.1 slice.41
  553.7 0.7 copy.43
  554.4 0.7 copy.44
  555.0 0.6 copy.45
  555.6 0.7 slice_reduce_fusion
  556.3 1.0 bitcast_convert_fusion
  557.4 0.0 copy-start.2
  557.4 0.0 copy-start.3
  557.4 1.2 pad_maximum_fusion.1
  558.7 0.7 copy-done.2
  559.4 0.5 copy-done.3
  559.8 1.9 pad_maximum_fusion
  561.7 0.1 copy-done.1
  561.9 1.1 copy.47
  (9 shorter events, 0.0 us)
Async XLA Ops:
  7.2 7.6 %copy-start.4 = (bf16[96,2304]{1,0:T(8,128)(2,1)S(1)}, bf16[96,2304]{1,0:T(8,128)(2,1)}, u32[]{:S(2)}) copy-start(bf16[96,2304]{1,0:T(8,128)(2,1)} %param.20) | copy-start | bytes 1327108
  7.2 7.6 %copy-start.5 = (bf16[96,768]{1,0:T(8,128)(2,1)S(1)}, bf16[96,768]{1,0:T(8,128)(2,1)}, u32[]{:S(2)}) copy-start(bf16[96,768]{1,0:T(8,128)(2,1)} %param.21) | copy-start | bytes 442372
  7.2 179.8 %all-gather.3.cloned.1.call-start = ((), (), s32[]{:S(2)}) async-start(), calls=%async_computation.2 | async-start | bytes 3538944 | tf_op jit(solution)/shard_map/all_gather | solution.py:1514
  50.9 224.8 %all-gather.5.cloned.1.call-start = ((), (), s32[]{:S(2)}) async-start(), calls=%async_computation.3 | async-start | bytes 3538944 | tf_op jit(solution)/shard_map/all_gather | solution.py:1514
  51.7 354.4 %reduce-scatter.3.cloned.1.call-start = ((), (), s32[]{:S(2)}) async-start(), calls=%async_computation.4 | async-start | bytes 3538944 | tf_op jit(solution)/shard_map/reduce_scatter | solution.py:1528
  275.6 280.7 %reduce-scatter.5.cloned.1.call-start = ((), (), s32[]{:S(2)}) async-start(), calls=%async_computation.5 | async-start | bytes 3538944 | tf_op jit(solution)/shard_map/reduce_scatter | solution.py:1533
  550.5 2.3 copy-start
  550.5 3.1 slice-start
  557.4 2.0 copy-start.2
  557.4 2.4 copy-start.3
  559.8 2.0 copy-start.1
Sparse Core Ops, SparseCore 0:
  51.0 74.8 all-gather.2
  128.1 81.2 all-gather.4
  275.7 107.1 reduce-scatter.2
  386.3 94.7 reduce-scatter.4
